TPU v7x, 32 devices: a whole 2x2x4 slice. The times are simulated.
32 devices in a mesh: group: 2 (over x), space: 16 (over z, y, core).
Axes of the slice: x: 2, y: 2, z: 4, core: 2. Of those that a mesh axis runs over, the one named last changes fastest.
Arguments:
- columns_in: bfloat16 [8192, 1024], P(('group', 'space')), parts along dimension 0, may hold values from -6 to 6
- cotangent: bfloat16 [8192, 1024], P(('group', 'space')), parts along dimension 0, may hold values from -6 to 6
- conv_weight: bfloat16 [7, 16, 16], replicated, may hold values from -0.5 to 0.5
- mix_weight: bfloat16 [1024, 1024], replicated, may hold values from -0.1875 to 0.1875
- neighbours: int32 [4096, 7], P('space'), may hold values from 0 to 4095, as said below
- rotations: int32 [4096], P('space'), may hold values from 0 to 5
- pentagons: int32 [4096], P('space'), may hold values 0 or 1
Outputs:
- grad_input: bfloat16 [8192, 1024], P(('group', 'space')), parts along dimension 0
- grad_mix: float32 [1024, 2048], P('space', 'group'), parts along dimension 1
- grad_conv: float32 [14, 16, 16], P('group'), parts along dimension 0
There are 2 independent parts, one for each index of `group`. A program takes and returns all parts, laid end to end along the dimension named above; an argument that names none is the same for every part. Nothing has to cross between parts.
Inputs may be any that keep to these rules, and one draw needn't show every extreme that they name: `neighbours`: entry 0 of each row is the column itself. Every other entry lies in the column's own grid row of 256 consecutive column indices or in the row just before or after it, the last row of the grid followed by the first. The relation is symmetric: if b is a neighbour of a, then a is a neighbour of b.
All inputs are finite; a program needn't handle non-finite values. No bound on the sum of `pentagons` on one device may be relied on, other than what follows from the above.
Results may differ from a plain program's by a relative error of at most 0.005.
Values may be sent and summed in bfloat16 or wider, within the bound.
No kernel may reach another device: no remote copies, remote signals or barrier semaphores. Data moves between devices by JAX's collectives and lax.ppermute only.
A program may use at most 128 MiB of HBM per device.

v0:
```python
import functools

import jax
import jax.numpy as jnp
from jax import lax
from jax.experimental import pallas as pl
from jax.experimental.pallas import tpu as pltpu
from jax.sharding import PartitionSpec as P


ROW = 256
WIDE = 256
TANH_SCALE = 0.7978845608028654
TANH_CUBE = 0.044715


f32 = jnp.float32
bf16 = jnp.bfloat16


def mm(a, b):
    return jnp.dot(a, b, preferred_element_type=f32)


def contract(a, b, dim_a, dim_b, **kw):
    return lax.dot_general(
        a, b, (((dim_a,), (dim_b,)), ((), ())), preferred_element_type=f32, **kw
    )


def iota(shape, dim):
    return lax.broadcasted_iota(jnp.int32, shape, dim)


def onehot(cond):
    return jnp.where(cond, 1.0, 0.0).astype(bf16)


def call(body, outs, cost, *args, scratch=(), scalars=0, far=()):
    space = lambda k: pltpu.SMEM if k < scalars else pltpu.HBM if k in far else pltpu.VMEM
    return pl.pallas_call(
        body,
        out_shape=[jax.ShapeDtypeStruct(s, d) for s, d in outs],
        in_specs=[pl.BlockSpec(memory_space=space(k)) for k in range(len(args))],
        out_specs=[pl.BlockSpec(memory_space=pltpu.VMEM)] * len(outs),
        scratch_shapes=list(scratch),
        cost_estimate=pl.CostEstimate(flops=cost, transcendentals=0, bytes_accessed=8 << 20),
        compiler_params=pltpu.CompilerParams(vmem_limit_bytes=12 << 20),
    )(*args)


def picked(local_t, turns, tap):
    turn = tap - 1 - turns
    slot = 1 + jnp.where(turn < 0, turn + 6, turn)
    source = jnp.full_like(slot, -1)
    for k in range(1, 7):
        source = jnp.where(slot == k, local_t[k : k + 1, :], source)
    return source


def early_kernel(
    place, near, turns, void, x_hbm, cot_hbm, conv_hbm, mix_hbm, up, halo_sel, back_sel, own, pre, wk, wkt, x, cot, conv, mix, sems
):
    copies = [
        pltpu.make_async_copy(src, dst, sems.at[k])
        for k, (src, dst) in enumerate(((conv_hbm, conv), (x_hbm, x), (cot_hbm, cot), (mix_hbm, mix)))
    ]
    for copy in copies:
        copy.start()
    n = x.shape[0]
    taps, c = conv.shape[:2]
    offset, total = place[0], place[1]
    moved = near[...] - offset + ROW
    moved = jnp.where(moved < 0, moved + total, moved)
    moved = jnp.where(moved >= total, moved - total, moved)
    dropped = (void[...] == 1) & (iota((taps, n), 0) == 6)
    local_t = jnp.where(dropped, -1, moved)
    sources = [picked(local_t, turns[...], tap) for tap in range(1, taps)]
    sources_t = jnp.concatenate(sources + [sources[0]] * (8 - len(sources)), axis=0)
    eye = jnp.where(iota((n, n), 0) == iota((n, n), 1), 1.0, 0.0)
    columns = contract(eye, sources_t.astype(f32), 1, 1, precision=lax.Precision.HIGHEST)
    columns = columns.astype(jnp.int32)

    copies[0].wait()
    repeat = onehot(iota((c, WIDE), 1) % c == iota((c, WIDE), 0))
    down = onehot(iota((WIDE, c), 0) % c == iota((WIDE, c), 1))
    same = iota((WIDE, WIDE), 0) // c == iota((WIDE, WIDE), 1) // c
    for tap in range(taps):
        for dim, out in ((1, wk), (0, wkt)):
            wide = contract(conv[tap], repeat, dim, 0).astype(bf16)
            out[tap * WIDE : (tap + 1) * WIDE, :] = jnp.where(same, mm(down, wide), 0.0).astype(bf16)
    copies[1].wait()
    for tap in range(1, taps):
        at = (tap - 1) * n
        source = columns[:, tap - 1 : tap]
        halo_sel[at : at + n, :ROW] = onehot(iota((n, ROW), 1) == source)
        halo_sel[at : at + n, ROW:] = onehot(iota((n, ROW), 1) + (ROW + n) == source)
        mine = onehot(iota((n, n), 1) + ROW == source)
        own[at : at + n, :] = mm(mine, x[...]).astype(bf16)
        back_sel[:, at : at + n] = onehot(iota((n + 2 * ROW, n), 0) == sources[tap - 1])
    for c in range(0, x.shape[1], WIDE):
        acc = mm(x[:, c : c + WIDE], wk[:WIDE, :])
        for tap in range(1, taps):
            acc += mm(own[(tap - 1) * n : tap * n, c : c + WIDE], wk[tap * WIDE : (tap + 1) * WIDE, :])
        pre[:, c : c + WIDE] = acc
    copies[2].wait()
    copies[3].wait()
    up[...] = contract(cot[...], mix[...], 1, 1)


def gelu_tanh(v):
    return jnp.tanh(TANH_SCALE * (v + TANH_CUBE * (v * v * v)))


def mix_rows(act_t, cot, bit, blocks, share):
    rows = [
        act_t[pl.ds(pl.multiple_of((2 * k + bit) * share, share), share), :] for k in range(blocks // 2)
    ]
    return mm(jnp.concatenate(rows, axis=0), cot[...])


def forward_kernel(blocks, me, low, high, halo_sel, pre_own, wk, cot, halo, pre, act_t, send):
    n, width = pre.shape
    taps = wk.shape[0] // WIDE
    for c in range(0, width, WIDE):
        both = jnp.concatenate([low[:, c : c + WIDE], high[:, c : c + WIDE]], axis=0)
        rows = mm(halo_sel[...], both).astype(bf16)
        halo[:, c : c + WIDE] = rows
        acc = pre_own[:, c : c + WIDE]
        for tap in range(1, taps):
            acc += mm(rows[(tap - 1) * n : tap * n], wk[tap * WIDE : (tap + 1) * WIDE, :])
        pre[:, c : c + WIDE] = acc
        active = (0.5 * acc) * (1.0 + gelu_tanh(acc))
        act_t[c : c + WIDE, :] = active.T.astype(bf16)
    share = width // blocks
    send[...] = mix_rows(act_t, cot, 1 - me[0], blocks, share).astype(bf16)


def keep_kernel(blocks, me, act_t, cot, keep):
    keep[...] = mix_rows(act_t, cot, me[0], blocks, act_t.shape[0] // blocks)


def merge_kernel(blocks, me, keep, got, send_a, keep_a, send_b, keep_b):
    share = keep.shape[0] * 2 // blocks
    half = keep.shape[1] // 2
    for first, send, kept in ((0, send_a, keep_a), (1, send_b, keep_b)):
        bit = me[1 + first]
        cols = slice(first * half, (first + 1) * half)
        for q in range(blocks // 4):
            base = (q >> first) * (2 << first) + (q & first)
            for value, out in ((1 - bit, send), (bit, kept)):
                at = pl.ds(pl.multiple_of((base + (value << first)) * share, share), share)
                out[q * share : (q + 1) * share, :] = (keep[at, cols] + got[at, cols].astype(f32)).astype(out.dtype)


def backward_kernel(channels, scale, up, pre, x, own, halo, wkt, back_sel, grad, terms, low, high, conv):
    n, width = pre.shape
    taps = wkt.shape[0] // WIDE
    acc = [jnp.zeros((WIDE, WIDE), f32) for _ in range(taps)]
    for c in range(0, width, WIDE):
        v = pre[:, c : c + WIDE]
        t = gelu_tanh(v)
        slope = 0.5 * (1.0 + t) + (0.5 * TANH_SCALE) * v * (1.0 - t * t) * (1.0 + (3 * TANH_CUBE) * (v * v))
        g32 = up[:, c : c + WIDE] * slope
        g = g32.astype(bf16)
        grad[:, c : c + WIDE] = g
        g_t = g32.T.astype(bf16)
        for tap in range(taps):
            if tap == 0:
                rows = x[:, c : c + WIDE]
            else:
                rows = own[(tap - 1) * n : tap * n, c : c + WIDE] + halo[(tap - 1) * n : tap * n, c : c + WIDE]
                terms[(tap - 1) * n : tap * n, c : c + WIDE] = mm(
                    g, wkt[tap * WIDE : (tap + 1) * WIDE, :]
                ).astype(bf16)
            acc[tap] += mm(g_t, rows)
        low[:, c : c + WIDE] = mm(back_sel[:ROW, :], terms[:, c : c + WIDE]).astype(bf16)
        high[:, c : c + WIDE] = mm(back_sel[ROW + n :, :], terms[:, c : c + WIDE]).astype(bf16)
    same = iota((WIDE, WIDE), 0) // channels == iota((WIDE, WIDE), 1) // channels
    fold = jnp.where(iota((WIDE, channels), 0) % channels == iota((WIDE, channels), 1), 1.0, 0.0)
    for tap in range(taps):
        block = jnp.where(same, acc[tap], 0.0)
        block = jnp.sum(block.reshape(WIDE // channels, channels, WIDE), axis=0)
        conv[:, tap * channels : (tap + 1) * channels] = (
            contract(block, fold, 1, 0, precision=lax.Precision.HIGHEST) * scale
        )


def inner_kernel(grad, terms, wkt, back_sel, cot, inner):
    n, width = grad.shape
    for c in range(0, width, WIDE):
        acc = mm(grad[:, c : c + WIDE], wkt[:WIDE, :]) + cot[:, c : c + WIDE].astype(f32)
        inner[:, c : c + WIDE] = acc + mm(back_sel[ROW : ROW + n, :], terms[:, c : c + WIDE])


def shards(columns_in, cotangent, conv_weight, mix_weight, neighbours, rotations, pentagons):
    n, width = columns_in.shape
    taps, channels = conv_weight.shape[:2]
    devices = lax.axis_size("space")
    place = lax.axis_index("space").astype(jnp.int32)
    total_cols = n * devices
    levels = width // channels
    bits = devices.bit_length() - 1

    def ring(value, by):
        return lax.ppermute(value, "space", [(i, (i + by) % devices) for i in range(devices)])

    def swap(value, bit):
        return lax.ppermute(value, "space", [(i, i ^ (1 << bit)) for i in range(devices)])

    below = ring(columns_in, 1)
    above = ring(columns_in, -1)
    pairs = (taps - 1) * n
    up, halo_sel, back_sel, own, pre_own, wk, wkt = call(
        early_kernel,
        [
            ((n, width), f32),
            ((pairs, 2 * ROW), bf16),
            ((n + 2 * ROW, pairs), bf16),
            ((pairs, width), bf16),
            ((n, width), f32),
            ((taps * WIDE, WIDE), bf16),
            ((taps * WIDE, WIDE), bf16),
        ],
        3 << 30,
        jnp.stack([place * n, jnp.int32(total_cols)]),
        neighbours.T,
        rotations[None, :],
        pentagons[None, :],
        columns_in,
        cotangent,
        conv_weight,
        mix_weight,
        scalars=1,
        far=(4, 5, 6, 7),
        scratch=[
            pltpu.VMEM(columns_in.shape, bf16),
            pltpu.VMEM(cotangent.shape, bf16),
            pltpu.VMEM(conv_weight.shape, bf16),
            pltpu.VMEM(mix_weight.shape, bf16),
            pltpu.SemaphoreType.DMA((4,)),
        ],
    )
    mine = jnp.stack([(place >> b) & 1 for b in range(3)])
    halo, pre, act_t, send = call(
        functools.partial(forward_kernel, devices),
        [
            ((pairs, width), bf16),
            ((n, width), f32),
            ((width, n), bf16),
            ((width // 2, width), bf16),
        ],
        3 << 30,
        mine,
        below,
        above,
        halo_sel,
        pre_own,
        wk,
        cotangent,
        scalars=1,
    )
    got = swap(send, 0)
    (keep,) = call(
        functools.partial(keep_kernel, devices),
        [((width // 2, width), f32)],
        1 << 29,
        mine,
        act_t,
        cotangent,
        scalars=1,
    )
    half = width // 2
    merged = call(
        functools.partial(merge_kernel, devices),
        [((width // 4, half), bf16), ((width // 4, half), f32)] * 2,
        1 << 20,
        mine,
        keep,
        got,
        scalars=1,
    )
    grad, terms, to_low, to_high, conv = call(
        functools.partial(backward_kernel, channels, 1.0 / float(total_cols * levels) ** 0.5),
        [
            ((n, width), bf16),
            ((pairs, width), bf16),
            ((ROW, width), bf16),
            ((ROW, width), bf16),
            ((channels, taps * channels), f32),
        ],
        4 << 30,
        up,
        pre,
        columns_in,
        own,
        halo,
        wkt,
        back_sel,
    )
    share = width // devices
    parts = []
    for first in (0, 1):
        order = list(range(1, bits))
        if first:
            order[0], order[1] = order[1], order[0]
        got = swap(merged[2 * first], order[0])
        left = [b for b in range(bits - 1, 0, -1) if b != order[0]]
        parts.append([merged[2 * first + 1], got, left, order])
    for stage in range(2, bits):
        for k, (kept, got, left, order) in enumerate(parts):
            bit = order[stage - 1]
            axis = left.index(bit)
            at = (place >> bit) & 1
            value = (kept + got.astype(f32)).reshape((2,) * len(left) + (share, half))
            sent = lax.dynamic_index_in_dim(value, 1 - at, axis, keepdims=False)
            kept = lax.dynamic_index_in_dim(value, at, axis, keepdims=False)
            flat = (share << (len(left) - 1), half)
            got = swap(sent.astype(bf16).reshape(flat), bit)
            parts[k] = [kept.reshape(flat), got, [b for b in left if b != bit], order]
    grad_mix = jnp.concatenate([p[0] + p[1].astype(f32) for p in parts], axis=1)
    grad_mix = grad_mix / jnp.sqrt(f32(total_cols))

    from_below = ring(to_high, 1)
    from_above = ring(to_low, -1)
    for bit in range(bits):
        conv = conv + swap(conv, bit)
    grad_conv = conv.reshape(channels, taps, channels).transpose(1, 2, 0)
    (inner,) = call(
        inner_kernel, [((n, width), f32)], 1 << 30, grad, terms, wkt, back_sel, cotangent
    )
    grad_input = (inner + from_below.astype(f32) + from_above.astype(f32)).astype(bf16)
    return grad_input, grad_mix, grad_conv


def solution(mesh):
    return jax.shard_map(
        shards,
        mesh=mesh,
        in_specs=(
            P(("group", "space"), None),
            P(("group", "space"), None),
            P(),
            P(),
            P("space", None),
            P("space"),
            P("space"),
        ),
        out_specs=(P(("group", "space"), None), P("space", "group"), P("group", None, None)),
        check_vma=False,
    )
```

profile of v0, /device:TPU:0, one launch (start us, length us, event | category | flops | bytes accessed | tf_op | source)
XLA Modules:
  0.0 81.8 jit_solution(4372288927529863031)
XLA Ops:
  1.2 5.0 %collective-permute-start.1 = (bf16[256,1024]{1,0:T(8,128)(2,1)}, bf16[256,1024]{1,0:T(8,128)(2,1)S(1)}, u32[]{:S(2)}, u32[]{:S(2)}) collective-permute-start(bf16[256,1024]{1,0:T(8,128)(2,1)} %x.1), channel_id=1, source_target_pairs={{0,15},{1,0},{2,1},{3,2},{4,3},{5,4},{6,5},{7,6},{8,7},{9,8},{10,9... | collective-permute-start | bytes 1572872 | tf_op jit(solution)/shard_map/ppermute | solution.py:206
  6.4 1.0 %copy-done.4 = bf16[256,1024]{1,0:T(8,128)(2,1)S(1)} copy-done((bf16[256,1024]{1,0:T(8,128)(2,1)S(1)}, bf16[256,1024]{1,0:T(8,128)(2,1)}, u32[]{:S(2)}) %copy-start.4) | copy-done | bytes 524312
  7.4 1.6 %copy-done.9 = bf16[1024,1024]{1,0:T(8,128)(2,1)S(1)} copy-done((bf16[1024,1024]{1,0:T(8,128)(2,1)S(1)}, bf16[1024,1024]{1,0:T(8,128)(2,1)}, u32[]{:S(2)}) %copy-start.9) | copy-done | bytes 2097176
  9.0 1.0 %copy-done.10 = bf16[256,1024]{1,0:T(8,128)(2,1)S(1)} copy-done((bf16[256,1024]{1,0:T(8,128)(2,1)S(1)}, bf16[256,1024]{1,0:T(8,128)(2,1)}, u32[]{:S(2)}) %copy-start.10) | copy-done | bytes 524312
  10.1 0.7 copy-done.12
  12.9 7.1 %shard_map.94 = (f32[256,1024]{1,0:T(8,128)S(1)}, bf16[1536,512]{1,0:T(8,128)(2,1)S(1)}, bf16[768,1536]{1,0:T(8,128)(2,1)S(1)}, bf16[1536,1024]{1,0:T(8,128)(2,1...) custom-call(s32[2]{0:T(128)S(1)} %pad_add_fusion.place, ...), custom_call_target="tpu_custom_call" | custom-call | flops 3221225472 | bytes 8388608 | tf_op jit(solution)/shard_map/pallas_call | solution.py:41
  20.0 6.0 %shard_map.95 = (bf16[1536,1024]{1,0:T(8,128)(2,1)S(1)}, f32[256,1024]{1,0:T(8,128)S(1)}, bf16[1024,256]{1,0:T(8,128)(2,1)S(1)}, bf16[512,1024]{1,0:T(8,128)(2,1)}) custom-call(s32[3]{0:T(128)S(1)} %pad_add_fusion.1.me, bf16[256,1024]{1,0:T(8,128)(2,1)S(1)} %collective-permute-done.low, bf16[256,1024]{1,0:T(8,128)(2,1)S(1)} %collective-permute-done.1.high, ...), custom_call_target="tpu_custom_call" | custom-call | flops 3221225472 | bytes 8388608 | tf_op jit(solution)/shard_map/pallas_call | solution.py:41
  26.0 0.8 copy-done.7
  26.8 4.9 %shard_map.96 = (bf16[256,1024]{1,0:T(8,128)(2,1)S(1)}, bf16[1536,1024]{1,0:T(8,128)(2,1)S(1)}, bf16[256,1024]{1,0:T(8,128)(2,1)}, bf16[256,1024]{1,0:T(8,128)(2,1)}, f32[16,112]{1,0:T(8,128)S(1)}) custom-call(f32[256,1024]{1,0:T(8,128)S(1)} %get-tuple-element.23.up, f32[256,1024]{1,0:T(8,128)S(1)} %get-tuple-element.27.pre, ...), custom_call_target="tpu_custom_call" | custom-call | flops 4294967296 | bytes 8388608 | tf_op jit(solution)/shard_map/pallas_call | solution.py:41
  31.7 1.6 %copy-done = bf16[1536,1024]{1,0:T(8,128)(2,1)} copy-done((bf16[1536,1024]{1,0:T(8,128)(2,1)}, bf16[1536,1024]{1,0:T(8,128)(2,1)S(1)}, u32[]{:S(2)}) %copy-start) | copy-done | bytes 3145752
  33.9 3.9 %collective-permute-start.3 = (bf16[256,1024]{1,0:T(8,128)(2,1)}, bf16[256,1024]{1,0:T(8,128)(2,1)}, u32[]{:S(2)}, u32[]{:S(2)}) collective-permute-start(bf16[256,1024]{1,0:T(8,128)(2,1)} %get-tuple-element.35), channel_id=1, source_target_pairs={{0,15},{1,0},{2,1},{3,2},{4,3},{5,4},{6,5},{7,6},{8,7},{9,8},{10,9... | collective-permute-start | bytes 1572872 | tf_op jit(solution)/shard_map/ppermute | solution.py:206
  37.8 1.2 %collective-permute-done.11 = f32[16,112]{1,0:T(8,128)S(1)} collective-permute-done((f32[16,112]{1,0:T(8,128)S(1)}, f32[16,112]{1,0:T(8,128)S(1)}, u32[]{:S(2)}, u32[]{:S(2)}) %collective-permute-start.11) | collective-permute-done | bytes 7200 | tf_op jit(solution)/shard_map/ppermute | solution.py:209
  39.0 9.7 %collective-permute-done.12 = f32[16,112]{1,0:T(8,128)S(1)} collective-permute-done((f32[16,112]{1,0:T(8,128)S(1)}, f32[16,112]{1,0:T(8,128)S(1)}, u32[]{:S(2)}, u32[]{:S(2)}) %collective-permute-start.12) | collective-permute-done | bytes 7200 | tf_op jit(solution)/shard_map/ppermute | solution.py:209
  49.1 1.9 %copy-done.1 = bf16[1536,1024]{1,0:T(8,128)(2,1)S(1)} copy-done((bf16[1536,1024]{1,0:T(8,128)(2,1)S(1)}, bf16[1536,1024]{1,0:T(8,128)(2,1)}, u32[]{:S(2)}) %copy-start.1) | copy-done | bytes 3145752
  50.9 1.7 %copy-done.3 = bf16[768,1536]{1,0:T(8,128)(2,1)S(1)} copy-done((bf16[768,1536]{1,0:T(8,128)(2,1)S(1)}, bf16[768,1536]{1,0:T(8,128)(2,1)}, u32[]{:S(2)}) %copy-start.3) | copy-done | bytes 2359320
  52.6 1.1 %shard_map.97 = f32[256,1024]{1,0:T(8,128)S(1)} custom-call(bf16[256,1024]{1,0:T(8,128)(2,1)S(1)} %get-tuple-element.32.grad, bf16[1536,1024]{1,0:T(8,128)(2,1)S(1)} %copy-done.1, bf16[1792,256]{1,0:T(8,128)(2,1)S(1)} %get-tuple-element.30.wkt, bf16[768,1536]{1,0:T(8,128)(2,1)S(1)} %copy-done.3, bf16[256,1024]{1,0:T(8,128)(2,1)S(1)} %copy-done.5), custom_call_target="tpu_custom_call" | custom-call | flops 1073741824 | bytes 8388608 | tf_op jit(solution)/shard_map/pallas_call | solution.py:41
  53.8 2.6 %collective-permute-start.14 = (f32[16,112]{1,0:T(8,128)S(1)}, f32[16,112]{1,0:T(8,128)S(1)}, u32[]{:S(2)}, u32[]{:S(2)}) collective-permute-start(f32[16,112]{1,0:T(8,128)S(1)} %add.77), channel_id=1, source_target_pairs={{0,8},{1,9},{2,10},{3,11},{4,12},{5,13},{6,14},{7,15},{8,0},{9,1},... | collective-permute-start | bytes 21512 | tf_op jit(solution)/shard_map/ppermute | solution.py:209
  56.4 1.0 %shard_map.98.keep = f32[512,1024]{1,0:T(8,128)S(1)} custom-call(s32[3]{0:T(128)S(1)} %pad_add_fusion.1.me, bf16[1024,256]{1,0:T(8,128)(2,1)S(1)} %copy-done.8, bf16[256,1024]{1,0:T(8,128)(2,1)S(1)} %copy-done.6), custom_call_target="tpu_custom_call" | custom-call | flops 536870912 | bytes 8388608 | tf_op jit(solution)/shard_map/pallas_call | solution.py:41
  57.4 1.0 %collective-permute-done.14 = f32[16,112]{1,0:T(8,128)S(1)} collective-permute-done((f32[16,112]{1,0:T(8,128)S(1)}, f32[16,112]{1,0:T(8,128)S(1)}, u32[]{:S(2)}, u32[]{:S(2)}) %collective-permute-start.14) | collective-permute-done | bytes 7200 | tf_op jit(solution)/shard_map/ppermute | solution.py:209
  58.4 0.7 copy.11
  59.2 1.4 %shard_map.99 = (bf16[256,512]{1,0:T(8,128)(2,1)S(1)}, f32[256,512]{1,0:T(8,128)S(1)}, bf16[256,512]{1,0:T(8,128)(2,1)S(1)}, f32[256,512]{1,0:T(8,128)S(1)}) custom-call(s32[3]{0:T(128)S(1)} %pad_add_fusion.1.me, f32[512,1024]{1,0:T(8,128)S(1)} %shard_map.98.keep, bf16[512,1024]{1,0:T(8,128)(2,1)} %collective-permute-done.4.got), custom_call_target="tpu_custom_call" | custom-call | flops 1048576 | bytes 8388608 | tf_op jit(solution)/shard_map/pallas_call | solution.py:41
  60.7 2.2 %add_convert_fusion = bf16[256,1024]{1,0:T(8,128)(2,1)} fusion(bf16[256,1024]{1,0:T(8,128)(2,1)} %collective-permute-done.3, f32[256,1024]{1,0:T(8,128)S(1)} %shard_map.97, bf16[256,1024]{1,0:T(8,128)(2,1)} %collective-permute-done.2), kind=kLoop, calls=%fused_computation | loop fusion | flops 1310720 | bytes 2621440 | tf_op jit(solution)/shard_map/convert_element_type | solution.py:332
  62.9 1.6 %collective-permute-start.8 = (bf16[256,512]{1,0:T(8,128)(2,1)S(1)}, bf16[256,512]{1,0:T(8,128)(2,1)S(1)}, u32[]{:S(2)}, u32[]{:S(2)}) collective-permute-start(bf16[256,512]{1,0:T(8,128)(2,1)S(1)} %get-tuple-element.41), channel_id=1, source_target_pairs={{0,4},{1,5},{2,6},{3,7},{4,0},{5,1},{6,2},{7,3},{8,12},{9,13},{10,... | collective-permute-start | bytes 786440 | tf_op jit(solution)/shard_map/ppermute | solution.py:209
  64.6 2.5 %collective-permute-done.5 = bf16[256,512]{1,0:T(8,128)(2,1)S(1)} collective-permute-done((bf16[256,512]{1,0:T(8,128)(2,1)S(1)}, bf16[256,512]{1,0:T(8,128)(2,1)S(1)}, u32[]{:S(2)}, u32[]{:S(2)}) %collective-permute-start.5) | collective-permute-done | bytes 262176 | tf_op jit(solution)/shard_map/ppermute | solution.py:209
  67.1 1.7 %collective-permute-start.6 = (bf16[128,512]{1,0:T(8,128)(2,1)S(1)}, bf16[128,512]{1,0:T(8,128)(2,1)S(1)}, u32[]{:S(2)}, u32[]{:S(2)}) collective-permute-start(bf16[128,512]{1,0:T(8,128)(2,1)S(1)} %bitcast.38), channel_id=1, source_target_pairs={{0,4},{1,5},{2,6},{3,7},{4,0},{5,1},{6,2},{7,3},{8,12},{9,13},{10,... | collective-permute-start | bytes 393224 | tf_op jit(solution)/shard_map/ppermute | solution.py:209
  68.9 1.8 %collective-permute-done.8 = bf16[256,512]{1,0:T(8,128)(2,1)S(1)} collective-permute-done((bf16[256,512]{1,0:T(8,128)(2,1)S(1)}, bf16[256,512]{1,0:T(8,128)(2,1)S(1)}, u32[]{:S(2)}, u32[]{:S(2)}) %collective-permute-start.8) | collective-permute-done | bytes 262176 | tf_op jit(solution)/shard_map/ppermute | solution.py:209
  70.8 1.2 %collective-permute-start.9 = (bf16[128,512]{1,0:T(8,128)(2,1)S(1)}, bf16[128,512]{1,0:T(8,128)(2,1)S(1)}, u32[]{:S(2)}, u32[]{:S(2)}) collective-permute-start(bf16[128,512]{1,0:T(8,128)(2,1)S(1)} %bitcast.39), channel_id=1, source_target_pairs={{0,2},{1,3},{2,0},{3,1},{4,6},{5,7},{6,4},{7,5},{8,10},{9,11},{10,... | collective-permute-start | bytes 393224 | tf_op jit(solution)/shard_map/ppermute | solution.py:209
  72.2 2.9 %collective-permute-start.7 = (bf16[64,512]{1,0:T(8,128)(2,1)S(1)}, bf16[64,512]{1,0:T(8,128)(2,1)S(1)}, u32[]{:S(2)}, u32[]{:S(2)}) collective-permute-start(bf16[64,512]{1,0:T(8,128)(2,1)S(1)} %fusion), channel_id=1, source_target_pairs={{0,8},{1,9},{2,10},{3,11},{4,12},{5,13},{6,14},{7,15},{8,0},{9,1},... | collective-permute-start | bytes 196616 | tf_op jit(solution)/shard_map/ppermute | solution.py:209
  75.1 0.7 collective-permute-done.9
  75.9 2.7 %collective-permute-start.10 = (bf16[64,512]{1,0:T(8,128)(2,1)S(1)}, bf16[64,512]{1,0:T(8,128)(2,1)S(1)}, u32[]{:S(2)}, u32[]{:S(2)}) collective-permute-start(bf16[64,512]{1,0:T(8,128)(2,1)S(1)} %fusion.1), channel_id=1, source_target_pairs={{0,8},{1,9},{2,10},{3,11},{4,12},{5,13},{6,14},{7,15},{8,0},{9,1},... | collective-permute-start | bytes 196616 | tf_op jit(solution)/shard_map/ppermute | solution.py:209
  78.6 2.5 %collective-permute-done.10 = bf16[64,512]{1,0:T(8,128)(2,1)S(1)} collective-permute-done((bf16[64,512]{1,0:T(8,128)(2,1)S(1)}, bf16[64,512]{1,0:T(8,128)(2,1)S(1)}, u32[]{:S(2)}, u32[]{:S(2)}) %collective-permute-start.10) | collective-permute-done | bytes 65568 | tf_op jit(solution)/shard_map/ppermute | solution.py:209
  81.1 0.7 maximum_multiply_fusion
  (58 shorter events, 4.3 us)
Async XLA Ops:
  0.6 19.4 %collective-permute-start = (bf16[256,1024]{1,0:T(8,128)(2,1)}, bf16[256,1024]{1,0:T(8,128)(2,1)S(1)}, u32[]{:S(2)}, u32[]{:S(2)}) collective-permute-start(bf16[256,1024]{1,0:T(8,128)(2,1)} %x.1), channel_id=1, source_target_pairs={{0,1},{1,2},{2,3},{3,4},{4,5},{5,6},{6,7},{7,8},{8,9},{9,10},{10,1... | collective-permute-start | bytes 1572872 | tf_op jit(solution)/shard_map/ppermute | solution.py:206
  1.2 18.8 %collective-permute-start.1 = (bf16[256,1024]{1,0:T(8,128)(2,1)}, bf16[256,1024]{1,0:T(8,128)(2,1)S(1)}, u32[]{:S(2)}, u32[]{:S(2)}) collective-permute-start(bf16[256,1024]{1,0:T(8,128)(2,1)} %x.1), channel_id=1, source_target_pairs={{0,15},{1,0},{2,1},{3,2},{4,3},{5,4},{6,5},{7,6},{8,7},{9,8},{10,9... | collective-permute-start | bytes 1572872 | tf_op jit(solution)/shard_map/ppermute | solution.py:206
  6.4 1.0 %copy-start.4 = (bf16[256,1024]{1,0:T(8,128)(2,1)S(1)}, bf16[256,1024]{1,0:T(8,128)(2,1)}, u32[]{:S(2)}) copy-start(bf16[256,1024]{1,0:T(8,128)(2,1)} %cot.5) | copy-start | bytes 1572868
  7.4 1.6 %copy-start.9 = (bf16[1024,1024]{1,0:T(8,128)(2,1)S(1)}, bf16[1024,1024]{1,0:T(8,128)(2,1)}, u32[]{:S(2)}) copy-start(bf16[1024,1024]{1,0:T(8,128)(2,1)} %mix_hbm.1) | copy-start | bytes 6291460
  9.0 1.0 %copy-start.10 = (bf16[256,1024]{1,0:T(8,128)(2,1)S(1)}, bf16[256,1024]{1,0:T(8,128)(2,1)}, u32[]{:S(2)}) copy-start(bf16[256,1024]{1,0:T(8,128)(2,1)} %x.1) | copy-start | bytes 1572868
  10.1 0.7 copy-start.12
  10.8 0.7 copy-start.13
  11.5 0.7 copy-start.14
  12.2 0.7 copy-start.15
  12.9 7.2 %copy-start.5 = (bf16[256,1024]{1,0:T(8,128)(2,1)S(1)}, bf16[256,1024]{1,0:T(8,128)(2,1)}, u32[]{:S(2)}) copy-start(bf16[256,1024]{1,0:T(8,128)(2,1)} %cot.5) | copy-start | bytes 1572868
  20.0 6.8 %copy-start.2 = (bf16[768,1536]{1,0:T(8,128)(2,1)}, bf16[768,1536]{1,0:T(8,128)(2,1)S(1)}, u32[]{:S(2)}) copy-start(bf16[768,1536]{1,0:T(8,128)(2,1)S(1)} %get-tuple-element.31.back_sel) | copy-start | bytes 7077892
  20.0 6.8 %copy-start.11 = (bf16[256,1024]{1,0:T(8,128)(2,1)S(1)}, bf16[256,1024]{1,0:T(8,128)(2,1)}, u32[]{:S(2)}) copy-start(bf16[256,1024]{1,0:T(8,128)(2,1)} %x.1) | copy-start | bytes 1572868
  26.0 0.8 copy-start.7
  26.8 32.4 %collective-permute-start.4 = (bf16[512,1024]{1,0:T(8,128)(2,1)}, bf16[512,1024]{1,0:T(8,128)(2,1)}, u32[]{:S(2)}, u32[]{:S(2)}) collective-permute-start(bf16[512,1024]{1,0:T(8,128)(2,1)} %get-tuple-element.37), channel_id=1, source_target_pairs={{0,1},{1,0},{2,3},{3,2},{4,5},{5,4},{6,7},{7,6},{8,9},{9,8},{10,11... | collective-permute-start | bytes 3145736 | tf_op jit(solution)/shard_map/ppermute | solution.py:209
  31.7 1.6 %copy-start = (bf16[1536,1024]{1,0:T(8,128)(2,1)}, bf16[1536,1024]{1,0:T(8,128)(2,1)S(1)}, u32[]{:S(2)}) copy-start(bf16[1536,1024]{1,0:T(8,128)(2,1)S(1)} %get-tuple-element.33.terms) | copy-start | bytes 9437188
  33.4 27.3 %collective-permute-start.2 = (bf16[256,1024]{1,0:T(8,128)(2,1)}, bf16[256,1024]{1,0:T(8,128)(2,1)}, u32[]{:S(2)}, u32[]{:S(2)}) collective-permute-start(bf16[256,1024]{1,0:T(8,128)(2,1)} %get-tuple-element.34), channel_id=1, source_target_pairs={{0,1},{1,2},{2,3},{3,4},{4,5},{5,6},{6,7},{7,8},{8,9},{9,10},{10,1... | collective-permute-start | bytes 1572872 | tf_op jit(solution)/shard_map/ppermute | solution.py:206
  33.9 26.8 %collective-permute-start.3 = (bf16[256,1024]{1,0:T(8,128)(2,1)}, bf16[256,1024]{1,0:T(8,128)(2,1)}, u32[]{:S(2)}, u32[]{:S(2)}) collective-permute-start(bf16[256,1024]{1,0:T(8,128)(2,1)} %get-tuple-element.35), channel_id=1, source_target_pairs={{0,15},{1,0},{2,1},{3,2},{4,3},{5,4},{6,5},{7,6},{8,7},{9,8},{10,9... | collective-permute-start | bytes 1572872 | tf_op jit(solution)/shard_map/ppermute | solution.py:206
  37.8 1.2 %collective-permute-start.11 = (f32[16,112]{1,0:T(8,128)S(1)}, f32[16,112]{1,0:T(8,128)S(1)}, u32[]{:S(2)}, u32[]{:S(2)}) collective-permute-start(f32[16,112]{1,0:T(8,128)S(1)} %get-tuple-element.42), channel_id=1, source_target_pairs={{0,1},{1,0},{2,3},{3,2},{4,5},{5,4},{6,7},{7,6},{8,9},{9,8},{10,11... | collective-permute-start | bytes 21512 | tf_op jit(solution)/shard_map/ppermute | solution.py:209
  39.0 9.7 %collective-permute-start.12 = (f32[16,112]{1,0:T(8,128)S(1)}, f32[16,112]{1,0:T(8,128)S(1)}, u32[]{:S(2)}, u32[]{:S(2)}) collective-permute-start(f32[16,112]{1,0:T(8,128)S(1)} %add.75), channel_id=1, source_target_pairs={{0,2},{1,3},{2,0},{3,1},{4,6},{5,7},{6,4},{7,5},{8,10},{9,11},{10,... | collective-permute-start | bytes 21512 | tf_op jit(solution)/shard_map/ppermute | solution.py:209
  48.7 5.1 %collective-permute-start.13 = (f32[16,112]{1,0:T(8,128)S(1)}, f32[16,112]{1,0:T(8,128)S(1)}, u32[]{:S(2)}, u32[]{:S(2)}) collective-permute-start(f32[16,112]{1,0:T(8,128)S(1)} %add.76), channel_id=1, source_target_pairs={{0,4},{1,5},{2,6},{3,7},{4,0},{5,1},{6,2},{7,3},{8,12},{9,13},{10,... | collective-permute-start | bytes 21512 | tf_op jit(solution)/shard_map/ppermute | solution.py:209
  49.1 1.9 %copy-start.1 = (bf16[1536,1024]{1,0:T(8,128)(2,1)S(1)}, bf16[1536,1024]{1,0:T(8,128)(2,1)}, u32[]{:S(2)}) copy-start(bf16[1536,1024]{1,0:T(8,128)(2,1)} %copy-done) | copy-start | bytes 9437188
  50.9 1.7 %copy-start.3 = (bf16[768,1536]{1,0:T(8,128)(2,1)S(1)}, bf16[768,1536]{1,0:T(8,128)(2,1)}, u32[]{:S(2)}) copy-start(bf16[768,1536]{1,0:T(8,128)(2,1)} %copy-done.2) | copy-start | bytes 7077892
  52.6 3.8 %copy-start.6 = (bf16[256,1024]{1,0:T(8,128)(2,1)S(1)}, bf16[256,1024]{1,0:T(8,128)(2,1)}, u32[]{:S(2)}) copy-start(bf16[256,1024]{1,0:T(8,128)(2,1)} %cot.5) | copy-start | bytes 1572868
  52.6 3.8 %copy-start.8 = (bf16[1024,256]{1,0:T(8,128)(2,1)S(1)}, bf16[1024,256]{1,0:T(8,128)(2,1)}, u32[]{:S(2)}) copy-start(bf16[1024,256]{1,0:T(8,128)(2,1)} %copy-done.7) | copy-start | bytes 1572868
  53.8 4.6 %collective-permute-start.14 = (f32[16,112]{1,0:T(8,128)S(1)}, f32[16,112]{1,0:T(8,128)S(1)}, u32[]{:S(2)}, u32[]{:S(2)}) collective-permute-start(f32[16,112]{1,0:T(8,128)S(1)} %add.77), channel_id=1, source_target_pairs={{0,8},{1,9},{2,10},{3,11},{4,12},{5,13},{6,14},{7,15},{8,0},{9,1},... | collective-permute-start | bytes 21512 | tf_op jit(solution)/shard_map/ppermute | solution.py:209
  60.6 6.4 %collective-permute-start.5 = (bf16[256,512]{1,0:T(8,128)(2,1)S(1)}, bf16[256,512]{1,0:T(8,128)(2,1)S(1)}, u32[]{:S(2)}, u32[]{:S(2)}) collective-permute-start(bf16[256,512]{1,0:T(8,128)(2,1)S(1)} %get-tuple-element.39), channel_id=1, source_target_pairs={{0,2},{1,3},{2,0},{3,1},{4,6},{5,7},{6,4},{7,5},{8,10},{9,11},{10,... | collective-permute-start | bytes 786440 | tf_op jit(solution)/shard_map/ppermute | solution.py:209
  62.9 7.7 %collective-permute-start.8 = (bf16[256,512]{1,0:T(8,128)(2,1)S(1)}, bf16[256,512]{1,0:T(8,128)(2,1)S(1)}, u32[]{:S(2)}, u32[]{:S(2)}) collective-permute-start(bf16[256,512]{1,0:T(8,128)(2,1)S(1)} %get-tuple-element.41), channel_id=1, source_target_pairs={{0,4},{1,5},{2,6},{3,7},{4,0},{5,1},{6,2},{7,3},{8,12},{9,13},{10,... | collective-permute-start | bytes 786440 | tf_op jit(solution)/shard_map/ppermute | solution.py:209
  67.1 5.0 %collective-permute-start.6 = (bf16[128,512]{1,0:T(8,128)(2,1)S(1)}, bf16[128,512]{1,0:T(8,128)(2,1)S(1)}, u32[]{:S(2)}, u32[]{:S(2)}) collective-permute-start(bf16[128,512]{1,0:T(8,128)(2,1)S(1)} %bitcast.38), channel_id=1, source_target_pairs={{0,4},{1,5},{2,6},{3,7},{4,0},{5,1},{6,2},{7,3},{8,12},{9,13},{10,... | collective-permute-start | bytes 393224 | tf_op jit(solution)/shard_map/ppermute | solution.py:209
  70.8 5.0 %collective-permute-start.9 = (bf16[128,512]{1,0:T(8,128)(2,1)S(1)}, bf16[128,512]{1,0:T(8,128)(2,1)S(1)}, u32[]{:S(2)}, u32[]{:S(2)}) collective-permute-start(bf16[128,512]{1,0:T(8,128)(2,1)S(1)} %bitcast.39), channel_id=1, source_target_pairs={{0,2},{1,3},{2,0},{3,1},{4,6},{5,7},{6,4},{7,5},{8,10},{9,11},{10,... | collective-permute-start | bytes 393224 | tf_op jit(solution)/shard_map/ppermute | solution.py:209
  72.2 6.3 %collective-permute-start.7 = (bf16[64,512]{1,0:T(8,128)(2,1)S(1)}, bf16[64,512]{1,0:T(8,128)(2,1)S(1)}, u32[]{:S(2)}, u32[]{:S(2)}) collective-permute-start(bf16[64,512]{1,0:T(8,128)(2,1)S(1)} %fusion), channel_id=1, source_target_pairs={{0,8},{1,9},{2,10},{3,11},{4,12},{5,13},{6,14},{7,15},{8,0},{9,1},... | collective-permute-start | bytes 196616 | tf_op jit(solution)/shard_map/ppermute | solution.py:209
  75.9 5.2 %collective-permute-start.10 = (bf16[64,512]{1,0:T(8,128)(2,1)S(1)}, bf16[64,512]{1,0:T(8,128)(2,1)S(1)}, u32[]{:S(2)}, u32[]{:S(2)}) collective-permute-start(bf16[64,512]{1,0:T(8,128)(2,1)S(1)} %fusion.1), channel_id=1, source_target_pairs={{0,8},{1,9},{2,10},{3,11},{4,12},{5,13},{6,14},{7,15},{8,0},{9,1},... | collective-permute-start | bytes 196616 | tf_op jit(solution)/shard_map/ppermute | solution.py:209
where the time goes:
time: 82.3 us; the launch traced here: 81.8 us
  starting transfers between devices  23.3 us (28%)
  Pallas kernels  21.5 us (26%)
  waiting for transfers between devices  19.5 us (24%)
  local copies, waits for them, and re-layouts  13.4 us (16%)
  other arithmetic  3.35 us (4%)
  between operations  0.84 us (1%)
    pallas_call x6, Pallas kernels, call(): pl.pallas_call(body, out_shape=[jax.ShapeDtypeStruct(s, d) for s, d in ou...  21.5 us
    ppermute x11, waiting for transfers between devices, swap(): lax.ppermute(value, 'space', [(i, i ^ 1 << bit) for i in range(devices)])  19.4 us
    ppermute x11, starting transfers between devices, swap(): lax.ppermute(value, 'space', [(i, i ^ 1 << bit) for i in range(devices)])  13.2 us
    unnamed x33, local copies, waits for them, and re-layouts  13.2 us
    ppermute x4, starting transfers between devices, ring(): lax.ppermute(value, 'space', [(i, (i + by) % devices) for i in range(devi...  10 us
    convert_element_type x1, other arithmetic, shards(): (inner + from_below.astype(f32) + from_above.astype(f32)).astype(bf16)  2.24 us
  transfers between devices with their start and end apart: 15, of which 8 were waited for; matrix products, arithmetic and copies ran while one was open for 4% of the time, Pallas kernels for 19%

commit v1 on v0

v1 whole, which is shorter than its diff:
```python
import functools

import jax
import jax.numpy as jnp
from jax import lax
from jax.experimental import pallas as pl
from jax.experimental.pallas import tpu as pltpu
from jax.sharding import PartitionSpec as P


ROW = 256
WIDE = 256
TANH_SCALE = 0.7978845608028654
TANH_CUBE = 0.044715


f32 = jnp.float32
bf16 = jnp.bfloat16


def mm(a, b):
    return jnp.dot(a, b, preferred_element_type=f32)


def contract(a, b, dim_a, dim_b, **kw):
    return lax.dot_general(
        a, b, (((dim_a,), (dim_b,)), ((), ())), preferred_element_type=f32, **kw
    )


def iota(shape, dim):
    return lax.broadcasted_iota(jnp.int32, shape, dim)


def onehot(cond):
    return jnp.where(cond, 1.0, 0.0).astype(bf16)


def call(body, outs, cost, *args, scratch=(), scalars=0, far=()):
    space = lambda k: pltpu.SMEM if k < scalars else pltpu.HBM if k in far else pltpu.VMEM
    return pl.pallas_call(
        body,
        out_shape=[jax.ShapeDtypeStruct(s, d) for s, d in outs],
        in_specs=[pl.BlockSpec(memory_space=space(k)) for k in range(len(args))],
        out_specs=[pl.BlockSpec(memory_space=pltpu.VMEM)] * len(outs),
        scratch_shapes=list(scratch),
        cost_estimate=pl.CostEstimate(flops=cost, transcendentals=0, bytes_accessed=8 << 20),
        compiler_params=pltpu.CompilerParams(vmem_limit_bytes=12 << 20),
    )(*args)


def picked(local_t, turns, tap):
    turn = tap - 1 - turns
    slot = 1 + jnp.where(turn < 0, turn + 6, turn)
    source = jnp.full_like(slot, -1)
    for k in range(1, 7):
        source = jnp.where(slot == k, local_t[k : k + 1, :], source)
    return source


def early_kernel(place, near, turns, void, x_hbm, conv_hbm, halo_sel, sources_out, own, wk, x, conv, sems):
    copies = [
        pltpu.make_async_copy(src, dst, sems.at[k])
        for k, (src, dst) in enumerate(((conv_hbm, conv), (x_hbm, x)))
    ]
    for copy in copies:
        copy.start()
    n = x.shape[0]
    taps, c = conv.shape[:2]
    offset, total = place[0], place[1]
    moved = near[...] - offset + ROW
    moved = jnp.where(moved < 0, moved + total, moved)
    moved = jnp.where(moved >= total, moved - total, moved)
    dropped = (void[...] == 1) & (iota((taps, n), 0) == 6)
    local_t = jnp.where(dropped, -1, moved)
    sources = [picked(local_t, turns[...], tap) for tap in range(1, taps)]
    sources_t = jnp.concatenate(sources + [sources[0]] * (8 - len(sources)), axis=0)
    sources_out[...] = sources_t
    eye = jnp.where(iota((n, n), 0) == iota((n, n), 1), 1.0, 0.0)
    columns = contract(eye, sources_t.astype(f32), 1, 1, precision=lax.Precision.HIGHEST)
    columns = columns.astype(jnp.int32)

    copies[0].wait()
    repeat = onehot(iota((c, WIDE), 1) % c == iota((c, WIDE), 0))
    down = onehot(iota((WIDE, c), 0) % c == iota((WIDE, c), 1))
    same = iota((WIDE, WIDE), 0) // c == iota((WIDE, WIDE), 1) // c
    for tap in range(taps):
        wide = mm(conv[tap], repeat).astype(bf16)
        wk[tap * WIDE : (tap + 1) * WIDE, :] = jnp.where(same, mm(down, wide), 0.0).astype(bf16)
    copies[1].wait()
    for tap in range(1, taps):
        at = (tap - 1) * n
        source = columns[:, tap - 1 : tap]
        halo_sel[at : at + n, :ROW] = onehot(iota((n, ROW), 1) == source)
        halo_sel[at : at + n, ROW:] = onehot(iota((n, ROW), 1) + (ROW + n) == source)
        mine = onehot(iota((n, n), 1) + ROW == source)
        own[at : at + n, :] = mm(mine, x[...]).astype(bf16)


def gelu_tanh(v):
    return jnp.tanh(TANH_SCALE * (v + TANH_CUBE * (v * v * v)))


def mix_rows(act_t, cot, bit, share):
    blocks = act_t.shape[0] // share
    rows = [
        act_t[pl.ds(pl.multiple_of((2 * k + bit) * share, share), share), :] for k in range(blocks // 2)
    ]
    return mm(jnp.concatenate(rows, axis=0), cot[...])


def front_kernel(share, me, low, high, halo_sel, own, wk, x, cot, rows_out, pre, act_t, send):
    n, width = pre.shape
    taps = wk.shape[0] // WIDE
    for c in range(0, width, WIDE):
        both = jnp.concatenate([low[:, c : c + WIDE], high[:, c : c + WIDE]], axis=0)
        rows = mm(halo_sel[...], both).astype(bf16) + own[:, c : c + WIDE]
        rows_out[:, c : c + WIDE] = rows
        acc = mm(x[:, c : c + WIDE], wk[:WIDE, :])
        for tap in range(1, taps):
            acc += mm(rows[(tap - 1) * n : tap * n], wk[tap * WIDE : (tap + 1) * WIDE, :])
        pre[:, c : c + WIDE] = acc
        active = (0.5 * acc) * (1.0 + gelu_tanh(acc))
        act_t[c : c + WIDE, :] = active.T.astype(bf16)
    send[...] = mix_rows(act_t, cot, 1 - me[0], share).astype(bf16)


def keep_kernel(share, me, act_t, cot, mix_hbm, keep, up, mix, sem):
    copy = pltpu.make_async_copy(mix_hbm, mix, sem.at[0])
    copy.start()
    keep[...] = mix_rows(act_t, cot, me[0], share)
    copy.wait()
    up[...] = contract(cot[...], mix[...], 1, 1)


def select_rows(sources, start, count, taps):
    n = sources.shape[1]
    return jnp.concatenate(
        [onehot(iota((count, n), 0) + start == sources[tap : tap + 1, :]) for tap in range(taps - 1)], axis=1
    )


def terms_kernel(up, pre, wk, sources, grad, terms, low, high, back_sel):
    n, width = pre.shape
    taps = wk.shape[0] // WIDE
    back_sel[:ROW, :] = select_rows(sources, 0, ROW, taps)
    back_sel[ROW:, :] = select_rows(sources, ROW + n, ROW, taps)
    for c in range(0, width, WIDE):
        v = pre[:, c : c + WIDE]
        t = gelu_tanh(v)
        slope = 0.5 * (1.0 + t) + (0.5 * TANH_SCALE) * v * (1.0 - t * t) * (1.0 + (3 * TANH_CUBE) * (v * v))
        g = (up[:, c : c + WIDE] * slope).astype(bf16)
        grad[:, c : c + WIDE] = g
        for tap in range(1, taps):
            terms[(tap - 1) * n : tap * n, c : c + WIDE] = contract(
                g, wk[tap * WIDE : (tap + 1) * WIDE, :], 1, 1
            ).astype(bf16)
        both = mm(back_sel[...], terms[:, c : c + WIDE]).astype(bf16)
        low[:, c : c + WIDE] = both[:ROW]
        high[:, c : c + WIDE] = both[ROW:]


def weights_kernel(channels, scale, grad, x, rows, conv):
    n, width = grad.shape
    taps = rows.shape[0] // n + 1
    acc = [jnp.zeros((WIDE, WIDE), f32) for _ in range(taps)]
    for c in range(0, width, WIDE):
        g_t = grad[:, c : c + WIDE].astype(f32).T.astype(bf16)
        acc[0] += mm(g_t, x[:, c : c + WIDE])
        for tap in range(1, taps):
            acc[tap] += mm(g_t, rows[(tap - 1) * n : tap * n, c : c + WIDE])
    same = iota((WIDE, WIDE), 0) // channels == iota((WIDE, WIDE), 1) // channels
    fold = jnp.where(iota((channels, WIDE), 1) % channels == iota((channels, WIDE), 0), 1.0, 0.0)
    for tap in range(taps):
        block = jnp.where(same, acc[tap], 0.0)
        block = jnp.sum(block.reshape(WIDE // channels, channels, WIDE), axis=0)
        conv[:, tap * channels : (tap + 1) * channels] = (
            contract(fold, block, 1, 1, precision=lax.Precision.HIGHEST) * scale
        )


def inner_kernel(grad, terms, wk, sources, cot, inner):
    n, width = grad.shape
    taps = wk.shape[0] // WIDE
    sel = select_rows(sources, ROW, n, taps)
    for c in range(0, width, WIDE):
        acc = contract(grad[:, c : c + WIDE], wk[:WIDE, :], 1, 1) + cot[:, c : c + WIDE].astype(f32)
        inner[:, c : c + WIDE] = acc + mm(sel, terms[:, c : c + WIDE])


def halve(share, bit, skip, kept, got, send, keep):
    for q in range(kept.shape[0] // share // 2):
        base = ((q >> skip) << (skip + 1)) | (q & ((1 << skip) - 1))
        for value, out in ((1 - bit, send), (bit, keep)):
            at = pl.ds(pl.multiple_of((base + (value << skip)) * share, share), share)
            out[q * share : (q + 1) * share, :] = (kept[at, :] + got[at, :].astype(f32)).astype(out.dtype)


def split_kernel(share, where, me, keep, got, *outs):
    half = keep.shape[1] // 2
    for k, (bit, skip) in enumerate(where):
        cols = slice(k * half, (k + 1) * half)
        halve(share, me[bit], skip, keep.at[:, cols], got.at[:, cols], outs[2 * k], outs[2 * k + 1])


def merge_kernel(share, where, me, *refs):
    for k, (bit, skip) in enumerate(where):
        halve(share, me[bit], skip, refs[2 * k], refs[2 * k + 1], refs[4 + 2 * k], refs[5 + 2 * k])


def finish_kernel(scale, kept_a, got_a, kept_b, got_b, out):
    half = kept_a.shape[1]
    out[:, :half] = (kept_a[...] + got_a[...].astype(f32)) * scale
    out[:, half:] = (kept_b[...] + got_b[...].astype(f32)) * scale


def total_kernel(inner, first, second, out):
    out[...] = (inner[...] + first[...].astype(f32) + second[...].astype(f32)).astype(bf16)


def shards(columns_in, cotangent, conv_weight, mix_weight, neighbours, rotations, pentagons):
    n, width = columns_in.shape
    taps, channels = conv_weight.shape[:2]
    devices = lax.axis_size("space")
    place = lax.axis_index("space").astype(jnp.int32)
    total_cols = n * devices
    levels = width // channels
    bits = devices.bit_length() - 1

    def ring(value, by):
        return lax.ppermute(value, "space", [(i, (i + by) % devices) for i in range(devices)])

    def swap(value, bit):
        return lax.ppermute(value, "space", [(i, i ^ (1 << bit)) for i in range(devices)])

    below = ring(columns_in, 1)
    above = ring(columns_in, -1)
    pairs = (taps - 1) * n
    share = width // devices
    half = width // 2
    mine = jnp.stack([(place >> b) & 1 for b in range(bits)])
    halo_sel, sources, own, wk = call(
        early_kernel,
        [((pairs, 2 * ROW), bf16), ((8, n), jnp.int32), ((pairs, width), bf16), ((taps * WIDE, WIDE), bf16)],
        1 << 30,
        jnp.stack([place * n, jnp.int32(total_cols)]),
        neighbours.T,
        rotations[None, :],
        pentagons[None, :],
        columns_in,
        conv_weight,
        scalars=1,
        far=(4, 5),
        scratch=[
            pltpu.VMEM(columns_in.shape, bf16),
            pltpu.VMEM(conv_weight.shape, bf16),
            pltpu.SemaphoreType.DMA((2,)),
        ],
    )
    rows, pre, act_t, send = call(
        functools.partial(front_kernel, share),
        [((pairs, width), bf16), ((n, width), f32), ((width, n), bf16), ((half, width), bf16)],
        3 << 30,
        mine,
        below,
        above,
        halo_sel,
        own,
        wk,
        columns_in,
        cotangent,
        scalars=1,
    )
    got = swap(send, 0)
    keep, up = call(
        functools.partial(keep_kernel, share),
        [((half, width), f32), ((n, width), f32)],
        1 << 30,
        mine,
        act_t,
        cotangent,
        mix_weight,
        scalars=1,
        far=(3,),
        scratch=[pltpu.VMEM(mix_weight.shape, bf16), pltpu.SemaphoreType.DMA((1,))],
    )
    orders = [list(range(1, bits)), list(range(2, bits)) + [1]]
    lefts = [list(range(bits - 1, 0, -1)) for _ in orders]

    def places(stage):
        where = []
        for order, left in zip(orders, lefts):
            bit = order[stage]
            where.append((bit, len(left) - 1 - left.index(bit)))
            left.remove(bit)
        return tuple(where)

    rows_left = half // 2
    parts = call(
        functools.partial(split_kernel, share, places(0)),
        [((rows_left, half), bf16), ((rows_left, half), f32)] * 2,
        1 << 20,
        mine,
        keep,
        got,
        scalars=1,
    )
    for stage in range(1, bits):
        gots = []
        for k in (0, 1):
            gots.append(swap(parts[2 * k], orders[k][stage - 1]))
        state = [parts[1], gots[0], parts[3], gots[1]]
        if stage < bits - 1:
            rows_left //= 2
            parts = call(
                functools.partial(merge_kernel, share, places(stage)),
                [((rows_left, half), bf16), ((rows_left, half), f32)] * 2,
                1 << 20,
                mine,
                *state,
                scalars=1,
            )
    (grad_mix,) = call(
        functools.partial(finish_kernel, 1.0 / float(total_cols) ** 0.5),
        [((share, width), f32)],
        1 << 20,
        *state,
    )
    grad, terms, to_low, to_high = call(
        terms_kernel,
        [((n, width), bf16), ((pairs, width), bf16), ((ROW, width), bf16), ((ROW, width), bf16)],
        3 << 30,
        up,
        pre,
        wk,
        sources,
        scratch=[pltpu.VMEM((2 * ROW, pairs), bf16)],
    )
    from_below = ring(to_high, 1)
    from_above = ring(to_low, -1)
    (conv,) = call(
        functools.partial(weights_kernel, channels, 1.0 / float(total_cols * levels) ** 0.5),
        [((channels, taps * channels), f32)],
        1 << 30,
        grad,
        columns_in,
        rows,
    )
    for bit in [0] + orders[1]:
        conv = conv + swap(conv, bit)
    grad_conv = conv.reshape(channels, taps, channels).transpose(1, 0, 2)
    (inner,) = call(inner_kernel, [((n, width), f32)], 1 << 30, grad, terms, wk, sources, cotangent)
    (grad_input,) = call(total_kernel, [((n, width), bf16)], 1 << 20, inner, from_below, from_above)
    return grad_input, grad_mix, grad_conv


def solution(mesh):
    return jax.shard_map(
        shards,
        mesh=mesh,
        in_specs=(
            P(("group", "space"), None),
            P(("group", "space"), None),
            P(),
            P(),
            P("space", None),
            P("space"),
            P("space"),
        ),
        out_specs=(P(("group", "space"), None), P("space", "group"), P("group", None, None)),
        check_vma=False,
    )
```

time: 82.3 us -> 72.6 us (0.88)
  waiting for transfers between devices: 19.5 us -> 28.5 us
  local copies, waits for them, and re-layouts: 13.4 us -> 4.57 us
  starting transfers between devices: 23.3 us -> 16.7 us
  other arithmetic: 3.35 us -> 0.17 us
    unnamed x33 -> x17, local copies, waits for them, and re-layouts: 13.2 us -> 4.49 us
    ppermute x11, starting transfers between devices: 13.2 us -> 6.77 us  [swap(): lax.ppermute(value, 'space', [(i, i ^ 1 << bit) for i in range(devices)])]
    ppermute x11, waiting for transfers between devices: 19.4 us -> 24.6 us  [swap(): lax.ppermute(value, 'space', [(i, i ^ 1 << bit) for i in range(devices)])]
    ppermute x4, waiting for transfers between devices: 0.01 us -> 3.98 us  [ring(): lax.ppermute(value, 'space', [(i, (i + by) % devices) for i in range(devi...]
    convert_element_type x1 -> x0, other arithmetic: 2.24 us -> none  [shards(): (inner + from_below.astype(f32) + from_above.astype(f32)).astype(bf16)]
    pallas_call x6 -> x11, Pallas kernels: 21.5 us -> 21.5 us  [call(): pl.pallas_call(body, out_shape=[jax.ShapeDtypeStruct(s, d) for s, d in ou...]
  transfers between devices with their start and end apart: 15 -> 15, of which waited for: 8 -> 6; matrix products, arithmetic and copies ran while one was open for 4% -> 1% of each run, Pallas kernels for 19% -> 22%
where the time goes in v1:
time: 72.6 us; the launch traced here: 72.3 us
  waiting for transfers between devices  28.5 us (39%)
  Pallas kernels  21.5 us (30%)
  starting transfers between devices  16.7 us (23%)
  local copies, waits for them, and re-layouts  4.57 us (6%)
  between operations  0.77 us (1%)
    ppermute x11, waiting for transfers between devices, swap(): lax.ppermute(value, 'space', [(i, i ^ 1 << bit) for i in range(devices)])  24.6 us
    pallas_call x11, Pallas kernels, call(): pl.pallas_call(body, out_shape=[jax.ShapeDtypeStruct(s, d) for s, d in ou...  21.5 us
    ppermute x4, starting transfers between devices, ring(): lax.ppermute(value, 'space', [(i, (i + by) % devices) for i in range(devi...  9.97 us
    ppermute x11, starting transfers between devices, swap(): lax.ppermute(value, 'space', [(i, i ^ 1 << bit) for i in range(devices)])  6.77 us
    unnamed x17, local copies, waits for them, and re-layouts  4.49 us
    ppermute x4, waiting for transfers between devices, ring(): lax.ppermute(value, 'space', [(i, (i + by) % devices) for i in range(devi...  3.98 us
  transfers between devices with their start and end apart: 15, of which 6 were waited for; matrix products, arithmetic and copies ran while one was open for 1% of the time, Pallas kernels for 22%

profile of v1, /device:TPU:0, one launch (start us, length us, event | category | flops | bytes accessed | tf_op | source)
XLA Modules:
  0.0 72.3 jit_solution(18943331441361006)
XLA Ops:
  0.6 5.5 %collective-permute-start.1 = (bf16[256,1024]{1,0:T(8,128)(2,1)}, bf16[256,1024]{1,0:T(8,128)(2,1)S(1)}, u32[]{:S(2)}, u32[]{:S(2)}) collective-permute-start(bf16[256,1024]{1,0:T(8,128)(2,1)} %x.3), channel_id=1, source_target_pairs={{0,15},{1,0},{2,1},{3,2},{4,3},{5,4},{6,5},{7,6},{8,7},{9,8},{10,9... | collective-permute-start | bytes 1572872 | tf_op jit(solution)/shard_map/ppermute | solution.py:231
  6.2 1.0 %copy-done.1 = bf16[256,1024]{1,0:T(8,128)(2,1)S(1)} copy-done((bf16[256,1024]{1,0:T(8,128)(2,1)S(1)}, bf16[256,1024]{1,0:T(8,128)(2,1)}, u32[]{:S(2)}) %copy-start.1) | copy-done | bytes 524312
  7.3 0.7 %copy-done.4 = bf16[7,16,16]{2,1,0:T(8,128)(2,1)S(1)} copy-done((bf16[7,16,16]{2,1,0:T(8,128)(2,1)S(1)}, bf16[7,16,16]{2,1,0:T(8,128)(2,1)}, u32[]{:S(2)}) %copy-start.4) | copy-done | bytes 3608
  8.0 0.7 copy-done.5
  8.7 0.7 copy-done.6
  9.4 0.7 copy-done.7
  10.1 3.5 %shard_map.94 = (bf16[1536,512]{1,0:T(8,128)(2,1)S(1)}, s32[8,256]{1,0:T(8,128)S(1)}, bf16[1536,1024]{1,0:T(8,128)(2,1)S(1)}, bf16[1792,256]{1,0:T(8,128)(2,1)S(1)}) custom-call(s32[2]{0:T(128)S(1)} %pad_add_fusion.1.place, s32[7,256]{1,0:T(8,128)S(1)} %bitcast.9, s32[1,256]{1,0:T(1,128)S(1)} %bitcast.10, s32[1,256]{1,0:T(1,128)S(1)} %bitcast.11, ...), custom_call_target="tpu_custom_call" | custom-call | flops 1073741824 | bytes 8388608 | tf_op jit(solution)/shard_map/pallas_call | solution.py:41
  13.7 4.0 %collective-permute-done.low = bf16[256,1024]{1,0:T(8,128)(2,1)S(1)} collective-permute-done((bf16[256,1024]{1,0:T(8,128)(2,1)}, bf16[256,1024]{1,0:T(8,128)(2,1)S(1)}, u32[]{:S(2)}, u32[]{:S(2)}) %collective-permute-start) | collective-permute-done | bytes 524320 | tf_op jit(solution)/shard_map/ppermute | solution.py:231
  17.7 5.2 %shard_map.95 = (bf16[1536,1024]{1,0:T(8,128)(2,1)S(1)}, f32[256,1024]{1,0:T(8,128)S(1)}, bf16[1024,256]{1,0:T(8,128)(2,1)S(1)}, bf16[512,1024]{1,0:T(8,128)(2,1)S(1)}) custom-call(s32[4]{0:T(128)S(1)} %pad_add_fusion.me, bf16[256,1024]{1,0:T(8,128)(2,1)S(1)} %collective-permute-done.low, bf16[256,1024]{1,0:T(8,128)(2,1)S(1)} %collective-permute-done.1.high, ...), custom_call_target="tpu_custom_call" | custom-call | flops 3221225472 | bytes 8388608 | tf_op jit(solution)/shard_map/pallas_call | solution.py:41
  23.0 1.9 %shard_map.96 = (f32[512,1024]{1,0:T(8,128)S(1)}, f32[256,1024]{1,0:T(8,128)S(1)}) custom-call(s32[4]{0:T(128)S(1)} %pad_add_fusion.me, bf16[1024,256]{1,0:T(8,128)(2,1)S(1)} %get-tuple-element.32.act_t, bf16[256,1024]{1,0:T(8,128)(2,1)S(1)} %copy-done, bf16[1024,1024]{1,0:T(8,128)(2,1)S(1)} %copy-done.3), custom_call_target="tpu_custom_call" | custom-call | flops 1073741824 | bytes 8388608 | tf_op jit(solution)/shard_map/pallas_call | solution.py:41
  24.9 3.8 %shard_map.97 = (bf16[256,1024]{1,0:T(8,128)(2,1)S(1)}, bf16[1536,1024]{1,0:T(8,128)(2,1)S(1)}, bf16[256,1024]{1,0:T(8,128)(2,1)S(1)}, bf16[256,1024]{1,0:T(8,128)(2,1)}) custom-call(f32[256,1024]{1,0:T(8,128)S(1)} %get-tuple-element.33.up, f32[256,1024]{1,0:T(8,128)S(1)} %get-tuple-element.34.pre, bf16[1792,256]{1,0:T(8,128)(2,1)S(1)} %get-tuple-element.31.wk, ...), custom_call_target="tpu_custom_call" | custom-call | flops 3221225472 | bytes 8388608 | tf_op jit(solution)/shard_map/pallas_call | solution.py:41
  28.7 0.5 collective-permute-start.2
  29.2 4.0 %collective-permute-start.3 = (bf16[256,1024]{1,0:T(8,128)(2,1)S(1)}, bf16[256,1024]{1,0:T(8,128)(2,1)S(1)}, u32[]{:S(2)}, u32[]{:S(2)}) collective-permute-start(bf16[256,1024]{1,0:T(8,128)(2,1)S(1)} %get-tuple-element.39), channel_id=1, source_target_pairs={{0,15},{1,0},{2,1},{3,2},{4,3},{5,4},{6,5},{7,6},{8,7},{9,8},{10,9... | collective-permute-start | bytes 1572872 | tf_op jit(solution)/shard_map/ppermute | solution.py:231
  33.2 0.8 %shard_map.100 = (bf16[256,512]{1,0:T(8,128)(2,1)S(1)}, f32[256,512]{1,0:T(8,128)S(1)}, bf16[256,512]{1,0:T(8,128)(2,1)S(1)}, f32[256,512]{1,0:T(8,128)S(1)}) custom-call(s32[4]{0:T(128)S(1)} %pad_add_fusion.me, f32[512,1024]{1,0:T(8,128)S(1)} %get-tuple-element.40.keep, bf16[512,1024]{1,0:T(8,128)(2,1)S(1)} %collective-permute-done.4.got), custom_call_target="tpu_custom_call" | custom-call | flops 1048576 | bytes 8388608 | tf_op jit(solution)/shard_map/pallas_call | solution.py:41
  34.1 15.3 %collective-permute-done.5.refs_1_ = bf16[256,512]{1,0:T(8,128)(2,1)S(1)} collective-permute-done((bf16[256,512]{1,0:T(8,128)(2,1)S(1)}, bf16[256,512]{1,0:T(8,128)(2,1)S(1)}, u32[]{:S(2)}, u32[]{:S(2)}) %collective-permute-start.5) | collective-permute-done | bytes 262176 | tf_op jit(solution)/shard_map/ppermute | solution.py:234
  49.4 0.6 shard_map.101
  50.0 0.8 %collective-permute-start.7 = (bf16[128,512]{1,0:T(8,128)(2,1)S(1)}, bf16[128,512]{1,0:T(8,128)(2,1)S(1)}, u32[]{:S(2)}, u32[]{:S(2)}) collective-permute-start(bf16[128,512]{1,0:T(8,128)(2,1)S(1)} %get-tuple-element.47), channel_id=1, source_target_pairs={{0,4},{1,5},{2,6},{3,7},{4,0},{5,1},{6,2},{7,3},{8,12},{9,13},{10,... | collective-permute-start | bytes 393224 | tf_op jit(solution)/shard_map/ppermute | solution.py:234
  50.8 2.6 %collective-permute-start.8 = (bf16[128,512]{1,0:T(8,128)(2,1)S(1)}, bf16[128,512]{1,0:T(8,128)(2,1)S(1)}, u32[]{:S(2)}, u32[]{:S(2)}) collective-permute-start(bf16[128,512]{1,0:T(8,128)(2,1)S(1)} %get-tuple-element.49), channel_id=1, source_target_pairs={{0,8},{1,9},{2,10},{3,11},{4,12},{5,13},{6,14},{7,15},{8,0},{9,1},... | collective-permute-start | bytes 393224 | tf_op jit(solution)/shard_map/ppermute | solution.py:234
  53.4 1.6 %shard_map.104 = f32[16,112]{1,0:T(8,128)S(1)} custom-call(bf16[256,1024]{1,0:T(8,128)(2,1)S(1)} %get-tuple-element.36.grad, bf16[256,1024]{1,0:T(8,128)(2,1)S(1)} %copy-done.2, bf16[1536,1024]{1,0:T(8,128)(2,1)S(1)} %get-tuple-element.54.rows), custom_call_target="tpu_custom_call" | custom-call | flops 1073741824 | bytes 8388608 | tf_op jit(solution)/shard_map/pallas_call | solution.py:41
  55.0 1.2 %collective-permute-done.11 = f32[16,112]{1,0:T(8,128)S(1)} collective-permute-done((f32[16,112]{1,0:T(8,128)S(1)}, f32[16,112]{1,0:T(8,128)S(1)}, u32[]{:S(2)}, u32[]{:S(2)}) %collective-permute-start.11) | collective-permute-done | bytes 7200 | tf_op jit(solution)/shard_map/ppermute | solution.py:234
  56.2 0.4 collective-permute-start.12
  56.6 3.2 %collective-permute-done.12 = f32[16,112]{1,0:T(8,128)S(1)} collective-permute-done((f32[16,112]{1,0:T(8,128)S(1)}, f32[16,112]{1,0:T(8,128)S(1)}, u32[]{:S(2)}, u32[]{:S(2)}) %collective-permute-start.12) | collective-permute-done | bytes 7200 | tf_op jit(solution)/shard_map/ppermute | solution.py:234
  59.8 0.3 collective-permute-start.13
  60.2 4.2 %collective-permute-done.13 = f32[16,112]{1,0:T(8,128)S(1)} collective-permute-done((f32[16,112]{1,0:T(8,128)S(1)}, f32[16,112]{1,0:T(8,128)S(1)}, u32[]{:S(2)}, u32[]{:S(2)}) %collective-permute-start.13) | collective-permute-done | bytes 7200 | tf_op jit(solution)/shard_map/ppermute | solution.py:234
  64.4 1.2 %shard_map.102 = (bf16[64,512]{1,0:T(8,128)(2,1)}, f32[64,512]{1,0:T(8,128)S(1)}, bf16[64,512]{1,0:T(8,128)(2,1)}, f32[64,512]{1,0:T(8,128)S(1)}) custom-call(s32[4]{0:T(128)S(1)} %pad_add_fusion.me, f32[128,512]{1,0:T(8,128)S(1)} %get-tuple-element.46.refs_0_, bf16[128,512]{1,0:T(8,128)(2,1)S(1)} %collective-permute-done.7.refs_1_, ...), custom_call_target="tpu_custom_call" | custom-call | flops 1048576 | bytes 8388608 | tf_op jit(solution)/shard_map/pallas_call | solution.py:41
  65.6 0.8 %collective-permute-start.9 = (bf16[64,512]{1,0:T(8,128)(2,1)}, bf16[64,512]{1,0:T(8,128)(2,1)S(1)}, u32[]{:S(2)}, u32[]{:S(2)}) collective-permute-start(bf16[64,512]{1,0:T(8,128)(2,1)} %get-tuple-element.51), channel_id=1, source_target_pairs={{0,8},{1,9},{2,10},{3,11},{4,12},{5,13},{6,14},{7,15},{8,0},{9,1},... | collective-permute-start | bytes 196616 | tf_op jit(solution)/shard_map/ppermute | solution.py:234
  66.4 1.6 %collective-permute-start.10 = (bf16[64,512]{1,0:T(8,128)(2,1)}, bf16[64,512]{1,0:T(8,128)(2,1)S(1)}, u32[]{:S(2)}, u32[]{:S(2)}) collective-permute-start(bf16[64,512]{1,0:T(8,128)(2,1)} %get-tuple-element.53), channel_id=1, source_target_pairs={{0,2},{1,3},{2,0},{3,1},{4,6},{5,7},{6,4},{7,5},{8,10},{9,11},{10,... | collective-permute-start | bytes 196616 | tf_op jit(solution)/shard_map/ppermute | solution.py:234
  68.0 1.2 %shard_map.98.inner = f32[256,1024]{1,0:T(8,128)S(1)} custom-call(bf16[256,1024]{1,0:T(8,128)(2,1)S(1)} %get-tuple-element.36.grad, bf16[1536,1024]{1,0:T(8,128)(2,1)S(1)} %get-tuple-element.37.terms, bf16[1792,256]{1,0:T(8,128)(2,1)S(1)} %get-tuple-element.31.wk, s32[8,256]{1,0:T(8,128)S(1)} %get-tuple-element.35.sources, bf16[256,1024]{1,0:T(8,128)(2,1)S(1)} %copy-done), custom_call_target="tpu_custom_call" | custom-call | flops 1073741824 | bytes 8388608 | tf_op jit(solution)/shard_map/pallas_call | solution.py:41
  69.3 0.6 copy.11
  69.9 0.9 %shard_map.99 = bf16[256,1024]{1,0:T(8,128)(2,1)} custom-call(f32[256,1024]{1,0:T(8,128)S(1)} %shard_map.98.inner, bf16[256,1024]{1,0:T(8,128)(2,1)S(1)} %collective-permute-done.2.first, bf16[256,1024]{1,0:T(8,128)(2,1)S(1)} %collective-permute-done.3.second), custom_call_target="tpu_custom_call" | custom-call | flops 1048576 | bytes 8388608 | tf_op jit(solution)/shard_map/pallas_call | solution.py:41
  70.9 0.7 collective-permute-done.9.got_a
  71.6 0.7 %shard_map.103 = f32[64,1024]{1,0:T(8,128)} custom-call(f32[64,512]{1,0:T(8,128)S(1)} %get-tuple-element.50.kept_a, bf16[64,512]{1,0:T(8,128)(2,1)S(1)} %collective-permute-done.9.got_a, f32[64,512]{1,0:T(8,128)S(1)} %get-tuple-element.52.kept_b, bf16[64,512]{1,0:T(8,128)(2,1)S(1)} %collective-permute-done.10.got_b), custom_call_target="tpu_custom_call" | custom-call | flops 1048576 | bytes 8388608 | tf_op jit(solution)/shard_map/pallas_call | solution.py:41
  (33 shorter events, 0.5 us)
Async XLA Ops:
  0.6 17.1 %copy-start = (bf16[256,1024]{1,0:T(8,128)(2,1)S(1)}, bf16[256,1024]{1,0:T(8,128)(2,1)}, u32[]{:S(2)}) copy-start(bf16[256,1024]{1,0:T(8,128)(2,1)} %cot.5) | copy-start | bytes 1572868
  0.6 13.1 %collective-permute-start.1 = (bf16[256,1024]{1,0:T(8,128)(2,1)}, bf16[256,1024]{1,0:T(8,128)(2,1)S(1)}, u32[]{:S(2)}, u32[]{:S(2)}) collective-permute-start(bf16[256,1024]{1,0:T(8,128)(2,1)} %x.3), channel_id=1, source_target_pairs={{0,15},{1,0},{2,1},{3,2},{4,3},{5,4},{6,5},{7,6},{8,7},{9,8},{10,9... | collective-permute-start | bytes 1572872 | tf_op jit(solution)/shard_map/ppermute | solution.py:231
  6.2 11.5 %collective-permute-start = (bf16[256,1024]{1,0:T(8,128)(2,1)}, bf16[256,1024]{1,0:T(8,128)(2,1)S(1)}, u32[]{:S(2)}, u32[]{:S(2)}) collective-permute-start(bf16[256,1024]{1,0:T(8,128)(2,1)} %x.3), channel_id=1, source_target_pairs={{0,1},{1,2},{2,3},{3,4},{4,5},{5,6},{6,7},{7,8},{8,9},{9,10},{10,1... | collective-permute-start | bytes 1572872 | tf_op jit(solution)/shard_map/ppermute | solution.py:231
  6.2 1.0 %copy-start.1 = (bf16[256,1024]{1,0:T(8,128)(2,1)S(1)}, bf16[256,1024]{1,0:T(8,128)(2,1)}, u32[]{:S(2)}) copy-start(bf16[256,1024]{1,0:T(8,128)(2,1)} %x.3) | copy-start | bytes 1572868
  7.3 0.7 %copy-start.4 = (bf16[7,16,16]{2,1,0:T(8,128)(2,1)S(1)}, bf16[7,16,16]{2,1,0:T(8,128)(2,1)}, u32[]{:S(2)}) copy-start(bf16[7,16,16]{2,1,0:T(8,128)(2,1)} %conv_hbm.1) | copy-start | bytes 10756
  8.0 0.7 copy-start.5
  8.7 0.7 copy-start.6
  9.4 0.7 copy-start.7
  10.1 7.6 %copy-start.2 = (bf16[256,1024]{1,0:T(8,128)(2,1)S(1)}, bf16[256,1024]{1,0:T(8,128)(2,1)}, u32[]{:S(2)}) copy-start(bf16[256,1024]{1,0:T(8,128)(2,1)} %x.3) | copy-start | bytes 1572868
  17.7 5.3 %copy-start.3 = (bf16[1024,1024]{1,0:T(8,128)(2,1)S(1)}, bf16[1024,1024]{1,0:T(8,128)(2,1)}, u32[]{:S(2)}) copy-start(bf16[1024,1024]{1,0:T(8,128)(2,1)} %mix_hbm.1) | copy-start | bytes 6291460
  22.9 10.3 %collective-permute-start.4 = (bf16[512,1024]{1,0:T(8,128)(2,1)S(1)}, bf16[512,1024]{1,0:T(8,128)(2,1)S(1)}, u32[]{:S(2)}, u32[]{:S(2)}) collective-permute-start(bf16[512,1024]{1,0:T(8,128)(2,1)S(1)} %get-tuple-element.41), channel_id=1, source_target_pairs={{0,1},{1,0},{2,3},{3,2},{4,5},{5,4},{6,7},{7,6},{8,9},{9,8},{10,11... | collective-permute-start | bytes 3145736 | tf_op jit(solution)/shard_map/ppermute | solution.py:234
  28.7 41.2 %collective-permute-start.2 = (bf16[256,1024]{1,0:T(8,128)(2,1)}, bf16[256,1024]{1,0:T(8,128)(2,1)S(1)}, u32[]{:S(2)}, u32[]{:S(2)}) collective-permute-start(bf16[256,1024]{1,0:T(8,128)(2,1)} %get-tuple-element.38), channel_id=1, source_target_pairs={{0,1},{1,2},{2,3},{3,4},{4,5},{5,6},{6,7},{7,8},{8,9},{9,10},{10,1... | collective-permute-start | bytes 1572872 | tf_op jit(solution)/shard_map/ppermute | solution.py:231
  29.2 40.7 %collective-permute-start.3 = (bf16[256,1024]{1,0:T(8,128)(2,1)S(1)}, bf16[256,1024]{1,0:T(8,128)(2,1)S(1)}, u32[]{:S(2)}, u32[]{:S(2)}) collective-permute-start(bf16[256,1024]{1,0:T(8,128)(2,1)S(1)} %get-tuple-element.39), channel_id=1, source_target_pairs={{0,15},{1,0},{2,1},{3,2},{4,3},{5,4},{6,5},{7,6},{8,7},{9,8},{10,9... | collective-permute-start | bytes 1572872 | tf_op jit(solution)/shard_map/ppermute | solution.py:231
  34.0 15.4 %collective-permute-start.5 = (bf16[256,512]{1,0:T(8,128)(2,1)S(1)}, bf16[256,512]{1,0:T(8,128)(2,1)S(1)}, u32[]{:S(2)}, u32[]{:S(2)}) collective-permute-start(bf16[256,512]{1,0:T(8,128)(2,1)S(1)} %get-tuple-element.43), channel_id=1, source_target_pairs={{0,2},{1,3},{2,0},{3,1},{4,6},{5,7},{6,4},{7,5},{8,10},{9,11},{10,... | collective-permute-start | bytes 786440 | tf_op jit(solution)/shard_map/ppermute | solution.py:234
  34.0 15.4 %collective-permute-start.6 = (bf16[256,512]{1,0:T(8,128)(2,1)S(1)}, bf16[256,512]{1,0:T(8,128)(2,1)S(1)}, u32[]{:S(2)}, u32[]{:S(2)}) collective-permute-start(bf16[256,512]{1,0:T(8,128)(2,1)S(1)} %get-tuple-element.45), channel_id=1, source_target_pairs={{0,4},{1,5},{2,6},{3,7},{4,0},{5,1},{6,2},{7,3},{8,12},{9,13},{10,... | collective-permute-start | bytes 786440 | tf_op jit(solution)/shard_map/ppermute | solution.py:234
  50.0 14.4 %collective-permute-start.7 = (bf16[128,512]{1,0:T(8,128)(2,1)S(1)}, bf16[128,512]{1,0:T(8,128)(2,1)S(1)}, u32[]{:S(2)}, u32[]{:S(2)}) collective-permute-start(bf16[128,512]{1,0:T(8,128)(2,1)S(1)} %get-tuple-element.47), channel_id=1, source_target_pairs={{0,4},{1,5},{2,6},{3,7},{4,0},{5,1},{6,2},{7,3},{8,12},{9,13},{10,... | collective-permute-start | bytes 393224 | tf_op jit(solution)/shard_map/ppermute | solution.py:234
  50.8 13.6 %collective-permute-start.8 = (bf16[128,512]{1,0:T(8,128)(2,1)S(1)}, bf16[128,512]{1,0:T(8,128)(2,1)S(1)}, u32[]{:S(2)}, u32[]{:S(2)}) collective-permute-start(bf16[128,512]{1,0:T(8,128)(2,1)S(1)} %get-tuple-element.49), channel_id=1, source_target_pairs={{0,8},{1,9},{2,10},{3,11},{4,12},{5,13},{6,14},{7,15},{8,0},{9,1},... | collective-permute-start | bytes 393224 | tf_op jit(solution)/shard_map/ppermute | solution.py:234
  55.0 1.2 %collective-permute-start.11 = (f32[16,112]{1,0:T(8,128)S(1)}, f32[16,112]{1,0:T(8,128)S(1)}, u32[]{:S(2)}, u32[]{:S(2)}) collective-permute-start(f32[16,112]{1,0:T(8,128)S(1)} %shard_map.104), channel_id=1, source_target_pairs={{0,1},{1,0},{2,3},{3,2},{4,5},{5,4},{6,7},{7,6},{8,9},{9,8},{10,11... | collective-permute-start | bytes 21512 | tf_op jit(solution)/shard_map/ppermute | solution.py:234
  56.2 3.7 %collective-permute-start.12 = (f32[16,112]{1,0:T(8,128)S(1)}, f32[16,112]{1,0:T(8,128)S(1)}, u32[]{:S(2)}, u32[]{:S(2)}) collective-permute-start(f32[16,112]{1,0:T(8,128)S(1)} %add.12), channel_id=1, source_target_pairs={{0,4},{1,5},{2,6},{3,7},{4,0},{5,1},{6,2},{7,3},{8,12},{9,13},{10,... | collective-permute-start | bytes 21512 | tf_op jit(solution)/shard_map/ppermute | solution.py:234
  59.8 4.5 %collective-permute-start.13 = (f32[16,112]{1,0:T(8,128)S(1)}, f32[16,112]{1,0:T(8,128)S(1)}, u32[]{:S(2)}, u32[]{:S(2)}) collective-permute-start(f32[16,112]{1,0:T(8,128)S(1)} %add.13), channel_id=1, source_target_pairs={{0,8},{1,9},{2,10},{3,11},{4,12},{5,13},{6,14},{7,15},{8,0},{9,1},... | collective-permute-start | bytes 21512 | tf_op jit(solution)/shard_map/ppermute | solution.py:234
  64.4 4.8 %collective-permute-start.14 = (f32[16,112]{1,0:T(8,128)S(1)}, f32[16,112]{1,0:T(8,128)S(1)}, u32[]{:S(2)}, u32[]{:S(2)}) collective-permute-start(f32[16,112]{1,0:T(8,128)S(1)} %add.14), channel_id=1, source_target_pairs={{0,2},{1,3},{2,0},{3,1},{4,6},{5,7},{6,4},{7,5},{8,10},{9,11},{10,... | collective-permute-start | bytes 21512 | tf_op jit(solution)/shard_map/ppermute | solution.py:234
  65.6 6.0 %collective-permute-start.9 = (bf16[64,512]{1,0:T(8,128)(2,1)}, bf16[64,512]{1,0:T(8,128)(2,1)S(1)}, u32[]{:S(2)}, u32[]{:S(2)}) collective-permute-start(bf16[64,512]{1,0:T(8,128)(2,1)} %get-tuple-element.51), channel_id=1, source_target_pairs={{0,8},{1,9},{2,10},{3,11},{4,12},{5,13},{6,14},{7,15},{8,0},{9,1},... | collective-permute-start | bytes 196616 | tf_op jit(solution)/shard_map/ppermute | solution.py:234
  66.4 5.2 %collective-permute-start.10 = (bf16[64,512]{1,0:T(8,128)(2,1)}, bf16[64,512]{1,0:T(8,128)(2,1)S(1)}, u32[]{:S(2)}, u32[]{:S(2)}) collective-permute-start(bf16[64,512]{1,0:T(8,128)(2,1)} %get-tuple-element.53), channel_id=1, source_target_pairs={{0,2},{1,3},{2,0},{3,1},{4,6},{5,7},{6,4},{7,5},{8,10},{9,11},{10,... | collective-permute-start | bytes 196616 | tf_op jit(solution)/shard_map/ppermute | solution.py:234

commit v2 on v1

--- a/solution.py
+++ b/solution.py
@@ -140,17 +140,38 @@
     )
 
 
-def terms_kernel(up, pre, wk, sources, grad, terms, low, high, back_sel):
-    n, width = pre.shape
+def weights_kernel(channels, scale, up, pre, x, rows, grad, conv):
+    n, width = grad.shape
+    taps = rows.shape[0] // n + 1
+    acc = [jnp.zeros((WIDE, WIDE), f32) for _ in range(taps)]
+    for c in range(0, width, WIDE):
+        v = pre[:, c : c + WIDE]
+        t = gelu_tanh(v)
+        slope = 0.5 * (1.0 + t) + (0.5 * TANH_SCALE) * v * (1.0 - t * t) * (1.0 + (3 * TANH_CUBE) * (v * v))
+        g = up[:, c : c + WIDE] * slope
+        grad[:, c : c + WIDE] = g.astype(bf16)
+        g_t = g.T.astype(bf16)
+        acc[0] += mm(g_t, x[:, c : c + WIDE])
+        for tap in range(1, taps):
+            acc[tap] += mm(g_t, rows[(tap - 1) * n : tap * n, c : c + WIDE])
+    same = iota((WIDE, WIDE), 0) // channels == iota((WIDE, WIDE), 1) // channels
+    conv[...] = jnp.zeros(conv.shape, f32)
+    fold = jnp.where(iota((channels, WIDE), 1) % channels == iota((channels, WIDE), 0), 1.0, 0.0)
+    for tap in range(taps):
+        block = jnp.where(same, acc[tap], 0.0)
+        block = jnp.sum(block.reshape(WIDE // channels, channels, WIDE), axis=0)
+        conv[:, tap * channels : (tap + 1) * channels] = (
+            contract(fold, block, 1, 1, precision=lax.Precision.HIGHEST) * scale
+        )
+
+
+def terms_kernel(grad, wk, sources, terms, low, high, back_sel):
+    n, width = grad.shape
     taps = wk.shape[0] // WIDE
     back_sel[:ROW, :] = select_rows(sources, 0, ROW, taps)
     back_sel[ROW:, :] = select_rows(sources, ROW + n, ROW, taps)
     for c in range(0, width, WIDE):
-        v = pre[:, c : c + WIDE]
-        t = gelu_tanh(v)
-        slope = 0.5 * (1.0 + t) + (0.5 * TANH_SCALE) * v * (1.0 - t * t) * (1.0 + (3 * TANH_CUBE) * (v * v))
-        g = (up[:, c : c + WIDE] * slope).astype(bf16)
-        grad[:, c : c + WIDE] = g
+        g = grad[:, c : c + WIDE]
         for tap in range(1, taps):
             terms[(tap - 1) * n : tap * n, c : c + WIDE] = contract(
                 g, wk[tap * WIDE : (tap + 1) * WIDE, :], 1, 1
@@ -160,25 +181,6 @@
         high[:, c : c + WIDE] = both[ROW:]
 
 
-def weights_kernel(channels, scale, grad, x, rows, conv):
-    n, width = grad.shape
-    taps = rows.shape[0] // n + 1
-    acc = [jnp.zeros((WIDE, WIDE), f32) for _ in range(taps)]
-    for c in range(0, width, WIDE):
-        g_t = grad[:, c : c + WIDE].astype(f32).T.astype(bf16)
-        acc[0] += mm(g_t, x[:, c : c + WIDE])
-        for tap in range(1, taps):
-            acc[tap] += mm(g_t, rows[(tap - 1) * n : tap * n, c : c + WIDE])
-    same = iota((WIDE, WIDE), 0) // channels == iota((WIDE, WIDE), 1) // channels
-    fold = jnp.where(iota((channels, WIDE), 1) % channels == iota((channels, WIDE), 0), 1.0, 0.0)
-    for tap in range(taps):
-        block = jnp.where(same, acc[tap], 0.0)
-        block = jnp.sum(block.reshape(WIDE // channels, channels, WIDE), axis=0)
-        conv[:, tap * channels : (tap + 1) * channels] = (
-            contract(fold, block, 1, 1, precision=lax.Precision.HIGHEST) * scale
-        )
-
-
 def inner_kernel(grad, terms, wk, sources, cot, inner):
     n, width = grad.shape
     taps = wk.shape[0] // WIDE
@@ -188,34 +190,49 @@
         inner[:, c : c + WIDE] = acc + mm(sel, terms[:, c : c + WIDE])
 
 
-def halve(share, bit, skip, kept, got, send, keep):
+def halve(share, bit, skip, kept, got, got_at, send, send_at, keep):
     for q in range(kept.shape[0] // share // 2):
         base = ((q >> skip) << (skip + 1)) | (q & ((1 << skip) - 1))
-        for value, out in ((1 - bit, send), (bit, keep)):
-            at = pl.ds(pl.multiple_of((base + (value << skip)) * share, share), share)
-            out[q * share : (q + 1) * share, :] = (kept[at, :] + got[at, :].astype(f32)).astype(out.dtype)
+        for value, out, out_at in ((1 - bit, send, send_at), (bit, keep, 0)):
+            at = pl.multiple_of((base + (value << skip)) * share, share)
+            came = got[pl.ds(pl.multiple_of(at + got_at, 16), share), :].astype(f32)
+            out[out_at + q * share : out_at + (q + 1) * share, :] = (
+                kept[pl.ds(at, share), :] + came
+            ).astype(out.dtype)
 
 
 def split_kernel(share, where, me, keep, got, *outs):
     half = keep.shape[1] // 2
     for k, (bit, skip) in enumerate(where):
         cols = slice(k * half, (k + 1) * half)
-        halve(share, me[bit], skip, keep.at[:, cols], got.at[:, cols], outs[2 * k], outs[2 * k + 1])
-
-
-def merge_kernel(share, where, me, *refs):
-    for k, (bit, skip) in enumerate(where):
-        halve(share, me[bit], skip, refs[2 * k], refs[2 * k + 1], refs[4 + 2 * k], refs[5 + 2 * k])
-
-
-def finish_kernel(scale, kept_a, got_a, kept_b, got_b, out):
+        halve(share, me[bit], skip, keep.at[:, cols], got.at[:, cols], 0, outs[2 * k], 0, outs[2 * k + 1])
+
+
+def parcel(ref):
+    return ref[:16, :128].astype(f32) + ref[:16, 128:256].astype(f32)
+
+
+def merge_kernel(share, where, first, me, kept_a, got_a, kept_b, got_b, conv, conv_got, send_a, keep_a, send_b, keep_b, conv_out):
+    whole = conv[...] + (conv_got[...] if first else parcel(got_a))
+    high = whole.astype(bf16)
+    low = (whole - high.astype(f32)).astype(bf16)
+    conv_out[...] = high.astype(f32) + low.astype(f32)
+    send_a[:16, :] = jnp.zeros((16, send_a.shape[1]), bf16)
+    send_a[:16, :128] = high
+    send_a[:16, 128:256] = low
+    (bit_a, skip_a), (bit_b, skip_b) = where
+    halve(share, me[bit_a], skip_a, kept_a, got_a, 0 if first else 16, send_a, 16, keep_a)
+    halve(share, me[bit_b], skip_b, kept_b, got_b, 0, send_b, 0, keep_b)
+
+
+def last_kernel(scale, channels, kept_a, got_a, kept_b, got_b, conv, inner, first, second, mix_out, conv_out, grad_out):
     half = kept_a.shape[1]
-    out[:, :half] = (kept_a[...] + got_a[...].astype(f32)) * scale
-    out[:, half:] = (kept_b[...] + got_b[...].astype(f32)) * scale
-
-
-def total_kernel(inner, first, second, out):
-    out[...] = (inner[...] + first[...].astype(f32) + second[...].astype(f32)).astype(bf16)
+    mix_out[:, :half] = (kept_a[...] + got_a[16:, :].astype(f32)) * scale
+    mix_out[:, half:] = (kept_b[...] + got_b[...].astype(f32)) * scale
+    whole = conv[...] + parcel(got_a)
+    for tap in range(conv_out.shape[0]):
+        conv_out[tap] = whole[:, tap * channels : (tap + 1) * channels]
+    grad_out[...] = (inner[...] + first[...].astype(f32) + second[...].astype(f32)).astype(bf16)
 
 
 def shards(columns_in, cotangent, conv_weight, mix_weight, neighbours, rotations, pentagons):
@@ -305,6 +322,28 @@
         got,
         scalars=1,
     )
+    grad, conv = call(
+        functools.partial(weights_kernel, channels, 1.0 / float(total_cols * levels) ** 0.5),
+        [((n, width), bf16), ((channels, 128), f32)],
+        2 << 30,
+        up,
+        pre,
+        columns_in,
+        rows,
+    )
+    terms, to_low, to_high = call(
+        terms_kernel,
+        [((pairs, width), bf16), ((ROW, width), bf16), ((ROW, width), bf16)],
+        3 << 30,
+        grad,
+        wk,
+        sources,
+        scratch=[pltpu.VMEM((2 * ROW, pairs), bf16)],
+    )
+    conv = conv + swap(conv, 0)
+    conv_got = swap(conv, 1)
+    from_below = ring(to_high, 1)
+    from_above = ring(to_low, -1)
     for stage in range(1, bits):
         gots = []
         for k in (0, 1):
@@ -312,45 +351,35 @@
         state = [parts[1], gots[0], parts[3], gots[1]]
         if stage < bits - 1:
             rows_left //= 2
-            parts = call(
-                functools.partial(merge_kernel, share, places(stage)),
-                [((rows_left, half), bf16), ((rows_left, half), f32)] * 2,
+            *parts, conv = call(
+                functools.partial(merge_kernel, share, places(stage), stage == 1),
+                [
+                    ((rows_left + 16, half), bf16),
+                    ((rows_left, half), f32),
+                    ((rows_left, half), bf16),
+                    ((rows_left, half), f32),
+                    ((channels, 128), f32),
+                ],
                 1 << 20,
                 mine,
                 *state,
+                conv,
+                conv_got,
                 scalars=1,
             )
-    (grad_mix,) = call(
-        functools.partial(finish_kernel, 1.0 / float(total_cols) ** 0.5),
-        [((share, width), f32)],
+    (inner,) = call(
+        inner_kernel, [((n, width), f32)], 1 << 30, grad, terms, wk, sources, cotangent
+    )
+    grad_mix, grad_conv, grad_input = call(
+        functools.partial(last_kernel, 1.0 / float(total_cols) ** 0.5, channels),
+        [((share, width), f32), ((taps, channels, channels), f32), ((n, width), bf16)],
         1 << 20,
         *state,
-    )
-    grad, terms, to_low, to_high = call(
-        terms_kernel,
-        [((n, width), bf16), ((pairs, width), bf16), ((ROW, width), bf16), ((ROW, width), bf16)],
-        3 << 30,
-        up,
-        pre,
-        wk,
-        sources,
-        scratch=[pltpu.VMEM((2 * ROW, pairs), bf16)],
-    )
-    from_below = ring(to_high, 1)
-    from_above = ring(to_low, -1)
-    (conv,) = call(
-        functools.partial(weights_kernel, channels, 1.0 / float(total_cols * levels) ** 0.5),
-        [((channels, taps * channels), f32)],
-        1 << 30,
-        grad,
-        columns_in,
-        rows,
-    )
-    for bit in [0] + orders[1]:
-        conv = conv + swap(conv, bit)
-    grad_conv = conv.reshape(channels, taps, channels).transpose(1, 0, 2)
-    (inner,) = call(inner_kernel, [((n, width), f32)], 1 << 30, grad, terms, wk, sources, cotangent)
-    (grad_input,) = call(total_kernel, [((n, width), bf16)], 1 << 20, inner, from_below, from_above)
+        conv,
+        inner,
+        from_below,
+        from_above,
+    )
     return grad_input, grad_mix, grad_conv
 
 

time: 72.6 us -> 67.6 us (0.931)
  waiting for transfers between devices: 28.5 us -> 23.7 us
  starting transfers between devices: 16.7 us -> 19.3 us
  Pallas kernels: 21.5 us -> 19.5 us
    ppermute x11 -> x9, waiting for transfers between devices: 24.6 us -> 19.7 us  [swap(): lax.ppermute(value, 'space', [(i, i ^ 1 << bit) for i in range(devices)])]
    ppermute x11 -> x9, starting transfers between devices: 6.77 us -> 9.26 us  [swap(): lax.ppermute(value, 'space', [(i, i ^ 1 << bit) for i in range(devices)])]
    pallas_call x11 -> x10, Pallas kernels: 21.5 us -> 19.5 us  [call(): pl.pallas_call(body, out_shape=[jax.ShapeDtypeStruct(s, d) for s, d in ou...]
    unnamed x17 -> x16, local copies, waits for them, and re-layouts: 4.49 us -> 3.85 us
  transfers between devices with their start and end apart: 15 -> 13, of which waited for: 6 -> 5; matrix products, arithmetic and copies ran while one was open for 1% -> 0% of each run, Pallas kernels for 22% -> 20%
where the time goes in v2:
time: 67.6 us; the launch traced here: 67.2 us
  waiting for transfers between devices  23.7 us (35%)
  Pallas kernels  19.5 us (29%)
  starting transfers between devices  19.3 us (29%)
  local copies, waits for them, and re-layouts  3.85 us (6%)
  between operations  0.78 us (1%)
    ppermute x9, waiting for transfers between devices, swap(): lax.ppermute(value, 'space', [(i, i ^ 1 << bit) for i in range(devices)])  19.7 us
    pallas_call x10, Pallas kernels, call(): pl.pallas_call(body, out_shape=[jax.ShapeDtypeStruct(s, d) for s, d in ou...  19.5 us
    ppermute x4, starting transfers between devices, ring(): lax.ppermute(value, 'space', [(i, (i + by) % devices) for i in range(devi...  10 us
    ppermute x9, starting transfers between devices, swap(): lax.ppermute(value, 'space', [(i, i ^ 1 << bit) for i in range(devices)])  9.26 us
    ppermute x4, waiting for transfers between devices, ring(): lax.ppermute(value, 'space', [(i, (i + by) % devices) for i in range(devi...  3.99 us
    unnamed x16, local copies, waits for them, and re-layouts  3.85 us
  transfers between devices with their start and end apart: 13, of which 5 were waited for; matrix products, arithmetic and copies ran while one was open for 0% of the time, Pallas kernels for 20%

profile of v2, /device:TPU:0, one launch (start us, length us, event | category | flops | bytes accessed | tf_op | source)
XLA Modules:
  0.0 67.2 jit_solution(6926931428001339425)
XLA Ops:
  0.6 5.5 %collective-permute-start.1 = (bf16[256,1024]{1,0:T(8,128)(2,1)}, bf16[256,1024]{1,0:T(8,128)(2,1)S(1)}, u32[]{:S(2)}, u32[]{:S(2)}) collective-permute-start(bf16[256,1024]{1,0:T(8,128)(2,1)} %x.3), channel_id=1, source_target_pairs={{0,15},{1,0},{2,1},{3,2},{4,3},{5,4},{6,5},{7,6},{8,7},{9,8},{10,9... | collective-permute-start | bytes 1572872 | tf_op jit(solution)/shard_map/ppermute | solution.py:248
  6.2 0.1 pad_add_fusion.1.place
  6.2 1.0 %copy-done.2 = bf16[256,1024]{1,0:T(8,128)(2,1)S(1)} copy-done((bf16[256,1024]{1,0:T(8,128)(2,1)S(1)}, bf16[256,1024]{1,0:T(8,128)(2,1)}, u32[]{:S(2)}) %copy-start.2) | copy-done | bytes 524312
  7.3 0.7 %copy-done.4 = bf16[7,16,16]{2,1,0:T(8,128)(2,1)S(1)} copy-done((bf16[7,16,16]{2,1,0:T(8,128)(2,1)S(1)}, bf16[7,16,16]{2,1,0:T(8,128)(2,1)}, u32[]{:S(2)}) %copy-start.4) | copy-done | bytes 3608
  8.0 0.7 %copy-done.5 = s32[256,7]{0,1:T(8,128)S(1)} copy-done((s32[256,7]{0,1:T(8,128)S(1)}, s32[256,7]{0,1:T(8,128)}, u32[]{:S(2)}) %copy-start.5) | copy-done | bytes 7192
  8.7 0.7 %copy-done.6 = s32[256]{0:T(256)S(1)} copy-done((s32[256]{0:T(256)S(1)}, s32[256]{0:T(256)}, u32[]{:S(2)}) %copy-start.6) | copy-done | bytes 1048
  9.4 0.7 %copy-done.7 = s32[256]{0:T(256)S(1)} copy-done((s32[256]{0:T(256)S(1)}, s32[256]{0:T(256)}, u32[]{:S(2)}) %copy-start.7) | copy-done | bytes 1048
  10.1 3.5 %shard_map.94 = (bf16[1536,512]{1,0:T(8,128)(2,1)S(1)}, s32[8,256]{1,0:T(8,128)S(1)}, bf16[1536,1024]{1,0:T(8,128)(2,1)S(1)}, bf16[1792,256]{1,0:T(8,128)(2,1)S(1)}) custom-call(s32[2]{0:T(128)S(1)} %pad_add_fusion.1.place, s32[7,256]{1,0:T(8,128)S(1)} %bitcast.8, s32[1,256]{1,0:T(1,128)S(1)} %bitcast.9, s32[1,256]{1,0:T(1,128)S(1)} %bitcast.10, ...), custom_call_target="tpu_custom_call" | custom-call | flops 1073741824 | bytes 8388608 | tf_op jit(solution)/shard_map/pallas_call | solution.py:41
  13.6 0.1 pad_add_fusion.me
  13.7 4.0 %collective-permute-done.low = bf16[256,1024]{1,0:T(8,128)(2,1)S(1)} collective-permute-done((bf16[256,1024]{1,0:T(8,128)(2,1)}, bf16[256,1024]{1,0:T(8,128)(2,1)S(1)}, u32[]{:S(2)}, u32[]{:S(2)}) %collective-permute-start) | collective-permute-done | bytes 524320 | tf_op jit(solution)/shard_map/ppermute | solution.py:248
  17.7 5.3 %shard_map.95 = (bf16[1536,1024]{1,0:T(8,128)(2,1)S(1)}, f32[256,1024]{1,0:T(8,128)S(1)}, bf16[1024,256]{1,0:T(8,128)(2,1)S(1)}, bf16[512,1024]{1,0:T(8,128)(2,1)S(1)}) custom-call(s32[4]{0:T(128)S(1)} %pad_add_fusion.me, bf16[256,1024]{1,0:T(8,128)(2,1)S(1)} %collective-permute-done.low, bf16[256,1024]{1,0:T(8,128)(2,1)S(1)} %collective-permute-done.1.high, ...), custom_call_target="tpu_custom_call" | custom-call | flops 3221225472 | bytes 8388608 | tf_op jit(solution)/shard_map/pallas_call | solution.py:41
  23.0 0.1 collective-permute-start.2
  23.1 1.9 %shard_map.96 = (f32[512,1024]{1,0:T(8,128)S(1)}, f32[256,1024]{1,0:T(8,128)S(1)}) custom-call(s32[4]{0:T(128)S(1)} %pad_add_fusion.me, bf16[1024,256]{1,0:T(8,128)(2,1)S(1)} %get-tuple-element.38.act_t, bf16[256,1024]{1,0:T(8,128)(2,1)S(1)} %copy-done, bf16[1024,1024]{1,0:T(8,128)(2,1)S(1)} %copy-done.1), custom_call_target="tpu_custom_call" | custom-call | flops 1073741824 | bytes 8388608 | tf_op jit(solution)/shard_map/pallas_call | solution.py:41
  24.9 1.9 %shard_map.98 = (bf16[256,1024]{1,0:T(8,128)(2,1)S(1)}, f32[16,128]{1,0:T(8,128)S(1)}) custom-call(f32[256,1024]{1,0:T(8,128)S(1)} %get-tuple-element.45.up, f32[256,1024]{1,0:T(8,128)S(1)} %get-tuple-element.46.pre, bf16[256,1024]{1,0:T(8,128)(2,1)S(1)} %copy-done.3, bf16[1536,1024]{1,0:T(8,128)(2,1)S(1)} %get-tuple-element.47.rows), custom_call_target="tpu_custom_call" | custom-call | flops 2147483648 | bytes 8388608 | tf_op jit(solution)/shard_map/pallas_call | solution.py:41
  26.9 2.7 %shard_map.101 = (bf16[1536,1024]{1,0:T(8,128)(2,1)S(1)}, bf16[256,1024]{1,0:T(8,128)(2,1)S(1)}, bf16[256,1024]{1,0:T(8,128)(2,1)S(1)}) custom-call(bf16[256,1024]{1,0:T(8,128)(2,1)S(1)} %get-tuple-element.59.grad, bf16[1792,256]{1,0:T(8,128)(2,1)S(1)} %get-tuple-element.37.wk, s32[8,256]{1,0:T(8,128)S(1)} %get-tuple-element.60.sources), custom_call_target="tpu_custom_call" | custom-call | flops 3221225472 | bytes 8388608 | tf_op jit(solution)/shard_map/pallas_call | solution.py:41
  29.6 0.5 collective-permute-start.11
  30.1 4.0 %collective-permute-start.12 = (bf16[256,1024]{1,0:T(8,128)(2,1)S(1)}, bf16[256,1024]{1,0:T(8,128)(2,1)S(1)}, u32[]{:S(2)}, u32[]{:S(2)}) collective-permute-start(bf16[256,1024]{1,0:T(8,128)(2,1)S(1)} %get-tuple-element.63), channel_id=1, source_target_pairs={{0,15},{1,0},{2,1},{3,2},{4,3},{5,4},{6,5},{7,6},{8,7},{9,8},{10,9... | collective-permute-start | bytes 1572872 | tf_op jit(solution)/shard_map/ppermute | solution.py:248
  34.1 0.7 %shard_map.97 = (bf16[256,512]{1,0:T(8,128)(2,1)S(1)}, f32[256,512]{1,0:T(8,128)S(1)}, bf16[256,512]{1,0:T(8,128)(2,1)S(1)}, f32[256,512]{1,0:T(8,128)S(1)}) custom-call(s32[4]{0:T(128)S(1)} %pad_add_fusion.me, f32[512,1024]{1,0:T(8,128)S(1)} %get-tuple-element.39.keep, bf16[512,1024]{1,0:T(8,128)(2,1)S(1)} %collective-permute-done.2.got), custom_call_target="tpu_custom_call" | custom-call | flops 1048576 | bytes 8388608 | tf_op jit(solution)/shard_map/pallas_call | solution.py:41
  34.8 0.1 collective-permute-start.3
  35.0 1.2 %collective-permute-done.5 = f32[16,128]{1,0:T(8,128)S(1)} collective-permute-done((f32[16,128]{1,0:T(8,128)S(1)}, f32[16,128]{1,0:T(8,128)S(1)}, u32[]{:S(2)}, u32[]{:S(2)}) %collective-permute-start.5) | collective-permute-done | bytes 8224 | tf_op jit(solution)/shard_map/ppermute | solution.py:251
  36.2 1.9 %collective-permute-start.6 = (f32[16,128]{1,0:T(8,128)S(1)}, f32[16,128]{1,0:T(8,128)S(1)}, u32[]{:S(2)}, u32[]{:S(2)}) collective-permute-start(f32[16,128]{1,0:T(8,128)S(1)} %add.3.conv), channel_id=1, source_target_pairs={{0,2},{1,3},{2,0},{3,1},{4,6},{5,7},{6,4},{7,5},{8,10},{9,11},{10,... | collective-permute-start | bytes 24584 | tf_op jit(solution)/shard_map/ppermute | solution.py:251
  38.0 12.4 %collective-permute-done.6.conv_got = f32[16,128]{1,0:T(8,128)S(1)} collective-permute-done((f32[16,128]{1,0:T(8,128)S(1)}, f32[16,128]{1,0:T(8,128)S(1)}, u32[]{:S(2)}, u32[]{:S(2)}) %collective-permute-start.6) | collective-permute-done | bytes 8224 | tf_op jit(solution)/shard_map/ppermute | solution.py:251
  50.4 0.6 shard_map.99
  51.1 0.6 collective-permute-start.7
  51.6 2.6 %collective-permute-start.8 = (bf16[128,512]{1,0:T(8,128)(2,1)S(1)}, bf16[128,512]{1,0:T(8,128)(2,1)S(1)}, u32[]{:S(2)}, u32[]{:S(2)}) collective-permute-start(bf16[128,512]{1,0:T(8,128)(2,1)S(1)} %get-tuple-element.52), channel_id=1, source_target_pairs={{0,8},{1,9},{2,10},{3,11},{4,12},{5,13},{6,14},{7,15},{8,0},{9,1},... | collective-permute-start | bytes 393224 | tf_op jit(solution)/shard_map/ppermute | solution.py:251
  54.2 3.5 %collective-permute-done.8.got_b = bf16[128,512]{1,0:T(8,128)(2,1)S(1)} collective-permute-done((bf16[128,512]{1,0:T(8,128)(2,1)S(1)}, bf16[128,512]{1,0:T(8,128)(2,1)S(1)}, u32[]{:S(2)}, u32[]{:S(2)}) %collective-permute-start.8) | collective-permute-done | bytes 131104 | tf_op jit(solution)/shard_map/ppermute | solution.py:251
  57.7 0.6 shard_map.100
  58.3 1.6 %collective-permute-start.10 = (bf16[64,512]{1,0:T(8,128)(2,1)S(1)}, bf16[64,512]{1,0:T(8,128)(2,1)S(1)}, u32[]{:S(2)}, u32[]{:S(2)}) collective-permute-start(bf16[64,512]{1,0:T(8,128)(2,1)S(1)} %get-tuple-element.57), channel_id=1, source_target_pairs={{0,2},{1,3},{2,0},{3,1},{4,6},{5,7},{6,4},{7,5},{8,10},{9,11},{10,... | collective-permute-start | bytes 196616 | tf_op jit(solution)/shard_map/ppermute | solution.py:251
  59.9 2.4 %collective-permute-start.9 = (bf16[80,512]{1,0:T(8,128)(2,1)S(1)}, bf16[80,512]{1,0:T(8,128)(2,1)S(1)}, u32[]{:S(2)}, u32[]{:S(2)}) collective-permute-start(bf16[80,512]{1,0:T(8,128)(2,1)S(1)} %get-tuple-element.55), channel_id=1, source_target_pairs={{0,8},{1,9},{2,10},{3,11},{4,12},{5,13},{6,14},{7,15},{8,0},{9,1},... | collective-permute-start | bytes 245768 | tf_op jit(solution)/shard_map/ppermute | solution.py:251
  62.3 1.2 %shard_map.102.inner = f32[256,1024]{1,0:T(8,128)S(1)} custom-call(bf16[256,1024]{1,0:T(8,128)(2,1)S(1)} %get-tuple-element.59.grad, bf16[1536,1024]{1,0:T(8,128)(2,1)S(1)} %get-tuple-element.61.terms, bf16[1792,256]{1,0:T(8,128)(2,1)S(1)} %get-tuple-element.37.wk, s32[8,256]{1,0:T(8,128)S(1)} %get-tuple-element.60.sources, bf16[256,1024]{1,0:T(8,128)(2,1)S(1)} %copy-done), custom_call_target="tpu_custom_call" | custom-call | flops 1073741824 | bytes 8388608 | tf_op jit(solution)/shard_map/pallas_call | solution.py:41
  63.5 2.6 %collective-permute-done.9.got_a = bf16[80,512]{1,0:T(8,128)(2,1)S(1)} collective-permute-done((bf16[80,512]{1,0:T(8,128)(2,1)S(1)}, bf16[80,512]{1,0:T(8,128)(2,1)S(1)}, u32[]{:S(2)}, u32[]{:S(2)}) %collective-permute-start.9) | collective-permute-done | bytes 81952 | tf_op jit(solution)/shard_map/ppermute | solution.py:251
  66.1 1.1 %shard_map.103 = (f32[64,1024]{1,0:T(8,128)}, f32[7,16,16]{2,1,0:T(8,128)}, bf16[256,1024]{1,0:T(8,128)(2,1)}) custom-call(f32[64,512]{1,0:T(8,128)S(1)} %get-tuple-element.54.kept_a, bf16[80,512]{1,0:T(8,128)(2,1)S(1)} %collective-permute-done.9.got_a, f32[64,512]{1,0:T(8,128)S(1)} %get-tuple-element.56.kept_b, ...), custom_call_target="tpu_custom_call" | custom-call | flops 1048576 | bytes 8388608 | tf_op jit(solution)/shard_map/pallas_call | solution.py:41
  (23 shorter events, 0.2 us)
Async XLA Ops:
  0.6 17.1 %copy-start = (bf16[256,1024]{1,0:T(8,128)(2,1)S(1)}, bf16[256,1024]{1,0:T(8,128)(2,1)}, u32[]{:S(2)}) copy-start(bf16[256,1024]{1,0:T(8,128)(2,1)} %cot.5) | copy-start | bytes 1572868
  0.6 13.1 %collective-permute-start.1 = (bf16[256,1024]{1,0:T(8,128)(2,1)}, bf16[256,1024]{1,0:T(8,128)(2,1)S(1)}, u32[]{:S(2)}, u32[]{:S(2)}) collective-permute-start(bf16[256,1024]{1,0:T(8,128)(2,1)} %x.3), channel_id=1, source_target_pairs={{0,15},{1,0},{2,1},{3,2},{4,3},{5,4},{6,5},{7,6},{8,7},{9,8},{10,9... | collective-permute-start | bytes 1572872 | tf_op jit(solution)/shard_map/ppermute | solution.py:248
  6.2 11.5 %collective-permute-start = (bf16[256,1024]{1,0:T(8,128)(2,1)}, bf16[256,1024]{1,0:T(8,128)(2,1)S(1)}, u32[]{:S(2)}, u32[]{:S(2)}) collective-permute-start(bf16[256,1024]{1,0:T(8,128)(2,1)} %x.3), channel_id=1, source_target_pairs={{0,1},{1,2},{2,3},{3,4},{4,5},{5,6},{6,7},{7,8},{8,9},{9,10},{10,1... | collective-permute-start | bytes 1572872 | tf_op jit(solution)/shard_map/ppermute | solution.py:248
  6.2 1.0 %copy-start.2 = (bf16[256,1024]{1,0:T(8,128)(2,1)S(1)}, bf16[256,1024]{1,0:T(8,128)(2,1)}, u32[]{:S(2)}) copy-start(bf16[256,1024]{1,0:T(8,128)(2,1)} %x.3) | copy-start | bytes 1572868
  7.3 0.7 %copy-start.4 = (bf16[7,16,16]{2,1,0:T(8,128)(2,1)S(1)}, bf16[7,16,16]{2,1,0:T(8,128)(2,1)}, u32[]{:S(2)}) copy-start(bf16[7,16,16]{2,1,0:T(8,128)(2,1)} %conv_hbm.1) | copy-start | bytes 10756
  8.0 0.7 %copy-start.5 = (s32[256,7]{0,1:T(8,128)S(1)}, s32[256,7]{0,1:T(8,128)}, u32[]{:S(2)}) copy-start(s32[256,7]{0,1:T(8,128)} %param.11) | copy-start | bytes 21508
  8.7 0.7 %copy-start.6 = (s32[256]{0:T(256)S(1)}, s32[256]{0:T(256)}, u32[]{:S(2)}) copy-start(s32[256]{0:T(256)} %param.12) | copy-start | bytes 3076
  9.4 0.7 %copy-start.7 = (s32[256]{0:T(256)S(1)}, s32[256]{0:T(256)}, u32[]{:S(2)}) copy-start(s32[256]{0:T(256)} %param.13) | copy-start | bytes 3076
  10.1 7.6 %copy-start.3 = (bf16[256,1024]{1,0:T(8,128)(2,1)S(1)}, bf16[256,1024]{1,0:T(8,128)(2,1)}, u32[]{:S(2)}) copy-start(bf16[256,1024]{1,0:T(8,128)(2,1)} %x.3) | copy-start | bytes 1572868
  17.7 5.4 %copy-start.1 = (bf16[1024,1024]{1,0:T(8,128)(2,1)S(1)}, bf16[1024,1024]{1,0:T(8,128)(2,1)}, u32[]{:S(2)}) copy-start(bf16[1024,1024]{1,0:T(8,128)(2,1)} %mix_hbm.1) | copy-start | bytes 6291460
  23.0 11.1 %collective-permute-start.2 = (bf16[512,1024]{1,0:T(8,128)(2,1)S(1)}, bf16[512,1024]{1,0:T(8,128)(2,1)S(1)}, u32[]{:S(2)}, u32[]{:S(2)}) collective-permute-start(bf16[512,1024]{1,0:T(8,128)(2,1)S(1)} %get-tuple-element.40), channel_id=1, source_target_pairs={{0,1},{1,0},{2,3},{3,2},{4,5},{5,4},{6,7},{7,6},{8,9},{9,8},{10,11... | collective-permute-start | bytes 3145736 | tf_op jit(solution)/shard_map/ppermute | solution.py:251
  29.6 33.9 %collective-permute-start.11 = (bf16[256,1024]{1,0:T(8,128)(2,1)S(1)}, bf16[256,1024]{1,0:T(8,128)(2,1)S(1)}, u32[]{:S(2)}, u32[]{:S(2)}) collective-permute-start(bf16[256,1024]{1,0:T(8,128)(2,1)S(1)} %get-tuple-element.62), channel_id=1, source_target_pairs={{0,1},{1,2},{2,3},{3,4},{4,5},{5,6},{6,7},{7,8},{8,9},{9,10},{10,1... | collective-permute-start | bytes 1572872 | tf_op jit(solution)/shard_map/ppermute | solution.py:248
  30.1 33.4 %collective-permute-start.12 = (bf16[256,1024]{1,0:T(8,128)(2,1)S(1)}, bf16[256,1024]{1,0:T(8,128)(2,1)S(1)}, u32[]{:S(2)}, u32[]{:S(2)}) collective-permute-start(bf16[256,1024]{1,0:T(8,128)(2,1)S(1)} %get-tuple-element.63), channel_id=1, source_target_pairs={{0,15},{1,0},{2,1},{3,2},{4,3},{5,4},{6,5},{7,6},{8,7},{9,8},{10,9... | collective-permute-start | bytes 1572872 | tf_op jit(solution)/shard_map/ppermute | solution.py:248
  34.8 15.7 %collective-permute-start.3 = (bf16[256,512]{1,0:T(8,128)(2,1)S(1)}, bf16[256,512]{1,0:T(8,128)(2,1)S(1)}, u32[]{:S(2)}, u32[]{:S(2)}) collective-permute-start(bf16[256,512]{1,0:T(8,128)(2,1)S(1)} %get-tuple-element.42), channel_id=1, source_target_pairs={{0,2},{1,3},{2,0},{3,1},{4,6},{5,7},{6,4},{7,5},{8,10},{9,11},{10,... | collective-permute-start | bytes 786440 | tf_op jit(solution)/shard_map/ppermute | solution.py:251
  34.8 15.6 %collective-permute-start.4 = (bf16[256,512]{1,0:T(8,128)(2,1)S(1)}, bf16[256,512]{1,0:T(8,128)(2,1)S(1)}, u32[]{:S(2)}, u32[]{:S(2)}) collective-permute-start(bf16[256,512]{1,0:T(8,128)(2,1)S(1)} %get-tuple-element.44), channel_id=1, source_target_pairs={{0,4},{1,5},{2,6},{3,7},{4,0},{5,1},{6,2},{7,3},{8,12},{9,13},{10,... | collective-permute-start | bytes 786440 | tf_op jit(solution)/shard_map/ppermute | solution.py:251
  34.9 1.2 %collective-permute-start.5 = (f32[16,128]{1,0:T(8,128)S(1)}, f32[16,128]{1,0:T(8,128)S(1)}, u32[]{:S(2)}, u32[]{:S(2)}) collective-permute-start(f32[16,128]{1,0:T(8,128)S(1)} %get-tuple-element.48), channel_id=1, source_target_pairs={{0,1},{1,0},{2,3},{3,2},{4,5},{5,4},{6,7},{7,6},{8,9},{9,8},{10,11... | collective-permute-start | bytes 24584 | tf_op jit(solution)/shard_map/ppermute | solution.py:251
  36.2 14.3 %collective-permute-start.6 = (f32[16,128]{1,0:T(8,128)S(1)}, f32[16,128]{1,0:T(8,128)S(1)}, u32[]{:S(2)}, u32[]{:S(2)}) collective-permute-start(f32[16,128]{1,0:T(8,128)S(1)} %add.3.conv), channel_id=1, source_target_pairs={{0,2},{1,3},{2,0},{3,1},{4,6},{5,7},{6,4},{7,5},{8,10},{9,11},{10,... | collective-permute-start | bytes 24584 | tf_op jit(solution)/shard_map/ppermute | solution.py:251
  51.1 6.7 %collective-permute-start.7 = (bf16[144,512]{1,0:T(8,128)(2,1)S(1)}, bf16[144,512]{1,0:T(8,128)(2,1)S(1)}, u32[]{:S(2)}, u32[]{:S(2)}) collective-permute-start(bf16[144,512]{1,0:T(8,128)(2,1)S(1)} %get-tuple-element.50), channel_id=1, source_target_pairs={{0,4},{1,5},{2,6},{3,7},{4,0},{5,1},{6,2},{7,3},{8,12},{9,13},{10,... | collective-permute-start | bytes 442376 | tf_op jit(solution)/shard_map/ppermute | solution.py:251
  51.6 6.1 %collective-permute-start.8 = (bf16[128,512]{1,0:T(8,128)(2,1)S(1)}, bf16[128,512]{1,0:T(8,128)(2,1)S(1)}, u32[]{:S(2)}, u32[]{:S(2)}) collective-permute-start(bf16[128,512]{1,0:T(8,128)(2,1)S(1)} %get-tuple-element.52), channel_id=1, source_target_pairs={{0,8},{1,9},{2,10},{3,11},{4,12},{5,13},{6,14},{7,15},{8,0},{9,1},... | collective-permute-start | bytes 393224 | tf_op jit(solution)/shard_map/ppermute | solution.py:251
  58.3 5.1 %collective-permute-start.10 = (bf16[64,512]{1,0:T(8,128)(2,1)S(1)}, bf16[64,512]{1,0:T(8,128)(2,1)S(1)}, u32[]{:S(2)}, u32[]{:S(2)}) collective-permute-start(bf16[64,512]{1,0:T(8,128)(2,1)S(1)} %get-tuple-element.57), channel_id=1, source_target_pairs={{0,2},{1,3},{2,0},{3,1},{4,6},{5,7},{6,4},{7,5},{8,10},{9,11},{10,... | collective-permute-start | bytes 196616 | tf_op jit(solution)/shard_map/ppermute | solution.py:251
  59.9 6.2 %collective-permute-start.9 = (bf16[80,512]{1,0:T(8,128)(2,1)S(1)}, bf16[80,512]{1,0:T(8,128)(2,1)S(1)}, u32[]{:S(2)}, u32[]{:S(2)}) collective-permute-start(bf16[80,512]{1,0:T(8,128)(2,1)S(1)} %get-tuple-element.55), channel_id=1, source_target_pairs={{0,8},{1,9},{2,10},{3,11},{4,12},{5,13},{6,14},{7,15},{8,0},{9,1},... | collective-permute-start | bytes 245768 | tf_op jit(solution)/shard_map/ppermute | solution.py:251

commit v3 on v2

--- a/solution.py
+++ b/solution.py
@@ -212,24 +212,65 @@
     return ref[:16, :128].astype(f32) + ref[:16, 128:256].astype(f32)
 
 
-def merge_kernel(share, where, first, me, kept_a, got_a, kept_b, got_b, conv, conv_got, send_a, keep_a, send_b, keep_b, conv_out):
-    whole = conv[...] + (conv_got[...] if first else parcel(got_a))
+def conv_sum(conv, gots):
+    one, two, three = [parcel(got) for got in gots]
+    return (conv[...] + one) + (two + three)
+
+
+def quarter(share, bits, skips, kept, gots, got_at, sends, send_at, keep):
+    (lo, hi), (bit_lo, bit_hi) = skips, bits
+    small, large = min(lo, hi), max(lo, hi)
+    for q in range(kept.shape[0] // share // 4):
+        base = ((q >> small) << (small + 1)) | (q & ((1 << small) - 1))
+        base = ((base >> large) << (large + 1)) | (base & ((1 << large) - 1))
+        for delta in range(4):
+            out, out_at = (keep, 0) if delta == 0 else (sends[delta - 1], send_at)
+            want_lo = 1 - bit_lo if delta & 1 else bit_lo
+            want_hi = 1 - bit_hi if delta & 2 else bit_hi
+            at = pl.multiple_of((base + (want_lo << lo) + (want_hi << hi)) * share, share)
+            value = kept[pl.ds(at, share), :]
+            for got in gots:
+                value += got[pl.ds(pl.multiple_of(at + got_at, 16), share), :].astype(f32)
+            out[out_at + q * share : out_at + (q + 1) * share, :] = value.astype(out.dtype)
+
+
+def quad_kernel(share, where, came, me, *refs):
+    first = came == 1
+    kept_a, gots_a, kept_b, gots_b = refs[0], refs[1 : 1 + came], refs[1 + came], refs[2 + came : 2 + 2 * came]
+    rest = refs[2 + 2 * came :]
+    if first:
+        whole = rest[0][...] + rest[1][...]
+        rest = rest[2:]
+    else:
+        whole = conv_sum(rest[0], gots_a)
+        rest = rest[1:]
+    sends_a, keep_a, sends_b, keep_b, conv_out = rest[:3], rest[3], rest[4:7], rest[7], rest[8]
     high = whole.astype(bf16)
     low = (whole - high.astype(f32)).astype(bf16)
     conv_out[...] = high.astype(f32) + low.astype(f32)
-    send_a[:16, :] = jnp.zeros((16, send_a.shape[1]), bf16)
-    send_a[:16, :128] = high
-    send_a[:16, 128:256] = low
-    (bit_a, skip_a), (bit_b, skip_b) = where
-    halve(share, me[bit_a], skip_a, kept_a, got_a, 0 if first else 16, send_a, 16, keep_a)
-    halve(share, me[bit_b], skip_b, kept_b, got_b, 0, send_b, 0, keep_b)
-
-
-def last_kernel(scale, channels, kept_a, got_a, kept_b, got_b, conv, inner, first, second, mix_out, conv_out, grad_out):
+    for send in sends_a:
+        send[:16, :] = jnp.zeros((16, send.shape[1]), bf16)
+        send[:16, :128] = high
+        send[:16, 128:256] = low
+    (bits_a, skips_a), (bits_b, skips_b) = where
+    chosen = lambda bits: (me[bits[0]], me[bits[1]])
+    quarter(share, chosen(bits_a), skips_a, kept_a, gots_a, 0 if first else 16, sends_a, 16, keep_a)
+    quarter(share, chosen(bits_b), skips_b, kept_b, gots_b, 0, sends_b, 0, keep_b)
+
+
+def last_kernel(scale, channels, *refs):
+    kept_a, gots_a, kept_b, gots_b = refs[0], refs[1:4], refs[4], refs[5:8]
+    conv, inner, first, second, mix_out, conv_out, grad_out = refs[8:]
     half = kept_a.shape[1]
-    mix_out[:, :half] = (kept_a[...] + got_a[16:, :].astype(f32)) * scale
-    mix_out[:, half:] = (kept_b[...] + got_b[...].astype(f32)) * scale
-    whole = conv[...] + parcel(got_a)
+    total = kept_a[...]
+    for got in gots_a:
+        total += got[16:, :].astype(f32)
+    mix_out[:, :half] = total * scale
+    total = kept_b[...]
+    for got in gots_b:
+        total += got[...].astype(f32)
+    mix_out[:, half:] = total * scale
+    whole = conv_sum(conv, gots_a)
     for tap in range(conv_out.shape[0]):
         conv_out[tap] = whole[:, tap * channels : (tap + 1) * channels]
     grad_out[...] = (inner[...] + first[...].astype(f32) + second[...].astype(f32)).astype(bf16)
@@ -247,8 +288,11 @@
     def ring(value, by):
         return lax.ppermute(value, "space", [(i, (i + by) % devices) for i in range(devices)])
 
+    def swap_by(value, mask):
+        return lax.ppermute(value, "space", [(i, i ^ mask) for i in range(devices)])
+
     def swap(value, bit):
-        return lax.ppermute(value, "space", [(i, i ^ (1 << bit)) for i in range(devices)])
+        return swap_by(value, 1 << bit)
 
     below = ring(columns_in, 1)
     above = ring(columns_in, -1)
@@ -304,17 +348,17 @@
     orders = [list(range(1, bits)), list(range(2, bits)) + [1]]
     lefts = [list(range(bits - 1, 0, -1)) for _ in orders]
 
-    def places(stage):
-        where = []
-        for order, left in zip(orders, lefts):
-            bit = order[stage]
-            where.append((bit, len(left) - 1 - left.index(bit)))
-            left.remove(bit)
-        return tuple(where)
+    def position(k, bit):
+        return len(lefts[k]) - 1 - lefts[k].index(bit)
+
+    def drop(k, *gone):
+        lefts[k] = [b for b in lefts[k] if b not in gone]
 
     rows_left = half // 2
     parts = call(
-        functools.partial(split_kernel, share, places(0)),
+        functools.partial(
+            split_kernel, share, tuple((order[0], position(k, order[0])) for k, order in enumerate(orders))
+        ),
         [((rows_left, half), bf16), ((rows_left, half), f32)] * 2,
         1 << 20,
         mine,
@@ -322,6 +366,10 @@
         got,
         scalars=1,
     )
+    kept, gots = [parts[1], parts[3]], []
+    for k in (0, 1):
+        gots.append([swap(parts[2 * k], orders[k][0])])
+        drop(k, orders[k][0])
     grad, conv = call(
         functools.partial(weights_kernel, channels, 1.0 / float(total_cols * levels) ** 0.5),
         [((n, width), bf16), ((channels, 128), f32)],
@@ -344,29 +392,34 @@
     conv_got = swap(conv, 1)
     from_below = ring(to_high, 1)
     from_above = ring(to_low, -1)
-    for stage in range(1, bits):
+    for stage in range(1, bits - 1, 2):
+        rows_left //= 4
+        pair = [order[stage : stage + 2] for order in orders]
+        where = tuple((tuple(p), tuple(position(k, b) for b in p)) for k, p in enumerate(pair))
+        outs = call(
+            functools.partial(quad_kernel, share, where, len(gots[0])),
+            [((rows_left + 16, half), bf16)] * 3
+            + [((rows_left, half), f32)]
+            + [((rows_left, half), bf16)] * 3
+            + [((rows_left, half), f32), ((channels, 128), f32)],
+            1 << 20,
+            mine,
+            kept[0],
+            *gots[0],
+            kept[1],
+            *gots[1],
+            conv,
+            *([conv_got] if stage == 1 else []),
+            scalars=1,
+        )
+        kept, conv = [outs[3], outs[7]], outs[8]
         gots = []
         for k in (0, 1):
-            gots.append(swap(parts[2 * k], orders[k][stage - 1]))
-        state = [parts[1], gots[0], parts[3], gots[1]]
-        if stage < bits - 1:
-            rows_left //= 2
-            *parts, conv = call(
-                functools.partial(merge_kernel, share, places(stage), stage == 1),
-                [
-                    ((rows_left + 16, half), bf16),
-                    ((rows_left, half), f32),
-                    ((rows_left, half), bf16),
-                    ((rows_left, half), f32),
-                    ((channels, 128), f32),
-                ],
-                1 << 20,
-                mine,
-                *state,
-                conv,
-                conv_got,
-                scalars=1,
-            )
+            came = []
+            for delta in (1, 2, 3):
+                came.append(swap_by(outs[4 * k + delta - 1], ((delta & 1) << pair[k][0]) | ((delta >> 1) << pair[k][1])))
+            gots.append(came)
+            drop(k, *pair[k])
     (inner,) = call(
         inner_kernel, [((n, width), f32)], 1 << 30, grad, terms, wk, sources, cotangent
     )
@@ -374,7 +427,10 @@
         functools.partial(last_kernel, 1.0 / float(total_cols) ** 0.5, channels),
         [((share, width), f32), ((taps, channels, channels), f32), ((n, width), bf16)],
         1 << 20,
-        *state,
+        kept[0],
+        *gots[0],
+        kept[1],
+        *gots[1],
         conv,
         inner,
         from_below,

time: 67.6 us -> 67.4 us (level)
  starting transfers between devices: 19.3 us -> 21.4 us
  waiting for transfers between devices: 23.7 us -> 21.9 us
    ppermute x9 -> x11, starting transfers between devices: 9.26 us -> 11.4 us  [swap_by(): return lax.ppermute(value, 'space', [(i, i ^ mask) for i in range(devices)])]
    ppermute x9 -> x11, waiting for transfers between devices: 19.7 us -> 17.9 us  [swap_by(): return lax.ppermute(value, 'space', [(i, i ^ mask) for i in range(devices)])]
    pallas_call x10 -> x9, Pallas kernels: 19.5 us -> 19 us  [call(): pl.pallas_call(body, out_shape=[jax.ShapeDtypeStruct(s, d) for s, d in ou...]
  transfers between devices with their start and end apart: 13 -> 15, of which waited for: 5 -> 4; matrix products, arithmetic and copies ran while one was open for 0% -> 0% of each run, Pallas kernels for 20% -> 19%
where the time goes in v3:
time: 67.4 us; the launch traced here: 67.1 us
  waiting for transfers between devices  21.9 us (32%)
  starting transfers between devices  21.4 us (32%)
  Pallas kernels  19 us (28%)
  local copies, waits for them, and re-layouts  3.85 us (6%)
  between operations  0.78 us (1%)
    pallas_call x9, Pallas kernels, call(): pl.pallas_call(body, out_shape=[jax.ShapeDtypeStruct(s, d) for s, d in ou...  19 us
    ppermute x11, waiting for transfers between devices, swap_by(): return lax.ppermute(value, 'space', [(i, i ^ mask) for i in range(devices)])  17.9 us
    ppermute x11, starting transfers between devices, swap_by(): return lax.ppermute(value, 'space', [(i, i ^ mask) for i in range(devices)])  11.4 us
    ppermute x4, starting transfers between devices, ring(): lax.ppermute(value, 'space', [(i, (i + by) % devices) for i in range(devi...  10 us
    ppermute x4, waiting for transfers between devices, ring(): lax.ppermute(value, 'space', [(i, (i + by) % devices) for i in range(devi...  3.99 us
    unnamed x16, local copies, waits for them, and re-layouts  3.85 us
  transfers between devices with their start and end apart: 15, of which 4 were waited for; matrix products, arithmetic and copies ran while one was open for 0% of the time, Pallas kernels for 19%

profile of v3, /device:TPU:0, one launch (start us, length us, event | category | flops | bytes accessed | tf_op | source)
XLA Modules:
  0.0 67.1 jit_solution(11526833448710408654)
XLA Ops:
  0.6 5.5 %collective-permute-start.1 = (bf16[256,1024]{1,0:T(8,128)(2,1)}, bf16[256,1024]{1,0:T(8,128)(2,1)S(1)}, u32[]{:S(2)}, u32[]{:S(2)}) collective-permute-start(bf16[256,1024]{1,0:T(8,128)(2,1)} %x.3), channel_id=1, source_target_pairs={{0,15},{1,0},{2,1},{3,2},{4,3},{5,4},{6,5},{7,6},{8,7},{9,8},{10,9... | collective-permute-start | bytes 1572872 | tf_op jit(solution)/shard_map/ppermute | solution.py:289
  6.2 0.1 pad_add_fusion.1.place
  6.2 1.0 %copy-done.2 = bf16[256,1024]{1,0:T(8,128)(2,1)S(1)} copy-done((bf16[256,1024]{1,0:T(8,128)(2,1)S(1)}, bf16[256,1024]{1,0:T(8,128)(2,1)}, u32[]{:S(2)}) %copy-start.2) | copy-done | bytes 524312
  7.3 0.7 %copy-done.4 = bf16[7,16,16]{2,1,0:T(8,128)(2,1)S(1)} copy-done((bf16[7,16,16]{2,1,0:T(8,128)(2,1)S(1)}, bf16[7,16,16]{2,1,0:T(8,128)(2,1)}, u32[]{:S(2)}) %copy-start.4) | copy-done | bytes 3608
  8.0 0.7 %copy-done.5 = s32[256,7]{0,1:T(8,128)S(1)} copy-done((s32[256,7]{0,1:T(8,128)S(1)}, s32[256,7]{0,1:T(8,128)}, u32[]{:S(2)}) %copy-start.5) | copy-done | bytes 7192
  8.7 0.7 %copy-done.6 = s32[256]{0:T(256)S(1)} copy-done((s32[256]{0:T(256)S(1)}, s32[256]{0:T(256)}, u32[]{:S(2)}) %copy-start.6) | copy-done | bytes 1048
  9.4 0.7 %copy-done.7 = s32[256]{0:T(256)S(1)} copy-done((s32[256]{0:T(256)S(1)}, s32[256]{0:T(256)}, u32[]{:S(2)}) %copy-start.7) | copy-done | bytes 1048
  10.1 3.5 %shard_map.94 = (bf16[1536,512]{1,0:T(8,128)(2,1)S(1)}, s32[8,256]{1,0:T(8,128)S(1)}, bf16[1536,1024]{1,0:T(8,128)(2,1)S(1)}, bf16[1792,256]{1,0:T(8,128)(2,1)S(1)}) custom-call(s32[2]{0:T(128)S(1)} %pad_add_fusion.1.place, s32[7,256]{1,0:T(8,128)S(1)} %bitcast.8, s32[1,256]{1,0:T(1,128)S(1)} %bitcast.9, s32[1,256]{1,0:T(1,128)S(1)} %bitcast.10, ...), custom_call_target="tpu_custom_call" | custom-call | flops 1073741824 | bytes 8388608 | tf_op jit(solution)/shard_map/pallas_call | solution.py:41
  13.6 0.1 pad_add_fusion.me
  13.7 4.0 %collective-permute-done.low = bf16[256,1024]{1,0:T(8,128)(2,1)S(1)} collective-permute-done((bf16[256,1024]{1,0:T(8,128)(2,1)}, bf16[256,1024]{1,0:T(8,128)(2,1)S(1)}, u32[]{:S(2)}, u32[]{:S(2)}) %collective-permute-start) | collective-permute-done | bytes 524320 | tf_op jit(solution)/shard_map/ppermute | solution.py:289
  17.7 5.3 %shard_map.95 = (bf16[1536,1024]{1,0:T(8,128)(2,1)S(1)}, f32[256,1024]{1,0:T(8,128)S(1)}, bf16[1024,256]{1,0:T(8,128)(2,1)S(1)}, bf16[512,1024]{1,0:T(8,128)(2,1)S(1)}) custom-call(s32[4]{0:T(128)S(1)} %pad_add_fusion.me, bf16[256,1024]{1,0:T(8,128)(2,1)S(1)} %collective-permute-done.low, bf16[256,1024]{1,0:T(8,128)(2,1)S(1)} %collective-permute-done.1.high, ...), custom_call_target="tpu_custom_call" | custom-call | flops 3221225472 | bytes 8388608 | tf_op jit(solution)/shard_map/pallas_call | solution.py:41
  23.0 0.1 collective-permute-start.2
  23.1 1.9 %shard_map.96 = (f32[512,1024]{1,0:T(8,128)S(1)}, f32[256,1024]{1,0:T(8,128)S(1)}) custom-call(s32[4]{0:T(128)S(1)} %pad_add_fusion.me, bf16[1024,256]{1,0:T(8,128)(2,1)S(1)} %get-tuple-element.37.act_t, bf16[256,1024]{1,0:T(8,128)(2,1)S(1)} %copy-done, bf16[1024,1024]{1,0:T(8,128)(2,1)S(1)} %copy-done.1), custom_call_target="tpu_custom_call" | custom-call | flops 1073741824 | bytes 8388608 | tf_op jit(solution)/shard_map/pallas_call | solution.py:41
  24.9 1.9 %shard_map.98 = (bf16[256,1024]{1,0:T(8,128)(2,1)S(1)}, f32[16,128]{1,0:T(8,128)S(1)}) custom-call(f32[256,1024]{1,0:T(8,128)S(1)} %get-tuple-element.44.up, f32[256,1024]{1,0:T(8,128)S(1)} %get-tuple-element.45.pre, bf16[256,1024]{1,0:T(8,128)(2,1)S(1)} %copy-done.3, bf16[1536,1024]{1,0:T(8,128)(2,1)S(1)} %get-tuple-element.46.rows), custom_call_target="tpu_custom_call" | custom-call | flops 2147483648 | bytes 8388608 | tf_op jit(solution)/shard_map/pallas_call | solution.py:41
  26.9 2.7 %shard_map.100 = (bf16[1536,1024]{1,0:T(8,128)(2,1)S(1)}, bf16[256,1024]{1,0:T(8,128)(2,1)S(1)}, bf16[256,1024]{1,0:T(8,128)(2,1)S(1)}) custom-call(bf16[256,1024]{1,0:T(8,128)(2,1)S(1)} %get-tuple-element.57.grad, bf16[1792,256]{1,0:T(8,128)(2,1)S(1)} %get-tuple-element.36.wk, s32[8,256]{1,0:T(8,128)S(1)} %get-tuple-element.58.sources), custom_call_target="tpu_custom_call" | custom-call | flops 3221225472 | bytes 8388608 | tf_op jit(solution)/shard_map/pallas_call | solution.py:41
  29.6 0.5 collective-permute-start.13
  30.1 4.0 %collective-permute-start.14 = (bf16[256,1024]{1,0:T(8,128)(2,1)S(1)}, bf16[256,1024]{1,0:T(8,128)(2,1)S(1)}, u32[]{:S(2)}, u32[]{:S(2)}) collective-permute-start(bf16[256,1024]{1,0:T(8,128)(2,1)S(1)} %get-tuple-element.61), channel_id=1, source_target_pairs={{0,15},{1,0},{2,1},{3,2},{4,3},{5,4},{6,5},{7,6},{8,7},{9,8},{10,9... | collective-permute-start | bytes 1572872 | tf_op jit(solution)/shard_map/ppermute | solution.py:289
  34.1 0.7 %shard_map.97 = (bf16[256,512]{1,0:T(8,128)(2,1)S(1)}, f32[256,512]{1,0:T(8,128)S(1)}, bf16[256,512]{1,0:T(8,128)(2,1)S(1)}, f32[256,512]{1,0:T(8,128)S(1)}) custom-call(s32[4]{0:T(128)S(1)} %pad_add_fusion.me, f32[512,1024]{1,0:T(8,128)S(1)} %get-tuple-element.38.keep, bf16[512,1024]{1,0:T(8,128)(2,1)S(1)} %collective-permute-done.2.got), custom_call_target="tpu_custom_call" | custom-call | flops 1048576 | bytes 8388608 | tf_op jit(solution)/shard_map/pallas_call | solution.py:41
  34.8 0.1 collective-permute-start.4
  34.9 0.1 collective-permute-start.5
  35.0 1.2 %collective-permute-done.5 = f32[16,128]{1,0:T(8,128)S(1)} collective-permute-done((f32[16,128]{1,0:T(8,128)S(1)}, f32[16,128]{1,0:T(8,128)S(1)}, u32[]{:S(2)}, u32[]{:S(2)}) %collective-permute-start.5) | collective-permute-done | bytes 8224 | tf_op jit(solution)/shard_map/ppermute | solution.py:292
  36.2 1.9 %collective-permute-start.6 = (f32[16,128]{1,0:T(8,128)S(1)}, f32[16,128]{1,0:T(8,128)S(1)}, u32[]{:S(2)}, u32[]{:S(2)}) collective-permute-start(f32[16,128]{1,0:T(8,128)S(1)} %add.3.refs_4_), channel_id=1, source_target_pairs={{0,2},{1,3},{2,0},{3,1},{4,6},{5,7},{6,4},{7,5},{8,10},{9,11},{10,... | collective-permute-start | bytes 24584 | tf_op jit(solution)/shard_map/ppermute | solution.py:292
  38.0 12.4 %collective-permute-done.6.refs_5_ = f32[16,128]{1,0:T(8,128)S(1)} collective-permute-done((f32[16,128]{1,0:T(8,128)S(1)}, f32[16,128]{1,0:T(8,128)S(1)}, u32[]{:S(2)}, u32[]{:S(2)}) %collective-permute-start.6) | collective-permute-done | bytes 8224 | tf_op jit(solution)/shard_map/ppermute | solution.py:292
  50.4 0.6 shard_map.99
  51.1 1.6 %collective-permute-start.10 = (bf16[64,512]{1,0:T(8,128)(2,1)S(1)}, bf16[64,512]{1,0:T(8,128)(2,1)S(1)}, u32[]{:S(2)}, u32[]{:S(2)}) collective-permute-start(bf16[64,512]{1,0:T(8,128)(2,1)S(1)} %get-tuple-element.53), channel_id=1, source_target_pairs={{0,8},{1,9},{2,10},{3,11},{4,12},{5,13},{6,14},{7,15},{8,0},{9,1},... | collective-permute-start | bytes 196616 | tf_op jit(solution)/shard_map/ppermute | solution.py:292
  52.6 2.9 %collective-permute-start.12 = (bf16[64,512]{1,0:T(8,128)(2,1)S(1)}, bf16[64,512]{1,0:T(8,128)(2,1)S(1)}, u32[]{:S(2)}, u32[]{:S(2)}) collective-permute-start(bf16[64,512]{1,0:T(8,128)(2,1)S(1)} %get-tuple-element.55), channel_id=1, source_target_pairs={{0,10},{1,11},{2,8},{3,9},{4,14},{5,15},{6,12},{7,13},{8,2},{9,3},... | collective-permute-start | bytes 196616 | tf_op jit(solution)/shard_map/ppermute | solution.py:292
  55.5 0.5 collective-permute-start.7
  56.0 2.6 %collective-permute-start.8 = (bf16[80,512]{1,0:T(8,128)(2,1)S(1)}, bf16[80,512]{1,0:T(8,128)(2,1)S(1)}, u32[]{:S(2)}, u32[]{:S(2)}) collective-permute-start(bf16[80,512]{1,0:T(8,128)(2,1)S(1)} %get-tuple-element.50), channel_id=1, source_target_pairs={{0,8},{1,9},{2,10},{3,11},{4,12},{5,13},{6,14},{7,15},{8,0},{9,1},... | collective-permute-start | bytes 245768 | tf_op jit(solution)/shard_map/ppermute | solution.py:292
  58.6 1.7 %collective-permute-start.9 = (bf16[80,512]{1,0:T(8,128)(2,1)S(1)}, bf16[80,512]{1,0:T(8,128)(2,1)S(1)}, u32[]{:S(2)}, u32[]{:S(2)}) collective-permute-start(bf16[80,512]{1,0:T(8,128)(2,1)S(1)} %get-tuple-element.51), channel_id=1, source_target_pairs={{0,12},{1,13},{2,14},{3,15},{4,8},{5,9},{6,10},{7,11},{8,4},{9,5},... | collective-permute-start | bytes 245768 | tf_op jit(solution)/shard_map/ppermute | solution.py:292
  60.3 1.2 %shard_map.101.refs_9_ = f32[256,1024]{1,0:T(8,128)S(1)} custom-call(bf16[256,1024]{1,0:T(8,128)(2,1)S(1)} %get-tuple-element.57.grad, bf16[1536,1024]{1,0:T(8,128)(2,1)S(1)} %get-tuple-element.59.terms, bf16[1792,256]{1,0:T(8,128)(2,1)S(1)} %get-tuple-element.36.wk, s32[8,256]{1,0:T(8,128)S(1)} %get-tuple-element.58.sources, bf16[256,1024]{1,0:T(8,128)(2,1)S(1)} %copy-done), custom_call_target="tpu_custom_call" | custom-call | flops 1073741824 | bytes 8388608 | tf_op jit(solution)/shard_map/pallas_call | solution.py:41
  61.5 4.4 %collective-permute-done.8.refs_2_ = bf16[80,512]{1,0:T(8,128)(2,1)S(1)} collective-permute-done((bf16[80,512]{1,0:T(8,128)(2,1)S(1)}, bf16[80,512]{1,0:T(8,128)(2,1)S(1)}, u32[]{:S(2)}, u32[]{:S(2)}) %collective-permute-start.8) | collective-permute-done | bytes 81952 | tf_op jit(solution)/shard_map/ppermute | solution.py:292
  65.9 1.2 %shard_map.102 = (f32[64,1024]{1,0:T(8,128)}, f32[7,16,16]{2,1,0:T(8,128)}, bf16[256,1024]{1,0:T(8,128)(2,1)}) custom-call(f32[64,512]{1,0:T(8,128)S(1)} %get-tuple-element.48.refs_0_, bf16[80,512]{1,0:T(8,128)(2,1)S(1)} %collective-permute-done.7.refs_1_, bf16[80,512]{1,0:T(8,128)(2,1)S(1)} %collective-permute-done.8.refs_2_, ...), custom_call_target="tpu_custom_call" | custom-call | flops 1048576 | bytes 8388608 | tf_op jit(solution)/shard_map/pallas_call | solution.py:41
  (26 shorter events, 0.1 us)
Async XLA Ops:
  0.6 17.1 %copy-start = (bf16[256,1024]{1,0:T(8,128)(2,1)S(1)}, bf16[256,1024]{1,0:T(8,128)(2,1)}, u32[]{:S(2)}) copy-start(bf16[256,1024]{1,0:T(8,128)(2,1)} %cot.5) | copy-start | bytes 1572868
  0.6 13.1 %collective-permute-start.1 = (bf16[256,1024]{1,0:T(8,128)(2,1)}, bf16[256,1024]{1,0:T(8,128)(2,1)S(1)}, u32[]{:S(2)}, u32[]{:S(2)}) collective-permute-start(bf16[256,1024]{1,0:T(8,128)(2,1)} %x.3), channel_id=1, source_target_pairs={{0,15},{1,0},{2,1},{3,2},{4,3},{5,4},{6,5},{7,6},{8,7},{9,8},{10,9... | collective-permute-start | bytes 1572872 | tf_op jit(solution)/shard_map/ppermute | solution.py:289
  6.2 11.5 %collective-permute-start = (bf16[256,1024]{1,0:T(8,128)(2,1)}, bf16[256,1024]{1,0:T(8,128)(2,1)S(1)}, u32[]{:S(2)}, u32[]{:S(2)}) collective-permute-start(bf16[256,1024]{1,0:T(8,128)(2,1)} %x.3), channel_id=1, source_target_pairs={{0,1},{1,2},{2,3},{3,4},{4,5},{5,6},{6,7},{7,8},{8,9},{9,10},{10,1... | collective-permute-start | bytes 1572872 | tf_op jit(solution)/shard_map/ppermute | solution.py:289
  6.2 1.0 %copy-start.2 = (bf16[256,1024]{1,0:T(8,128)(2,1)S(1)}, bf16[256,1024]{1,0:T(8,128)(2,1)}, u32[]{:S(2)}) copy-start(bf16[256,1024]{1,0:T(8,128)(2,1)} %x.3) | copy-start | bytes 1572868
  7.3 0.7 %copy-start.4 = (bf16[7,16,16]{2,1,0:T(8,128)(2,1)S(1)}, bf16[7,16,16]{2,1,0:T(8,128)(2,1)}, u32[]{:S(2)}) copy-start(bf16[7,16,16]{2,1,0:T(8,128)(2,1)} %conv_hbm.1) | copy-start | bytes 10756
  8.0 0.7 %copy-start.5 = (s32[256,7]{0,1:T(8,128)S(1)}, s32[256,7]{0,1:T(8,128)}, u32[]{:S(2)}) copy-start(s32[256,7]{0,1:T(8,128)} %param.11) | copy-start | bytes 21508
  8.7 0.7 %copy-start.6 = (s32[256]{0:T(256)S(1)}, s32[256]{0:T(256)}, u32[]{:S(2)}) copy-start(s32[256]{0:T(256)} %param.12) | copy-start | bytes 3076
  9.4 0.7 %copy-start.7 = (s32[256]{0:T(256)S(1)}, s32[256]{0:T(256)}, u32[]{:S(2)}) copy-start(s32[256]{0:T(256)} %param.13) | copy-start | bytes 3076
  10.1 7.6 %copy-start.3 = (bf16[256,1024]{1,0:T(8,128)(2,1)S(1)}, bf16[256,1024]{1,0:T(8,128)(2,1)}, u32[]{:S(2)}) copy-start(bf16[256,1024]{1,0:T(8,128)(2,1)} %x.3) | copy-start | bytes 1572868
  17.7 5.4 %copy-start.1 = (bf16[1024,1024]{1,0:T(8,128)(2,1)S(1)}, bf16[1024,1024]{1,0:T(8,128)(2,1)}, u32[]{:S(2)}) copy-start(bf16[1024,1024]{1,0:T(8,128)(2,1)} %mix_hbm.1) | copy-start | bytes 6291460
  23.0 11.1 %collective-permute-start.2 = (bf16[512,1024]{1,0:T(8,128)(2,1)S(1)}, bf16[512,1024]{1,0:T(8,128)(2,1)S(1)}, u32[]{:S(2)}, u32[]{:S(2)}) collective-permute-start(bf16[512,1024]{1,0:T(8,128)(2,1)S(1)} %get-tuple-element.39), channel_id=1, source_target_pairs={{0,1},{1,0},{2,3},{3,2},{4,5},{5,4},{6,7},{7,6},{8,9},{9,8},{10,11... | collective-permute-start | bytes 3145736 | tf_op jit(solution)/shard_map/ppermute | solution.py:292
  29.6 26.0 %collective-permute-start.13 = (bf16[256,1024]{1,0:T(8,128)(2,1)S(1)}, bf16[256,1024]{1,0:T(8,128)(2,1)S(1)}, u32[]{:S(2)}, u32[]{:S(2)}) collective-permute-start(bf16[256,1024]{1,0:T(8,128)(2,1)S(1)} %get-tuple-element.60), channel_id=1, source_target_pairs={{0,1},{1,2},{2,3},{3,4},{4,5},{5,6},{6,7},{7,8},{8,9},{9,10},{10,1... | collective-permute-start | bytes 1572872 | tf_op jit(solution)/shard_map/ppermute | solution.py:289
  30.1 25.9 %collective-permute-start.14 = (bf16[256,1024]{1,0:T(8,128)(2,1)S(1)}, bf16[256,1024]{1,0:T(8,128)(2,1)S(1)}, u32[]{:S(2)}, u32[]{:S(2)}) collective-permute-start(bf16[256,1024]{1,0:T(8,128)(2,1)S(1)} %get-tuple-element.61), channel_id=1, source_target_pairs={{0,15},{1,0},{2,1},{3,2},{4,3},{5,4},{6,5},{7,6},{8,7},{9,8},{10,9... | collective-permute-start | bytes 1572872 | tf_op jit(solution)/shard_map/ppermute | solution.py:289
  34.8 15.7 %collective-permute-start.3 = (bf16[256,512]{1,0:T(8,128)(2,1)S(1)}, bf16[256,512]{1,0:T(8,128)(2,1)S(1)}, u32[]{:S(2)}, u32[]{:S(2)}) collective-permute-start(bf16[256,512]{1,0:T(8,128)(2,1)S(1)} %get-tuple-element.41), channel_id=1, source_target_pairs={{0,2},{1,3},{2,0},{3,1},{4,6},{5,7},{6,4},{7,5},{8,10},{9,11},{10,... | collective-permute-start | bytes 786440 | tf_op jit(solution)/shard_map/ppermute | solution.py:292
  34.8 15.6 %collective-permute-start.4 = (bf16[256,512]{1,0:T(8,128)(2,1)S(1)}, bf16[256,512]{1,0:T(8,128)(2,1)S(1)}, u32[]{:S(2)}, u32[]{:S(2)}) collective-permute-start(bf16[256,512]{1,0:T(8,128)(2,1)S(1)} %get-tuple-element.43), channel_id=1, source_target_pairs={{0,4},{1,5},{2,6},{3,7},{4,0},{5,1},{6,2},{7,3},{8,12},{9,13},{10,... | collective-permute-start | bytes 786440 | tf_op jit(solution)/shard_map/ppermute | solution.py:292
  34.9 1.2 %collective-permute-start.5 = (f32[16,128]{1,0:T(8,128)S(1)}, f32[16,128]{1,0:T(8,128)S(1)}, u32[]{:S(2)}, u32[]{:S(2)}) collective-permute-start(f32[16,128]{1,0:T(8,128)S(1)} %get-tuple-element.47), channel_id=1, source_target_pairs={{0,1},{1,0},{2,3},{3,2},{4,5},{5,4},{6,7},{7,6},{8,9},{9,8},{10,11... | collective-permute-start | bytes 24584 | tf_op jit(solution)/shard_map/ppermute | solution.py:292
  36.2 14.3 %collective-permute-start.6 = (f32[16,128]{1,0:T(8,128)S(1)}, f32[16,128]{1,0:T(8,128)S(1)}, u32[]{:S(2)}, u32[]{:S(2)}) collective-permute-start(f32[16,128]{1,0:T(8,128)S(1)} %add.3.refs_4_), channel_id=1, source_target_pairs={{0,2},{1,3},{2,0},{3,1},{4,6},{5,7},{6,4},{7,5},{8,10},{9,11},{10,... | collective-permute-start | bytes 24584 | tf_op jit(solution)/shard_map/ppermute | solution.py:292
  51.1 7.5 %collective-permute-start.10 = (bf16[64,512]{1,0:T(8,128)(2,1)S(1)}, bf16[64,512]{1,0:T(8,128)(2,1)S(1)}, u32[]{:S(2)}, u32[]{:S(2)}) collective-permute-start(bf16[64,512]{1,0:T(8,128)(2,1)S(1)} %get-tuple-element.53), channel_id=1, source_target_pairs={{0,8},{1,9},{2,10},{3,11},{4,12},{5,13},{6,14},{7,15},{8,0},{9,1},... | collective-permute-start | bytes 196616 | tf_op jit(solution)/shard_map/ppermute | solution.py:292
  52.6 8.9 %collective-permute-start.11 = (bf16[64,512]{1,0:T(8,128)(2,1)S(1)}, bf16[64,512]{1,0:T(8,128)(2,1)S(1)}, u32[]{:S(2)}, u32[]{:S(2)}) collective-permute-start(bf16[64,512]{1,0:T(8,128)(2,1)S(1)} %get-tuple-element.54), channel_id=1, source_target_pairs={{0,2},{1,3},{2,0},{3,1},{4,6},{5,7},{6,4},{7,5},{8,10},{9,11},{10,... | collective-permute-start | bytes 196616 | tf_op jit(solution)/shard_map/ppermute | solution.py:292
  52.6 8.9 %collective-permute-start.12 = (bf16[64,512]{1,0:T(8,128)(2,1)S(1)}, bf16[64,512]{1,0:T(8,128)(2,1)S(1)}, u32[]{:S(2)}, u32[]{:S(2)}) collective-permute-start(bf16[64,512]{1,0:T(8,128)(2,1)S(1)} %get-tuple-element.55), channel_id=1, source_target_pairs={{0,10},{1,11},{2,8},{3,9},{4,14},{5,15},{6,12},{7,13},{8,2},{9,3},... | collective-permute-start | bytes 196616 | tf_op jit(solution)/shard_map/ppermute | solution.py:292
  55.5 6.0 %collective-permute-start.7 = (bf16[80,512]{1,0:T(8,128)(2,1)S(1)}, bf16[80,512]{1,0:T(8,128)(2,1)S(1)}, u32[]{:S(2)}, u32[]{:S(2)}) collective-permute-start(bf16[80,512]{1,0:T(8,128)(2,1)S(1)} %get-tuple-element.49), channel_id=1, source_target_pairs={{0,4},{1,5},{2,6},{3,7},{4,0},{5,1},{6,2},{7,3},{8,12},{9,13},{10,... | collective-permute-start | bytes 245768 | tf_op jit(solution)/shard_map/ppermute | solution.py:292
  56.0 9.9 %collective-permute-start.8 = (bf16[80,512]{1,0:T(8,128)(2,1)S(1)}, bf16[80,512]{1,0:T(8,128)(2,1)S(1)}, u32[]{:S(2)}, u32[]{:S(2)}) collective-permute-start(bf16[80,512]{1,0:T(8,128)(2,1)S(1)} %get-tuple-element.50), channel_id=1, source_target_pairs={{0,8},{1,9},{2,10},{3,11},{4,12},{5,13},{6,14},{7,15},{8,0},{9,1},... | collective-permute-start | bytes 245768 | tf_op jit(solution)/shard_map/ppermute | solution.py:292
  58.6 7.3 %collective-permute-start.9 = (bf16[80,512]{1,0:T(8,128)(2,1)S(1)}, bf16[80,512]{1,0:T(8,128)(2,1)S(1)}, u32[]{:S(2)}, u32[]{:S(2)}) collective-permute-start(bf16[80,512]{1,0:T(8,128)(2,1)S(1)} %get-tuple-element.51), channel_id=1, source_target_pairs={{0,12},{1,13},{2,14},{3,15},{4,8},{5,9},{6,10},{7,11},{8,4},{9,5},... | collective-permute-start | bytes 245768 | tf_op jit(solution)/shard_map/ppermute | solution.py:292

commit v4 on v3

--- a/solution.py
+++ b/solution.py
@@ -101,15 +101,7 @@
     return jnp.tanh(TANH_SCALE * (v + TANH_CUBE * (v * v * v)))
 
 
-def mix_rows(act_t, cot, bit, share):
-    blocks = act_t.shape[0] // share
-    rows = [
-        act_t[pl.ds(pl.multiple_of((2 * k + bit) * share, share), share), :] for k in range(blocks // 2)
-    ]
-    return mm(jnp.concatenate(rows, axis=0), cot[...])
-
-
-def front_kernel(share, me, low, high, halo_sel, own, wk, x, cot, rows_out, pre, act_t, send):
+def front_kernel(share, me, low, high, halo_sel, own, wk, x, rows_out, pre, act_keep, act_send, act_t):
     n, width = pre.shape
     taps = wk.shape[0] // WIDE
     for c in range(0, width, WIDE):
@@ -122,15 +114,29 @@
         pre[:, c : c + WIDE] = acc
         active = (0.5 * acc) * (1.0 + gelu_tanh(acc))
         act_t[c : c + WIDE, :] = active.T.astype(bf16)
-    send[...] = mix_rows(act_t, cot, 1 - me[0], share).astype(bf16)
-
-
-def keep_kernel(share, me, act_t, cot, mix_hbm, keep, up, mix, sem):
-    copy = pltpu.make_async_copy(mix_hbm, mix, sem.at[0])
-    copy.start()
-    keep[...] = mix_rows(act_t, cot, me[0], share)
-    copy.wait()
+    for k in range(width // share // 2):
+        for bit, out in ((me[0], act_keep), (1 - me[0], act_send)):
+            at = pl.multiple_of((2 * k + bit) * share, share)
+            out[k * share : (k + 1) * share, :] = act_t[pl.ds(at, share), :]
+
+
+def up_kernel(cot, mix, up):
     up[...] = contract(cot[...], mix[...], 1, 1)
+
+
+def mix_kernel(share, where, me, act, act_got, cot, cot_got, *outs):
+    half = cot.shape[1] // 2
+    blocks = act.shape[0] // share
+    for k, (bit, skip) in enumerate(where):
+        cols = slice(k * half, (k + 1) * half)
+        both = jnp.concatenate([cot[:, cols], cot_got[:, cols]], axis=0)
+        for want, out in ((1 - me[bit], outs[2 * k]), (me[bit], outs[2 * k + 1])):
+            pieces = []
+            for q in range(blocks // 2):
+                base = ((q >> skip) << (skip + 1)) | (q & ((1 << skip) - 1))
+                at = pl.ds(pl.multiple_of((base + (want << skip)) * share, share), share)
+                pieces.append(jnp.concatenate([act[at, :], act_got[at, :]], axis=1))
+            out[...] = mm(jnp.concatenate(pieces, axis=0), both).astype(out.dtype)
 
 
 def select_rows(sources, start, count, taps):
@@ -190,24 +196,6 @@
         inner[:, c : c + WIDE] = acc + mm(sel, terms[:, c : c + WIDE])
 
 
-def halve(share, bit, skip, kept, got, got_at, send, send_at, keep):
-    for q in range(kept.shape[0] // share // 2):
-        base = ((q >> skip) << (skip + 1)) | (q & ((1 << skip) - 1))
-        for value, out, out_at in ((1 - bit, send, send_at), (bit, keep, 0)):
-            at = pl.multiple_of((base + (value << skip)) * share, share)
-            came = got[pl.ds(pl.multiple_of(at + got_at, 16), share), :].astype(f32)
-            out[out_at + q * share : out_at + (q + 1) * share, :] = (
-                kept[pl.ds(at, share), :] + came
-            ).astype(out.dtype)
-
-
-def split_kernel(share, where, me, keep, got, *outs):
-    half = keep.shape[1] // 2
-    for k, (bit, skip) in enumerate(where):
-        cols = slice(k * half, (k + 1) * half)
-        halve(share, me[bit], skip, keep.at[:, cols], got.at[:, cols], 0, outs[2 * k], 0, outs[2 * k + 1])
-
-
 def parcel(ref):
     return ref[:16, :128].astype(f32) + ref[:16, 128:256].astype(f32)
 
@@ -296,6 +284,7 @@
 
     below = ring(columns_in, 1)
     above = ring(columns_in, -1)
+    cot_got = swap(cotangent, 0)
     pairs = (taps - 1) * n
     share = width // devices
     half = width // 2
@@ -318,9 +307,10 @@
             pltpu.SemaphoreType.DMA((2,)),
         ],
     )
-    rows, pre, act_t, send = call(
+    (up,) = call(up_kernel, [((n, width), f32)], 1 << 29, cotangent, mix_weight)
+    rows, pre, act, act_send = call(
         functools.partial(front_kernel, share),
-        [((pairs, width), bf16), ((n, width), f32), ((width, n), bf16), ((half, width), bf16)],
+        [((pairs, width), bf16), ((n, width), f32), ((half, n), bf16), ((half, n), bf16)],
         3 << 30,
         mine,
         below,
@@ -329,22 +319,10 @@
         own,
         wk,
         columns_in,
-        cotangent,
         scalars=1,
-    )
-    got = swap(send, 0)
-    keep, up = call(
-        functools.partial(keep_kernel, share),
-        [((half, width), f32), ((n, width), f32)],
-        1 << 30,
-        mine,
-        act_t,
-        cotangent,
-        mix_weight,
-        scalars=1,
-        far=(3,),
-        scratch=[pltpu.VMEM(mix_weight.shape, bf16), pltpu.SemaphoreType.DMA((1,))],
-    )
+        scratch=[pltpu.VMEM((width, n), bf16)],
+    )
+    act_got = swap(act_send, 0)
     orders = [list(range(1, bits)), list(range(2, bits)) + [1]]
     lefts = [list(range(bits - 1, 0, -1)) for _ in orders]
 
@@ -357,13 +335,15 @@
     rows_left = half // 2
     parts = call(
         functools.partial(
-            split_kernel, share, tuple((order[0], position(k, order[0])) for k, order in enumerate(orders))
+            mix_kernel, share, tuple((order[0], position(k, order[0])) for k, order in enumerate(orders))
         ),
         [((rows_left, half), bf16), ((rows_left, half), f32)] * 2,
-        1 << 20,
+        1 << 30,
         mine,
-        keep,
-        got,
+        act,
+        act_got,
+        cotangent,
+        cot_got,
         scalars=1,
     )
     kept, gots = [parts[1], parts[3]], []

time: 67.4 us -> 66 us (0.979)
  starting transfers between devices: 21.4 us -> 23.5 us
  waiting for transfers between devices: 21.9 us -> 20.4 us
  Pallas kernels: 19 us -> 18 us
  local copies, waits for them, and re-layouts: 3.85 us -> 2.86 us
    ppermute x4, waiting for transfers between devices: 3.99 us -> 0.01 us  [ring(): lax.ppermute(value, 'space', [(i, (i + by) % devices) for i in range(devi...]
    ppermute x11 -> x12, waiting for transfers between devices: 17.9 us -> 20.4 us  [swap_by(): return lax.ppermute(value, 'space', [(i, i ^ mask) for i in range(devices)])]
    ppermute x11 -> x12, starting transfers between devices: 11.4 us -> 13.5 us  [swap_by(): return lax.ppermute(value, 'space', [(i, i ^ mask) for i in range(devices)])]
    unnamed x16, local copies, waits for them, and re-layouts: 3.85 us -> 2.86 us
    pallas_call x9, Pallas kernels: 19 us -> 18 us  [call(): pl.pallas_call(body, out_shape=[jax.ShapeDtypeStruct(s, d) for s, d in ou...]
  transfers between devices with their start and end apart: 15 -> 16, of which waited for: 4 -> 5; matrix products, arithmetic and copies ran while one was open for 0% -> 0% of each run, Pallas kernels for 19% -> 26%
where the time goes in v4:
time: 66 us; the launch traced here: 65.8 us
  starting transfers between devices  23.5 us (36%)
  waiting for transfers between devices  20.4 us (31%)
  Pallas kernels  18 us (27%)
  local copies, waits for them, and re-layouts  2.86 us (4%)
  between operations  0.77 us (1%)
    ppermute x12, waiting for transfers between devices, swap_by(): return lax.ppermute(value, 'space', [(i, i ^ mask) for i in range(devices)])  20.4 us
    pallas_call x9, Pallas kernels, call(): pl.pallas_call(body, out_shape=[jax.ShapeDtypeStruct(s, d) for s, d in ou...  18 us
    ppermute x12, starting transfers between devices, swap_by(): return lax.ppermute(value, 'space', [(i, i ^ mask) for i in range(devices)])  13.5 us
    ppermute x4, starting transfers between devices, ring(): lax.ppermute(value, 'space', [(i, (i + by) % devices) for i in range(devi...  10.1 us
    unnamed x16, local copies, waits for them, and re-layouts  2.86 us
  transfers between devices with their start and end apart: 16, of which 5 were waited for; matrix products, arithmetic and copies ran while one was open for 0% of the time, Pallas kernels for 26%

profile of v4, /device:TPU:0, one launch (start us, length us, event | category | flops | bytes accessed | tf_op | source)
XLA Modules:
  0.0 65.8 jit_solution(17453353043644416277)
XLA Ops:
  0.7 0.5 collective-permute-start
  1.2 5.0 %collective-permute-start.1 = (bf16[256,1024]{1,0:T(8,128)(2,1)}, bf16[256,1024]{1,0:T(8,128)(2,1)S(1)}, u32[]{:S(2)}, u32[]{:S(2)}) collective-permute-start(bf16[256,1024]{1,0:T(8,128)(2,1)} %x.3), channel_id=1, source_target_pairs={{0,15},{1,0},{2,1},{3,2},{4,3},{5,4},{6,5},{7,6},{8,7},{9,8},{10,9... | collective-permute-start | bytes 1572872 | tf_op jit(solution)/shard_map/ppermute | solution.py:277
  6.3 1.0 %copy-done = bf16[256,1024]{1,0:T(8,128)(2,1)S(1)} copy-done((bf16[256,1024]{1,0:T(8,128)(2,1)S(1)}, bf16[256,1024]{1,0:T(8,128)(2,1)}, u32[]{:S(2)}) %copy-start) | copy-done | bytes 524312
  7.3 1.6 %copy-done.2 = bf16[1024,1024]{1,0:T(8,128)(2,1)S(1)} copy-done((bf16[1024,1024]{1,0:T(8,128)(2,1)S(1)}, bf16[1024,1024]{1,0:T(8,128)(2,1)}, u32[]{:S(2)}) %copy-start.2) | copy-done | bytes 2097176
  8.9 0.7 %shard_map.97.up = f32[256,1024]{1,0:T(8,128)S(1)} custom-call(bf16[256,1024]{1,0:T(8,128)(2,1)S(1)} %copy-done, bf16[1024,1024]{1,0:T(8,128)(2,1)S(1)} %copy-done.2), custom_call_target="tpu_custom_call" | custom-call | flops 536870912 | bytes 8388608 | tf_op jit(solution)/shard_map/pallas_call | solution.py:41
  9.6 0.1 pad_add_fusion.1.place
  9.7 0.2 copy-done.3
  9.9 3.5 %shard_map.94 = (bf16[1536,512]{1,0:T(8,128)(2,1)S(1)}, s32[8,256]{1,0:T(8,128)S(1)}, bf16[1536,1024]{1,0:T(8,128)(2,1)S(1)}, bf16[1792,256]{1,0:T(8,128)(2,1)S(1)}) custom-call(s32[2]{0:T(128)S(1)} %pad_add_fusion.1.place, s32[7,256]{1,0:T(8,128)S(1)} %bitcast.8, s32[1,256]{1,0:T(1,128)S(1)} %bitcast.9, s32[1,256]{1,0:T(1,128)S(1)} %bitcast.10, ...), custom_call_target="tpu_custom_call" | custom-call | flops 1073741824 | bytes 8388608 | tf_op jit(solution)/shard_map/pallas_call | solution.py:41
  13.5 0.1 pad_add_fusion.me
  13.5 4.9 %shard_map.95 = (bf16[1536,1024]{1,0:T(8,128)(2,1)S(1)}, f32[256,1024]{1,0:T(8,128)S(1)}, bf16[512,256]{1,0:T(8,128)(2,1)S(1)}, bf16[512,256]{1,0:T(8,128)(2,1)S(1)}) custom-call(s32[4]{0:T(128)S(1)} %pad_add_fusion.me, bf16[256,1024]{1,0:T(8,128)(2,1)S(1)} %collective-permute-done.low, bf16[256,1024]{1,0:T(8,128)(2,1)S(1)} %collective-permute-done.1.high, ...), custom_call_target="tpu_custom_call" | custom-call | flops 3221225472 | bytes 8388608 | tf_op jit(solution)/shard_map/pallas_call | solution.py:41
  18.5 4.8 %collective-permute-start.2 = (bf16[512,256]{1,0:T(8,128)(2,1)S(1)}, bf16[512,256]{1,0:T(8,128)(2,1)S(1)}, u32[]{:S(2)}, u32[]{:S(2)}) collective-permute-start(bf16[512,256]{1,0:T(8,128)(2,1)S(1)} %get-tuple-element.36), channel_id=1, source_target_pairs={{0,1},{1,0},{2,3},{3,2},{4,5},{5,4},{6,7},{7,6},{8,9},{9,8},{10,11... | collective-permute-start | bytes 786440 | tf_op jit(solution)/shard_map/ppermute | solution.py:280
  23.2 1.9 %shard_map.98 = (bf16[256,1024]{1,0:T(8,128)(2,1)S(1)}, f32[16,128]{1,0:T(8,128)S(1)}) custom-call(f32[256,1024]{1,0:T(8,128)S(1)} %shard_map.97.up, f32[256,1024]{1,0:T(8,128)S(1)} %get-tuple-element.41.pre, bf16[256,1024]{1,0:T(8,128)(2,1)S(1)} %copy-done.3, bf16[1536,1024]{1,0:T(8,128)(2,1)S(1)} %get-tuple-element.42.rows), custom_call_target="tpu_custom_call" | custom-call | flops 2147483648 | bytes 8388608 | tf_op jit(solution)/shard_map/pallas_call | solution.py:41
  25.2 2.7 %shard_map.100 = (bf16[1536,1024]{1,0:T(8,128)(2,1)S(1)}, bf16[256,1024]{1,0:T(8,128)(2,1)S(1)}, bf16[256,1024]{1,0:T(8,128)(2,1)S(1)}) custom-call(bf16[256,1024]{1,0:T(8,128)(2,1)S(1)} %get-tuple-element.53.grad, bf16[1792,256]{1,0:T(8,128)(2,1)S(1)} %get-tuple-element.34.wk, s32[8,256]{1,0:T(8,128)S(1)} %get-tuple-element.54.sources), custom_call_target="tpu_custom_call" | custom-call | flops 3221225472 | bytes 8388608 | tf_op jit(solution)/shard_map/pallas_call | solution.py:41
  27.9 0.1 collective-permute-start.14
  27.9 4.4 %collective-permute-start.15 = (bf16[256,1024]{1,0:T(8,128)(2,1)S(1)}, bf16[256,1024]{1,0:T(8,128)(2,1)S(1)}, u32[]{:S(2)}, u32[]{:S(2)}) collective-permute-start(bf16[256,1024]{1,0:T(8,128)(2,1)S(1)} %get-tuple-element.57), channel_id=1, source_target_pairs={{0,15},{1,0},{2,1},{3,2},{4,3},{5,4},{6,5},{7,6},{8,7},{9,8},{10,9... | collective-permute-start | bytes 1572872 | tf_op jit(solution)/shard_map/ppermute | solution.py:277
  32.4 1.2 %shard_map.96 = (bf16[256,512]{1,0:T(8,128)(2,1)S(1)}, f32[256,512]{1,0:T(8,128)S(1)}, bf16[256,512]{1,0:T(8,128)(2,1)S(1)}, f32[256,512]{1,0:T(8,128)S(1)}) custom-call(s32[4]{0:T(128)S(1)} %pad_add_fusion.me, bf16[512,256]{1,0:T(8,128)(2,1)S(1)} %get-tuple-element.35.act, bf16[512,256]{1,0:T(8,128)(2,1)S(1)} %collective-permute-done.2.act_got, ...), custom_call_target="tpu_custom_call" | custom-call | flops 1073741824 | bytes 8388608 | tf_op jit(solution)/shard_map/pallas_call | solution.py:41
  33.6 0.1 collective-permute-start.4
  33.7 0.1 collective-permute-start.5
  33.8 0.1 collective-permute-start.6
  33.9 1.2 %collective-permute-done.6 = f32[16,128]{1,0:T(8,128)S(1)} collective-permute-done((f32[16,128]{1,0:T(8,128)S(1)}, f32[16,128]{1,0:T(8,128)S(1)}, u32[]{:S(2)}, u32[]{:S(2)}) %collective-permute-start.6) | collective-permute-done | bytes 8224 | tf_op jit(solution)/shard_map/ppermute | solution.py:280
  35.0 1.9 %collective-permute-start.7 = (f32[16,128]{1,0:T(8,128)S(1)}, f32[16,128]{1,0:T(8,128)S(1)}, u32[]{:S(2)}, u32[]{:S(2)}) collective-permute-start(f32[16,128]{1,0:T(8,128)S(1)} %add.3.refs_4_), channel_id=1, source_target_pairs={{0,2},{1,3},{2,0},{3,1},{4,6},{5,7},{6,4},{7,5},{8,10},{9,11},{10,... | collective-permute-start | bytes 24584 | tf_op jit(solution)/shard_map/ppermute | solution.py:280
  36.9 11.5 %collective-permute-done.7.refs_5_ = f32[16,128]{1,0:T(8,128)S(1)} collective-permute-done((f32[16,128]{1,0:T(8,128)S(1)}, f32[16,128]{1,0:T(8,128)S(1)}, u32[]{:S(2)}, u32[]{:S(2)}) %collective-permute-start.7) | collective-permute-done | bytes 8224 | tf_op jit(solution)/shard_map/ppermute | solution.py:280
  48.4 0.6 shard_map.99
  49.0 2.2 %collective-permute-start.11 = (bf16[64,512]{1,0:T(8,128)(2,1)S(1)}, bf16[64,512]{1,0:T(8,128)(2,1)S(1)}, u32[]{:S(2)}, u32[]{:S(2)}) collective-permute-start(bf16[64,512]{1,0:T(8,128)(2,1)S(1)} %get-tuple-element.49), channel_id=1, source_target_pairs={{0,8},{1,9},{2,10},{3,11},{4,12},{5,13},{6,14},{7,15},{8,0},{9,1},... | collective-permute-start | bytes 196616 | tf_op jit(solution)/shard_map/ppermute | solution.py:280
  51.2 1.3 %collective-permute-start.10 = (bf16[80,512]{1,0:T(8,128)(2,1)S(1)}, bf16[80,512]{1,0:T(8,128)(2,1)S(1)}, u32[]{:S(2)}, u32[]{:S(2)}) collective-permute-start(bf16[80,512]{1,0:T(8,128)(2,1)S(1)} %get-tuple-element.47), channel_id=1, source_target_pairs={{0,12},{1,13},{2,14},{3,15},{4,8},{5,9},{6,10},{7,11},{8,4},{9,5},... | collective-permute-start | bytes 245768 | tf_op jit(solution)/shard_map/ppermute | solution.py:280
  52.6 0.2 collective-permute-start.8
  52.8 2.8 %collective-permute-start.9 = (bf16[80,512]{1,0:T(8,128)(2,1)S(1)}, bf16[80,512]{1,0:T(8,128)(2,1)S(1)}, u32[]{:S(2)}, u32[]{:S(2)}) collective-permute-start(bf16[80,512]{1,0:T(8,128)(2,1)S(1)} %get-tuple-element.46), channel_id=1, source_target_pairs={{0,8},{1,9},{2,10},{3,11},{4,12},{5,13},{6,14},{7,15},{8,0},{9,1},... | collective-permute-start | bytes 245768 | tf_op jit(solution)/shard_map/ppermute | solution.py:280
  55.6 2.2 %collective-permute-done.11.refs_5_ = bf16[64,512]{1,0:T(8,128)(2,1)S(1)} collective-permute-done((bf16[64,512]{1,0:T(8,128)(2,1)S(1)}, bf16[64,512]{1,0:T(8,128)(2,1)S(1)}, u32[]{:S(2)}, u32[]{:S(2)}) %collective-permute-start.11) | collective-permute-done | bytes 65568 | tf_op jit(solution)/shard_map/ppermute | solution.py:280
  57.8 1.2 %shard_map.101.refs_9_ = f32[256,1024]{1,0:T(8,128)S(1)} custom-call(bf16[256,1024]{1,0:T(8,128)(2,1)S(1)} %get-tuple-element.53.grad, bf16[1536,1024]{1,0:T(8,128)(2,1)S(1)} %get-tuple-element.55.terms, bf16[1792,256]{1,0:T(8,128)(2,1)S(1)} %get-tuple-element.34.wk, s32[8,256]{1,0:T(8,128)S(1)} %get-tuple-element.54.sources, bf16[256,1024]{1,0:T(8,128)(2,1)S(1)} %copy-done.1), custom_call_target="tpu_custom_call" | custom-call | flops 1073741824 | bytes 8388608 | tf_op jit(solution)/shard_map/pallas_call | solution.py:41
  59.0 0.9 %collective-permute-done.12.refs_6_ = bf16[64,512]{1,0:T(8,128)(2,1)S(1)} collective-permute-done((bf16[64,512]{1,0:T(8,128)(2,1)S(1)}, bf16[64,512]{1,0:T(8,128)(2,1)S(1)}, u32[]{:S(2)}, u32[]{:S(2)}) %collective-permute-start.12) | collective-permute-done | bytes 65568 | tf_op jit(solution)/shard_map/ppermute | solution.py:280
  59.9 4.7 %collective-permute-done.13.refs_7_ = bf16[64,512]{1,0:T(8,128)(2,1)S(1)} collective-permute-done((bf16[64,512]{1,0:T(8,128)(2,1)S(1)}, bf16[64,512]{1,0:T(8,128)(2,1)S(1)}, u32[]{:S(2)}, u32[]{:S(2)}) %collective-permute-start.13) | collective-permute-done | bytes 65568 | tf_op jit(solution)/shard_map/ppermute | solution.py:280
  64.6 1.2 %shard_map.102 = (f32[64,1024]{1,0:T(8,128)}, f32[7,16,16]{2,1,0:T(8,128)}, bf16[256,1024]{1,0:T(8,128)(2,1)}) custom-call(f32[64,512]{1,0:T(8,128)S(1)} %get-tuple-element.44.refs_0_, bf16[80,512]{1,0:T(8,128)(2,1)S(1)} %collective-permute-done.8.refs_1_, bf16[80,512]{1,0:T(8,128)(2,1)S(1)} %collective-permute-done.9.refs_2_, ...), custom_call_target="tpu_custom_call" | custom-call | flops 1048576 | bytes 8388608 | tf_op jit(solution)/shard_map/pallas_call | solution.py:41
  (28 shorter events, 0.1 us)
Async XLA Ops:
  0.6 9.1 %copy-start.5 = (s32[256,7]{0,1:T(8,128)S(1)}, s32[256,7]{0,1:T(8,128)}, u32[]{:S(2)}) copy-start(s32[256,7]{0,1:T(8,128)} %param.11) | copy-start | bytes 21508
  0.6 9.1 %copy-start.6 = (s32[256]{0:T(256)S(1)}, s32[256]{0:T(256)}, u32[]{:S(2)}) copy-start(s32[256]{0:T(256)} %param.12) | copy-start | bytes 3076
  0.7 9.1 %copy-start.7 = (s32[256]{0:T(256)S(1)}, s32[256]{0:T(256)}, u32[]{:S(2)}) copy-start(s32[256]{0:T(256)} %param.13) | copy-start | bytes 3076
  0.7 12.9 %collective-permute-start = (bf16[256,1024]{1,0:T(8,128)(2,1)}, bf16[256,1024]{1,0:T(8,128)(2,1)S(1)}, u32[]{:S(2)}, u32[]{:S(2)}) collective-permute-start(bf16[256,1024]{1,0:T(8,128)(2,1)} %x.3), channel_id=1, source_target_pairs={{0,1},{1,2},{2,3},{3,4},{4,5},{5,6},{6,7},{7,8},{8,9},{9,10},{10,1... | collective-permute-start | bytes 1572872 | tf_op jit(solution)/shard_map/ppermute | solution.py:277
  1.2 12.3 %collective-permute-start.1 = (bf16[256,1024]{1,0:T(8,128)(2,1)}, bf16[256,1024]{1,0:T(8,128)(2,1)S(1)}, u32[]{:S(2)}, u32[]{:S(2)}) collective-permute-start(bf16[256,1024]{1,0:T(8,128)(2,1)} %x.3), channel_id=1, source_target_pairs={{0,15},{1,0},{2,1},{3,2},{4,3},{5,4},{6,5},{7,6},{8,7},{9,8},{10,9... | collective-permute-start | bytes 1572872 | tf_op jit(solution)/shard_map/ppermute | solution.py:277
  6.3 26.1 %collective-permute-start.3 = (bf16[256,1024]{1,0:T(8,128)(2,1)}, bf16[256,1024]{1,0:T(8,128)(2,1)S(1)}, u32[]{:S(2)}, u32[]{:S(2)}) collective-permute-start(bf16[256,1024]{1,0:T(8,128)(2,1)} %cot.5), channel_id=1, source_target_pairs={{0,1},{1,0},{2,3},{3,2},{4,5},{5,4},{6,7},{7,6},{8,9},{9,8},{10,11... | collective-permute-start | bytes 1572872 | tf_op jit(solution)/shard_map/ppermute | solution.py:280
  6.3 1.0 %copy-start = (bf16[256,1024]{1,0:T(8,128)(2,1)S(1)}, bf16[256,1024]{1,0:T(8,128)(2,1)}, u32[]{:S(2)}) copy-start(bf16[256,1024]{1,0:T(8,128)(2,1)} %cot.5) | copy-start | bytes 1572868
  7.3 1.6 %copy-start.2 = (bf16[1024,1024]{1,0:T(8,128)(2,1)S(1)}, bf16[1024,1024]{1,0:T(8,128)(2,1)}, u32[]{:S(2)}) copy-start(bf16[1024,1024]{1,0:T(8,128)(2,1)} %mix.1) | copy-start | bytes 6291460
  8.9 1.0 %copy-start.3 = (bf16[256,1024]{1,0:T(8,128)(2,1)S(1)}, bf16[256,1024]{1,0:T(8,128)(2,1)}, u32[]{:S(2)}) copy-start(bf16[256,1024]{1,0:T(8,128)(2,1)} %x.3) | copy-start | bytes 1572868
  8.9 1.0 %copy-start.4 = (bf16[7,16,16]{2,1,0:T(8,128)(2,1)S(1)}, bf16[7,16,16]{2,1,0:T(8,128)(2,1)}, u32[]{:S(2)}) copy-start(bf16[7,16,16]{2,1,0:T(8,128)(2,1)} %conv_hbm.1) | copy-start | bytes 10756
  18.5 13.9 %collective-permute-start.2 = (bf16[512,256]{1,0:T(8,128)(2,1)S(1)}, bf16[512,256]{1,0:T(8,128)(2,1)S(1)}, u32[]{:S(2)}, u32[]{:S(2)}) collective-permute-start(bf16[512,256]{1,0:T(8,128)(2,1)S(1)} %get-tuple-element.36), channel_id=1, source_target_pairs={{0,1},{1,0},{2,3},{3,2},{4,5},{5,4},{6,7},{7,6},{8,9},{9,8},{10,11... | collective-permute-start | bytes 786440 | tf_op jit(solution)/shard_map/ppermute | solution.py:280
  25.2 7.2 %copy-start.1 = (bf16[256,1024]{1,0:T(8,128)(2,1)S(1)}, bf16[256,1024]{1,0:T(8,128)(2,1)}, u32[]{:S(2)}) copy-start(bf16[256,1024]{1,0:T(8,128)(2,1)} %cot.5) | copy-start | bytes 1572868
  27.9 24.9 %collective-permute-start.14 = (bf16[256,1024]{1,0:T(8,128)(2,1)S(1)}, bf16[256,1024]{1,0:T(8,128)(2,1)S(1)}, u32[]{:S(2)}, u32[]{:S(2)}) collective-permute-start(bf16[256,1024]{1,0:T(8,128)(2,1)S(1)} %get-tuple-element.56), channel_id=1, source_target_pairs={{0,1},{1,2},{2,3},{3,4},{4,5},{5,6},{6,7},{7,8},{8,9},{9,10},{10,1... | collective-permute-start | bytes 1572872 | tf_op jit(solution)/shard_map/ppermute | solution.py:277
  27.9 27.7 %collective-permute-start.15 = (bf16[256,1024]{1,0:T(8,128)(2,1)S(1)}, bf16[256,1024]{1,0:T(8,128)(2,1)S(1)}, u32[]{:S(2)}, u32[]{:S(2)}) collective-permute-start(bf16[256,1024]{1,0:T(8,128)(2,1)S(1)} %get-tuple-element.57), channel_id=1, source_target_pairs={{0,15},{1,0},{2,1},{3,2},{4,3},{5,4},{6,5},{7,6},{8,7},{9,8},{10,9... | collective-permute-start | bytes 1572872 | tf_op jit(solution)/shard_map/ppermute | solution.py:277
  33.6 14.7 %collective-permute-start.4 = (bf16[256,512]{1,0:T(8,128)(2,1)S(1)}, bf16[256,512]{1,0:T(8,128)(2,1)S(1)}, u32[]{:S(2)}, u32[]{:S(2)}) collective-permute-start(bf16[256,512]{1,0:T(8,128)(2,1)S(1)} %get-tuple-element.38), channel_id=1, source_target_pairs={{0,2},{1,3},{2,0},{3,1},{4,6},{5,7},{6,4},{7,5},{8,10},{9,11},{10,... | collective-permute-start | bytes 786440 | tf_op jit(solution)/shard_map/ppermute | solution.py:280
  33.7 14.7 %collective-permute-start.5 = (bf16[256,512]{1,0:T(8,128)(2,1)S(1)}, bf16[256,512]{1,0:T(8,128)(2,1)S(1)}, u32[]{:S(2)}, u32[]{:S(2)}) collective-permute-start(bf16[256,512]{1,0:T(8,128)(2,1)S(1)} %get-tuple-element.40), channel_id=1, source_target_pairs={{0,4},{1,5},{2,6},{3,7},{4,0},{5,1},{6,2},{7,3},{8,12},{9,13},{10,... | collective-permute-start | bytes 786440 | tf_op jit(solution)/shard_map/ppermute | solution.py:280
  33.8 1.2 %collective-permute-start.6 = (f32[16,128]{1,0:T(8,128)S(1)}, f32[16,128]{1,0:T(8,128)S(1)}, u32[]{:S(2)}, u32[]{:S(2)}) collective-permute-start(f32[16,128]{1,0:T(8,128)S(1)} %get-tuple-element.43), channel_id=1, source_target_pairs={{0,1},{1,0},{2,3},{3,2},{4,5},{5,4},{6,7},{7,6},{8,9},{9,8},{10,11... | collective-permute-start | bytes 24584 | tf_op jit(solution)/shard_map/ppermute | solution.py:280
  35.0 13.3 %collective-permute-start.7 = (f32[16,128]{1,0:T(8,128)S(1)}, f32[16,128]{1,0:T(8,128)S(1)}, u32[]{:S(2)}, u32[]{:S(2)}) collective-permute-start(f32[16,128]{1,0:T(8,128)S(1)} %add.3.refs_4_), channel_id=1, source_target_pairs={{0,2},{1,3},{2,0},{3,1},{4,6},{5,7},{6,4},{7,5},{8,10},{9,11},{10,... | collective-permute-start | bytes 24584 | tf_op jit(solution)/shard_map/ppermute | solution.py:280
  49.0 8.8 %collective-permute-start.11 = (bf16[64,512]{1,0:T(8,128)(2,1)S(1)}, bf16[64,512]{1,0:T(8,128)(2,1)S(1)}, u32[]{:S(2)}, u32[]{:S(2)}) collective-permute-start(bf16[64,512]{1,0:T(8,128)(2,1)S(1)} %get-tuple-element.49), channel_id=1, source_target_pairs={{0,8},{1,9},{2,10},{3,11},{4,12},{5,13},{6,14},{7,15},{8,0},{9,1},... | collective-permute-start | bytes 196616 | tf_op jit(solution)/shard_map/ppermute | solution.py:280
  51.2 13.4 %collective-permute-start.10 = (bf16[80,512]{1,0:T(8,128)(2,1)S(1)}, bf16[80,512]{1,0:T(8,128)(2,1)S(1)}, u32[]{:S(2)}, u32[]{:S(2)}) collective-permute-start(bf16[80,512]{1,0:T(8,128)(2,1)S(1)} %get-tuple-element.47), channel_id=1, source_target_pairs={{0,12},{1,13},{2,14},{3,15},{4,8},{5,9},{6,10},{7,11},{8,4},{9,5},... | collective-permute-start | bytes 245768 | tf_op jit(solution)/shard_map/ppermute | solution.py:280
  52.6 12.0 %collective-permute-start.8 = (bf16[80,512]{1,0:T(8,128)(2,1)S(1)}, bf16[80,512]{1,0:T(8,128)(2,1)S(1)}, u32[]{:S(2)}, u32[]{:S(2)}) collective-permute-start(bf16[80,512]{1,0:T(8,128)(2,1)S(1)} %get-tuple-element.45), channel_id=1, source_target_pairs={{0,4},{1,5},{2,6},{3,7},{4,0},{5,1},{6,2},{7,3},{8,12},{9,13},{10,... | collective-permute-start | bytes 245768 | tf_op jit(solution)/shard_map/ppermute | solution.py:280
  52.8 11.8 %collective-permute-start.9 = (bf16[80,512]{1,0:T(8,128)(2,1)S(1)}, bf16[80,512]{1,0:T(8,128)(2,1)S(1)}, u32[]{:S(2)}, u32[]{:S(2)}) collective-permute-start(bf16[80,512]{1,0:T(8,128)(2,1)S(1)} %get-tuple-element.46), channel_id=1, source_target_pairs={{0,8},{1,9},{2,10},{3,11},{4,12},{5,13},{6,14},{7,15},{8,0},{9,1},... | collective-permute-start | bytes 245768 | tf_op jit(solution)/shard_map/ppermute | solution.py:280
  55.6 4.3 %collective-permute-start.12 = (bf16[64,512]{1,0:T(8,128)(2,1)S(1)}, bf16[64,512]{1,0:T(8,128)(2,1)S(1)}, u32[]{:S(2)}, u32[]{:S(2)}) collective-permute-start(bf16[64,512]{1,0:T(8,128)(2,1)S(1)} %get-tuple-element.50), channel_id=1, source_target_pairs={{0,2},{1,3},{2,0},{3,1},{4,6},{5,7},{6,4},{7,5},{8,10},{9,11},{10,... | collective-permute-start | bytes 196616 | tf_op jit(solution)/shard_map/ppermute | solution.py:280
  57.8 6.8 %collective-permute-start.13 = (bf16[64,512]{1,0:T(8,128)(2,1)S(1)}, bf16[64,512]{1,0:T(8,128)(2,1)S(1)}, u32[]{:S(2)}, u32[]{:S(2)}) collective-permute-start(bf16[64,512]{1,0:T(8,128)(2,1)S(1)} %get-tuple-element.51), channel_id=1, source_target_pairs={{0,10},{1,11},{2,8},{3,9},{4,14},{5,15},{6,12},{7,13},{8,2},{9,3},... | collective-permute-start | bytes 196616 | tf_op jit(solution)/shard_map/ppermute | solution.py:280

commit v5 on v4

--- a/solution.py
+++ b/solution.py
@@ -68,6 +68,7 @@
     n = x.shape[0]
     taps, c = conv.shape[:2]
     offset, total = place[0], place[1]
+    base_far, base_near = place[2], place[3]
     moved = near[...] - offset + ROW
     moved = jnp.where(moved < 0, moved + total, moved)
     moved = jnp.where(moved >= total, moved - total, moved)
@@ -91,8 +92,8 @@
     for tap in range(1, taps):
         at = (tap - 1) * n
         source = columns[:, tap - 1 : tap]
-        halo_sel[at : at + n, :ROW] = onehot(iota((n, ROW), 1) == source)
-        halo_sel[at : at + n, ROW:] = onehot(iota((n, ROW), 1) + (ROW + n) == source)
+        halo_sel[at : at + n, :ROW] = onehot(iota((n, ROW), 1) == source - base_far)
+        halo_sel[at : at + n, ROW:] = onehot(iota((n, ROW), 1) == source - base_near)
         mine = onehot(iota((n, n), 1) + ROW == source)
         own[at : at + n, :] = mm(mine, x[...]).astype(bf16)
 
@@ -101,11 +102,11 @@
     return jnp.tanh(TANH_SCALE * (v + TANH_CUBE * (v * v * v)))
 
 
-def front_kernel(share, me, low, high, halo_sel, own, wk, x, rows_out, pre, act_keep, act_send, act_t):
+def front_kernel(share, me, far, near, halo_sel, own, wk, x, rows_out, pre, act_keep, act_send, act_t):
     n, width = pre.shape
     taps = wk.shape[0] // WIDE
     for c in range(0, width, WIDE):
-        both = jnp.concatenate([low[:, c : c + WIDE], high[:, c : c + WIDE]], axis=0)
+        both = jnp.concatenate([far[:, c : c + WIDE], near[:, c : c + WIDE]], axis=0)
         rows = mm(halo_sel[...], both).astype(bf16) + own[:, c : c + WIDE]
         rows_out[:, c : c + WIDE] = rows
         acc = mm(x[:, c : c + WIDE], wk[:WIDE, :])
@@ -142,7 +143,7 @@
 def select_rows(sources, start, count, taps):
     n = sources.shape[1]
     return jnp.concatenate(
-        [onehot(iota((count, n), 0) + start == sources[tap : tap + 1, :]) for tap in range(taps - 1)], axis=1
+        [onehot(iota((count, n), 0) == sources[tap : tap + 1, :] - start) for tap in range(taps - 1)], axis=1
     )
 
 
@@ -171,11 +172,11 @@
         )
 
 
-def terms_kernel(grad, wk, sources, terms, low, high, back_sel):
+def terms_kernel(place, grad, wk, sources, terms, far, near, back_sel):
     n, width = grad.shape
     taps = wk.shape[0] // WIDE
-    back_sel[:ROW, :] = select_rows(sources, 0, ROW, taps)
-    back_sel[ROW:, :] = select_rows(sources, ROW + n, ROW, taps)
+    back_sel[:ROW, :] = select_rows(sources, place[2], ROW, taps)
+    back_sel[ROW:, :] = select_rows(sources, place[3], ROW, taps)
     for c in range(0, width, WIDE):
         g = grad[:, c : c + WIDE]
         for tap in range(1, taps):
@@ -183,8 +184,8 @@
                 g, wk[tap * WIDE : (tap + 1) * WIDE, :], 1, 1
             ).astype(bf16)
         both = mm(back_sel[...], terms[:, c : c + WIDE]).astype(bf16)
-        low[:, c : c + WIDE] = both[:ROW]
-        high[:, c : c + WIDE] = both[ROW:]
+        far[:, c : c + WIDE] = both[:ROW]
+        near[:, c : c + WIDE] = both[ROW:]
 
 
 def inner_kernel(grad, terms, wk, sources, cot, inner):
@@ -273,8 +274,12 @@
     levels = width // channels
     bits = devices.bit_length() - 1
 
-    def ring(value, by):
-        return lax.ppermute(value, "space", [(i, (i + by) % devices) for i in range(devices)])
+    def near_swap(value):
+        return lax.ppermute(value, "space", [(i, i ^ 1) for i in range(devices)])
+
+    def far_swap(value):
+        other = lambda i: (i + 1 if i % 2 else i - 1) % devices
+        return lax.ppermute(value, "space", [(i, other(i)) for i in range(devices)])
 
     def swap_by(value, mask):
         return lax.ppermute(value, "space", [(i, i ^ mask) for i in range(devices)])
@@ -282,8 +287,10 @@
     def swap(value, bit):
         return swap_by(value, 1 << bit)
 
-    below = ring(columns_in, 1)
-    above = ring(columns_in, -1)
+    far = far_swap(columns_in)
+    near = near_swap(columns_in)
+    odd = place & 1
+    spots = jnp.stack([place * n, jnp.int32(total_cols), odd * (ROW + n), (1 - odd) * (ROW + n)])
     cot_got = swap(cotangent, 0)
     pairs = (taps - 1) * n
     share = width // devices
@@ -293,7 +300,7 @@
         early_kernel,
         [((pairs, 2 * ROW), bf16), ((8, n), jnp.int32), ((pairs, width), bf16), ((taps * WIDE, WIDE), bf16)],
         1 << 30,
-        jnp.stack([place * n, jnp.int32(total_cols)]),
+        spots,
         neighbours.T,
         rotations[None, :],
         pentagons[None, :],
@@ -313,8 +320,8 @@
         [((pairs, width), bf16), ((n, width), f32), ((half, n), bf16), ((half, n), bf16)],
         3 << 30,
         mine,
-        below,
-        above,
+        far,
+        near,
         halo_sel,
         own,
         wk,
@@ -359,19 +366,21 @@
         columns_in,
         rows,
     )
-    terms, to_low, to_high = call(
+    terms, to_far, to_near = call(
         terms_kernel,
         [((pairs, width), bf16), ((ROW, width), bf16), ((ROW, width), bf16)],
         3 << 30,
+        spots,
         grad,
         wk,
         sources,
+        scalars=1,
         scratch=[pltpu.VMEM((2 * ROW, pairs), bf16)],
     )
     conv = conv + swap(conv, 0)
     conv_got = swap(conv, 1)
-    from_below = ring(to_high, 1)
-    from_above = ring(to_low, -1)
+    from_far = far_swap(to_far)
+    from_near = near_swap(to_near)
     for stage in range(1, bits - 1, 2):
         rows_left //= 4
         pair = [order[stage : stage + 2] for order in orders]
@@ -413,8 +422,8 @@
         *gots[1],
         conv,
         inner,
-        from_below,
-        from_above,
+        from_far,
+        from_near,
     )
     return grad_input, grad_mix, grad_conv
 

time: 66 us -> 64.9 us (0.983)
  waiting for transfers between devices: 20.4 us -> 17.9 us
  starting transfers between devices: 23.5 us -> 24.5 us
    ppermute x12, waiting for transfers between devices: 20.4 us -> 17.9 us  [swap_by(): return lax.ppermute(value, 'space', [(i, i ^ mask) for i in range(devices)])]
    ppermute x12, starting transfers between devices: 13.5 us -> 14.1 us  [swap_by(): return lax.ppermute(value, 'space', [(i, i ^ mask) for i in range(devices)])]
  transfers between devices with their start and end apart: 16 -> 16, of which waited for: 5 -> 4; matrix products, arithmetic and copies ran while one was open for 0% -> 0% of each run, Pallas kernels for 26% -> 27%
where the time goes in v5:
time: 64.9 us; the launch traced here: 64.7 us
  starting transfers between devices  24.5 us (38%)
  Pallas kernels  18.5 us (29%)
  waiting for transfers between devices  17.9 us (28%)
  local copies, waits for them, and re-layouts  2.85 us (4%)
  between operations  0.77 us (1%)
    pallas_call x9, Pallas kernels, call(): pl.pallas_call(body, out_shape=[jax.ShapeDtypeStruct(s, d) for s, d in ou...  18.5 us
    ppermute x12, waiting for transfers between devices, swap_by(): return lax.ppermute(value, 'space', [(i, i ^ mask) for i in range(devices)])  17.9 us
    ppermute x12, starting transfers between devices, swap_by(): return lax.ppermute(value, 'space', [(i, i ^ mask) for i in range(devices)])  14.1 us
    ppermute x2, starting transfers between devices, far_swap(): return lax.ppermute(value, 'space', [(i, other(i)) for i in range(devices)])  10.4 us
    unnamed x16, local copies, waits for them, and re-layouts  2.85 us
  transfers between devices with their start and end apart: 16, of which 4 were waited for; matrix products, arithmetic and copies ran while one was open for 0% of the time, Pallas kernels for 27%

profile of v5, /device:TPU:0, one launch (start us, length us, event | category | flops | bytes accessed | tf_op | source)
XLA Modules:
  0.0 64.7 jit_solution(4793787012386028619)
XLA Ops:
  0.7 5.5 %collective-permute-start = (bf16[256,1024]{1,0:T(8,128)(2,1)}, bf16[256,1024]{1,0:T(8,128)(2,1)S(1)}, u32[]{:S(2)}, u32[]{:S(2)}) collective-permute-start(bf16[256,1024]{1,0:T(8,128)(2,1)} %x.3), channel_id=1, source_target_pairs={{0,15},{1,2},{2,1},{3,4},{4,3},{5,6},{6,5},{7,8},{8,7},{9,10},{10,... | collective-permute-start | bytes 1572872 | tf_op jit(solution)/shard_map/ppermute | solution.py:282
  6.2 0.0 collective-permute-start.1
  6.2 0.5 collective-permute-start.3
  6.7 1.0 %copy-done = bf16[256,1024]{1,0:T(8,128)(2,1)S(1)} copy-done((bf16[256,1024]{1,0:T(8,128)(2,1)S(1)}, bf16[256,1024]{1,0:T(8,128)(2,1)}, u32[]{:S(2)}) %copy-start) | copy-done | bytes 524312
  7.8 1.6 %copy-done.2 = bf16[1024,1024]{1,0:T(8,128)(2,1)S(1)} copy-done((bf16[1024,1024]{1,0:T(8,128)(2,1)S(1)}, bf16[1024,1024]{1,0:T(8,128)(2,1)}, u32[]{:S(2)}) %copy-start.2) | copy-done | bytes 2097176
  9.3 0.7 %shard_map.97.up = f32[256,1024]{1,0:T(8,128)S(1)} custom-call(bf16[256,1024]{1,0:T(8,128)(2,1)S(1)} %copy-done, bf16[1024,1024]{1,0:T(8,128)(2,1)S(1)} %copy-done.2), custom_call_target="tpu_custom_call" | custom-call | flops 536870912 | bytes 8388608 | tf_op jit(solution)/shard_map/pallas_call | solution.py:41
  10.1 0.1 pad_add_fusion.1.place
  10.2 0.2 copy-done.3
  10.4 3.5 %shard_map.94 = (bf16[1536,512]{1,0:T(8,128)(2,1)S(1)}, s32[8,256]{1,0:T(8,128)S(1)}, bf16[1536,1024]{1,0:T(8,128)(2,1)S(1)}, bf16[1792,256]{1,0:T(8,128)(2,1)S(1)}) custom-call(s32[4]{0:T(128)S(1)} %pad_add_fusion.1.place, s32[7,256]{1,0:T(8,128)S(1)} %bitcast.10, s32[1,256]{1,0:T(1,128)S(1)} %bitcast.11, s32[1,256]{1,0:T(1,128)S(1)} %bitcast.12, ...), custom_call_target="tpu_custom_call" | custom-call | flops 1073741824 | bytes 8388608 | tf_op jit(solution)/shard_map/pallas_call | solution.py:41
  13.9 0.1 pad_add_fusion.me
  14.0 4.9 %shard_map.95 = (bf16[1536,1024]{1,0:T(8,128)(2,1)S(1)}, f32[256,1024]{1,0:T(8,128)S(1)}, bf16[512,256]{1,0:T(8,128)(2,1)S(1)}, bf16[512,256]{1,0:T(8,128)(2,1)S(1)}) custom-call(s32[4]{0:T(128)S(1)} %pad_add_fusion.me, bf16[256,1024]{1,0:T(8,128)(2,1)S(1)} %collective-permute-done.far, bf16[256,1024]{1,0:T(8,128)(2,1)S(1)} %collective-permute-done.1.near, ...), custom_call_target="tpu_custom_call" | custom-call | flops 3221225472 | bytes 8388608 | tf_op jit(solution)/shard_map/pallas_call | solution.py:41
  18.9 2.6 %collective-permute-start.2 = (bf16[512,256]{1,0:T(8,128)(2,1)S(1)}, bf16[512,256]{1,0:T(8,128)(2,1)S(1)}, u32[]{:S(2)}, u32[]{:S(2)}) collective-permute-start(bf16[512,256]{1,0:T(8,128)(2,1)S(1)} %get-tuple-element.36), channel_id=1, source_target_pairs={{0,1},{1,0},{2,3},{3,2},{4,5},{5,4},{6,7},{7,6},{8,9},{9,8},{10,11... | collective-permute-start | bytes 786440 | tf_op jit(solution)/shard_map/ppermute | solution.py:285
  21.5 1.9 %shard_map.98 = (bf16[256,1024]{1,0:T(8,128)(2,1)S(1)}, f32[16,128]{1,0:T(8,128)S(1)}) custom-call(f32[256,1024]{1,0:T(8,128)S(1)} %shard_map.97.up, f32[256,1024]{1,0:T(8,128)S(1)} %get-tuple-element.41.pre, bf16[256,1024]{1,0:T(8,128)(2,1)S(1)} %copy-done.3, bf16[1536,1024]{1,0:T(8,128)(2,1)S(1)} %get-tuple-element.42.rows), custom_call_target="tpu_custom_call" | custom-call | flops 2147483648 | bytes 8388608 | tf_op jit(solution)/shard_map/pallas_call | solution.py:41
  23.4 3.2 %shard_map.100 = (bf16[1536,1024]{1,0:T(8,128)(2,1)S(1)}, bf16[256,1024]{1,0:T(8,128)(2,1)S(1)}, bf16[256,1024]{1,0:T(8,128)(2,1)S(1)}) custom-call(s32[4]{0:T(128)S(1)} %pad_add_fusion.1.place, bf16[256,1024]{1,0:T(8,128)(2,1)S(1)} %get-tuple-element.53.grad, bf16[1792,256]{1,0:T(8,128)(2,1)S(1)} %get-tuple-element.34.wk, ...), custom_call_target="tpu_custom_call" | custom-call | flops 3221225472 | bytes 8388608 | tf_op jit(solution)/shard_map/pallas_call | solution.py:41
  26.6 4.9 %collective-permute-start.14 = (bf16[256,1024]{1,0:T(8,128)(2,1)S(1)}, bf16[256,1024]{1,0:T(8,128)(2,1)S(1)}, u32[]{:S(2)}, u32[]{:S(2)}) collective-permute-start(bf16[256,1024]{1,0:T(8,128)(2,1)S(1)} %get-tuple-element.56), channel_id=1, source_target_pairs={{0,15},{1,2},{2,1},{3,4},{4,3},{5,6},{6,5},{7,8},{8,7},{9,10},{10,... | collective-permute-start | bytes 1572872 | tf_op jit(solution)/shard_map/ppermute | solution.py:282
  31.5 1.2 %shard_map.96 = (bf16[256,512]{1,0:T(8,128)(2,1)S(1)}, f32[256,512]{1,0:T(8,128)S(1)}, bf16[256,512]{1,0:T(8,128)(2,1)S(1)}, f32[256,512]{1,0:T(8,128)S(1)}) custom-call(s32[4]{0:T(128)S(1)} %pad_add_fusion.me, bf16[512,256]{1,0:T(8,128)(2,1)S(1)} %get-tuple-element.35.act, bf16[512,256]{1,0:T(8,128)(2,1)S(1)} %collective-permute-done.2.act_got, ...), custom_call_target="tpu_custom_call" | custom-call | flops 1073741824 | bytes 8388608 | tf_op jit(solution)/shard_map/pallas_call | solution.py:41
  32.8 0.1 collective-permute-start.4
  32.9 0.1 collective-permute-start.5
  32.9 0.6 collective-permute-start.6
  33.5 0.8 %collective-permute-done.6 = f32[16,128]{1,0:T(8,128)S(1)} collective-permute-done((f32[16,128]{1,0:T(8,128)S(1)}, f32[16,128]{1,0:T(8,128)S(1)}, u32[]{:S(2)}, u32[]{:S(2)}) %collective-permute-start.6) | collective-permute-done | bytes 8224 | tf_op jit(solution)/shard_map/ppermute | solution.py:285
  34.3 1.7 %collective-permute-start.7 = (f32[16,128]{1,0:T(8,128)S(1)}, f32[16,128]{1,0:T(8,128)S(1)}, u32[]{:S(2)}, u32[]{:S(2)}) collective-permute-start(f32[16,128]{1,0:T(8,128)S(1)} %add.3.refs_4_), channel_id=1, source_target_pairs={{0,2},{1,3},{2,0},{3,1},{4,6},{5,7},{6,4},{7,5},{8,10},{9,11},{10,... | collective-permute-start | bytes 24584 | tf_op jit(solution)/shard_map/ppermute | solution.py:285
  36.0 10.9 %collective-permute-done.7.refs_5_ = f32[16,128]{1,0:T(8,128)S(1)} collective-permute-done((f32[16,128]{1,0:T(8,128)S(1)}, f32[16,128]{1,0:T(8,128)S(1)}, u32[]{:S(2)}, u32[]{:S(2)}) %collective-permute-start.7) | collective-permute-done | bytes 8224 | tf_op jit(solution)/shard_map/ppermute | solution.py:285
  47.0 0.6 shard_map.99
  47.6 2.6 %collective-permute-start.11 = (bf16[64,512]{1,0:T(8,128)(2,1)S(1)}, bf16[64,512]{1,0:T(8,128)(2,1)S(1)}, u32[]{:S(2)}, u32[]{:S(2)}) collective-permute-start(bf16[64,512]{1,0:T(8,128)(2,1)S(1)} %get-tuple-element.49), channel_id=1, source_target_pairs={{0,8},{1,9},{2,10},{3,11},{4,12},{5,13},{6,14},{7,15},{8,0},{9,1},... | collective-permute-start | bytes 196616 | tf_op jit(solution)/shard_map/ppermute | solution.py:285
  50.3 1.3 %collective-permute-start.10 = (bf16[80,512]{1,0:T(8,128)(2,1)S(1)}, bf16[80,512]{1,0:T(8,128)(2,1)S(1)}, u32[]{:S(2)}, u32[]{:S(2)}) collective-permute-start(bf16[80,512]{1,0:T(8,128)(2,1)S(1)} %get-tuple-element.47), channel_id=1, source_target_pairs={{0,12},{1,13},{2,14},{3,15},{4,8},{5,9},{6,10},{7,11},{8,4},{9,5},... | collective-permute-start | bytes 245768 | tf_op jit(solution)/shard_map/ppermute | solution.py:285
  51.6 0.2 collective-permute-start.8
  51.8 2.8 %collective-permute-start.9 = (bf16[80,512]{1,0:T(8,128)(2,1)S(1)}, bf16[80,512]{1,0:T(8,128)(2,1)S(1)}, u32[]{:S(2)}, u32[]{:S(2)}) collective-permute-start(bf16[80,512]{1,0:T(8,128)(2,1)S(1)} %get-tuple-element.46), channel_id=1, source_target_pairs={{0,8},{1,9},{2,10},{3,11},{4,12},{5,13},{6,14},{7,15},{8,0},{9,1},... | collective-permute-start | bytes 245768 | tf_op jit(solution)/shard_map/ppermute | solution.py:285
  54.7 1.6 %collective-permute-start.13 = (bf16[64,512]{1,0:T(8,128)(2,1)S(1)}, bf16[64,512]{1,0:T(8,128)(2,1)S(1)}, u32[]{:S(2)}, u32[]{:S(2)}) collective-permute-start(bf16[64,512]{1,0:T(8,128)(2,1)S(1)} %get-tuple-element.51), channel_id=1, source_target_pairs={{0,10},{1,11},{2,8},{3,9},{4,14},{5,15},{6,12},{7,13},{8,2},{9,3},... | collective-permute-start | bytes 196616 | tf_op jit(solution)/shard_map/ppermute | solution.py:285
  56.2 1.2 %shard_map.101.refs_9_ = f32[256,1024]{1,0:T(8,128)S(1)} custom-call(bf16[256,1024]{1,0:T(8,128)(2,1)S(1)} %get-tuple-element.53.grad, bf16[1536,1024]{1,0:T(8,128)(2,1)S(1)} %get-tuple-element.55.terms, bf16[1792,256]{1,0:T(8,128)(2,1)S(1)} %get-tuple-element.34.wk, s32[8,256]{1,0:T(8,128)S(1)} %get-tuple-element.54.sources, bf16[256,1024]{1,0:T(8,128)(2,1)S(1)} %copy-done.1), custom_call_target="tpu_custom_call" | custom-call | flops 1073741824 | bytes 8388608 | tf_op jit(solution)/shard_map/pallas_call | solution.py:41
  57.4 1.5 %collective-permute-done.12.refs_6_ = bf16[64,512]{1,0:T(8,128)(2,1)S(1)} collective-permute-done((bf16[64,512]{1,0:T(8,128)(2,1)S(1)}, bf16[64,512]{1,0:T(8,128)(2,1)S(1)}, u32[]{:S(2)}, u32[]{:S(2)}) %collective-permute-start.12) | collective-permute-done | bytes 65568 | tf_op jit(solution)/shard_map/ppermute | solution.py:285
  58.9 4.6 %collective-permute-done.13.refs_7_ = bf16[64,512]{1,0:T(8,128)(2,1)S(1)} collective-permute-done((bf16[64,512]{1,0:T(8,128)(2,1)S(1)}, bf16[64,512]{1,0:T(8,128)(2,1)S(1)}, u32[]{:S(2)}, u32[]{:S(2)}) %collective-permute-start.13) | collective-permute-done | bytes 65568 | tf_op jit(solution)/shard_map/ppermute | solution.py:285
  63.5 1.2 %shard_map.102 = (f32[64,1024]{1,0:T(8,128)}, f32[7,16,16]{2,1,0:T(8,128)}, bf16[256,1024]{1,0:T(8,128)(2,1)}) custom-call(f32[64,512]{1,0:T(8,128)S(1)} %get-tuple-element.44.refs_0_, bf16[80,512]{1,0:T(8,128)(2,1)S(1)} %collective-permute-done.8.refs_1_, bf16[80,512]{1,0:T(8,128)(2,1)S(1)} %collective-permute-done.9.refs_2_, ...), custom_call_target="tpu_custom_call" | custom-call | flops 1048576 | bytes 8388608 | tf_op jit(solution)/shard_map/pallas_call | solution.py:41
  (28 shorter events, 0.1 us)
Async XLA Ops:
  0.6 9.5 %copy-start.6 = (s32[256]{0:T(256)S(1)}, s32[256]{0:T(256)}, u32[]{:S(2)}) copy-start(s32[256]{0:T(256)} %param.12) | copy-start | bytes 3076
  0.6 9.5 %copy-start.7 = (s32[256]{0:T(256)S(1)}, s32[256]{0:T(256)}, u32[]{:S(2)}) copy-start(s32[256]{0:T(256)} %param.13) | copy-start | bytes 3076
  0.7 9.5 %copy-start.4 = (bf16[7,16,16]{2,1,0:T(8,128)(2,1)S(1)}, bf16[7,16,16]{2,1,0:T(8,128)(2,1)}, u32[]{:S(2)}) copy-start(bf16[7,16,16]{2,1,0:T(8,128)(2,1)} %conv_hbm.1) | copy-start | bytes 10756
  0.7 13.3 %collective-permute-start = (bf16[256,1024]{1,0:T(8,128)(2,1)}, bf16[256,1024]{1,0:T(8,128)(2,1)S(1)}, u32[]{:S(2)}, u32[]{:S(2)}) collective-permute-start(bf16[256,1024]{1,0:T(8,128)(2,1)} %x.3), channel_id=1, source_target_pairs={{0,15},{1,2},{2,1},{3,4},{4,3},{5,6},{6,5},{7,8},{8,7},{9,10},{10,... | collective-permute-start | bytes 1572872 | tf_op jit(solution)/shard_map/ppermute | solution.py:282
  6.2 7.8 %collective-permute-start.1 = (bf16[256,1024]{1,0:T(8,128)(2,1)}, bf16[256,1024]{1,0:T(8,128)(2,1)S(1)}, u32[]{:S(2)}, u32[]{:S(2)}) collective-permute-start(bf16[256,1024]{1,0:T(8,128)(2,1)} %x.3), channel_id=1, source_target_pairs={{0,1},{1,0},{2,3},{3,2},{4,5},{5,4},{6,7},{7,6},{8,9},{9,8},{10,11... | collective-permute-start | bytes 1572872 | tf_op jit(solution)/shard_map/ppermute | solution.py:278
  6.2 25.3 %collective-permute-start.3 = (bf16[256,1024]{1,0:T(8,128)(2,1)}, bf16[256,1024]{1,0:T(8,128)(2,1)S(1)}, u32[]{:S(2)}, u32[]{:S(2)}) collective-permute-start(bf16[256,1024]{1,0:T(8,128)(2,1)} %cot.5), channel_id=1, source_target_pairs={{0,1},{1,0},{2,3},{3,2},{4,5},{5,4},{6,7},{7,6},{8,9},{9,8},{10,11... | collective-permute-start | bytes 1572872 | tf_op jit(solution)/shard_map/ppermute | solution.py:285
  6.7 1.0 %copy-start = (bf16[256,1024]{1,0:T(8,128)(2,1)S(1)}, bf16[256,1024]{1,0:T(8,128)(2,1)}, u32[]{:S(2)}) copy-start(bf16[256,1024]{1,0:T(8,128)(2,1)} %cot.5) | copy-start | bytes 1572868
  7.8 1.6 %copy-start.2 = (bf16[1024,1024]{1,0:T(8,128)(2,1)S(1)}, bf16[1024,1024]{1,0:T(8,128)(2,1)}, u32[]{:S(2)}) copy-start(bf16[1024,1024]{1,0:T(8,128)(2,1)} %mix.1) | copy-start | bytes 6291460
  9.3 1.0 %copy-start.3 = (bf16[256,1024]{1,0:T(8,128)(2,1)S(1)}, bf16[256,1024]{1,0:T(8,128)(2,1)}, u32[]{:S(2)}) copy-start(bf16[256,1024]{1,0:T(8,128)(2,1)} %x.3) | copy-start | bytes 1572868
  9.3 1.0 %copy-start.5 = (s32[256,7]{0,1:T(8,128)S(1)}, s32[256,7]{0,1:T(8,128)}, u32[]{:S(2)}) copy-start(s32[256,7]{0,1:T(8,128)} %param.11) | copy-start | bytes 21508
  18.9 12.6 %collective-permute-start.2 = (bf16[512,256]{1,0:T(8,128)(2,1)S(1)}, bf16[512,256]{1,0:T(8,128)(2,1)S(1)}, u32[]{:S(2)}, u32[]{:S(2)}) collective-permute-start(bf16[512,256]{1,0:T(8,128)(2,1)S(1)} %get-tuple-element.36), channel_id=1, source_target_pairs={{0,1},{1,0},{2,3},{3,2},{4,5},{5,4},{6,7},{7,6},{8,9},{9,8},{10,11... | collective-permute-start | bytes 786440 | tf_op jit(solution)/shard_map/ppermute | solution.py:285
  23.4 8.1 %copy-start.1 = (bf16[256,1024]{1,0:T(8,128)(2,1)S(1)}, bf16[256,1024]{1,0:T(8,128)(2,1)}, u32[]{:S(2)}) copy-start(bf16[256,1024]{1,0:T(8,128)(2,1)} %cot.5) | copy-start | bytes 1572868
  26.6 25.2 %collective-permute-start.14 = (bf16[256,1024]{1,0:T(8,128)(2,1)S(1)}, bf16[256,1024]{1,0:T(8,128)(2,1)S(1)}, u32[]{:S(2)}, u32[]{:S(2)}) collective-permute-start(bf16[256,1024]{1,0:T(8,128)(2,1)S(1)} %get-tuple-element.56), channel_id=1, source_target_pairs={{0,15},{1,2},{2,1},{3,4},{4,3},{5,6},{6,5},{7,8},{8,7},{9,10},{10,... | collective-permute-start | bytes 1572872 | tf_op jit(solution)/shard_map/ppermute | solution.py:282
  31.5 23.2 %collective-permute-start.15 = (bf16[256,1024]{1,0:T(8,128)(2,1)S(1)}, bf16[256,1024]{1,0:T(8,128)(2,1)S(1)}, u32[]{:S(2)}, u32[]{:S(2)}) collective-permute-start(bf16[256,1024]{1,0:T(8,128)(2,1)S(1)} %get-tuple-element.57), channel_id=1, source_target_pairs={{0,1},{1,0},{2,3},{3,2},{4,5},{5,4},{6,7},{7,6},{8,9},{9,8},{10,11... | collective-permute-start | bytes 1572872 | tf_op jit(solution)/shard_map/ppermute | solution.py:278
  32.8 14.2 %collective-permute-start.4 = (bf16[256,512]{1,0:T(8,128)(2,1)S(1)}, bf16[256,512]{1,0:T(8,128)(2,1)S(1)}, u32[]{:S(2)}, u32[]{:S(2)}) collective-permute-start(bf16[256,512]{1,0:T(8,128)(2,1)S(1)} %get-tuple-element.38), channel_id=1, source_target_pairs={{0,2},{1,3},{2,0},{3,1},{4,6},{5,7},{6,4},{7,5},{8,10},{9,11},{10,... | collective-permute-start | bytes 786440 | tf_op jit(solution)/shard_map/ppermute | solution.py:285
  32.9 14.1 %collective-permute-start.5 = (bf16[256,512]{1,0:T(8,128)(2,1)S(1)}, bf16[256,512]{1,0:T(8,128)(2,1)S(1)}, u32[]{:S(2)}, u32[]{:S(2)}) collective-permute-start(bf16[256,512]{1,0:T(8,128)(2,1)S(1)} %get-tuple-element.40), channel_id=1, source_target_pairs={{0,4},{1,5},{2,6},{3,7},{4,0},{5,1},{6,2},{7,3},{8,12},{9,13},{10,... | collective-permute-start | bytes 786440 | tf_op jit(solution)/shard_map/ppermute | solution.py:285
  32.9 1.4 %collective-permute-start.6 = (f32[16,128]{1,0:T(8,128)S(1)}, f32[16,128]{1,0:T(8,128)S(1)}, u32[]{:S(2)}, u32[]{:S(2)}) collective-permute-start(f32[16,128]{1,0:T(8,128)S(1)} %get-tuple-element.43), channel_id=1, source_target_pairs={{0,1},{1,0},{2,3},{3,2},{4,5},{5,4},{6,7},{7,6},{8,9},{9,8},{10,11... | collective-permute-start | bytes 24584 | tf_op jit(solution)/shard_map/ppermute | solution.py:285
  34.3 12.6 %collective-permute-start.7 = (f32[16,128]{1,0:T(8,128)S(1)}, f32[16,128]{1,0:T(8,128)S(1)}, u32[]{:S(2)}, u32[]{:S(2)}) collective-permute-start(f32[16,128]{1,0:T(8,128)S(1)} %add.3.refs_4_), channel_id=1, source_target_pairs={{0,2},{1,3},{2,0},{3,1},{4,6},{5,7},{6,4},{7,5},{8,10},{9,11},{10,... | collective-permute-start | bytes 24584 | tf_op jit(solution)/shard_map/ppermute | solution.py:285
  47.6 7.1 %collective-permute-start.11 = (bf16[64,512]{1,0:T(8,128)(2,1)S(1)}, bf16[64,512]{1,0:T(8,128)(2,1)S(1)}, u32[]{:S(2)}, u32[]{:S(2)}) collective-permute-start(bf16[64,512]{1,0:T(8,128)(2,1)S(1)} %get-tuple-element.49), channel_id=1, source_target_pairs={{0,8},{1,9},{2,10},{3,11},{4,12},{5,13},{6,14},{7,15},{8,0},{9,1},... | collective-permute-start | bytes 196616 | tf_op jit(solution)/shard_map/ppermute | solution.py:285
  50.3 13.3 %collective-permute-start.10 = (bf16[80,512]{1,0:T(8,128)(2,1)S(1)}, bf16[80,512]{1,0:T(8,128)(2,1)S(1)}, u32[]{:S(2)}, u32[]{:S(2)}) collective-permute-start(bf16[80,512]{1,0:T(8,128)(2,1)S(1)} %get-tuple-element.47), channel_id=1, source_target_pairs={{0,12},{1,13},{2,14},{3,15},{4,8},{5,9},{6,10},{7,11},{8,4},{9,5},... | collective-permute-start | bytes 245768 | tf_op jit(solution)/shard_map/ppermute | solution.py:285
  51.6 11.9 %collective-permute-start.8 = (bf16[80,512]{1,0:T(8,128)(2,1)S(1)}, bf16[80,512]{1,0:T(8,128)(2,1)S(1)}, u32[]{:S(2)}, u32[]{:S(2)}) collective-permute-start(bf16[80,512]{1,0:T(8,128)(2,1)S(1)} %get-tuple-element.45), channel_id=1, source_target_pairs={{0,4},{1,5},{2,6},{3,7},{4,0},{5,1},{6,2},{7,3},{8,12},{9,13},{10,... | collective-permute-start | bytes 245768 | tf_op jit(solution)/shard_map/ppermute | solution.py:285
  51.8 11.7 %collective-permute-start.9 = (bf16[80,512]{1,0:T(8,128)(2,1)S(1)}, bf16[80,512]{1,0:T(8,128)(2,1)S(1)}, u32[]{:S(2)}, u32[]{:S(2)}) collective-permute-start(bf16[80,512]{1,0:T(8,128)(2,1)S(1)} %get-tuple-element.46), channel_id=1, source_target_pairs={{0,8},{1,9},{2,10},{3,11},{4,12},{5,13},{6,14},{7,15},{8,0},{9,1},... | collective-permute-start | bytes 245768 | tf_op jit(solution)/shard_map/ppermute | solution.py:285
  54.7 4.3 %collective-permute-start.12 = (bf16[64,512]{1,0:T(8,128)(2,1)S(1)}, bf16[64,512]{1,0:T(8,128)(2,1)S(1)}, u32[]{:S(2)}, u32[]{:S(2)}) collective-permute-start(bf16[64,512]{1,0:T(8,128)(2,1)S(1)} %get-tuple-element.50), channel_id=1, source_target_pairs={{0,2},{1,3},{2,0},{3,1},{4,6},{5,7},{6,4},{7,5},{8,10},{9,11},{10,... | collective-permute-start | bytes 196616 | tf_op jit(solution)/shard_map/ppermute | solution.py:285
  54.7 8.9 %collective-permute-start.13 = (bf16[64,512]{1,0:T(8,128)(2,1)S(1)}, bf16[64,512]{1,0:T(8,128)(2,1)S(1)}, u32[]{:S(2)}, u32[]{:S(2)}) collective-permute-start(bf16[64,512]{1,0:T(8,128)(2,1)S(1)} %get-tuple-element.51), channel_id=1, source_target_pairs={{0,10},{1,11},{2,8},{3,9},{4,14},{5,15},{6,12},{7,13},{8,2},{9,3},... | collective-permute-start | bytes 196616 | tf_op jit(solution)/shard_map/ppermute | solution.py:285

commit v6 on v5

--- a/solution.py
+++ b/solution.py
@@ -125,19 +125,83 @@
     up[...] = contract(cot[...], mix[...], 1, 1)
 
 
-def mix_kernel(share, where, me, act, act_got, cot, cot_got, *outs):
-    half = cot.shape[1] // 2
-    blocks = act.shape[0] // share
-    for k, (bit, skip) in enumerate(where):
-        cols = slice(k * half, (k + 1) * half)
-        both = jnp.concatenate([cot[:, cols], cot_got[:, cols]], axis=0)
-        for want, out in ((1 - me[bit], outs[2 * k]), (me[bit], outs[2 * k + 1])):
-            pieces = []
-            for q in range(blocks // 2):
-                base = ((q >> skip) << (skip + 1)) | (q & ((1 << skip) - 1))
-                at = pl.ds(pl.multiple_of((base + (want << skip)) * share, share), share)
-                pieces.append(jnp.concatenate([act[at, :], act_got[at, :]], axis=1))
-            out[...] = mm(jnp.concatenate(pieces, axis=0), both).astype(out.dtype)
+def blocks_of(count, bits, skips, me):
+    groups = []
+    for delta in range(1 << len(bits)):
+        offset = 0
+        for k, (bit, skip) in enumerate(zip(bits, skips)):
+            offset += ((1 - me[bit]) if (delta >> k) & 1 else me[bit]) << skip
+        group = []
+        for q in range(count >> len(bits)):
+            base = q
+            for skip in sorted(skips):
+                base = ((base >> skip) << (skip + 1)) | (base & ((1 << skip) - 1))
+            group.append(base + offset)
+        groups.append(group)
+    return groups
+
+
+def parcel(ref):
+    return ref[:16, :128].astype(f32) + ref[:16, 128:256].astype(f32)
+
+
+def pack(whole, sends, kept):
+    high = whole.astype(bf16)
+    low = (whole - high.astype(f32)).astype(bf16)
+    kept[...] = high.astype(f32) + low.astype(f32)
+    for send in sends:
+        send[:16, :] = jnp.zeros((16, send.shape[1]), bf16)
+        send[:16, :128] = high
+        send[:16, 128:256] = low
+
+
+def conv_sum(conv, gots):
+    if len(gots) == 1:
+        return conv[...] + parcel(gots[0])
+    one, two, three = [parcel(got) for got in gots]
+    return (conv[...] + one) + (two + three)
+
+
+def mix_kernel(share, bits, skips, me, act, act_got, cot, cot_got, conv, conv_got, *outs):
+    *sends, keep, conv_out = outs
+    pack(conv[...] + conv_got[...], sends, conv_out)
+    groups = blocks_of(act.shape[0] // share, bits, skips, me)
+    both = jnp.concatenate([cot[...], cot_got[...]], axis=0)
+    pieces = []
+    for group in groups:
+        for block in group:
+            at = pl.ds(pl.multiple_of(block * share, share), share)
+            pieces.append(jnp.concatenate([act[at, :], act_got[at, :]], axis=1))
+    total = mm(jnp.concatenate(pieces, axis=0), both)
+    rows = keep.shape[0]
+    keep[...] = total[:rows]
+    for k, send in enumerate(sends):
+        send[16:, :] = total[(k + 1) * rows : (k + 2) * rows].astype(bf16)
+
+
+def stage_kernel(share, bits, skips, came, me, kept, *refs):
+    gots, conv, (*sends, keep, conv_out) = refs[:came], refs[came], refs[came + 1 :]
+    pack(conv_sum(conv, gots), sends, conv_out)
+    groups = blocks_of(kept.shape[0] // share, bits, skips, me)
+    for group, out, out_at in zip(groups, [keep] + sends, [0] + [16] * len(sends)):
+        for q, block in enumerate(group):
+            at = pl.multiple_of(block * share, share)
+            value = kept[pl.ds(at, share), :]
+            for got in gots:
+                value += got[pl.ds(pl.multiple_of(at + 16, 16), share), :].astype(f32)
+            out[out_at + q * share : out_at + (q + 1) * share, :] = value.astype(out.dtype)
+
+
+def last_kernel(scale, channels, came, kept, *refs):
+    gots, (conv, inner, first, second, mix_out, conv_out, grad_out) = refs[:came], refs[came:]
+    total = kept[...]
+    for got in gots:
+        total += got[16:, :].astype(f32)
+    mix_out[...] = total * scale
+    whole = conv_sum(conv, gots)
+    for tap in range(conv_out.shape[0]):
+        conv_out[tap] = whole[:, tap * channels : (tap + 1) * channels]
+    grad_out[...] = (inner[...] + first[...].astype(f32) + second[...].astype(f32)).astype(bf16)
 
 
 def select_rows(sources, start, count, taps):
@@ -172,11 +236,15 @@
         )
 
 
-def terms_kernel(place, grad, wk, sources, terms, far, near, back_sel):
+def pick_kernel(place, sources, back_sel):
+    taps = back_sel.shape[1] // sources.shape[1] + 1
+    back_sel[:ROW, :] = select_rows(sources, place[2], ROW, taps)
+    back_sel[ROW:, :] = select_rows(sources, place[3], ROW, taps)
+
+
+def terms_kernel(grad, wk, back_sel, terms, far, near):
     n, width = grad.shape
     taps = wk.shape[0] // WIDE
-    back_sel[:ROW, :] = select_rows(sources, place[2], ROW, taps)
-    back_sel[ROW:, :] = select_rows(sources, place[3], ROW, taps)
     for c in range(0, width, WIDE):
         g = grad[:, c : c + WIDE]
         for tap in range(1, taps):
@@ -195,74 +263,6 @@
     for c in range(0, width, WIDE):
         acc = contract(grad[:, c : c + WIDE], wk[:WIDE, :], 1, 1) + cot[:, c : c + WIDE].astype(f32)
         inner[:, c : c + WIDE] = acc + mm(sel, terms[:, c : c + WIDE])
-
-
-def parcel(ref):
-    return ref[:16, :128].astype(f32) + ref[:16, 128:256].astype(f32)
-
-
-def conv_sum(conv, gots):
-    one, two, three = [parcel(got) for got in gots]
-    return (conv[...] + one) + (two + three)
-
-
-def quarter(share, bits, skips, kept, gots, got_at, sends, send_at, keep):
-    (lo, hi), (bit_lo, bit_hi) = skips, bits
-    small, large = min(lo, hi), max(lo, hi)
-    for q in range(kept.shape[0] // share // 4):
-        base = ((q >> small) << (small + 1)) | (q & ((1 << small) - 1))
-        base = ((base >> large) << (large + 1)) | (base & ((1 << large) - 1))
-        for delta in range(4):
-            out, out_at = (keep, 0) if delta == 0 else (sends[delta - 1], send_at)
-            want_lo = 1 - bit_lo if delta & 1 else bit_lo
-            want_hi = 1 - bit_hi if delta & 2 else bit_hi
-            at = pl.multiple_of((base + (want_lo << lo) + (want_hi << hi)) * share, share)
-            value = kept[pl.ds(at, share), :]
-            for got in gots:
-                value += got[pl.ds(pl.multiple_of(at + got_at, 16), share), :].astype(f32)
-            out[out_at + q * share : out_at + (q + 1) * share, :] = value.astype(out.dtype)
-
-
-def quad_kernel(share, where, came, me, *refs):
-    first = came == 1
-    kept_a, gots_a, kept_b, gots_b = refs[0], refs[1 : 1 + came], refs[1 + came], refs[2 + came : 2 + 2 * came]
-    rest = refs[2 + 2 * came :]
-    if first:
-        whole = rest[0][...] + rest[1][...]
-        rest = rest[2:]
-    else:
-        whole = conv_sum(rest[0], gots_a)
-        rest = rest[1:]
-    sends_a, keep_a, sends_b, keep_b, conv_out = rest[:3], rest[3], rest[4:7], rest[7], rest[8]
-    high = whole.astype(bf16)
-    low = (whole - high.astype(f32)).astype(bf16)
-    conv_out[...] = high.astype(f32) + low.astype(f32)
-    for send in sends_a:
-        send[:16, :] = jnp.zeros((16, send.shape[1]), bf16)
-        send[:16, :128] = high
-        send[:16, 128:256] = low
-    (bits_a, skips_a), (bits_b, skips_b) = where
-    chosen = lambda bits: (me[bits[0]], me[bits[1]])
-    quarter(share, chosen(bits_a), skips_a, kept_a, gots_a, 0 if first else 16, sends_a, 16, keep_a)
-    quarter(share, chosen(bits_b), skips_b, kept_b, gots_b, 0, sends_b, 0, keep_b)
-
-
-def last_kernel(scale, channels, *refs):
-    kept_a, gots_a, kept_b, gots_b = refs[0], refs[1:4], refs[4], refs[5:8]
-    conv, inner, first, second, mix_out, conv_out, grad_out = refs[8:]
-    half = kept_a.shape[1]
-    total = kept_a[...]
-    for got in gots_a:
-        total += got[16:, :].astype(f32)
-    mix_out[:, :half] = total * scale
-    total = kept_b[...]
-    for got in gots_b:
-        total += got[...].astype(f32)
-    mix_out[:, half:] = total * scale
-    whole = conv_sum(conv, gots_a)
-    for tap in range(conv_out.shape[0]):
-        conv_out[tap] = whole[:, tap * channels : (tap + 1) * channels]
-    grad_out[...] = (inner[...] + first[...].astype(f32) + second[...].astype(f32)).astype(bf16)
 
 
 def shards(columns_in, cotangent, conv_weight, mix_weight, neighbours, rotations, pentagons):
@@ -330,33 +330,12 @@
         scratch=[pltpu.VMEM((width, n), bf16)],
     )
     act_got = swap(act_send, 0)
-    orders = [list(range(1, bits)), list(range(2, bits)) + [1]]
-    lefts = [list(range(bits - 1, 0, -1)) for _ in orders]
-
-    def position(k, bit):
-        return len(lefts[k]) - 1 - lefts[k].index(bit)
-
-    def drop(k, *gone):
-        lefts[k] = [b for b in lefts[k] if b not in gone]
-
-    rows_left = half // 2
-    parts = call(
-        functools.partial(
-            mix_kernel, share, tuple((order[0], position(k, order[0])) for k, order in enumerate(orders))
-        ),
-        [((rows_left, half), bf16), ((rows_left, half), f32)] * 2,
-        1 << 30,
-        mine,
-        act,
-        act_got,
-        cotangent,
-        cot_got,
-        scalars=1,
-    )
-    kept, gots = [parts[1], parts[3]], []
-    for k in (0, 1):
-        gots.append([swap(parts[2 * k], orders[k][0])])
-        drop(k, orders[k][0])
+    left = list(range(bits - 1, 0, -1))
+    stages = [left[::-1][k : k + 2] for k in range(0, len(left), 2)]
+
+    def skips_of(pair):
+        return tuple(len(left) - 1 - left.index(b) for b in pair)
+
     grad, conv = call(
         functools.partial(weights_kernel, channels, 1.0 / float(total_cols * levels) ** 0.5),
         [((n, width), bf16), ((channels, 128), f32)],
@@ -366,60 +345,61 @@
         columns_in,
         rows,
     )
+    conv_got = swap(conv, 0)
+    (back_sel,) = call(pick_kernel, [((2 * ROW, pairs), bf16)], 1 << 26, spots, sources, scalars=1)
+    kept, gots = None, []
+    rows_left = half
+    for stage, pair in enumerate(stages):
+        ways = 1 << len(pair)
+        rows_left //= ways
+        outs = [((rows_left + 16, width), bf16)] * (ways - 1) + [((rows_left, width), f32), ((channels, 128), f32)]
+        if stage == 0:
+            *sends, kept, conv = call(
+                functools.partial(mix_kernel, share, tuple(pair), skips_of(pair)),
+                outs,
+                1 << 30,
+                mine,
+                act,
+                act_got,
+                cotangent,
+                cot_got,
+                conv,
+                conv_got,
+                scalars=1,
+            )
+        else:
+            *sends, kept, conv = call(
+                functools.partial(stage_kernel, share, tuple(pair), skips_of(pair), len(gots)),
+                outs,
+                1 << 20,
+                mine,
+                kept,
+                *gots,
+                conv,
+                scalars=1,
+            )
+        gots = []
+        for delta in range(ways - 1, 0, -1):
+            mask = sum(1 << b for k, b in enumerate(pair) if (delta >> k) & 1)
+            gots.insert(0, swap_by(sends[delta - 1], mask))
+        left = [b for b in left if b not in pair]
     terms, to_far, to_near = call(
         terms_kernel,
         [((pairs, width), bf16), ((ROW, width), bf16), ((ROW, width), bf16)],
         3 << 30,
-        spots,
         grad,
         wk,
-        sources,
-        scalars=1,
-        scratch=[pltpu.VMEM((2 * ROW, pairs), bf16)],
-    )
-    conv = conv + swap(conv, 0)
-    conv_got = swap(conv, 1)
+        back_sel,
+    )
     from_far = far_swap(to_far)
     from_near = near_swap(to_near)
-    for stage in range(1, bits - 1, 2):
-        rows_left //= 4
-        pair = [order[stage : stage + 2] for order in orders]
-        where = tuple((tuple(p), tuple(position(k, b) for b in p)) for k, p in enumerate(pair))
-        outs = call(
-            functools.partial(quad_kernel, share, where, len(gots[0])),
-            [((rows_left + 16, half), bf16)] * 3
-            + [((rows_left, half), f32)]
-            + [((rows_left, half), bf16)] * 3
-            + [((rows_left, half), f32), ((channels, 128), f32)],
-            1 << 20,
-            mine,
-            kept[0],
-            *gots[0],
-            kept[1],
-            *gots[1],
-            conv,
-            *([conv_got] if stage == 1 else []),
-            scalars=1,
-        )
-        kept, conv = [outs[3], outs[7]], outs[8]
-        gots = []
-        for k in (0, 1):
-            came = []
-            for delta in (1, 2, 3):
-                came.append(swap_by(outs[4 * k + delta - 1], ((delta & 1) << pair[k][0]) | ((delta >> 1) << pair[k][1])))
-            gots.append(came)
-            drop(k, *pair[k])
-    (inner,) = call(
-        inner_kernel, [((n, width), f32)], 1 << 30, grad, terms, wk, sources, cotangent
-    )
+    (inner,) = call(inner_kernel, [((n, width), f32)], 1 << 30, grad, terms, wk, sources, cotangent)
     grad_mix, grad_conv, grad_input = call(
-        functools.partial(last_kernel, 1.0 / float(total_cols) ** 0.5, channels),
+        functools.partial(last_kernel, 1.0 / float(total_cols) ** 0.5, channels, len(gots)),
         [((share, width), f32), ((taps, channels, channels), f32), ((n, width), bf16)],
         1 << 20,
-        kept[0],
-        *gots[0],
-        kept[1],
-        *gots[1],
+        kept,
+        *gots,
         conv,
         inner,
         from_far,

time: 64.9 us -> 66.4 us (1.023)
  starting transfers between devices: 24.5 us -> 18.4 us
  waiting for transfers between devices: 17.9 us -> 23.4 us
  local copies, waits for them, and re-layouts: 2.85 us -> 3.86 us
  Pallas kernels: 18.5 us -> 19.5 us
    ppermute x12 -> x7, starting transfers between devices: 14.1 us -> 7.58 us  [swap_by(): return lax.ppermute(value, 'space', [(i, i ^ mask) for i in range(devices)])]
    ppermute x12 -> x7, waiting for transfers between devices: 17.9 us -> 23.4 us  [swap_by(): return lax.ppermute(value, 'space', [(i, i ^ mask) for i in range(devices)])]
    unnamed x16, local copies, waits for them, and re-layouts: 2.85 us -> 3.86 us
    pallas_call x9 -> x10, Pallas kernels: 18.5 us -> 19.5 us  [call(): pl.pallas_call(body, out_shape=[jax.ShapeDtypeStruct(s, d) for s, d in ou...]
  transfers between devices with their start and end apart: 16 -> 11, of which waited for: 4 -> 2; matrix products, arithmetic and copies ran while one was open for 0% -> 0% of each run, Pallas kernels for 27% -> 28%
where the time goes in v6:
time: 66.4 us; the launch traced here: 66.1 us
  waiting for transfers between devices  23.4 us (35%)
  Pallas kernels  19.5 us (29%)
  starting transfers between devices  18.4 us (28%)
  local copies, waits for them, and re-layouts  3.86 us (6%)
  between operations  0.78 us (1%)
    ppermute x7, waiting for transfers between devices, swap_by(): return lax.ppermute(value, 'space', [(i, i ^ mask) for i in range(devices)])  23.4 us
    pallas_call x10, Pallas kernels, call(): pl.pallas_call(body, out_shape=[jax.ShapeDtypeStruct(s, d) for s, d in ou...  19.5 us
    ppermute x2, starting transfers between devices, far_swap(): return lax.ppermute(value, 'space', [(i, other(i)) for i in range(devices)])  10.3 us
    ppermute x7, starting transfers between devices, swap_by(): return lax.ppermute(value, 'space', [(i, i ^ mask) for i in range(devices)])  7.58 us
    unnamed x16, local copies, waits for them, and re-layouts  3.86 us
  transfers between devices with their start and end apart: 11, of which 2 were waited for; matrix products, arithmetic and copies ran while one was open for 0% of the time, Pallas kernels for 28%

profile of v6, /device:TPU:0, one launch (start us, length us, event | category | flops | bytes accessed | tf_op | source)
XLA Modules:
  0.0 66.1 jit_solution(5513130806467005043)
XLA Ops:
  0.7 5.5 %collective-permute-start = (bf16[256,1024]{1,0:T(8,128)(2,1)}, bf16[256,1024]{1,0:T(8,128)(2,1)}, u32[]{:S(2)}, u32[]{:S(2)}) collective-permute-start(bf16[256,1024]{1,0:T(8,128)(2,1)} %x.3), channel_id=1, source_target_pairs={{0,15},{1,2},{2,1},{3,4},{4,3},{5,6},{6,5},{7,8},{8,7},{9,10},{10,... | collective-permute-start | bytes 1572872 | tf_op jit(solution)/shard_map/ppermute | solution.py:282
  6.2 0.0 collective-permute-start.1
  6.2 0.5 collective-permute-start.3
  6.7 0.1 pad_add_fusion.1.place
  6.8 1.0 %copy-done.2 = bf16[256,1024]{1,0:T(8,128)(2,1)S(1)} copy-done((bf16[256,1024]{1,0:T(8,128)(2,1)S(1)}, bf16[256,1024]{1,0:T(8,128)(2,1)}, u32[]{:S(2)}) %copy-start.2) | copy-done | bytes 524312
  7.8 0.7 %copy-done.4 = bf16[7,16,16]{2,1,0:T(8,128)(2,1)S(1)} copy-done((bf16[7,16,16]{2,1,0:T(8,128)(2,1)S(1)}, bf16[7,16,16]{2,1,0:T(8,128)(2,1)}, u32[]{:S(2)}) %copy-start.4) | copy-done | bytes 3608
  8.6 0.7 %copy-done.5 = s32[256,7]{0,1:T(8,128)S(1)} copy-done((s32[256,7]{0,1:T(8,128)S(1)}, s32[256,7]{0,1:T(8,128)}, u32[]{:S(2)}) %copy-start.5) | copy-done | bytes 7192
  9.3 0.7 %copy-done.6 = s32[256]{0:T(256)S(1)} copy-done((s32[256]{0:T(256)S(1)}, s32[256]{0:T(256)}, u32[]{:S(2)}) %copy-start.6) | copy-done | bytes 1048
  9.9 0.7 %copy-done.7 = s32[256]{0:T(256)S(1)} copy-done((s32[256]{0:T(256)S(1)}, s32[256]{0:T(256)}, u32[]{:S(2)}) %copy-start.7) | copy-done | bytes 1048
  10.6 3.5 %shard_map.94 = (bf16[1536,512]{1,0:T(8,128)(2,1)S(1)}, s32[8,256]{1,0:T(8,128)S(1)}, bf16[1536,1024]{1,0:T(8,128)(2,1)S(1)}, bf16[1792,256]{1,0:T(8,128)(2,1)S(1)}) custom-call(s32[4]{0:T(128)S(1)} %pad_add_fusion.1.place, s32[7,256]{1,0:T(8,128)S(1)} %bitcast.10, s32[1,256]{1,0:T(1,128)S(1)} %bitcast.11, s32[1,256]{1,0:T(1,128)S(1)} %bitcast.12, ...), custom_call_target="tpu_custom_call" | custom-call | flops 1073741824 | bytes 8388608 | tf_op jit(solution)/shard_map/pallas_call | solution.py:41
  14.2 0.0 copy-start.3
  14.2 0.8 %shard_map.100.back_sel = bf16[512,1536]{1,0:T(8,128)(2,1)S(1)} custom-call(s32[4]{0:T(128)S(1)} %pad_add_fusion.1.place, s32[8,256]{1,0:T(8,128)S(1)} %get-tuple-element.44.sources), custom_call_target="tpu_custom_call" | custom-call | flops 67108864 | bytes 8388608 | tf_op jit(solution)/shard_map/pallas_call | solution.py:41
  15.0 0.7 %shard_map.96.up = f32[256,1024]{1,0:T(8,128)S(1)} custom-call(bf16[256,1024]{1,0:T(8,128)(2,1)S(1)} %copy-done, bf16[1024,1024]{1,0:T(8,128)(2,1)S(1)} %copy-done.1), custom_call_target="tpu_custom_call" | custom-call | flops 536870912 | bytes 8388608 | tf_op jit(solution)/shard_map/pallas_call | solution.py:41
  15.8 0.1 pad_add_fusion.me
  15.8 0.0 collective-permute-done.far
  15.8 5.6 %shard_map.95 = (bf16[1536,1024]{1,0:T(8,128)(2,1)S(1)}, f32[256,1024]{1,0:T(8,128)S(1)}, bf16[512,256]{1,0:T(8,128)(2,1)S(1)}, bf16[512,256]{1,0:T(8,128)(2,1)S(1)}) custom-call(s32[4]{0:T(128)S(1)} %pad_add_fusion.me, bf16[256,1024]{1,0:T(8,128)(2,1)} %collective-permute-done.far, bf16[256,1024]{1,0:T(8,128)(2,1)} %collective-permute-done.1.near, ...), custom_call_target="tpu_custom_call" | custom-call | flops 3221225472 | bytes 8388608 | tf_op jit(solution)/shard_map/pallas_call | solution.py:41
  21.4 1.9 %shard_map.97 = (bf16[256,1024]{1,0:T(8,128)(2,1)S(1)}, f32[16,128]{1,0:T(8,128)S(1)}) custom-call(f32[256,1024]{1,0:T(8,128)S(1)} %shard_map.96.up, f32[256,1024]{1,0:T(8,128)S(1)} %get-tuple-element.32.pre, bf16[256,1024]{1,0:T(8,128)(2,1)S(1)} %copy-done.3, bf16[1536,1024]{1,0:T(8,128)(2,1)S(1)} %get-tuple-element.33.rows), custom_call_target="tpu_custom_call" | custom-call | flops 2147483648 | bytes 8388608 | tf_op jit(solution)/shard_map/pallas_call | solution.py:41
  23.3 0.8 %collective-permute-start.4 = (f32[16,128]{1,0:T(8,128)S(1)}, f32[16,128]{1,0:T(8,128)S(1)}, u32[]{:S(2)}, u32[]{:S(2)}) collective-permute-start(f32[16,128]{1,0:T(8,128)S(1)} %get-tuple-element.34.conv), channel_id=1, source_target_pairs={{0,1},{1,0},{2,3},{3,2},{4,5},{5,4},{6,7},{7,6},{8,9},{9,8},{10,11... | collective-permute-start | bytes 24584 | tf_op jit(solution)/shard_map/ppermute | solution.py:285
  24.1 0.1 collective-permute-start.2
  24.2 2.7 %shard_map.101 = (bf16[1536,1024]{1,0:T(8,128)(2,1)S(1)}, bf16[256,1024]{1,0:T(8,128)(2,1)S(1)}, bf16[256,1024]{1,0:T(8,128)(2,1)S(1)}) custom-call(bf16[256,1024]{1,0:T(8,128)(2,1)S(1)} %get-tuple-element.43.grad, bf16[1792,256]{1,0:T(8,128)(2,1)S(1)} %get-tuple-element.29.wk, bf16[512,1536]{1,0:T(8,128)(2,1)S(1)} %shard_map.100.back_sel), custom_call_target="tpu_custom_call" | custom-call | flops 3221225472 | bytes 8388608 | tf_op jit(solution)/shard_map/pallas_call | solution.py:41
  26.9 0.5 collective-permute-start.10
  27.4 4.8 %collective-permute-start.9 = (bf16[256,1024]{1,0:T(8,128)(2,1)S(1)}, bf16[256,1024]{1,0:T(8,128)(2,1)S(1)}, u32[]{:S(2)}, u32[]{:S(2)}) collective-permute-start(bf16[256,1024]{1,0:T(8,128)(2,1)S(1)} %get-tuple-element.46), channel_id=1, source_target_pairs={{0,15},{1,2},{2,1},{3,4},{4,3},{5,6},{6,5},{7,8},{8,7},{9,10},{10,... | collective-permute-start | bytes 1572872 | tf_op jit(solution)/shard_map/ppermute | solution.py:282
  32.2 1.2 %shard_map.98 = (bf16[144,1024]{1,0:T(8,128)(2,1)S(1)}, bf16[144,1024]{1,0:T(8,128)(2,1)S(1)}, bf16[144,1024]{1,0:T(8,128)(2,1)S(1)}, f32[128,1024]{1,0:T(8,128)S(1)}, f32[16,128]{1,0:T(8,128)S(1)}) custom-call(s32[4]{0:T(128)S(1)} %pad_add_fusion.me, bf16[512,256]{1,0:T(8,128)(2,1)S(1)} %get-tuple-element.30.act, ...), custom_call_target="tpu_custom_call" | custom-call | flops 1073741824 | bytes 8388608 | tf_op jit(solution)/shard_map/pallas_call | solution.py:41
  33.5 0.1 collective-permute-start.5
  33.5 0.1 collective-permute-start.6
  33.6 3.4 %collective-permute-start.7 = (bf16[144,1024]{1,0:T(8,128)(2,1)S(1)}, bf16[144,1024]{1,0:T(8,128)(2,1)S(1)}, u32[]{:S(2)}, u32[]{:S(2)}) collective-permute-start(bf16[144,1024]{1,0:T(8,128)(2,1)S(1)} %get-tuple-element.38), channel_id=1, source_target_pairs={{0,6},{1,7},{2,4},{3,5},{4,2},{5,3},{6,0},{7,1},{8,14},{9,15},{10,... | collective-permute-start | bytes 884744 | tf_op jit(solution)/shard_map/ppermute | solution.py:285
  37.0 17.5 %collective-permute-done.5.refs_0_ = bf16[144,1024]{1,0:T(8,128)(2,1)S(1)} collective-permute-done((bf16[144,1024]{1,0:T(8,128)(2,1)S(1)}, bf16[144,1024]{1,0:T(8,128)(2,1)S(1)}, u32[]{:S(2)}, u32[]{:S(2)}) %collective-permute-start.5) | collective-permute-done | bytes 294944 | tf_op jit(solution)/shard_map/ppermute | solution.py:285
  54.6 0.7 %shard_map.99 = (bf16[80,1024]{1,0:T(8,128)(2,1)S(1)}, f32[64,1024]{1,0:T(8,128)S(1)}, f32[16,128]{1,0:T(8,128)S(1)}) custom-call(s32[4]{0:T(128)S(1)} %pad_add_fusion.me, f32[128,1024]{1,0:T(8,128)S(1)} %get-tuple-element.35.kept, bf16[144,1024]{1,0:T(8,128)(2,1)S(1)} %collective-permute-done.5.refs_0_, ...), custom_call_target="tpu_custom_call" | custom-call | flops 1048576 | bytes 8388608 | tf_op jit(solution)/shard_map/pallas_call | solution.py:41
  55.3 2.7 %collective-permute-start.8 = (bf16[80,1024]{1,0:T(8,128)(2,1)S(1)}, bf16[80,1024]{1,0:T(8,128)(2,1)S(1)}, u32[]{:S(2)}, u32[]{:S(2)}) collective-permute-start(bf16[80,1024]{1,0:T(8,128)(2,1)S(1)} %get-tuple-element.41), channel_id=1, source_target_pairs={{0,8},{1,9},{2,10},{3,11},{4,12},{5,13},{6,14},{7,15},{8,0},{9,1},... | collective-permute-start | bytes 491528 | tf_op jit(solution)/shard_map/ppermute | solution.py:285
  57.9 1.1 %shard_map.102.refs_2_ = f32[256,1024]{1,0:T(8,128)S(1)} custom-call(bf16[256,1024]{1,0:T(8,128)(2,1)S(1)} %get-tuple-element.43.grad, bf16[1536,1024]{1,0:T(8,128)(2,1)S(1)} %get-tuple-element.45.terms, bf16[1792,256]{1,0:T(8,128)(2,1)S(1)} %get-tuple-element.29.wk, s32[8,256]{1,0:T(8,128)S(1)} %get-tuple-element.44.sources, bf16[256,1024]{1,0:T(8,128)(2,1)S(1)} %copy-done), custom_call_target="tpu_custom_call" | custom-call | flops 1073741824 | bytes 8388608 | tf_op jit(solution)/shard_map/pallas_call | solution.py:41
  59.1 5.8 %collective-permute-done.8.refs_0_ = bf16[80,1024]{1,0:T(8,128)(2,1)S(1)} collective-permute-done((bf16[80,1024]{1,0:T(8,128)(2,1)S(1)}, bf16[80,1024]{1,0:T(8,128)(2,1)S(1)}, u32[]{:S(2)}, u32[]{:S(2)}) %collective-permute-start.8) | collective-permute-done | bytes 163872 | tf_op jit(solution)/shard_map/ppermute | solution.py:285
  64.9 1.1 %shard_map.103 = (f32[64,1024]{1,0:T(8,128)}, f32[7,16,16]{2,1,0:T(8,128)}, bf16[256,1024]{1,0:T(8,128)(2,1)}) custom-call(f32[64,1024]{1,0:T(8,128)S(1)} %get-tuple-element.40.kept, bf16[80,1024]{1,0:T(8,128)(2,1)S(1)} %collective-permute-done.8.refs_0_, f32[16,128]{1,0:T(8,128)S(1)} %get-tuple-element.42.refs_1_, f32[256,1024]{1,0:T(8,128)S(1)} %shard_map.102.refs_2_, ...), custom_call_target="tpu_custom_call" | custom-call | flops 1048576 | bytes 8388608 | tf_op jit(solution)/shard_map/pallas_call | solution.py:41
  (18 shorter events, 0.0 us)
Async XLA Ops:
  0.6 14.4 %copy-start = (bf16[256,1024]{1,0:T(8,128)(2,1)S(1)}, bf16[256,1024]{1,0:T(8,128)(2,1)}, u32[]{:S(2)}) copy-start(bf16[256,1024]{1,0:T(8,128)(2,1)} %cot.5) | copy-start | bytes 1572868
  0.6 14.4 %copy-start.1 = (bf16[1024,1024]{1,0:T(8,128)(2,1)S(1)}, bf16[1024,1024]{1,0:T(8,128)(2,1)}, u32[]{:S(2)}) copy-start(bf16[1024,1024]{1,0:T(8,128)(2,1)} %mix.1) | copy-start | bytes 6291460
  0.7 15.2 %collective-permute-start = (bf16[256,1024]{1,0:T(8,128)(2,1)}, bf16[256,1024]{1,0:T(8,128)(2,1)}, u32[]{:S(2)}, u32[]{:S(2)}) collective-permute-start(bf16[256,1024]{1,0:T(8,128)(2,1)} %x.3), channel_id=1, source_target_pairs={{0,15},{1,2},{2,1},{3,4},{4,3},{5,6},{6,5},{7,8},{8,7},{9,10},{10,... | collective-permute-start | bytes 1572872 | tf_op jit(solution)/shard_map/ppermute | solution.py:282
  6.2 9.7 %collective-permute-start.1 = (bf16[256,1024]{1,0:T(8,128)(2,1)}, bf16[256,1024]{1,0:T(8,128)(2,1)}, u32[]{:S(2)}, u32[]{:S(2)}) collective-permute-start(bf16[256,1024]{1,0:T(8,128)(2,1)} %x.3), channel_id=1, source_target_pairs={{0,1},{1,0},{2,3},{3,2},{4,5},{5,4},{6,7},{7,6},{8,9},{9,8},{10,11... | collective-permute-start | bytes 1572872 | tf_op jit(solution)/shard_map/ppermute | solution.py:278
  6.2 26.0 %collective-permute-start.3 = (bf16[256,1024]{1,0:T(8,128)(2,1)}, bf16[256,1024]{1,0:T(8,128)(2,1)S(1)}, u32[]{:S(2)}, u32[]{:S(2)}) collective-permute-start(bf16[256,1024]{1,0:T(8,128)(2,1)} %cot.5), channel_id=1, source_target_pairs={{0,1},{1,0},{2,3},{3,2},{4,5},{5,4},{6,7},{7,6},{8,9},{9,8},{10,11... | collective-permute-start | bytes 1572872 | tf_op jit(solution)/shard_map/ppermute | solution.py:285
  6.8 1.0 %copy-start.2 = (bf16[256,1024]{1,0:T(8,128)(2,1)S(1)}, bf16[256,1024]{1,0:T(8,128)(2,1)}, u32[]{:S(2)}) copy-start(bf16[256,1024]{1,0:T(8,128)(2,1)} %x.3) | copy-start | bytes 1572868
  7.8 0.7 %copy-start.4 = (bf16[7,16,16]{2,1,0:T(8,128)(2,1)S(1)}, bf16[7,16,16]{2,1,0:T(8,128)(2,1)}, u32[]{:S(2)}) copy-start(bf16[7,16,16]{2,1,0:T(8,128)(2,1)} %conv_hbm.1) | copy-start | bytes 10756
  8.6 0.7 %copy-start.5 = (s32[256,7]{0,1:T(8,128)S(1)}, s32[256,7]{0,1:T(8,128)}, u32[]{:S(2)}) copy-start(s32[256,7]{0,1:T(8,128)} %param.11) | copy-start | bytes 21508
  9.3 0.7 %copy-start.6 = (s32[256]{0:T(256)S(1)}, s32[256]{0:T(256)}, u32[]{:S(2)}) copy-start(s32[256]{0:T(256)} %param.12) | copy-start | bytes 3076
  9.9 0.7 %copy-start.7 = (s32[256]{0:T(256)S(1)}, s32[256]{0:T(256)}, u32[]{:S(2)}) copy-start(s32[256]{0:T(256)} %param.13) | copy-start | bytes 3076
  14.2 1.7 %copy-start.3 = (bf16[256,1024]{1,0:T(8,128)(2,1)S(1)}, bf16[256,1024]{1,0:T(8,128)(2,1)}, u32[]{:S(2)}) copy-start(bf16[256,1024]{1,0:T(8,128)(2,1)} %x.3) | copy-start | bytes 1572868
  23.3 8.9 %collective-permute-start.4 = (f32[16,128]{1,0:T(8,128)S(1)}, f32[16,128]{1,0:T(8,128)S(1)}, u32[]{:S(2)}, u32[]{:S(2)}) collective-permute-start(f32[16,128]{1,0:T(8,128)S(1)} %get-tuple-element.34.conv), channel_id=1, source_target_pairs={{0,1},{1,0},{2,3},{3,2},{4,5},{5,4},{6,7},{7,6},{8,9},{9,8},{10,11... | collective-permute-start | bytes 24584 | tf_op jit(solution)/shard_map/ppermute | solution.py:285
  24.1 8.1 %collective-permute-start.2 = (bf16[512,256]{1,0:T(8,128)(2,1)S(1)}, bf16[512,256]{1,0:T(8,128)(2,1)S(1)}, u32[]{:S(2)}, u32[]{:S(2)}) collective-permute-start(bf16[512,256]{1,0:T(8,128)(2,1)S(1)} %get-tuple-element.31), channel_id=1, source_target_pairs={{0,1},{1,0},{2,3},{3,2},{4,5},{5,4},{6,7},{7,6},{8,9},{9,8},{10,11... | collective-permute-start | bytes 786440 | tf_op jit(solution)/shard_map/ppermute | solution.py:285
  26.9 32.1 %collective-permute-start.10 = (bf16[256,1024]{1,0:T(8,128)(2,1)S(1)}, bf16[256,1024]{1,0:T(8,128)(2,1)S(1)}, u32[]{:S(2)}, u32[]{:S(2)}) collective-permute-start(bf16[256,1024]{1,0:T(8,128)(2,1)S(1)} %get-tuple-element.47), channel_id=1, source_target_pairs={{0,1},{1,0},{2,3},{3,2},{4,5},{5,4},{6,7},{7,6},{8,9},{9,8},{10,11... | collective-permute-start | bytes 1572872 | tf_op jit(solution)/shard_map/ppermute | solution.py:278
  27.4 31.7 %collective-permute-start.9 = (bf16[256,1024]{1,0:T(8,128)(2,1)S(1)}, bf16[256,1024]{1,0:T(8,128)(2,1)S(1)}, u32[]{:S(2)}, u32[]{:S(2)}) collective-permute-start(bf16[256,1024]{1,0:T(8,128)(2,1)S(1)} %get-tuple-element.46), channel_id=1, source_target_pairs={{0,15},{1,2},{2,1},{3,4},{4,3},{5,6},{6,5},{7,8},{8,7},{9,10},{10,... | collective-permute-start | bytes 1572872 | tf_op jit(solution)/shard_map/ppermute | solution.py:282
  33.5 21.1 %collective-permute-start.5 = (bf16[144,1024]{1,0:T(8,128)(2,1)S(1)}, bf16[144,1024]{1,0:T(8,128)(2,1)S(1)}, u32[]{:S(2)}, u32[]{:S(2)}) collective-permute-start(bf16[144,1024]{1,0:T(8,128)(2,1)S(1)} %get-tuple-element.36), channel_id=1, source_target_pairs={{0,2},{1,3},{2,0},{3,1},{4,6},{5,7},{6,4},{7,5},{8,10},{9,11},{10,... | collective-permute-start | bytes 884744 | tf_op jit(solution)/shard_map/ppermute | solution.py:285
  33.5 21.0 %collective-permute-start.6 = (bf16[144,1024]{1,0:T(8,128)(2,1)S(1)}, bf16[144,1024]{1,0:T(8,128)(2,1)S(1)}, u32[]{:S(2)}, u32[]{:S(2)}) collective-permute-start(bf16[144,1024]{1,0:T(8,128)(2,1)S(1)} %get-tuple-element.37), channel_id=1, source_target_pairs={{0,4},{1,5},{2,6},{3,7},{4,0},{5,1},{6,2},{7,3},{8,12},{9,13},{10,... | collective-permute-start | bytes 884744 | tf_op jit(solution)/shard_map/ppermute | solution.py:285
  33.6 20.9 %collective-permute-start.7 = (bf16[144,1024]{1,0:T(8,128)(2,1)S(1)}, bf16[144,1024]{1,0:T(8,128)(2,1)S(1)}, u32[]{:S(2)}, u32[]{:S(2)}) collective-permute-start(bf16[144,1024]{1,0:T(8,128)(2,1)S(1)} %get-tuple-element.38), channel_id=1, source_target_pairs={{0,6},{1,7},{2,4},{3,5},{4,2},{5,3},{6,0},{7,1},{8,14},{9,15},{10,... | collective-permute-start | bytes 884744 | tf_op jit(solution)/shard_map/ppermute | solution.py:285
  55.3 9.7 %collective-permute-start.8 = (bf16[80,1024]{1,0:T(8,128)(2,1)S(1)}, bf16[80,1024]{1,0:T(8,128)(2,1)S(1)}, u32[]{:S(2)}, u32[]{:S(2)}) collective-permute-start(bf16[80,1024]{1,0:T(8,128)(2,1)S(1)} %get-tuple-element.41), channel_id=1, source_target_pairs={{0,8},{1,9},{2,10},{3,11},{4,12},{5,13},{6,14},{7,15},{8,0},{9,1},... | collective-permute-start | bytes 491528 | tf_op jit(solution)/shard_map/ppermute | solution.py:285

commit v7 on v5

--- a/solution.py
+++ b/solution.py
@@ -172,11 +172,15 @@
         )
 
 
-def terms_kernel(place, grad, wk, sources, terms, far, near, back_sel):
+def pick_kernel(place, sources, back_sel):
+    taps = back_sel.shape[1] // sources.shape[1] + 1
+    back_sel[:ROW, :] = select_rows(sources, place[2], ROW, taps)
+    back_sel[ROW:, :] = select_rows(sources, place[3], ROW, taps)
+
+
+def terms_kernel(grad, wk, back_sel, terms, far, near):
     n, width = grad.shape
     taps = wk.shape[0] // WIDE
-    back_sel[:ROW, :] = select_rows(sources, place[2], ROW, taps)
-    back_sel[ROW:, :] = select_rows(sources, place[3], ROW, taps)
     for c in range(0, width, WIDE):
         g = grad[:, c : c + WIDE]
         for tap in range(1, taps):
@@ -197,69 +201,39 @@
         inner[:, c : c + WIDE] = acc + mm(sel, terms[:, c : c + WIDE])
 
 
+def halve(share, bit, skip, kept, got, got_at, send, send_at, keep):
+    for q in range(kept.shape[0] // share // 2):
+        base = ((q >> skip) << (skip + 1)) | (q & ((1 << skip) - 1))
+        for value, out, out_at in ((1 - bit, send, send_at), (bit, keep, 0)):
+            at = pl.multiple_of((base + (value << skip)) * share, share)
+            came = got[pl.ds(pl.multiple_of(at + got_at, 16), share), :].astype(f32)
+            out[out_at + q * share : out_at + (q + 1) * share, :] = (
+                kept[pl.ds(at, share), :] + came
+            ).astype(out.dtype)
+
+
 def parcel(ref):
     return ref[:16, :128].astype(f32) + ref[:16, 128:256].astype(f32)
 
 
-def conv_sum(conv, gots):
-    one, two, three = [parcel(got) for got in gots]
-    return (conv[...] + one) + (two + three)
-
-
-def quarter(share, bits, skips, kept, gots, got_at, sends, send_at, keep):
-    (lo, hi), (bit_lo, bit_hi) = skips, bits
-    small, large = min(lo, hi), max(lo, hi)
-    for q in range(kept.shape[0] // share // 4):
-        base = ((q >> small) << (small + 1)) | (q & ((1 << small) - 1))
-        base = ((base >> large) << (large + 1)) | (base & ((1 << large) - 1))
-        for delta in range(4):
-            out, out_at = (keep, 0) if delta == 0 else (sends[delta - 1], send_at)
-            want_lo = 1 - bit_lo if delta & 1 else bit_lo
-            want_hi = 1 - bit_hi if delta & 2 else bit_hi
-            at = pl.multiple_of((base + (want_lo << lo) + (want_hi << hi)) * share, share)
-            value = kept[pl.ds(at, share), :]
-            for got in gots:
-                value += got[pl.ds(pl.multiple_of(at + got_at, 16), share), :].astype(f32)
-            out[out_at + q * share : out_at + (q + 1) * share, :] = value.astype(out.dtype)
-
-
-def quad_kernel(share, where, came, me, *refs):
-    first = came == 1
-    kept_a, gots_a, kept_b, gots_b = refs[0], refs[1 : 1 + came], refs[1 + came], refs[2 + came : 2 + 2 * came]
-    rest = refs[2 + 2 * came :]
-    if first:
-        whole = rest[0][...] + rest[1][...]
-        rest = rest[2:]
-    else:
-        whole = conv_sum(rest[0], gots_a)
-        rest = rest[1:]
-    sends_a, keep_a, sends_b, keep_b, conv_out = rest[:3], rest[3], rest[4:7], rest[7], rest[8]
+def merge_kernel(share, where, first, me, kept_a, got_a, kept_b, got_b, conv, conv_got, send_a, keep_a, send_b, keep_b, conv_out):
+    whole = conv[...] + (conv_got[...] if first else parcel(got_a))
     high = whole.astype(bf16)
     low = (whole - high.astype(f32)).astype(bf16)
     conv_out[...] = high.astype(f32) + low.astype(f32)
-    for send in sends_a:
-        send[:16, :] = jnp.zeros((16, send.shape[1]), bf16)
-        send[:16, :128] = high
-        send[:16, 128:256] = low
-    (bits_a, skips_a), (bits_b, skips_b) = where
-    chosen = lambda bits: (me[bits[0]], me[bits[1]])
-    quarter(share, chosen(bits_a), skips_a, kept_a, gots_a, 0 if first else 16, sends_a, 16, keep_a)
-    quarter(share, chosen(bits_b), skips_b, kept_b, gots_b, 0, sends_b, 0, keep_b)
-
-
-def last_kernel(scale, channels, *refs):
-    kept_a, gots_a, kept_b, gots_b = refs[0], refs[1:4], refs[4], refs[5:8]
-    conv, inner, first, second, mix_out, conv_out, grad_out = refs[8:]
+    send_a[:16, :] = jnp.zeros((16, send_a.shape[1]), bf16)
+    send_a[:16, :128] = high
+    send_a[:16, 128:256] = low
+    (bit_a, skip_a), (bit_b, skip_b) = where
+    halve(share, me[bit_a], skip_a, kept_a, got_a, 0 if first else 16, send_a, 16, keep_a)
+    halve(share, me[bit_b], skip_b, kept_b, got_b, 0, send_b, 0, keep_b)
+
+
+def last_kernel(scale, channels, kept_a, got_a, kept_b, got_b, conv, inner, first, second, mix_out, conv_out, grad_out):
     half = kept_a.shape[1]
-    total = kept_a[...]
-    for got in gots_a:
-        total += got[16:, :].astype(f32)
-    mix_out[:, :half] = total * scale
-    total = kept_b[...]
-    for got in gots_b:
-        total += got[...].astype(f32)
-    mix_out[:, half:] = total * scale
-    whole = conv_sum(conv, gots_a)
+    mix_out[:, :half] = (kept_a[...] + got_a[16:, :].astype(f32)) * scale
+    mix_out[:, half:] = (kept_b[...] + got_b[...].astype(f32)) * scale
+    whole = conv[...] + parcel(got_a)
     for tap in range(conv_out.shape[0]):
         conv_out[tap] = whole[:, tap * channels : (tap + 1) * channels]
     grad_out[...] = (inner[...] + first[...].astype(f32) + second[...].astype(f32)).astype(bf16)
@@ -315,6 +289,7 @@
         ],
     )
     (up,) = call(up_kernel, [((n, width), f32)], 1 << 29, cotangent, mix_weight)
+    (back_sel,) = call(pick_kernel, [((2 * ROW, pairs), bf16)], 1 << 26, spots, sources, scalars=1)
     rows, pre, act, act_send = call(
         functools.partial(front_kernel, share),
         [((pairs, width), bf16), ((n, width), f32), ((half, n), bf16), ((half, n), bf16)],
@@ -370,27 +345,26 @@
         terms_kernel,
         [((pairs, width), bf16), ((ROW, width), bf16), ((ROW, width), bf16)],
         3 << 30,
-        spots,
         grad,
         wk,
-        sources,
-        scalars=1,
-        scratch=[pltpu.VMEM((2 * ROW, pairs), bf16)],
+        back_sel,
     )
     conv = conv + swap(conv, 0)
     conv_got = swap(conv, 1)
     from_far = far_swap(to_far)
     from_near = near_swap(to_near)
-    for stage in range(1, bits - 1, 2):
-        rows_left //= 4
-        pair = [order[stage : stage + 2] for order in orders]
-        where = tuple((tuple(p), tuple(position(k, b) for b in p)) for k, p in enumerate(pair))
-        outs = call(
-            functools.partial(quad_kernel, share, where, len(gots[0])),
-            [((rows_left + 16, half), bf16)] * 3
-            + [((rows_left, half), f32)]
-            + [((rows_left, half), bf16)] * 3
-            + [((rows_left, half), f32), ((channels, 128), f32)],
+    for stage in range(1, bits - 1):
+        rows_left //= 2
+        where = tuple((order[stage], position(k, order[stage])) for k, order in enumerate(orders))
+        *outs, conv = call(
+            functools.partial(merge_kernel, share, where, stage == 1),
+            [
+                ((rows_left + 16, half), bf16),
+                ((rows_left, half), f32),
+                ((rows_left, half), bf16),
+                ((rows_left, half), f32),
+                ((channels, 128), f32),
+            ],
             1 << 20,
             mine,
             kept[0],
@@ -398,17 +372,13 @@
             kept[1],
             *gots[1],
             conv,
-            *([conv_got] if stage == 1 else []),
+            conv_got,
             scalars=1,
         )
-        kept, conv = [outs[3], outs[7]], outs[8]
-        gots = []
+        kept, gots = [outs[1], outs[3]], []
         for k in (0, 1):
-            came = []
-            for delta in (1, 2, 3):
-                came.append(swap_by(outs[4 * k + delta - 1], ((delta & 1) << pair[k][0]) | ((delta >> 1) << pair[k][1])))
-            gots.append(came)
-            drop(k, *pair[k])
+            gots.append([swap(outs[2 * k], orders[k][stage])])
+            drop(k, orders[k][stage])
     (inner,) = call(
         inner_kernel, [((n, width), f32)], 1 << 30, grad, terms, wk, sources, cotangent
     )

time: 64.9 us -> 64.8 us (level)
  starting transfers between devices: 24.5 us -> 21.3 us
  Pallas kernels: 18.5 us -> 20.1 us
  local copies, waits for them, and re-layouts: 2.85 us -> 3.86 us
    ppermute x12 -> x10, starting transfers between devices: 14.1 us -> 10.9 us  [swap_by(): return lax.ppermute(value, 'space', [(i, i ^ mask) for i in range(devices)])]
    pallas_call x9 -> x11, Pallas kernels: 18.5 us -> 20.1 us  [call(): pl.pallas_call(body, out_shape=[jax.ShapeDtypeStruct(s, d) for s, d in ou...]
    unnamed x16, local copies, waits for them, and re-layouts: 2.85 us -> 3.86 us
    ppermute x12 -> x10, waiting for transfers between devices: 17.9 us -> 18.4 us  [swap_by(): return lax.ppermute(value, 'space', [(i, i ^ mask) for i in range(devices)])]
  transfers between devices with their start and end apart: 16 -> 14, of which waited for: 4 -> 4; matrix products, arithmetic and copies ran while one was open for 0% -> 0% of each run, Pallas kernels for 27% -> 29%
where the time goes in v7:
time: 64.8 us; the launch traced here: 64.5 us
  starting transfers between devices  21.3 us (33%)
  Pallas kernels  20.1 us (31%)
  waiting for transfers between devices  18.4 us (28%)
  local copies, waits for them, and re-layouts  3.86 us (6%)
  between operations  0.79 us (1%)
    pallas_call x11, Pallas kernels, call(): pl.pallas_call(body, out_shape=[jax.ShapeDtypeStruct(s, d) for s, d in ou...  20.1 us
    ppermute x10, waiting for transfers between devices, swap_by(): return lax.ppermute(value, 'space', [(i, i ^ mask) for i in range(devices)])  18.4 us
    ppermute x10, starting transfers between devices, swap_by(): return lax.ppermute(value, 'space', [(i, i ^ mask) for i in range(devices)])  10.9 us
    ppermute x2, starting transfers between devices, far_swap(): return lax.ppermute(value, 'space', [(i, other(i)) for i in range(devices)])  10.4 us
    unnamed x16, local copies, waits for them, and re-layouts  3.86 us
  transfers between devices with their start and end apart: 14, of which 4 were waited for; matrix products, arithmetic and copies ran while one was open for 0% of the time, Pallas kernels for 29%

profile of v7, /device:TPU:0, one launch (start us, length us, event | category | flops | bytes accessed | tf_op | source)
XLA Modules:
  0.0 64.5 jit_solution(12132789894301036927)
XLA Ops:
  0.7 5.5 %collective-permute-start = (bf16[256,1024]{1,0:T(8,128)(2,1)}, bf16[256,1024]{1,0:T(8,128)(2,1)}, u32[]{:S(2)}, u32[]{:S(2)}) collective-permute-start(bf16[256,1024]{1,0:T(8,128)(2,1)} %x.3), channel_id=1, source_target_pairs={{0,15},{1,2},{2,1},{3,4},{4,3},{5,6},{6,5},{7,8},{8,7},{9,10},{10,... | collective-permute-start | bytes 1572872 | tf_op jit(solution)/shard_map/ppermute | solution.py:256
  6.2 0.5 collective-permute-start.3
  6.7 0.1 pad_add_fusion.1.place
  6.8 1.0 %copy-done.2 = bf16[256,1024]{1,0:T(8,128)(2,1)S(1)} copy-done((bf16[256,1024]{1,0:T(8,128)(2,1)S(1)}, bf16[256,1024]{1,0:T(8,128)(2,1)}, u32[]{:S(2)}) %copy-start.2) | copy-done | bytes 524312
  7.8 0.7 %copy-done.4 = bf16[7,16,16]{2,1,0:T(8,128)(2,1)S(1)} copy-done((bf16[7,16,16]{2,1,0:T(8,128)(2,1)S(1)}, bf16[7,16,16]{2,1,0:T(8,128)(2,1)}, u32[]{:S(2)}) %copy-start.4) | copy-done | bytes 3608
  8.6 0.7 %copy-done.5 = s32[256,7]{0,1:T(8,128)S(1)} copy-done((s32[256,7]{0,1:T(8,128)S(1)}, s32[256,7]{0,1:T(8,128)}, u32[]{:S(2)}) %copy-start.5) | copy-done | bytes 7192
  9.3 0.7 %copy-done.6 = s32[256]{0:T(256)S(1)} copy-done((s32[256]{0:T(256)S(1)}, s32[256]{0:T(256)}, u32[]{:S(2)}) %copy-start.6) | copy-done | bytes 1048
  9.9 0.7 %copy-done.7 = s32[256]{0:T(256)S(1)} copy-done((s32[256]{0:T(256)S(1)}, s32[256]{0:T(256)}, u32[]{:S(2)}) %copy-start.7) | copy-done | bytes 1048
  10.6 3.5 %shard_map.94 = (bf16[1536,512]{1,0:T(8,128)(2,1)S(1)}, s32[8,256]{1,0:T(8,128)S(1)}, bf16[1536,1024]{1,0:T(8,128)(2,1)S(1)}, bf16[1792,256]{1,0:T(8,128)(2,1)S(1)}) custom-call(s32[4]{0:T(128)S(1)} %pad_add_fusion.1.place, s32[7,256]{1,0:T(8,128)S(1)} %bitcast.10, s32[1,256]{1,0:T(1,128)S(1)} %bitcast.11, s32[1,256]{1,0:T(1,128)S(1)} %bitcast.12, ...), custom_call_target="tpu_custom_call" | custom-call | flops 1073741824 | bytes 8388608 | tf_op jit(solution)/shard_map/pallas_call | solution.py:41
  14.2 0.8 %shard_map.101.back_sel = bf16[512,1536]{1,0:T(8,128)(2,1)S(1)} custom-call(s32[4]{0:T(128)S(1)} %pad_add_fusion.1.place, s32[8,256]{1,0:T(8,128)S(1)} %get-tuple-element.56.sources), custom_call_target="tpu_custom_call" | custom-call | flops 67108864 | bytes 8388608 | tf_op jit(solution)/shard_map/pallas_call | solution.py:41
  15.0 0.7 %shard_map.97.up = f32[256,1024]{1,0:T(8,128)S(1)} custom-call(bf16[256,1024]{1,0:T(8,128)(2,1)S(1)} %copy-done, bf16[1024,1024]{1,0:T(8,128)(2,1)S(1)} %copy-done.1), custom_call_target="tpu_custom_call" | custom-call | flops 536870912 | bytes 8388608 | tf_op jit(solution)/shard_map/pallas_call | solution.py:41
  15.8 0.1 pad_add_fusion.me
  15.8 5.6 %shard_map.95 = (bf16[1536,1024]{1,0:T(8,128)(2,1)S(1)}, f32[256,1024]{1,0:T(8,128)S(1)}, bf16[512,256]{1,0:T(8,128)(2,1)S(1)}, bf16[512,256]{1,0:T(8,128)(2,1)S(1)}) custom-call(s32[4]{0:T(128)S(1)} %pad_add_fusion.me, bf16[256,1024]{1,0:T(8,128)(2,1)} %collective-permute-done.far, bf16[256,1024]{1,0:T(8,128)(2,1)} %collective-permute-done.1.near, ...), custom_call_target="tpu_custom_call" | custom-call | flops 3221225472 | bytes 8388608 | tf_op jit(solution)/shard_map/pallas_call | solution.py:41
  21.4 0.8 %collective-permute-start.2 = (bf16[512,256]{1,0:T(8,128)(2,1)S(1)}, bf16[512,256]{1,0:T(8,128)(2,1)S(1)}, u32[]{:S(2)}, u32[]{:S(2)}) collective-permute-start(bf16[512,256]{1,0:T(8,128)(2,1)S(1)} %get-tuple-element.37), channel_id=1, source_target_pairs={{0,1},{1,0},{2,3},{3,2},{4,5},{5,4},{6,7},{7,6},{8,9},{9,8},{10,11... | collective-permute-start | bytes 786440 | tf_op jit(solution)/shard_map/ppermute | solution.py:259
  22.3 1.9 %shard_map.98 = (bf16[256,1024]{1,0:T(8,128)(2,1)S(1)}, f32[16,128]{1,0:T(8,128)S(1)}) custom-call(f32[256,1024]{1,0:T(8,128)S(1)} %shard_map.97.up, f32[256,1024]{1,0:T(8,128)S(1)} %get-tuple-element.42.pre, bf16[256,1024]{1,0:T(8,128)(2,1)S(1)} %copy-done.3, bf16[1536,1024]{1,0:T(8,128)(2,1)S(1)} %get-tuple-element.43.rows), custom_call_target="tpu_custom_call" | custom-call | flops 2147483648 | bytes 8388608 | tf_op jit(solution)/shard_map/pallas_call | solution.py:41
  24.2 2.7 %shard_map.102 = (bf16[1536,1024]{1,0:T(8,128)(2,1)S(1)}, bf16[256,1024]{1,0:T(8,128)(2,1)S(1)}, bf16[256,1024]{1,0:T(8,128)(2,1)S(1)}) custom-call(bf16[256,1024]{1,0:T(8,128)(2,1)S(1)} %get-tuple-element.55.grad, bf16[1792,256]{1,0:T(8,128)(2,1)S(1)} %get-tuple-element.35.wk, bf16[512,1536]{1,0:T(8,128)(2,1)S(1)} %shard_map.101.back_sel), custom_call_target="tpu_custom_call" | custom-call | flops 3221225472 | bytes 8388608 | tf_op jit(solution)/shard_map/pallas_call | solution.py:41
  26.9 4.8 %collective-permute-start.12 = (bf16[256,1024]{1,0:T(8,128)(2,1)S(1)}, bf16[256,1024]{1,0:T(8,128)(2,1)S(1)}, u32[]{:S(2)}, u32[]{:S(2)}) collective-permute-start(bf16[256,1024]{1,0:T(8,128)(2,1)S(1)} %get-tuple-element.58), channel_id=1, source_target_pairs={{0,15},{1,2},{2,1},{3,4},{4,3},{5,6},{6,5},{7,8},{8,7},{9,10},{10,... | collective-permute-start | bytes 1572872 | tf_op jit(solution)/shard_map/ppermute | solution.py:256
  31.8 1.2 %shard_map.96 = (bf16[256,512]{1,0:T(8,128)(2,1)S(1)}, f32[256,512]{1,0:T(8,128)S(1)}, bf16[256,512]{1,0:T(8,128)(2,1)S(1)}, f32[256,512]{1,0:T(8,128)S(1)}) custom-call(s32[4]{0:T(128)S(1)} %pad_add_fusion.me, bf16[512,256]{1,0:T(8,128)(2,1)S(1)} %get-tuple-element.36.act, bf16[512,256]{1,0:T(8,128)(2,1)S(1)} %collective-permute-done.2.act_got, ...), custom_call_target="tpu_custom_call" | custom-call | flops 1073741824 | bytes 8388608 | tf_op jit(solution)/shard_map/pallas_call | solution.py:41
  33.2 0.6 collective-permute-start.6
  33.8 0.8 %collective-permute-done.6 = f32[16,128]{1,0:T(8,128)S(1)} collective-permute-done((f32[16,128]{1,0:T(8,128)S(1)}, f32[16,128]{1,0:T(8,128)S(1)}, u32[]{:S(2)}, u32[]{:S(2)}) %collective-permute-start.6) | collective-permute-done | bytes 8224 | tf_op jit(solution)/shard_map/ppermute | solution.py:259
  34.6 1.7 %collective-permute-start.7 = (f32[16,128]{1,0:T(8,128)S(1)}, f32[16,128]{1,0:T(8,128)S(1)}, u32[]{:S(2)}, u32[]{:S(2)}) collective-permute-start(f32[16,128]{1,0:T(8,128)S(1)} %add.3.conv), channel_id=1, source_target_pairs={{0,2},{1,3},{2,0},{3,1},{4,6},{5,7},{6,4},{7,5},{8,10},{9,11},{10,... | collective-permute-start | bytes 24584 | tf_op jit(solution)/shard_map/ppermute | solution.py:259
  36.3 10.9 %collective-permute-done.7.conv_got = f32[16,128]{1,0:T(8,128)S(1)} collective-permute-done((f32[16,128]{1,0:T(8,128)S(1)}, f32[16,128]{1,0:T(8,128)S(1)}, u32[]{:S(2)}, u32[]{:S(2)}) %collective-permute-start.7) | collective-permute-done | bytes 8224 | tf_op jit(solution)/shard_map/ppermute | solution.py:259
  47.2 0.6 %shard_map.99 = (bf16[144,512]{1,0:T(8,128)(2,1)S(1)}, f32[128,512]{1,0:T(8,128)S(1)}, bf16[128,512]{1,0:T(8,128)(2,1)S(1)}, f32[128,512]{1,0:T(8,128)S(1)}, f32[16,128]{1,0:T(8,128)S(1)}) custom-call(s32[4]{0:T(128)S(1)} %pad_add_fusion.me, f32[256,512]{1,0:T(8,128)S(1)} %get-tuple-element.38.kept_a, bf16[256,512]{1,0:T(8,128)(2,1)S(1)} %collective-permute-done.4.got_a, ...), custom_call_target="tpu_custom_call" | custom-call | flops 1048576 | bytes 8388608 | tf_op jit(solution)/shard_map/pallas_call | solution.py:41
  47.8 1.6 %collective-permute-start.8 = (bf16[144,512]{1,0:T(8,128)(2,1)S(1)}, bf16[144,512]{1,0:T(8,128)(2,1)S(1)}, u32[]{:S(2)}, u32[]{:S(2)}) collective-permute-start(bf16[144,512]{1,0:T(8,128)(2,1)S(1)} %get-tuple-element.46), channel_id=1, source_target_pairs={{0,4},{1,5},{2,6},{3,7},{4,0},{5,1},{6,2},{7,3},{8,12},{9,13},{10,... | collective-permute-start | bytes 442376 | tf_op jit(solution)/shard_map/ppermute | solution.py:259
  49.5 2.6 %collective-permute-start.9 = (bf16[128,512]{1,0:T(8,128)(2,1)S(1)}, bf16[128,512]{1,0:T(8,128)(2,1)S(1)}, u32[]{:S(2)}, u32[]{:S(2)}) collective-permute-start(bf16[128,512]{1,0:T(8,128)(2,1)S(1)} %get-tuple-element.48), channel_id=1, source_target_pairs={{0,8},{1,9},{2,10},{3,11},{4,12},{5,13},{6,14},{7,15},{8,0},{9,1},... | collective-permute-start | bytes 393224 | tf_op jit(solution)/shard_map/ppermute | solution.py:259
  52.1 4.1 %collective-permute-done.9.got_b = bf16[128,512]{1,0:T(8,128)(2,1)S(1)} collective-permute-done((bf16[128,512]{1,0:T(8,128)(2,1)S(1)}, bf16[128,512]{1,0:T(8,128)(2,1)S(1)}, u32[]{:S(2)}, u32[]{:S(2)}) %collective-permute-start.9) | collective-permute-done | bytes 131104 | tf_op jit(solution)/shard_map/ppermute | solution.py:259
  56.3 0.6 shard_map.100
  56.8 2.3 %collective-permute-start.10 = (bf16[80,512]{1,0:T(8,128)(2,1)S(1)}, bf16[80,512]{1,0:T(8,128)(2,1)S(1)}, u32[]{:S(2)}, u32[]{:S(2)}) collective-permute-start(bf16[80,512]{1,0:T(8,128)(2,1)S(1)} %get-tuple-element.51), channel_id=1, source_target_pairs={{0,8},{1,9},{2,10},{3,11},{4,12},{5,13},{6,14},{7,15},{8,0},{9,1},... | collective-permute-start | bytes 245768 | tf_op jit(solution)/shard_map/ppermute | solution.py:259
  59.1 0.6 collective-permute-start.11
  59.7 1.1 %shard_map.103.inner = f32[256,1024]{1,0:T(8,128)S(1)} custom-call(bf16[256,1024]{1,0:T(8,128)(2,1)S(1)} %get-tuple-element.55.grad, bf16[1536,1024]{1,0:T(8,128)(2,1)S(1)} %get-tuple-element.57.terms, bf16[1792,256]{1,0:T(8,128)(2,1)S(1)} %get-tuple-element.35.wk, s32[8,256]{1,0:T(8,128)S(1)} %get-tuple-element.56.sources, bf16[256,1024]{1,0:T(8,128)(2,1)S(1)} %copy-done), custom_call_target="tpu_custom_call" | custom-call | flops 1073741824 | bytes 8388608 | tf_op jit(solution)/shard_map/pallas_call | solution.py:41
  60.9 2.5 %collective-permute-done.11.got_b = bf16[64,512]{1,0:T(8,128)(2,1)S(1)} collective-permute-done((bf16[64,512]{1,0:T(8,128)(2,1)S(1)}, bf16[64,512]{1,0:T(8,128)(2,1)S(1)}, u32[]{:S(2)}, u32[]{:S(2)}) %collective-permute-start.11) | collective-permute-done | bytes 65568 | tf_op jit(solution)/shard_map/ppermute | solution.py:259
  63.4 1.1 %shard_map.104 = (f32[64,1024]{1,0:T(8,128)}, f32[7,16,16]{2,1,0:T(8,128)}, bf16[256,1024]{1,0:T(8,128)(2,1)}) custom-call(f32[64,512]{1,0:T(8,128)S(1)} %get-tuple-element.50.kept_a, bf16[80,512]{1,0:T(8,128)(2,1)S(1)} %collective-permute-done.10.got_a, f32[64,512]{1,0:T(8,128)S(1)} %get-tuple-element.52.kept_b, ...), custom_call_target="tpu_custom_call" | custom-call | flops 1048576 | bytes 8388608 | tf_op jit(solution)/shard_map/pallas_call | solution.py:41
  (26 shorter events, 0.2 us)
Async XLA Ops:
  0.6 14.4 %copy-start = (bf16[256,1024]{1,0:T(8,128)(2,1)S(1)}, bf16[256,1024]{1,0:T(8,128)(2,1)}, u32[]{:S(2)}) copy-start(bf16[256,1024]{1,0:T(8,128)(2,1)} %cot.5) | copy-start | bytes 1572868
  0.6 14.4 %copy-start.1 = (bf16[1024,1024]{1,0:T(8,128)(2,1)S(1)}, bf16[1024,1024]{1,0:T(8,128)(2,1)}, u32[]{:S(2)}) copy-start(bf16[1024,1024]{1,0:T(8,128)(2,1)} %mix.1) | copy-start | bytes 6291460
  0.7 15.2 %collective-permute-start = (bf16[256,1024]{1,0:T(8,128)(2,1)}, bf16[256,1024]{1,0:T(8,128)(2,1)}, u32[]{:S(2)}, u32[]{:S(2)}) collective-permute-start(bf16[256,1024]{1,0:T(8,128)(2,1)} %x.3), channel_id=1, source_target_pairs={{0,15},{1,2},{2,1},{3,4},{4,3},{5,6},{6,5},{7,8},{8,7},{9,10},{10,... | collective-permute-start | bytes 1572872 | tf_op jit(solution)/shard_map/ppermute | solution.py:256
  6.2 9.7 %collective-permute-start.1 = (bf16[256,1024]{1,0:T(8,128)(2,1)}, bf16[256,1024]{1,0:T(8,128)(2,1)}, u32[]{:S(2)}, u32[]{:S(2)}) collective-permute-start(bf16[256,1024]{1,0:T(8,128)(2,1)} %x.3), channel_id=1, source_target_pairs={{0,1},{1,0},{2,3},{3,2},{4,5},{5,4},{6,7},{7,6},{8,9},{9,8},{10,11... | collective-permute-start | bytes 1572872 | tf_op jit(solution)/shard_map/ppermute | solution.py:252
  6.2 25.6 %collective-permute-start.3 = (bf16[256,1024]{1,0:T(8,128)(2,1)}, bf16[256,1024]{1,0:T(8,128)(2,1)S(1)}, u32[]{:S(2)}, u32[]{:S(2)}) collective-permute-start(bf16[256,1024]{1,0:T(8,128)(2,1)} %cot.5), channel_id=1, source_target_pairs={{0,1},{1,0},{2,3},{3,2},{4,5},{5,4},{6,7},{7,6},{8,9},{9,8},{10,11... | collective-permute-start | bytes 1572872 | tf_op jit(solution)/shard_map/ppermute | solution.py:259
  6.8 1.0 %copy-start.2 = (bf16[256,1024]{1,0:T(8,128)(2,1)S(1)}, bf16[256,1024]{1,0:T(8,128)(2,1)}, u32[]{:S(2)}) copy-start(bf16[256,1024]{1,0:T(8,128)(2,1)} %x.3) | copy-start | bytes 1572868
  7.8 0.7 %copy-start.4 = (bf16[7,16,16]{2,1,0:T(8,128)(2,1)S(1)}, bf16[7,16,16]{2,1,0:T(8,128)(2,1)}, u32[]{:S(2)}) copy-start(bf16[7,16,16]{2,1,0:T(8,128)(2,1)} %conv_hbm.1) | copy-start | bytes 10756
  8.6 0.7 %copy-start.5 = (s32[256,7]{0,1:T(8,128)S(1)}, s32[256,7]{0,1:T(8,128)}, u32[]{:S(2)}) copy-start(s32[256,7]{0,1:T(8,128)} %param.11) | copy-start | bytes 21508
  9.3 0.7 %copy-start.6 = (s32[256]{0:T(256)S(1)}, s32[256]{0:T(256)}, u32[]{:S(2)}) copy-start(s32[256]{0:T(256)} %param.12) | copy-start | bytes 3076
  9.9 0.7 %copy-start.7 = (s32[256]{0:T(256)S(1)}, s32[256]{0:T(256)}, u32[]{:S(2)}) copy-start(s32[256]{0:T(256)} %param.13) | copy-start | bytes 3076
  14.2 1.7 %copy-start.3 = (bf16[256,1024]{1,0:T(8,128)(2,1)S(1)}, bf16[256,1024]{1,0:T(8,128)(2,1)}, u32[]{:S(2)}) copy-start(bf16[256,1024]{1,0:T(8,128)(2,1)} %x.3) | copy-start | bytes 1572868
  21.4 10.4 %collective-permute-start.2 = (bf16[512,256]{1,0:T(8,128)(2,1)S(1)}, bf16[512,256]{1,0:T(8,128)(2,1)S(1)}, u32[]{:S(2)}, u32[]{:S(2)}) collective-permute-start(bf16[512,256]{1,0:T(8,128)(2,1)S(1)} %get-tuple-element.37), channel_id=1, source_target_pairs={{0,1},{1,0},{2,3},{3,2},{4,5},{5,4},{6,7},{7,6},{8,9},{9,8},{10,11... | collective-permute-start | bytes 786440 | tf_op jit(solution)/shard_map/ppermute | solution.py:259
  26.9 33.9 %collective-permute-start.12 = (bf16[256,1024]{1,0:T(8,128)(2,1)S(1)}, bf16[256,1024]{1,0:T(8,128)(2,1)S(1)}, u32[]{:S(2)}, u32[]{:S(2)}) collective-permute-start(bf16[256,1024]{1,0:T(8,128)(2,1)S(1)} %get-tuple-element.58), channel_id=1, source_target_pairs={{0,15},{1,2},{2,1},{3,4},{4,3},{5,6},{6,5},{7,8},{8,7},{9,10},{10,... | collective-permute-start | bytes 1572872 | tf_op jit(solution)/shard_map/ppermute | solution.py:256
  31.8 29.1 %collective-permute-start.13 = (bf16[256,1024]{1,0:T(8,128)(2,1)S(1)}, bf16[256,1024]{1,0:T(8,128)(2,1)S(1)}, u32[]{:S(2)}, u32[]{:S(2)}) collective-permute-start(bf16[256,1024]{1,0:T(8,128)(2,1)S(1)} %get-tuple-element.59), channel_id=1, source_target_pairs={{0,1},{1,0},{2,3},{3,2},{4,5},{5,4},{6,7},{7,6},{8,9},{9,8},{10,11... | collective-permute-start | bytes 1572872 | tf_op jit(solution)/shard_map/ppermute | solution.py:252
  33.0 14.1 %collective-permute-start.4 = (bf16[256,512]{1,0:T(8,128)(2,1)S(1)}, bf16[256,512]{1,0:T(8,128)(2,1)S(1)}, u32[]{:S(2)}, u32[]{:S(2)}) collective-permute-start(bf16[256,512]{1,0:T(8,128)(2,1)S(1)} %get-tuple-element.39), channel_id=1, source_target_pairs={{0,2},{1,3},{2,0},{3,1},{4,6},{5,7},{6,4},{7,5},{8,10},{9,11},{10,... | collective-permute-start | bytes 786440 | tf_op jit(solution)/shard_map/ppermute | solution.py:259
  33.1 14.1 %collective-permute-start.5 = (bf16[256,512]{1,0:T(8,128)(2,1)S(1)}, bf16[256,512]{1,0:T(8,128)(2,1)S(1)}, u32[]{:S(2)}, u32[]{:S(2)}) collective-permute-start(bf16[256,512]{1,0:T(8,128)(2,1)S(1)} %get-tuple-element.41), channel_id=1, source_target_pairs={{0,4},{1,5},{2,6},{3,7},{4,0},{5,1},{6,2},{7,3},{8,12},{9,13},{10,... | collective-permute-start | bytes 786440 | tf_op jit(solution)/shard_map/ppermute | solution.py:259
  33.2 1.4 %collective-permute-start.6 = (f32[16,128]{1,0:T(8,128)S(1)}, f32[16,128]{1,0:T(8,128)S(1)}, u32[]{:S(2)}, u32[]{:S(2)}) collective-permute-start(f32[16,128]{1,0:T(8,128)S(1)} %get-tuple-element.44), channel_id=1, source_target_pairs={{0,1},{1,0},{2,3},{3,2},{4,5},{5,4},{6,7},{7,6},{8,9},{9,8},{10,11... | collective-permute-start | bytes 24584 | tf_op jit(solution)/shard_map/ppermute | solution.py:259
  34.6 12.6 %collective-permute-start.7 = (f32[16,128]{1,0:T(8,128)S(1)}, f32[16,128]{1,0:T(8,128)S(1)}, u32[]{:S(2)}, u32[]{:S(2)}) collective-permute-start(f32[16,128]{1,0:T(8,128)S(1)} %add.3.conv), channel_id=1, source_target_pairs={{0,2},{1,3},{2,0},{3,1},{4,6},{5,7},{6,4},{7,5},{8,10},{9,11},{10,... | collective-permute-start | bytes 24584 | tf_op jit(solution)/shard_map/ppermute | solution.py:259
  47.8 8.4 %collective-permute-start.8 = (bf16[144,512]{1,0:T(8,128)(2,1)S(1)}, bf16[144,512]{1,0:T(8,128)(2,1)S(1)}, u32[]{:S(2)}, u32[]{:S(2)}) collective-permute-start(bf16[144,512]{1,0:T(8,128)(2,1)S(1)} %get-tuple-element.46), channel_id=1, source_target_pairs={{0,4},{1,5},{2,6},{3,7},{4,0},{5,1},{6,2},{7,3},{8,12},{9,13},{10,... | collective-permute-start | bytes 442376 | tf_op jit(solution)/shard_map/ppermute | solution.py:259
  49.5 6.8 %collective-permute-start.9 = (bf16[128,512]{1,0:T(8,128)(2,1)S(1)}, bf16[128,512]{1,0:T(8,128)(2,1)S(1)}, u32[]{:S(2)}, u32[]{:S(2)}) collective-permute-start(bf16[128,512]{1,0:T(8,128)(2,1)S(1)} %get-tuple-element.48), channel_id=1, source_target_pairs={{0,8},{1,9},{2,10},{3,11},{4,12},{5,13},{6,14},{7,15},{8,0},{9,1},... | collective-permute-start | bytes 393224 | tf_op jit(solution)/shard_map/ppermute | solution.py:259
  56.8 6.5 %collective-permute-start.10 = (bf16[80,512]{1,0:T(8,128)(2,1)S(1)}, bf16[80,512]{1,0:T(8,128)(2,1)S(1)}, u32[]{:S(2)}, u32[]{:S(2)}) collective-permute-start(bf16[80,512]{1,0:T(8,128)(2,1)S(1)} %get-tuple-element.51), channel_id=1, source_target_pairs={{0,8},{1,9},{2,10},{3,11},{4,12},{5,13},{6,14},{7,15},{8,0},{9,1},... | collective-permute-start | bytes 245768 | tf_op jit(solution)/shard_map/ppermute | solution.py:259
  59.1 4.3 %collective-permute-start.11 = (bf16[64,512]{1,0:T(8,128)(2,1)S(1)}, bf16[64,512]{1,0:T(8,128)(2,1)S(1)}, u32[]{:S(2)}, u32[]{:S(2)}) collective-permute-start(bf16[64,512]{1,0:T(8,128)(2,1)S(1)} %get-tuple-element.53), channel_id=1, source_target_pairs={{0,2},{1,3},{2,0},{3,1},{4,6},{5,7},{6,4},{7,5},{8,10},{9,11},{10,... | collective-permute-start | bytes 196616 | tf_op jit(solution)/shard_map/ppermute | solution.py:259

commit v8 on v5

--- a/solution.py
+++ b/solution.py
@@ -106,15 +106,18 @@
     n, width = pre.shape
     taps = wk.shape[0] // WIDE
     for c in range(0, width, WIDE):
-        both = jnp.concatenate([far[:, c : c + WIDE], near[:, c : c + WIDE]], axis=0)
-        rows = mm(halo_sel[...], both).astype(bf16) + own[:, c : c + WIDE]
-        rows_out[:, c : c + WIDE] = rows
-        acc = mm(x[:, c : c + WIDE], wk[:WIDE, :])
+        cols = slice(c, c + WIDE)
+        both = jnp.concatenate([far[:, cols], near[:, cols]], axis=0)
         for tap in range(1, taps):
-            acc += mm(rows[(tap - 1) * n : tap * n], wk[tap * WIDE : (tap + 1) * WIDE, :])
-        pre[:, c : c + WIDE] = acc
+            at = slice((tap - 1) * n, tap * n)
+            rows_out[at, cols] = mm(halo_sel[at, :], both).astype(bf16) + own[at, cols]
+    for c in range(0, width, WIDE):
+        cols = slice(c, c + WIDE)
+        wide = [x[:, cols]] + [rows_out[(tap - 1) * n : tap * n, cols] for tap in range(1, taps)]
+        acc = mm(jnp.concatenate(wide, axis=1), wk[...])
+        pre[:, cols] = acc
         active = (0.5 * acc) * (1.0 + gelu_tanh(acc))
-        act_t[c : c + WIDE, :] = active.T.astype(bf16)
+        act_t[cols, :] = active.T.astype(bf16)
     for k in range(width // share // 2):
         for bit, out in ((me[0], act_keep), (1 - me[0], act_send)):
             at = pl.multiple_of((2 * k + bit) * share, share)
@@ -131,13 +134,16 @@
     for k, (bit, skip) in enumerate(where):
         cols = slice(k * half, (k + 1) * half)
         both = jnp.concatenate([cot[:, cols], cot_got[:, cols]], axis=0)
-        for want, out in ((1 - me[bit], outs[2 * k]), (me[bit], outs[2 * k + 1])):
-            pieces = []
+        pieces = []
+        for want in (1 - me[bit], me[bit]):
             for q in range(blocks // 2):
                 base = ((q >> skip) << (skip + 1)) | (q & ((1 << skip) - 1))
                 at = pl.ds(pl.multiple_of((base + (want << skip)) * share, share), share)
                 pieces.append(jnp.concatenate([act[at, :], act_got[at, :]], axis=1))
-            out[...] = mm(jnp.concatenate(pieces, axis=0), both).astype(out.dtype)
+        total = mm(jnp.concatenate(pieces, axis=0), both)
+        rows = total.shape[0] // 2
+        outs[2 * k][...] = total[:rows].astype(bf16)
+        outs[2 * k + 1][...] = total[rows:]
 
 
 def select_rows(sources, start, count, taps):
@@ -150,17 +156,19 @@
 def weights_kernel(channels, scale, up, pre, x, rows, grad, conv):
     n, width = grad.shape
     taps = rows.shape[0] // n + 1
-    acc = [jnp.zeros((WIDE, WIDE), f32) for _ in range(taps)]
+    turned = []
     for c in range(0, width, WIDE):
         v = pre[:, c : c + WIDE]
         t = gelu_tanh(v)
         slope = 0.5 * (1.0 + t) + (0.5 * TANH_SCALE) * v * (1.0 - t * t) * (1.0 + (3 * TANH_CUBE) * (v * v))
         g = up[:, c : c + WIDE] * slope
         grad[:, c : c + WIDE] = g.astype(bf16)
-        g_t = g.T.astype(bf16)
-        acc[0] += mm(g_t, x[:, c : c + WIDE])
-        for tap in range(1, taps):
-            acc[tap] += mm(g_t, rows[(tap - 1) * n : tap * n, c : c + WIDE])
+        turned.append(g.T.astype(bf16))
+    turned = jnp.concatenate(turned, axis=1)
+    acc = []
+    for tap in range(taps):
+        part = x[...] if tap == 0 else rows[(tap - 1) * n : tap * n, :]
+        acc.append(mm(turned, jnp.concatenate([part[:, c : c + WIDE] for c in range(0, width, WIDE)], axis=0)))
     same = iota((WIDE, WIDE), 0) // channels == iota((WIDE, WIDE), 1) // channels
     conv[...] = jnp.zeros(conv.shape, f32)
     fold = jnp.where(iota((channels, WIDE), 1) % channels == iota((channels, WIDE), 0), 1.0, 0.0)
@@ -172,11 +180,15 @@
         )
 
 
-def terms_kernel(place, grad, wk, sources, terms, far, near, back_sel):
+def pick_kernel(place, sources, back_sel):
+    taps = back_sel.shape[1] // sources.shape[1] + 1
+    back_sel[:ROW, :] = select_rows(sources, place[2], ROW, taps)
+    back_sel[ROW:, :] = select_rows(sources, place[3], ROW, taps)
+
+
+def terms_kernel(grad, wk, back_sel, terms, far, near):
     n, width = grad.shape
     taps = wk.shape[0] // WIDE
-    back_sel[:ROW, :] = select_rows(sources, place[2], ROW, taps)
-    back_sel[ROW:, :] = select_rows(sources, place[3], ROW, taps)
     for c in range(0, width, WIDE):
         g = grad[:, c : c + WIDE]
         for tap in range(1, taps):
@@ -315,6 +327,7 @@
         ],
     )
     (up,) = call(up_kernel, [((n, width), f32)], 1 << 29, cotangent, mix_weight)
+    (back_sel,) = call(pick_kernel, [((2 * ROW, pairs), bf16)], 1 << 26, spots, sources, scalars=1)
     rows, pre, act, act_send = call(
         functools.partial(front_kernel, share),
         [((pairs, width), bf16), ((n, width), f32), ((half, n), bf16), ((half, n), bf16)],
@@ -370,12 +383,9 @@
         terms_kernel,
         [((pairs, width), bf16), ((ROW, width), bf16), ((ROW, width), bf16)],
         3 << 30,
-        spots,
         grad,
         wk,
-        sources,
-        scalars=1,
-        scratch=[pltpu.VMEM((2 * ROW, pairs), bf16)],
+        back_sel,
     )
     conv = conv + swap(conv, 0)
     conv_got = swap(conv, 1)

time: 64.9 us -> 64.2 us (0.989)
  starting transfers between devices: 24.5 us -> 22.8 us
  local copies, waits for them, and re-layouts: 2.85 us -> 3.86 us
    ppermute x12, starting transfers between devices: 14.1 us -> 12.4 us  [swap_by(): return lax.ppermute(value, 'space', [(i, i ^ mask) for i in range(devices)])]
    unnamed x16, local copies, waits for them, and re-layouts: 2.85 us -> 3.86 us
    pallas_call x9 -> x10, Pallas kernels: 18.5 us -> 18.4 us  [call(): pl.pallas_call(body, out_shape=[jax.ShapeDtypeStruct(s, d) for s, d in ou...]
where the time goes in v8:
time: 64.2 us; the launch traced here: 63.8 us
  starting transfers between devices  22.8 us (36%)
  Pallas kernels  18.4 us (29%)
  waiting for transfers between devices  17.9 us (28%)
  local copies, waits for them, and re-layouts  3.86 us (6%)
  between operations  0.78 us (1%)
    pallas_call x10, Pallas kernels, call(): pl.pallas_call(body, out_shape=[jax.ShapeDtypeStruct(s, d) for s, d in ou...  18.4 us
    ppermute x12, waiting for transfers between devices, swap_by(): return lax.ppermute(value, 'space', [(i, i ^ mask) for i in range(devices)])  17.9 us
    ppermute x12, starting transfers between devices, swap_by(): return lax.ppermute(value, 'space', [(i, i ^ mask) for i in range(devices)])  12.4 us
    ppermute x2, starting transfers between devices, far_swap(): return lax.ppermute(value, 'space', [(i, other(i)) for i in range(devices)])  10.4 us
    unnamed x16, local copies, waits for them, and re-layouts  3.86 us
  transfers between devices with their start and end apart: 16, of which 4 were waited for; matrix products, arithmetic and copies ran while one was open for 0% of the time, Pallas kernels for 27%

profile of v8, /device:TPU:0, one launch (start us, length us, event | category | flops | bytes accessed | tf_op | source)
XLA Modules:
  0.0 63.8 jit_solution(922606948558387720)
XLA Ops:
  0.7 5.5 %collective-permute-start = (bf16[256,1024]{1,0:T(8,128)(2,1)}, bf16[256,1024]{1,0:T(8,128)(2,1)}, u32[]{:S(2)}, u32[]{:S(2)}) collective-permute-start(bf16[256,1024]{1,0:T(8,128)(2,1)} %x.3), channel_id=1, source_target_pairs={{0,15},{1,2},{2,1},{3,4},{4,3},{5,6},{6,5},{7,8},{8,7},{9,10},{10,... | collective-permute-start | bytes 1572872 | tf_op jit(solution)/shard_map/ppermute | solution.py:294
  6.2 0.5 collective-permute-start.3
  6.7 0.1 pad_add_fusion.1.place
  6.8 1.0 %copy-done.2 = bf16[256,1024]{1,0:T(8,128)(2,1)S(1)} copy-done((bf16[256,1024]{1,0:T(8,128)(2,1)S(1)}, bf16[256,1024]{1,0:T(8,128)(2,1)}, u32[]{:S(2)}) %copy-start.2) | copy-done | bytes 524312
  7.8 0.7 %copy-done.4 = bf16[7,16,16]{2,1,0:T(8,128)(2,1)S(1)} copy-done((bf16[7,16,16]{2,1,0:T(8,128)(2,1)S(1)}, bf16[7,16,16]{2,1,0:T(8,128)(2,1)}, u32[]{:S(2)}) %copy-start.4) | copy-done | bytes 3608
  8.6 0.7 %copy-done.5 = s32[256,7]{0,1:T(8,128)S(1)} copy-done((s32[256,7]{0,1:T(8,128)S(1)}, s32[256,7]{0,1:T(8,128)}, u32[]{:S(2)}) %copy-start.5) | copy-done | bytes 7192
  9.3 0.7 %copy-done.6 = s32[256]{0:T(256)S(1)} copy-done((s32[256]{0:T(256)S(1)}, s32[256]{0:T(256)}, u32[]{:S(2)}) %copy-start.6) | copy-done | bytes 1048
  9.9 0.7 %copy-done.7 = s32[256]{0:T(256)S(1)} copy-done((s32[256]{0:T(256)S(1)}, s32[256]{0:T(256)}, u32[]{:S(2)}) %copy-start.7) | copy-done | bytes 1048
  10.6 3.5 %shard_map.94 = (bf16[1536,512]{1,0:T(8,128)(2,1)S(1)}, s32[8,256]{1,0:T(8,128)S(1)}, bf16[1536,1024]{1,0:T(8,128)(2,1)S(1)}, bf16[1792,256]{1,0:T(8,128)(2,1)S(1)}) custom-call(s32[4]{0:T(128)S(1)} %pad_add_fusion.1.place, s32[7,256]{1,0:T(8,128)S(1)} %bitcast.10, s32[1,256]{1,0:T(1,128)S(1)} %bitcast.11, s32[1,256]{1,0:T(1,128)S(1)} %bitcast.12, ...), custom_call_target="tpu_custom_call" | custom-call | flops 1073741824 | bytes 8388608 | tf_op jit(solution)/shard_map/pallas_call | solution.py:41
  14.2 0.8 %shard_map.100.back_sel = bf16[512,1536]{1,0:T(8,128)(2,1)S(1)} custom-call(s32[4]{0:T(128)S(1)} %pad_add_fusion.1.place, s32[8,256]{1,0:T(8,128)S(1)} %get-tuple-element.54.sources), custom_call_target="tpu_custom_call" | custom-call | flops 67108864 | bytes 8388608 | tf_op jit(solution)/shard_map/pallas_call | solution.py:41
  15.0 0.7 %shard_map.97.up = f32[256,1024]{1,0:T(8,128)S(1)} custom-call(bf16[256,1024]{1,0:T(8,128)(2,1)S(1)} %copy-done, bf16[1024,1024]{1,0:T(8,128)(2,1)S(1)} %copy-done.1), custom_call_target="tpu_custom_call" | custom-call | flops 536870912 | bytes 8388608 | tf_op jit(solution)/shard_map/pallas_call | solution.py:41
  15.8 0.1 pad_add_fusion.me
  15.8 4.3 %shard_map.95 = (bf16[1536,1024]{1,0:T(8,128)(2,1)S(1)}, f32[256,1024]{1,0:T(8,128)S(1)}, bf16[512,256]{1,0:T(8,128)(2,1)S(1)}, bf16[512,256]{1,0:T(8,128)(2,1)S(1)}) custom-call(s32[4]{0:T(128)S(1)} %pad_add_fusion.me, bf16[256,1024]{1,0:T(8,128)(2,1)} %collective-permute-done.far, bf16[256,1024]{1,0:T(8,128)(2,1)} %collective-permute-done.1.near, ...), custom_call_target="tpu_custom_call" | custom-call | flops 3221225472 | bytes 8388608 | tf_op jit(solution)/shard_map/pallas_call | solution.py:41
  20.2 0.8 %collective-permute-start.2 = (bf16[512,256]{1,0:T(8,128)(2,1)S(1)}, bf16[512,256]{1,0:T(8,128)(2,1)S(1)}, u32[]{:S(2)}, u32[]{:S(2)}) collective-permute-start(bf16[512,256]{1,0:T(8,128)(2,1)S(1)} %get-tuple-element.36), channel_id=1, source_target_pairs={{0,1},{1,0},{2,3},{3,2},{4,5},{5,4},{6,7},{7,6},{8,9},{9,8},{10,11... | collective-permute-start | bytes 786440 | tf_op jit(solution)/shard_map/ppermute | solution.py:297
  21.0 2.0 %shard_map.98 = (bf16[256,1024]{1,0:T(8,128)(2,1)S(1)}, f32[16,128]{1,0:T(8,128)S(1)}) custom-call(f32[256,1024]{1,0:T(8,128)S(1)} %shard_map.97.up, f32[256,1024]{1,0:T(8,128)S(1)} %get-tuple-element.41.pre, bf16[256,1024]{1,0:T(8,128)(2,1)S(1)} %copy-done.3, bf16[1536,1024]{1,0:T(8,128)(2,1)S(1)} %get-tuple-element.42.rows), custom_call_target="tpu_custom_call" | custom-call | flops 2147483648 | bytes 8388608 | tf_op jit(solution)/shard_map/pallas_call | solution.py:41
  23.1 2.7 %shard_map.101 = (bf16[1536,1024]{1,0:T(8,128)(2,1)S(1)}, bf16[256,1024]{1,0:T(8,128)(2,1)S(1)}, bf16[256,1024]{1,0:T(8,128)(2,1)S(1)}) custom-call(bf16[256,1024]{1,0:T(8,128)(2,1)S(1)} %get-tuple-element.53.grad, bf16[1792,256]{1,0:T(8,128)(2,1)S(1)} %get-tuple-element.34.wk, bf16[512,1536]{1,0:T(8,128)(2,1)S(1)} %shard_map.100.back_sel), custom_call_target="tpu_custom_call" | custom-call | flops 3221225472 | bytes 8388608 | tf_op jit(solution)/shard_map/pallas_call | solution.py:41
  25.8 4.8 %collective-permute-start.14 = (bf16[256,1024]{1,0:T(8,128)(2,1)S(1)}, bf16[256,1024]{1,0:T(8,128)(2,1)S(1)}, u32[]{:S(2)}, u32[]{:S(2)}) collective-permute-start(bf16[256,1024]{1,0:T(8,128)(2,1)S(1)} %get-tuple-element.56), channel_id=1, source_target_pairs={{0,15},{1,2},{2,1},{3,4},{4,3},{5,6},{6,5},{7,8},{8,7},{9,10},{10,... | collective-permute-start | bytes 1572872 | tf_op jit(solution)/shard_map/ppermute | solution.py:294
  30.7 1.3 %shard_map.96 = (bf16[256,512]{1,0:T(8,128)(2,1)S(1)}, f32[256,512]{1,0:T(8,128)S(1)}, bf16[256,512]{1,0:T(8,128)(2,1)S(1)}, f32[256,512]{1,0:T(8,128)S(1)}) custom-call(s32[4]{0:T(128)S(1)} %pad_add_fusion.me, bf16[512,256]{1,0:T(8,128)(2,1)S(1)} %get-tuple-element.35.act, bf16[512,256]{1,0:T(8,128)(2,1)S(1)} %collective-permute-done.2.act_got, ...), custom_call_target="tpu_custom_call" | custom-call | flops 1073741824 | bytes 8388608 | tf_op jit(solution)/shard_map/pallas_call | solution.py:41
  32.1 0.6 collective-permute-start.6
  32.6 0.8 %collective-permute-done.6 = f32[16,128]{1,0:T(8,128)S(1)} collective-permute-done((f32[16,128]{1,0:T(8,128)S(1)}, f32[16,128]{1,0:T(8,128)S(1)}, u32[]{:S(2)}, u32[]{:S(2)}) %collective-permute-start.6) | collective-permute-done | bytes 8224 | tf_op jit(solution)/shard_map/ppermute | solution.py:297
  33.5 1.7 %collective-permute-start.7 = (f32[16,128]{1,0:T(8,128)S(1)}, f32[16,128]{1,0:T(8,128)S(1)}, u32[]{:S(2)}, u32[]{:S(2)}) collective-permute-start(f32[16,128]{1,0:T(8,128)S(1)} %add.3.refs_4_), channel_id=1, source_target_pairs={{0,2},{1,3},{2,0},{3,1},{4,6},{5,7},{6,4},{7,5},{8,10},{9,11},{10,... | collective-permute-start | bytes 24584 | tf_op jit(solution)/shard_map/ppermute | solution.py:297
  35.2 10.9 %collective-permute-done.7.refs_5_ = f32[16,128]{1,0:T(8,128)S(1)} collective-permute-done((f32[16,128]{1,0:T(8,128)S(1)}, f32[16,128]{1,0:T(8,128)S(1)}, u32[]{:S(2)}, u32[]{:S(2)}) %collective-permute-start.7) | collective-permute-done | bytes 8224 | tf_op jit(solution)/shard_map/ppermute | solution.py:297
  46.1 0.6 %shard_map.99 = (bf16[80,512]{1,0:T(8,128)(2,1)S(1)}, bf16[80,512]{1,0:T(8,128)(2,1)S(1)}, bf16[80,512]{1,0:T(8,128)(2,1)S(1)}, f32[64,512]{1,0:T(8,128)S(1)}, b...) custom-call(s32[4]{0:T(128)S(1)} %pad_add_fusion.me, ...), custom_call_target="tpu_custom_call" | custom-call | flops 1048576 | bytes 8388608 | tf_op jit(solution)/shard_map/pallas_call | solution.py:41
  46.8 2.7 %collective-permute-start.11 = (bf16[64,512]{1,0:T(8,128)(2,1)S(1)}, bf16[64,512]{1,0:T(8,128)(2,1)S(1)}, u32[]{:S(2)}, u32[]{:S(2)}) collective-permute-start(bf16[64,512]{1,0:T(8,128)(2,1)S(1)} %get-tuple-element.49), channel_id=1, source_target_pairs={{0,8},{1,9},{2,10},{3,11},{4,12},{5,13},{6,14},{7,15},{8,0},{9,1},... | collective-permute-start | bytes 196616 | tf_op jit(solution)/shard_map/ppermute | solution.py:297
  49.4 1.3 %collective-permute-start.10 = (bf16[80,512]{1,0:T(8,128)(2,1)S(1)}, bf16[80,512]{1,0:T(8,128)(2,1)S(1)}, u32[]{:S(2)}, u32[]{:S(2)}) collective-permute-start(bf16[80,512]{1,0:T(8,128)(2,1)S(1)} %get-tuple-element.47), channel_id=1, source_target_pairs={{0,12},{1,13},{2,14},{3,15},{4,8},{5,9},{6,10},{7,11},{8,4},{9,5},... | collective-permute-start | bytes 245768 | tf_op jit(solution)/shard_map/ppermute | solution.py:297
  50.8 0.2 collective-permute-start.8
  51.0 2.8 %collective-permute-start.9 = (bf16[80,512]{1,0:T(8,128)(2,1)S(1)}, bf16[80,512]{1,0:T(8,128)(2,1)S(1)}, u32[]{:S(2)}, u32[]{:S(2)}) collective-permute-start(bf16[80,512]{1,0:T(8,128)(2,1)S(1)} %get-tuple-element.46), channel_id=1, source_target_pairs={{0,8},{1,9},{2,10},{3,11},{4,12},{5,13},{6,14},{7,15},{8,0},{9,1},... | collective-permute-start | bytes 245768 | tf_op jit(solution)/shard_map/ppermute | solution.py:297
  53.8 1.6 %collective-permute-start.13 = (bf16[64,512]{1,0:T(8,128)(2,1)S(1)}, bf16[64,512]{1,0:T(8,128)(2,1)S(1)}, u32[]{:S(2)}, u32[]{:S(2)}) collective-permute-start(bf16[64,512]{1,0:T(8,128)(2,1)S(1)} %get-tuple-element.51), channel_id=1, source_target_pairs={{0,10},{1,11},{2,8},{3,9},{4,14},{5,15},{6,12},{7,13},{8,2},{9,3},... | collective-permute-start | bytes 196616 | tf_op jit(solution)/shard_map/ppermute | solution.py:297
  55.4 1.1 %shard_map.102.refs_9_ = f32[256,1024]{1,0:T(8,128)S(1)} custom-call(bf16[256,1024]{1,0:T(8,128)(2,1)S(1)} %get-tuple-element.53.grad, bf16[1536,1024]{1,0:T(8,128)(2,1)S(1)} %get-tuple-element.55.terms, bf16[1792,256]{1,0:T(8,128)(2,1)S(1)} %get-tuple-element.34.wk, s32[8,256]{1,0:T(8,128)S(1)} %get-tuple-element.54.sources, bf16[256,1024]{1,0:T(8,128)(2,1)S(1)} %copy-done), custom_call_target="tpu_custom_call" | custom-call | flops 1073741824 | bytes 8388608 | tf_op jit(solution)/shard_map/pallas_call | solution.py:41
  56.5 1.5 %collective-permute-done.12.refs_6_ = bf16[64,512]{1,0:T(8,128)(2,1)S(1)} collective-permute-done((bf16[64,512]{1,0:T(8,128)(2,1)S(1)}, bf16[64,512]{1,0:T(8,128)(2,1)S(1)}, u32[]{:S(2)}, u32[]{:S(2)}) %collective-permute-start.12) | collective-permute-done | bytes 65568 | tf_op jit(solution)/shard_map/ppermute | solution.py:297
  58.1 4.6 %collective-permute-done.13.refs_7_ = bf16[64,512]{1,0:T(8,128)(2,1)S(1)} collective-permute-done((bf16[64,512]{1,0:T(8,128)(2,1)S(1)}, bf16[64,512]{1,0:T(8,128)(2,1)S(1)}, u32[]{:S(2)}, u32[]{:S(2)}) %collective-permute-start.13) | collective-permute-done | bytes 65568 | tf_op jit(solution)/shard_map/ppermute | solution.py:297
  62.7 1.2 %shard_map.103 = (f32[64,1024]{1,0:T(8,128)}, f32[7,16,16]{2,1,0:T(8,128)}, bf16[256,1024]{1,0:T(8,128)(2,1)}) custom-call(f32[64,512]{1,0:T(8,128)S(1)} %get-tuple-element.44.refs_0_, bf16[80,512]{1,0:T(8,128)(2,1)S(1)} %collective-permute-done.8.refs_1_, bf16[80,512]{1,0:T(8,128)(2,1)S(1)} %collective-permute-done.9.refs_2_, ...), custom_call_target="tpu_custom_call" | custom-call | flops 1048576 | bytes 8388608 | tf_op jit(solution)/shard_map/pallas_call | solution.py:41
  (29 shorter events, 0.2 us)
Async XLA Ops:
  0.6 14.4 %copy-start = (bf16[256,1024]{1,0:T(8,128)(2,1)S(1)}, bf16[256,1024]{1,0:T(8,128)(2,1)}, u32[]{:S(2)}) copy-start(bf16[256,1024]{1,0:T(8,128)(2,1)} %cot.5) | copy-start | bytes 1572868
  0.6 14.4 %copy-start.1 = (bf16[1024,1024]{1,0:T(8,128)(2,1)S(1)}, bf16[1024,1024]{1,0:T(8,128)(2,1)}, u32[]{:S(2)}) copy-start(bf16[1024,1024]{1,0:T(8,128)(2,1)} %mix.1) | copy-start | bytes 6291460
  0.7 15.2 %collective-permute-start = (bf16[256,1024]{1,0:T(8,128)(2,1)}, bf16[256,1024]{1,0:T(8,128)(2,1)}, u32[]{:S(2)}, u32[]{:S(2)}) collective-permute-start(bf16[256,1024]{1,0:T(8,128)(2,1)} %x.3), channel_id=1, source_target_pairs={{0,15},{1,2},{2,1},{3,4},{4,3},{5,6},{6,5},{7,8},{8,7},{9,10},{10,... | collective-permute-start | bytes 1572872 | tf_op jit(solution)/shard_map/ppermute | solution.py:294
  6.2 9.7 %collective-permute-start.1 = (bf16[256,1024]{1,0:T(8,128)(2,1)}, bf16[256,1024]{1,0:T(8,128)(2,1)}, u32[]{:S(2)}, u32[]{:S(2)}) collective-permute-start(bf16[256,1024]{1,0:T(8,128)(2,1)} %x.3), channel_id=1, source_target_pairs={{0,1},{1,0},{2,3},{3,2},{4,5},{5,4},{6,7},{7,6},{8,9},{9,8},{10,11... | collective-permute-start | bytes 1572872 | tf_op jit(solution)/shard_map/ppermute | solution.py:290
  6.2 24.5 %collective-permute-start.3 = (bf16[256,1024]{1,0:T(8,128)(2,1)}, bf16[256,1024]{1,0:T(8,128)(2,1)S(1)}, u32[]{:S(2)}, u32[]{:S(2)}) collective-permute-start(bf16[256,1024]{1,0:T(8,128)(2,1)} %cot.5), channel_id=1, source_target_pairs={{0,1},{1,0},{2,3},{3,2},{4,5},{5,4},{6,7},{7,6},{8,9},{9,8},{10,11... | collective-permute-start | bytes 1572872 | tf_op jit(solution)/shard_map/ppermute | solution.py:297
  6.8 1.0 %copy-start.2 = (bf16[256,1024]{1,0:T(8,128)(2,1)S(1)}, bf16[256,1024]{1,0:T(8,128)(2,1)}, u32[]{:S(2)}) copy-start(bf16[256,1024]{1,0:T(8,128)(2,1)} %x.3) | copy-start | bytes 1572868
  7.8 0.7 %copy-start.4 = (bf16[7,16,16]{2,1,0:T(8,128)(2,1)S(1)}, bf16[7,16,16]{2,1,0:T(8,128)(2,1)}, u32[]{:S(2)}) copy-start(bf16[7,16,16]{2,1,0:T(8,128)(2,1)} %conv_hbm.1) | copy-start | bytes 10756
  8.6 0.7 %copy-start.5 = (s32[256,7]{0,1:T(8,128)S(1)}, s32[256,7]{0,1:T(8,128)}, u32[]{:S(2)}) copy-start(s32[256,7]{0,1:T(8,128)} %param.11) | copy-start | bytes 21508
  9.3 0.7 %copy-start.6 = (s32[256]{0:T(256)S(1)}, s32[256]{0:T(256)}, u32[]{:S(2)}) copy-start(s32[256]{0:T(256)} %param.12) | copy-start | bytes 3076
  9.9 0.7 %copy-start.7 = (s32[256]{0:T(256)S(1)}, s32[256]{0:T(256)}, u32[]{:S(2)}) copy-start(s32[256]{0:T(256)} %param.13) | copy-start | bytes 3076
  14.2 1.7 %copy-start.3 = (bf16[256,1024]{1,0:T(8,128)(2,1)S(1)}, bf16[256,1024]{1,0:T(8,128)(2,1)}, u32[]{:S(2)}) copy-start(bf16[256,1024]{1,0:T(8,128)(2,1)} %x.3) | copy-start | bytes 1572868
  20.2 10.5 %collective-permute-start.2 = (bf16[512,256]{1,0:T(8,128)(2,1)S(1)}, bf16[512,256]{1,0:T(8,128)(2,1)S(1)}, u32[]{:S(2)}, u32[]{:S(2)}) collective-permute-start(bf16[512,256]{1,0:T(8,128)(2,1)S(1)} %get-tuple-element.36), channel_id=1, source_target_pairs={{0,1},{1,0},{2,3},{3,2},{4,5},{5,4},{6,7},{7,6},{8,9},{9,8},{10,11... | collective-permute-start | bytes 786440 | tf_op jit(solution)/shard_map/ppermute | solution.py:297
  25.8 25.2 %collective-permute-start.14 = (bf16[256,1024]{1,0:T(8,128)(2,1)S(1)}, bf16[256,1024]{1,0:T(8,128)(2,1)S(1)}, u32[]{:S(2)}, u32[]{:S(2)}) collective-permute-start(bf16[256,1024]{1,0:T(8,128)(2,1)S(1)} %get-tuple-element.56), channel_id=1, source_target_pairs={{0,15},{1,2},{2,1},{3,4},{4,3},{5,6},{6,5},{7,8},{8,7},{9,10},{10,... | collective-permute-start | bytes 1572872 | tf_op jit(solution)/shard_map/ppermute | solution.py:294
  30.6 23.2 %collective-permute-start.15 = (bf16[256,1024]{1,0:T(8,128)(2,1)S(1)}, bf16[256,1024]{1,0:T(8,128)(2,1)S(1)}, u32[]{:S(2)}, u32[]{:S(2)}) collective-permute-start(bf16[256,1024]{1,0:T(8,128)(2,1)S(1)} %get-tuple-element.57), channel_id=1, source_target_pairs={{0,1},{1,0},{2,3},{3,2},{4,5},{5,4},{6,7},{7,6},{8,9},{9,8},{10,11... | collective-permute-start | bytes 1572872 | tf_op jit(solution)/shard_map/ppermute | solution.py:290
  31.9 14.2 %collective-permute-start.4 = (bf16[256,512]{1,0:T(8,128)(2,1)S(1)}, bf16[256,512]{1,0:T(8,128)(2,1)S(1)}, u32[]{:S(2)}, u32[]{:S(2)}) collective-permute-start(bf16[256,512]{1,0:T(8,128)(2,1)S(1)} %get-tuple-element.38), channel_id=1, source_target_pairs={{0,2},{1,3},{2,0},{3,1},{4,6},{5,7},{6,4},{7,5},{8,10},{9,11},{10,... | collective-permute-start | bytes 786440 | tf_op jit(solution)/shard_map/ppermute | solution.py:297
  32.0 14.1 %collective-permute-start.5 = (bf16[256,512]{1,0:T(8,128)(2,1)S(1)}, bf16[256,512]{1,0:T(8,128)(2,1)S(1)}, u32[]{:S(2)}, u32[]{:S(2)}) collective-permute-start(bf16[256,512]{1,0:T(8,128)(2,1)S(1)} %get-tuple-element.40), channel_id=1, source_target_pairs={{0,4},{1,5},{2,6},{3,7},{4,0},{5,1},{6,2},{7,3},{8,12},{9,13},{10,... | collective-permute-start | bytes 786440 | tf_op jit(solution)/shard_map/ppermute | solution.py:297
  32.1 1.4 %collective-permute-start.6 = (f32[16,128]{1,0:T(8,128)S(1)}, f32[16,128]{1,0:T(8,128)S(1)}, u32[]{:S(2)}, u32[]{:S(2)}) collective-permute-start(f32[16,128]{1,0:T(8,128)S(1)} %get-tuple-element.43), channel_id=1, source_target_pairs={{0,1},{1,0},{2,3},{3,2},{4,5},{5,4},{6,7},{7,6},{8,9},{9,8},{10,11... | collective-permute-start | bytes 24584 | tf_op jit(solution)/shard_map/ppermute | solution.py:297
  33.5 12.6 %collective-permute-start.7 = (f32[16,128]{1,0:T(8,128)S(1)}, f32[16,128]{1,0:T(8,128)S(1)}, u32[]{:S(2)}, u32[]{:S(2)}) collective-permute-start(f32[16,128]{1,0:T(8,128)S(1)} %add.3.refs_4_), channel_id=1, source_target_pairs={{0,2},{1,3},{2,0},{3,1},{4,6},{5,7},{6,4},{7,5},{8,10},{9,11},{10,... | collective-permute-start | bytes 24584 | tf_op jit(solution)/shard_map/ppermute | solution.py:297
  46.8 7.1 %collective-permute-start.11 = (bf16[64,512]{1,0:T(8,128)(2,1)S(1)}, bf16[64,512]{1,0:T(8,128)(2,1)S(1)}, u32[]{:S(2)}, u32[]{:S(2)}) collective-permute-start(bf16[64,512]{1,0:T(8,128)(2,1)S(1)} %get-tuple-element.49), channel_id=1, source_target_pairs={{0,8},{1,9},{2,10},{3,11},{4,12},{5,13},{6,14},{7,15},{8,0},{9,1},... | collective-permute-start | bytes 196616 | tf_op jit(solution)/shard_map/ppermute | solution.py:297
  49.4 13.2 %collective-permute-start.10 = (bf16[80,512]{1,0:T(8,128)(2,1)S(1)}, bf16[80,512]{1,0:T(8,128)(2,1)S(1)}, u32[]{:S(2)}, u32[]{:S(2)}) collective-permute-start(bf16[80,512]{1,0:T(8,128)(2,1)S(1)} %get-tuple-element.47), channel_id=1, source_target_pairs={{0,12},{1,13},{2,14},{3,15},{4,8},{5,9},{6,10},{7,11},{8,4},{9,5},... | collective-permute-start | bytes 245768 | tf_op jit(solution)/shard_map/ppermute | solution.py:297
  50.8 11.9 %collective-permute-start.8 = (bf16[80,512]{1,0:T(8,128)(2,1)S(1)}, bf16[80,512]{1,0:T(8,128)(2,1)S(1)}, u32[]{:S(2)}, u32[]{:S(2)}) collective-permute-start(bf16[80,512]{1,0:T(8,128)(2,1)S(1)} %get-tuple-element.45), channel_id=1, source_target_pairs={{0,4},{1,5},{2,6},{3,7},{4,0},{5,1},{6,2},{7,3},{8,12},{9,13},{10,... | collective-permute-start | bytes 245768 | tf_op jit(solution)/shard_map/ppermute | solution.py:297
  51.0 11.7 %collective-permute-start.9 = (bf16[80,512]{1,0:T(8,128)(2,1)S(1)}, bf16[80,512]{1,0:T(8,128)(2,1)S(1)}, u32[]{:S(2)}, u32[]{:S(2)}) collective-permute-start(bf16[80,512]{1,0:T(8,128)(2,1)S(1)} %get-tuple-element.46), channel_id=1, source_target_pairs={{0,8},{1,9},{2,10},{3,11},{4,12},{5,13},{6,14},{7,15},{8,0},{9,1},... | collective-permute-start | bytes 245768 | tf_op jit(solution)/shard_map/ppermute | solution.py:297
  53.8 4.3 %collective-permute-start.12 = (bf16[64,512]{1,0:T(8,128)(2,1)S(1)}, bf16[64,512]{1,0:T(8,128)(2,1)S(1)}, u32[]{:S(2)}, u32[]{:S(2)}) collective-permute-start(bf16[64,512]{1,0:T(8,128)(2,1)S(1)} %get-tuple-element.50), channel_id=1, source_target_pairs={{0,2},{1,3},{2,0},{3,1},{4,6},{5,7},{6,4},{7,5},{8,10},{9,11},{10,... | collective-permute-start | bytes 196616 | tf_op jit(solution)/shard_map/ppermute | solution.py:297
  53.8 8.8 %collective-permute-start.13 = (bf16[64,512]{1,0:T(8,128)(2,1)S(1)}, bf16[64,512]{1,0:T(8,128)(2,1)S(1)}, u32[]{:S(2)}, u32[]{:S(2)}) collective-permute-start(bf16[64,512]{1,0:T(8,128)(2,1)S(1)} %get-tuple-element.51), channel_id=1, source_target_pairs={{0,10},{1,11},{2,8},{3,9},{4,14},{5,15},{6,12},{7,13},{8,2},{9,3},... | collective-permute-start | bytes 196616 | tf_op jit(solution)/shard_map/ppermute | solution.py:297

commit v9 on v8

--- a/solution.py
+++ b/solution.py
@@ -218,60 +218,60 @@
     return (conv[...] + one) + (two + three)
 
 
-def quarter(share, bits, skips, kept, gots, got_at, sends, send_at, keep):
+def quarter(share, bits, skips, kept, gots, sends, keep):
     (lo, hi), (bit_lo, bit_hi) = skips, bits
     small, large = min(lo, hi), max(lo, hi)
     for q in range(kept.shape[0] // share // 4):
         base = ((q >> small) << (small + 1)) | (q & ((1 << small) - 1))
         base = ((base >> large) << (large + 1)) | (base & ((1 << large) - 1))
         for delta in range(4):
-            out, out_at = (keep, 0) if delta == 0 else (sends[delta - 1], send_at)
+            out, out_at = (keep, 0) if delta == 0 else sends[delta - 1]
             want_lo = 1 - bit_lo if delta & 1 else bit_lo
             want_hi = 1 - bit_hi if delta & 2 else bit_hi
             at = pl.multiple_of((base + (want_lo << lo) + (want_hi << hi)) * share, share)
             value = kept[pl.ds(at, share), :]
-            for got in gots:
+            for got, got_at in gots:
                 value += got[pl.ds(pl.multiple_of(at + got_at, 16), share), :].astype(f32)
             out[out_at + q * share : out_at + (q + 1) * share, :] = value.astype(out.dtype)
 
 
-def quad_kernel(share, where, came, me, *refs):
-    first = came == 1
-    kept_a, gots_a, kept_b, gots_b = refs[0], refs[1 : 1 + came], refs[1 + came], refs[2 + came : 2 + 2 * came]
-    rest = refs[2 + 2 * came :]
+def quad_kernel(share, where, first, me, *refs):
     if first:
-        whole = rest[0][...] + rest[1][...]
-        rest = rest[2:]
+        kept_a, got_a, kept_b, got_b, conv, conv_got, *outs = refs
+        gots_a, gots_b = [(got_a, 0)], [(got_b, 0)]
+        whole = conv[...] + conv_got[...]
     else:
-        whole = conv_sum(rest[0], gots_a)
-        rest = rest[1:]
-    sends_a, keep_a, sends_b, keep_b, conv_out = rest[:3], rest[3], rest[4:7], rest[7], rest[8]
+        kept_a, one, shared, three, kept_b, two_b, three_b, conv, *outs = refs
+        gots_a = [(one, 16), (shared, 16), (three, 16)]
+        gots_b = [(shared, 16 + kept_b.shape[0]), (two_b, 0), (three_b, 0)]
+        whole = conv_sum(conv, (one, shared, three))
+    send_one, send_shared, send_three, keep_a, send_two_b, send_three_b, keep_b, conv_out = outs
     high = whole.astype(bf16)
     low = (whole - high.astype(f32)).astype(bf16)
     conv_out[...] = high.astype(f32) + low.astype(f32)
-    for send in sends_a:
+    for send in (send_one, send_shared, send_three):
         send[:16, :] = jnp.zeros((16, send.shape[1]), bf16)
         send[:16, :128] = high
         send[:16, 128:256] = low
     (bits_a, skips_a), (bits_b, skips_b) = where
     chosen = lambda bits: (me[bits[0]], me[bits[1]])
-    quarter(share, chosen(bits_a), skips_a, kept_a, gots_a, 0 if first else 16, sends_a, 16, keep_a)
-    quarter(share, chosen(bits_b), skips_b, kept_b, gots_b, 0, sends_b, 0, keep_b)
-
-
-def last_kernel(scale, channels, *refs):
-    kept_a, gots_a, kept_b, gots_b = refs[0], refs[1:4], refs[4], refs[5:8]
-    conv, inner, first, second, mix_out, conv_out, grad_out = refs[8:]
-    half = kept_a.shape[1]
+    sends_a = [(send_one, 16), (send_shared, 16), (send_three, 16)]
+    sends_b = [(send_shared, 16 + keep_b.shape[0]), (send_two_b, 0), (send_three_b, 0)]
+    quarter(share, chosen(bits_a), skips_a, kept_a, gots_a, sends_a, keep_a)
+    quarter(share, chosen(bits_b), skips_b, kept_b, gots_b, sends_b, keep_b)
+
+
+def last_kernel(scale, channels, kept_a, one, shared, three, kept_b, two_b, three_b, conv, inner, first, second, mix_out, conv_out, grad_out):
+    rows, half = kept_a.shape
     total = kept_a[...]
-    for got in gots_a:
-        total += got[16:, :].astype(f32)
+    for got in (one, shared, three):
+        total += got[16 : 16 + rows, :].astype(f32)
     mix_out[:, :half] = total * scale
-    total = kept_b[...]
-    for got in gots_b:
+    total = kept_b[...] + shared[16 + rows :, :].astype(f32)
+    for got in (two_b, three_b):
         total += got[...].astype(f32)
     mix_out[:, half:] = total * scale
-    whole = conv_sum(conv, gots_a)
+    whole = conv_sum(conv, (one, shared, three))
     for tap in range(conv_out.shape[0]):
         conv_out[tap] = whole[:, tap * channels : (tap + 1) * channels]
     grad_out[...] = (inner[...] + first[...].astype(f32) + second[...].astype(f32)).astype(bf16)
@@ -391,33 +391,36 @@
     conv_got = swap(conv, 1)
     from_far = far_swap(to_far)
     from_near = near_swap(to_near)
+    state = [kept[0], *gots[0], kept[1], *gots[1], conv, conv_got]
     for stage in range(1, bits - 1, 2):
         rows_left //= 4
         pair = [order[stage : stage + 2] for order in orders]
         where = tuple((tuple(p), tuple(position(k, b) for b in p)) for k, p in enumerate(pair))
-        outs = call(
-            functools.partial(quad_kernel, share, where, len(gots[0])),
-            [((rows_left + 16, half), bf16)] * 3
-            + [((rows_left, half), f32)]
-            + [((rows_left, half), bf16)] * 3
-            + [((rows_left, half), f32), ((channels, 128), f32)],
+        one, shared, three, keep_a, two_b, three_b, keep_b, conv = call(
+            functools.partial(quad_kernel, share, where, stage == 1),
+            [
+                ((rows_left + 16, half), bf16),
+                ((2 * rows_left + 16, half), bf16),
+                ((rows_left + 16, half), bf16),
+                ((rows_left, half), f32),
+                ((rows_left, half), bf16),
+                ((rows_left, half), bf16),
+                ((rows_left, half), f32),
+                ((channels, 128), f32),
+            ],
             1 << 20,
             mine,
-            kept[0],
-            *gots[0],
-            kept[1],
-            *gots[1],
-            conv,
-            *([conv_got] if stage == 1 else []),
+            *state,
             scalars=1,
         )
-        kept, conv = [outs[3], outs[7]], outs[8]
-        gots = []
+        (a_lo, both_bit), (_, b_hi) = pair
+        shared = swap(shared, both_bit)
+        three = swap_by(three, 1 << a_lo | 1 << both_bit)
+        three_b = swap_by(three_b, 1 << both_bit | 1 << b_hi)
+        two_b = swap(two_b, b_hi)
+        one = swap(one, a_lo)
+        state = [keep_a, one, shared, three, keep_b, two_b, three_b, conv]
         for k in (0, 1):
-            came = []
-            for delta in (1, 2, 3):
-                came.append(swap_by(outs[4 * k + delta - 1], ((delta & 1) << pair[k][0]) | ((delta >> 1) << pair[k][1])))
-            gots.append(came)
             drop(k, *pair[k])
     (inner,) = call(
         inner_kernel, [((n, width), f32)], 1 << 30, grad, terms, wk, sources, cotangent
@@ -426,11 +429,7 @@
         functools.partial(last_kernel, 1.0 / float(total_cols) ** 0.5, channels),
         [((share, width), f32), ((taps, channels, channels), f32), ((n, width), bf16)],
         1 << 20,
-        kept[0],
-        *gots[0],
-        kept[1],
-        *gots[1],
-        conv,
+        *state,
         inner,
         from_far,
         from_near,

time: 64.2 us -> 63.8 us (level)
    ppermute x12 -> x11, waiting for transfers between devices: 17.9 us -> 17.5 us  [swap_by(): return lax.ppermute(value, 'space', [(i, i ^ mask) for i in range(devices)])]
    ppermute x12 -> x11, starting transfers between devices: 12.4 us -> 12.3 us  [swap_by(): return lax.ppermute(value, 'space', [(i, i ^ mask) for i in range(devices)])]
  transfers between devices with their start and end apart: 16 -> 15, of which waited for: 4 -> 3; matrix products, arithmetic and copies ran while one was open for 0% -> 0% of each run, Pallas kernels for 27% -> 27%
where the time goes in v9:
time: 63.8 us; the launch traced here: 63.4 us
  starting transfers between devices  22.7 us (36%)
  Pallas kernels  18.4 us (29%)
  waiting for transfers between devices  17.5 us (27%)
  local copies, waits for them, and re-layouts  3.86 us (6%)
  between operations  0.78 us (1%)
    pallas_call x10, Pallas kernels, call(): pl.pallas_call(body, out_shape=[jax.ShapeDtypeStruct(s, d) for s, d in ou...  18.4 us
    ppermute x11, waiting for transfers between devices, swap_by(): return lax.ppermute(value, 'space', [(i, i ^ mask) for i in range(devices)])  17.5 us
    ppermute x11, starting transfers between devices, swap_by(): return lax.ppermute(value, 'space', [(i, i ^ mask) for i in range(devices)])  12.3 us
    ppermute x2, starting transfers between devices, far_swap(): return lax.ppermute(value, 'space', [(i, other(i)) for i in range(devices)])  10.4 us
    unnamed x16, local copies, waits for them, and re-layouts  3.86 us
  transfers between devices with their start and end apart: 15, of which 3 were waited for; matrix products, arithmetic and copies ran while one was open for 0% of the time, Pallas kernels for 27%

profile of v9, /device:TPU:0, one launch (start us, length us, event | category | flops | bytes accessed | tf_op | source)
XLA Modules:
  0.0 63.4 jit_solution(16467228444571143814)
XLA Ops:
  0.7 5.5 %collective-permute-start = (bf16[256,1024]{1,0:T(8,128)(2,1)}, bf16[256,1024]{1,0:T(8,128)(2,1)}, u32[]{:S(2)}, u32[]{:S(2)}) collective-permute-start(bf16[256,1024]{1,0:T(8,128)(2,1)} %x.3), channel_id=1, source_target_pairs={{0,15},{1,2},{2,1},{3,4},{4,3},{5,6},{6,5},{7,8},{8,7},{9,10},{10,... | collective-permute-start | bytes 1572872 | tf_op jit(solution)/shard_map/ppermute | solution.py:294
  6.2 0.5 collective-permute-start.3
  6.7 0.1 pad_add_fusion.1.place
  6.8 1.0 %copy-done.2 = bf16[256,1024]{1,0:T(8,128)(2,1)S(1)} copy-done((bf16[256,1024]{1,0:T(8,128)(2,1)S(1)}, bf16[256,1024]{1,0:T(8,128)(2,1)}, u32[]{:S(2)}) %copy-start.2) | copy-done | bytes 524312
  7.8 0.7 %copy-done.4 = bf16[7,16,16]{2,1,0:T(8,128)(2,1)S(1)} copy-done((bf16[7,16,16]{2,1,0:T(8,128)(2,1)S(1)}, bf16[7,16,16]{2,1,0:T(8,128)(2,1)}, u32[]{:S(2)}) %copy-start.4) | copy-done | bytes 3608
  8.6 0.7 %copy-done.5 = s32[256,7]{0,1:T(8,128)S(1)} copy-done((s32[256,7]{0,1:T(8,128)S(1)}, s32[256,7]{0,1:T(8,128)}, u32[]{:S(2)}) %copy-start.5) | copy-done | bytes 7192
  9.3 0.7 %copy-done.6 = s32[256]{0:T(256)S(1)} copy-done((s32[256]{0:T(256)S(1)}, s32[256]{0:T(256)}, u32[]{:S(2)}) %copy-start.6) | copy-done | bytes 1048
  9.9 0.7 %copy-done.7 = s32[256]{0:T(256)S(1)} copy-done((s32[256]{0:T(256)S(1)}, s32[256]{0:T(256)}, u32[]{:S(2)}) %copy-start.7) | copy-done | bytes 1048
  10.6 3.5 %shard_map.94 = (bf16[1536,512]{1,0:T(8,128)(2,1)S(1)}, s32[8,256]{1,0:T(8,128)S(1)}, bf16[1536,1024]{1,0:T(8,128)(2,1)S(1)}, bf16[1792,256]{1,0:T(8,128)(2,1)S(1)}) custom-call(s32[4]{0:T(128)S(1)} %pad_add_fusion.1.place, s32[7,256]{1,0:T(8,128)S(1)} %bitcast.10, s32[1,256]{1,0:T(1,128)S(1)} %bitcast.11, s32[1,256]{1,0:T(1,128)S(1)} %bitcast.12, ...), custom_call_target="tpu_custom_call" | custom-call | flops 1073741824 | bytes 8388608 | tf_op jit(solution)/shard_map/pallas_call | solution.py:41
  14.2 0.8 %shard_map.100.back_sel = bf16[512,1536]{1,0:T(8,128)(2,1)S(1)} custom-call(s32[4]{0:T(128)S(1)} %pad_add_fusion.1.place, s32[8,256]{1,0:T(8,128)S(1)} %get-tuple-element.52.sources), custom_call_target="tpu_custom_call" | custom-call | flops 67108864 | bytes 8388608 | tf_op jit(solution)/shard_map/pallas_call | solution.py:41
  15.0 0.7 %shard_map.97.up = f32[256,1024]{1,0:T(8,128)S(1)} custom-call(bf16[256,1024]{1,0:T(8,128)(2,1)S(1)} %copy-done, bf16[1024,1024]{1,0:T(8,128)(2,1)S(1)} %copy-done.1), custom_call_target="tpu_custom_call" | custom-call | flops 536870912 | bytes 8388608 | tf_op jit(solution)/shard_map/pallas_call | solution.py:41
  15.8 0.1 pad_add_fusion.me
  15.8 4.3 %shard_map.95 = (bf16[1536,1024]{1,0:T(8,128)(2,1)S(1)}, f32[256,1024]{1,0:T(8,128)S(1)}, bf16[512,256]{1,0:T(8,128)(2,1)S(1)}, bf16[512,256]{1,0:T(8,128)(2,1)S(1)}) custom-call(s32[4]{0:T(128)S(1)} %pad_add_fusion.me, bf16[256,1024]{1,0:T(8,128)(2,1)} %collective-permute-done.far, bf16[256,1024]{1,0:T(8,128)(2,1)} %collective-permute-done.1.near, ...), custom_call_target="tpu_custom_call" | custom-call | flops 3221225472 | bytes 8388608 | tf_op jit(solution)/shard_map/pallas_call | solution.py:41
  20.2 0.8 %collective-permute-start.2 = (bf16[512,256]{1,0:T(8,128)(2,1)S(1)}, bf16[512,256]{1,0:T(8,128)(2,1)S(1)}, u32[]{:S(2)}, u32[]{:S(2)}) collective-permute-start(bf16[512,256]{1,0:T(8,128)(2,1)S(1)} %get-tuple-element.35), channel_id=1, source_target_pairs={{0,1},{1,0},{2,3},{3,2},{4,5},{5,4},{6,7},{7,6},{8,9},{9,8},{10,11... | collective-permute-start | bytes 786440 | tf_op jit(solution)/shard_map/ppermute | solution.py:297
  21.0 2.0 %shard_map.98 = (bf16[256,1024]{1,0:T(8,128)(2,1)S(1)}, f32[16,128]{1,0:T(8,128)S(1)}) custom-call(f32[256,1024]{1,0:T(8,128)S(1)} %shard_map.97.up, f32[256,1024]{1,0:T(8,128)S(1)} %get-tuple-element.40.pre, bf16[256,1024]{1,0:T(8,128)(2,1)S(1)} %copy-done.3, bf16[1536,1024]{1,0:T(8,128)(2,1)S(1)} %get-tuple-element.41.rows), custom_call_target="tpu_custom_call" | custom-call | flops 2147483648 | bytes 8388608 | tf_op jit(solution)/shard_map/pallas_call | solution.py:41
  23.1 2.7 %shard_map.101 = (bf16[1536,1024]{1,0:T(8,128)(2,1)S(1)}, bf16[256,1024]{1,0:T(8,128)(2,1)S(1)}, bf16[256,1024]{1,0:T(8,128)(2,1)S(1)}) custom-call(bf16[256,1024]{1,0:T(8,128)(2,1)S(1)} %get-tuple-element.51.grad, bf16[1792,256]{1,0:T(8,128)(2,1)S(1)} %get-tuple-element.33.wk, bf16[512,1536]{1,0:T(8,128)(2,1)S(1)} %shard_map.100.back_sel), custom_call_target="tpu_custom_call" | custom-call | flops 3221225472 | bytes 8388608 | tf_op jit(solution)/shard_map/pallas_call | solution.py:41
  25.8 4.8 %collective-permute-start.13 = (bf16[256,1024]{1,0:T(8,128)(2,1)S(1)}, bf16[256,1024]{1,0:T(8,128)(2,1)S(1)}, u32[]{:S(2)}, u32[]{:S(2)}) collective-permute-start(bf16[256,1024]{1,0:T(8,128)(2,1)S(1)} %get-tuple-element.54), channel_id=1, source_target_pairs={{0,15},{1,2},{2,1},{3,4},{4,3},{5,6},{6,5},{7,8},{8,7},{9,10},{10,... | collective-permute-start | bytes 1572872 | tf_op jit(solution)/shard_map/ppermute | solution.py:294
  30.7 1.3 %shard_map.96 = (bf16[256,512]{1,0:T(8,128)(2,1)S(1)}, f32[256,512]{1,0:T(8,128)S(1)}, bf16[256,512]{1,0:T(8,128)(2,1)S(1)}, f32[256,512]{1,0:T(8,128)S(1)}) custom-call(s32[4]{0:T(128)S(1)} %pad_add_fusion.me, bf16[512,256]{1,0:T(8,128)(2,1)S(1)} %get-tuple-element.34.act, bf16[512,256]{1,0:T(8,128)(2,1)S(1)} %collective-permute-done.2.act_got, ...), custom_call_target="tpu_custom_call" | custom-call | flops 1073741824 | bytes 8388608 | tf_op jit(solution)/shard_map/pallas_call | solution.py:41
  31.9 0.1 collective-permute-start.4
  32.0 0.1 collective-permute-start.5
  32.1 0.6 collective-permute-start.6
  32.6 0.8 %collective-permute-done.6 = f32[16,128]{1,0:T(8,128)S(1)} collective-permute-done((f32[16,128]{1,0:T(8,128)S(1)}, f32[16,128]{1,0:T(8,128)S(1)}, u32[]{:S(2)}, u32[]{:S(2)}) %collective-permute-start.6) | collective-permute-done | bytes 8224 | tf_op jit(solution)/shard_map/ppermute | solution.py:297
  33.5 1.7 %collective-permute-start.7 = (f32[16,128]{1,0:T(8,128)S(1)}, f32[16,128]{1,0:T(8,128)S(1)}, u32[]{:S(2)}, u32[]{:S(2)}) collective-permute-start(f32[16,128]{1,0:T(8,128)S(1)} %add.3.refs_4_), channel_id=1, source_target_pairs={{0,2},{1,3},{2,0},{3,1},{4,6},{5,7},{6,4},{7,5},{8,10},{9,11},{10,... | collective-permute-start | bytes 24584 | tf_op jit(solution)/shard_map/ppermute | solution.py:297
  35.2 10.9 %collective-permute-done.7.refs_5_ = f32[16,128]{1,0:T(8,128)S(1)} collective-permute-done((f32[16,128]{1,0:T(8,128)S(1)}, f32[16,128]{1,0:T(8,128)S(1)}, u32[]{:S(2)}, u32[]{:S(2)}) %collective-permute-start.7) | collective-permute-done | bytes 8224 | tf_op jit(solution)/shard_map/ppermute | solution.py:297
  46.1 0.6 %shard_map.99 = (bf16[80,512]{1,0:T(8,128)(2,1)S(1)}, bf16[144,512]{1,0:T(8,128)(2,1)S(1)}, bf16[80,512]{1,0:T(8,128)(2,1)S(1)}, f32[64,512]{1,0:T(8,128)S(1)}, ...) custom-call(s32[4]{0:T(128)S(1)} %pad_add_fusion.me, ...), custom_call_target="tpu_custom_call" | custom-call | flops 1048576 | bytes 8388608 | tf_op jit(solution)/shard_map/pallas_call | solution.py:41
  46.8 2.7 %collective-permute-start.9 = (bf16[144,512]{1,0:T(8,128)(2,1)S(1)}, bf16[144,512]{1,0:T(8,128)(2,1)S(1)}, u32[]{:S(2)}, u32[]{:S(2)}) collective-permute-start(bf16[144,512]{1,0:T(8,128)(2,1)S(1)} %get-tuple-element.45), channel_id=1, source_target_pairs={{0,8},{1,9},{2,10},{3,11},{4,12},{5,13},{6,14},{7,15},{8,0},{9,1},... | collective-permute-start | bytes 442376 | tf_op jit(solution)/shard_map/ppermute | solution.py:297
  49.4 1.3 %collective-permute-start.10 = (bf16[80,512]{1,0:T(8,128)(2,1)S(1)}, bf16[80,512]{1,0:T(8,128)(2,1)S(1)}, u32[]{:S(2)}, u32[]{:S(2)}) collective-permute-start(bf16[80,512]{1,0:T(8,128)(2,1)S(1)} %get-tuple-element.46), channel_id=1, source_target_pairs={{0,12},{1,13},{2,14},{3,15},{4,8},{5,9},{6,10},{7,11},{8,4},{9,5},... | collective-permute-start | bytes 245768 | tf_op jit(solution)/shard_map/ppermute | solution.py:297
  50.8 0.2 collective-permute-start.8
  51.0 4.3 %collective-permute-start.12 = (bf16[64,512]{1,0:T(8,128)(2,1)S(1)}, bf16[64,512]{1,0:T(8,128)(2,1)S(1)}, u32[]{:S(2)}, u32[]{:S(2)}) collective-permute-start(bf16[64,512]{1,0:T(8,128)(2,1)S(1)} %get-tuple-element.49), channel_id=1, source_target_pairs={{0,10},{1,11},{2,8},{3,9},{4,14},{5,15},{6,12},{7,13},{8,2},{9,3},... | collective-permute-start | bytes 196616 | tf_op jit(solution)/shard_map/ppermute | solution.py:297
  55.3 1.1 %shard_map.102.inner = f32[256,1024]{1,0:T(8,128)S(1)} custom-call(bf16[256,1024]{1,0:T(8,128)(2,1)S(1)} %get-tuple-element.51.grad, bf16[1536,1024]{1,0:T(8,128)(2,1)S(1)} %get-tuple-element.53.terms, bf16[1792,256]{1,0:T(8,128)(2,1)S(1)} %get-tuple-element.33.wk, s32[8,256]{1,0:T(8,128)S(1)} %get-tuple-element.52.sources, bf16[256,1024]{1,0:T(8,128)(2,1)S(1)} %copy-done), custom_call_target="tpu_custom_call" | custom-call | flops 1073741824 | bytes 8388608 | tf_op jit(solution)/shard_map/pallas_call | solution.py:41
  56.4 5.8 %collective-permute-done.12.three_b = bf16[64,512]{1,0:T(8,128)(2,1)S(1)} collective-permute-done((bf16[64,512]{1,0:T(8,128)(2,1)S(1)}, bf16[64,512]{1,0:T(8,128)(2,1)S(1)}, u32[]{:S(2)}, u32[]{:S(2)}) %collective-permute-start.12) | collective-permute-done | bytes 65568 | tf_op jit(solution)/shard_map/ppermute | solution.py:297
  62.2 1.2 %shard_map.103 = (f32[64,1024]{1,0:T(8,128)}, f32[7,16,16]{2,1,0:T(8,128)}, bf16[256,1024]{1,0:T(8,128)(2,1)}) custom-call(f32[64,512]{1,0:T(8,128)S(1)} %get-tuple-element.43.kept_a, bf16[80,512]{1,0:T(8,128)(2,1)S(1)} %collective-permute-done.8.one, bf16[144,512]{1,0:T(8,128)(2,1)S(1)} %collective-permute-done.9.shared, ...), custom_call_target="tpu_custom_call" | custom-call | flops 1048576 | bytes 8388608 | tf_op jit(solution)/shard_map/pallas_call | solution.py:41
  (27 shorter events, 0.1 us)
Async XLA Ops:
  0.6 14.4 %copy-start = (bf16[256,1024]{1,0:T(8,128)(2,1)S(1)}, bf16[256,1024]{1,0:T(8,128)(2,1)}, u32[]{:S(2)}) copy-start(bf16[256,1024]{1,0:T(8,128)(2,1)} %cot.5) | copy-start | bytes 1572868
  0.6 14.4 %copy-start.1 = (bf16[1024,1024]{1,0:T(8,128)(2,1)S(1)}, bf16[1024,1024]{1,0:T(8,128)(2,1)}, u32[]{:S(2)}) copy-start(bf16[1024,1024]{1,0:T(8,128)(2,1)} %mix.1) | copy-start | bytes 6291460
  0.7 15.2 %collective-permute-start = (bf16[256,1024]{1,0:T(8,128)(2,1)}, bf16[256,1024]{1,0:T(8,128)(2,1)}, u32[]{:S(2)}, u32[]{:S(2)}) collective-permute-start(bf16[256,1024]{1,0:T(8,128)(2,1)} %x.3), channel_id=1, source_target_pairs={{0,15},{1,2},{2,1},{3,4},{4,3},{5,6},{6,5},{7,8},{8,7},{9,10},{10,... | collective-permute-start | bytes 1572872 | tf_op jit(solution)/shard_map/ppermute | solution.py:294
  6.2 9.7 %collective-permute-start.1 = (bf16[256,1024]{1,0:T(8,128)(2,1)}, bf16[256,1024]{1,0:T(8,128)(2,1)}, u32[]{:S(2)}, u32[]{:S(2)}) collective-permute-start(bf16[256,1024]{1,0:T(8,128)(2,1)} %x.3), channel_id=1, source_target_pairs={{0,1},{1,0},{2,3},{3,2},{4,5},{5,4},{6,7},{7,6},{8,9},{9,8},{10,11... | collective-permute-start | bytes 1572872 | tf_op jit(solution)/shard_map/ppermute | solution.py:290
  6.2 24.5 %collective-permute-start.3 = (bf16[256,1024]{1,0:T(8,128)(2,1)}, bf16[256,1024]{1,0:T(8,128)(2,1)S(1)}, u32[]{:S(2)}, u32[]{:S(2)}) collective-permute-start(bf16[256,1024]{1,0:T(8,128)(2,1)} %cot.5), channel_id=1, source_target_pairs={{0,1},{1,0},{2,3},{3,2},{4,5},{5,4},{6,7},{7,6},{8,9},{9,8},{10,11... | collective-permute-start | bytes 1572872 | tf_op jit(solution)/shard_map/ppermute | solution.py:297
  6.8 1.0 %copy-start.2 = (bf16[256,1024]{1,0:T(8,128)(2,1)S(1)}, bf16[256,1024]{1,0:T(8,128)(2,1)}, u32[]{:S(2)}) copy-start(bf16[256,1024]{1,0:T(8,128)(2,1)} %x.3) | copy-start | bytes 1572868
  7.8 0.7 %copy-start.4 = (bf16[7,16,16]{2,1,0:T(8,128)(2,1)S(1)}, bf16[7,16,16]{2,1,0:T(8,128)(2,1)}, u32[]{:S(2)}) copy-start(bf16[7,16,16]{2,1,0:T(8,128)(2,1)} %conv_hbm.1) | copy-start | bytes 10756
  8.6 0.7 %copy-start.5 = (s32[256,7]{0,1:T(8,128)S(1)}, s32[256,7]{0,1:T(8,128)}, u32[]{:S(2)}) copy-start(s32[256,7]{0,1:T(8,128)} %param.11) | copy-start | bytes 21508
  9.3 0.7 %copy-start.6 = (s32[256]{0:T(256)S(1)}, s32[256]{0:T(256)}, u32[]{:S(2)}) copy-start(s32[256]{0:T(256)} %param.12) | copy-start | bytes 3076
  9.9 0.7 %copy-start.7 = (s32[256]{0:T(256)S(1)}, s32[256]{0:T(256)}, u32[]{:S(2)}) copy-start(s32[256]{0:T(256)} %param.13) | copy-start | bytes 3076
  14.2 1.7 %copy-start.3 = (bf16[256,1024]{1,0:T(8,128)(2,1)S(1)}, bf16[256,1024]{1,0:T(8,128)(2,1)}, u32[]{:S(2)}) copy-start(bf16[256,1024]{1,0:T(8,128)(2,1)} %x.3) | copy-start | bytes 1572868
  20.2 10.5 %collective-permute-start.2 = (bf16[512,256]{1,0:T(8,128)(2,1)S(1)}, bf16[512,256]{1,0:T(8,128)(2,1)S(1)}, u32[]{:S(2)}, u32[]{:S(2)}) collective-permute-start(bf16[512,256]{1,0:T(8,128)(2,1)S(1)} %get-tuple-element.35), channel_id=1, source_target_pairs={{0,1},{1,0},{2,3},{3,2},{4,5},{5,4},{6,7},{7,6},{8,9},{9,8},{10,11... | collective-permute-start | bytes 786440 | tf_op jit(solution)/shard_map/ppermute | solution.py:297
  25.8 25.2 %collective-permute-start.13 = (bf16[256,1024]{1,0:T(8,128)(2,1)S(1)}, bf16[256,1024]{1,0:T(8,128)(2,1)S(1)}, u32[]{:S(2)}, u32[]{:S(2)}) collective-permute-start(bf16[256,1024]{1,0:T(8,128)(2,1)S(1)} %get-tuple-element.54), channel_id=1, source_target_pairs={{0,15},{1,2},{2,1},{3,4},{4,3},{5,6},{6,5},{7,8},{8,7},{9,10},{10,... | collective-permute-start | bytes 1572872 | tf_op jit(solution)/shard_map/ppermute | solution.py:294
  30.6 20.4 %collective-permute-start.14 = (bf16[256,1024]{1,0:T(8,128)(2,1)S(1)}, bf16[256,1024]{1,0:T(8,128)(2,1)S(1)}, u32[]{:S(2)}, u32[]{:S(2)}) collective-permute-start(bf16[256,1024]{1,0:T(8,128)(2,1)S(1)} %get-tuple-element.55), channel_id=1, source_target_pairs={{0,1},{1,0},{2,3},{3,2},{4,5},{5,4},{6,7},{7,6},{8,9},{9,8},{10,11... | collective-permute-start | bytes 1572872 | tf_op jit(solution)/shard_map/ppermute | solution.py:290
  31.9 14.2 %collective-permute-start.4 = (bf16[256,512]{1,0:T(8,128)(2,1)S(1)}, bf16[256,512]{1,0:T(8,128)(2,1)S(1)}, u32[]{:S(2)}, u32[]{:S(2)}) collective-permute-start(bf16[256,512]{1,0:T(8,128)(2,1)S(1)} %get-tuple-element.37), channel_id=1, source_target_pairs={{0,2},{1,3},{2,0},{3,1},{4,6},{5,7},{6,4},{7,5},{8,10},{9,11},{10,... | collective-permute-start | bytes 786440 | tf_op jit(solution)/shard_map/ppermute | solution.py:297
  32.0 14.1 %collective-permute-start.5 = (bf16[256,512]{1,0:T(8,128)(2,1)S(1)}, bf16[256,512]{1,0:T(8,128)(2,1)S(1)}, u32[]{:S(2)}, u32[]{:S(2)}) collective-permute-start(bf16[256,512]{1,0:T(8,128)(2,1)S(1)} %get-tuple-element.39), channel_id=1, source_target_pairs={{0,4},{1,5},{2,6},{3,7},{4,0},{5,1},{6,2},{7,3},{8,12},{9,13},{10,... | collective-permute-start | bytes 786440 | tf_op jit(solution)/shard_map/ppermute | solution.py:297
  32.1 1.4 %collective-permute-start.6 = (f32[16,128]{1,0:T(8,128)S(1)}, f32[16,128]{1,0:T(8,128)S(1)}, u32[]{:S(2)}, u32[]{:S(2)}) collective-permute-start(f32[16,128]{1,0:T(8,128)S(1)} %get-tuple-element.42), channel_id=1, source_target_pairs={{0,1},{1,0},{2,3},{3,2},{4,5},{5,4},{6,7},{7,6},{8,9},{9,8},{10,11... | collective-permute-start | bytes 24584 | tf_op jit(solution)/shard_map/ppermute | solution.py:297
  33.5 12.6 %collective-permute-start.7 = (f32[16,128]{1,0:T(8,128)S(1)}, f32[16,128]{1,0:T(8,128)S(1)}, u32[]{:S(2)}, u32[]{:S(2)}) collective-permute-start(f32[16,128]{1,0:T(8,128)S(1)} %add.3.refs_4_), channel_id=1, source_target_pairs={{0,2},{1,3},{2,0},{3,1},{4,6},{5,7},{6,4},{7,5},{8,10},{9,11},{10,... | collective-permute-start | bytes 24584 | tf_op jit(solution)/shard_map/ppermute | solution.py:297
  46.8 15.4 %collective-permute-start.9 = (bf16[144,512]{1,0:T(8,128)(2,1)S(1)}, bf16[144,512]{1,0:T(8,128)(2,1)S(1)}, u32[]{:S(2)}, u32[]{:S(2)}) collective-permute-start(bf16[144,512]{1,0:T(8,128)(2,1)S(1)} %get-tuple-element.45), channel_id=1, source_target_pairs={{0,8},{1,9},{2,10},{3,11},{4,12},{5,13},{6,14},{7,15},{8,0},{9,1},... | collective-permute-start | bytes 442376 | tf_op jit(solution)/shard_map/ppermute | solution.py:297
  49.4 12.8 %collective-permute-start.10 = (bf16[80,512]{1,0:T(8,128)(2,1)S(1)}, bf16[80,512]{1,0:T(8,128)(2,1)S(1)}, u32[]{:S(2)}, u32[]{:S(2)}) collective-permute-start(bf16[80,512]{1,0:T(8,128)(2,1)S(1)} %get-tuple-element.46), channel_id=1, source_target_pairs={{0,12},{1,13},{2,14},{3,15},{4,8},{5,9},{6,10},{7,11},{8,4},{9,5},... | collective-permute-start | bytes 245768 | tf_op jit(solution)/shard_map/ppermute | solution.py:297
  50.8 11.4 %collective-permute-start.8 = (bf16[80,512]{1,0:T(8,128)(2,1)S(1)}, bf16[80,512]{1,0:T(8,128)(2,1)S(1)}, u32[]{:S(2)}, u32[]{:S(2)}) collective-permute-start(bf16[80,512]{1,0:T(8,128)(2,1)S(1)} %get-tuple-element.44), channel_id=1, source_target_pairs={{0,4},{1,5},{2,6},{3,7},{4,0},{5,1},{6,2},{7,3},{8,12},{9,13},{10,... | collective-permute-start | bytes 245768 | tf_op jit(solution)/shard_map/ppermute | solution.py:297
  51.0 5.4 %collective-permute-start.11 = (bf16[64,512]{1,0:T(8,128)(2,1)S(1)}, bf16[64,512]{1,0:T(8,128)(2,1)S(1)}, u32[]{:S(2)}, u32[]{:S(2)}) collective-permute-start(bf16[64,512]{1,0:T(8,128)(2,1)S(1)} %get-tuple-element.48), channel_id=1, source_target_pairs={{0,2},{1,3},{2,0},{3,1},{4,6},{5,7},{6,4},{7,5},{8,10},{9,11},{10,... | collective-permute-start | bytes 196616 | tf_op jit(solution)/shard_map/ppermute | solution.py:297
  51.0 11.2 %collective-permute-start.12 = (bf16[64,512]{1,0:T(8,128)(2,1)S(1)}, bf16[64,512]{1,0:T(8,128)(2,1)S(1)}, u32[]{:S(2)}, u32[]{:S(2)}) collective-permute-start(bf16[64,512]{1,0:T(8,128)(2,1)S(1)} %get-tuple-element.49), channel_id=1, source_target_pairs={{0,10},{1,11},{2,8},{3,9},{4,14},{5,15},{6,12},{7,13},{8,2},{9,3},... | collective-permute-start | bytes 196616 | tf_op jit(solution)/shard_map/ppermute | solution.py:297

commit v10 on v9

--- a/solution.py
+++ b/solution.py
@@ -261,7 +261,7 @@
     quarter(share, chosen(bits_b), skips_b, kept_b, gots_b, sends_b, keep_b)
 
 
-def last_kernel(scale, channels, kept_a, one, shared, three, kept_b, two_b, three_b, conv, inner, first, second, mix_out, conv_out, grad_out):
+def last_kernel(scale, channels, kept_a, one, shared, three, kept_b, two_b, three_b, conv, mix_out, conv_out):
     rows, half = kept_a.shape
     total = kept_a[...]
     for got in (one, shared, three):
@@ -274,6 +274,9 @@
     whole = conv_sum(conv, (one, shared, three))
     for tap in range(conv_out.shape[0]):
         conv_out[tap] = whole[:, tap * channels : (tap + 1) * channels]
+
+
+def total_kernel(inner, first, second, grad_out):
     grad_out[...] = (inner[...] + first[...].astype(f32) + second[...].astype(f32)).astype(bf16)
 
 
@@ -425,14 +428,12 @@
     (inner,) = call(
         inner_kernel, [((n, width), f32)], 1 << 30, grad, terms, wk, sources, cotangent
     )
-    grad_mix, grad_conv, grad_input = call(
+    (grad_input,) = call(total_kernel, [((n, width), bf16)], 1 << 20, inner, from_far, from_near)
+    grad_mix, grad_conv = call(
         functools.partial(last_kernel, 1.0 / float(total_cols) ** 0.5, channels),
-        [((share, width), f32), ((taps, channels, channels), f32), ((n, width), bf16)],
+        [((share, width), f32), ((taps, channels, channels), f32)],
         1 << 20,
         *state,
-        inner,
-        from_far,
-        from_near,
     )
     return grad_input, grad_mix, grad_conv
 

time: 63.8 us -> 63.4 us (level)
  starting transfers between devices: 22.7 us -> 21.8 us
    ppermute x11, starting transfers between devices: 12.3 us -> 11.4 us  [swap_by(): return lax.ppermute(value, 'space', [(i, i ^ mask) for i in range(devices)])]
    pallas_call x10 -> x11, Pallas kernels: 18.4 us -> 19 us  [call(): pl.pallas_call(body, out_shape=[jax.ShapeDtypeStruct(s, d) for s, d in ou...]
  transfers between devices with their start and end apart: 15 -> 15, of which waited for: 3 -> 3; matrix products, arithmetic and copies ran while one was open for 0% -> 0% of each run, Pallas kernels for 27% -> 29%
where the time goes in v10:
time: 63.4 us; the launch traced here: 63 us
  starting transfers between devices  21.8 us (34%)
  Pallas kernels  19 us (30%)
  waiting for transfers between devices  17.4 us (27%)
  local copies, waits for them, and re-layouts  3.86 us (6%)
  between operations  0.77 us (1%)
    pallas_call x11, Pallas kernels, call(): pl.pallas_call(body, out_shape=[jax.ShapeDtypeStruct(s, d) for s, d in ou...  19 us
    ppermute x11, waiting for transfers between devices, swap_by(): return lax.ppermute(value, 'space', [(i, i ^ mask) for i in range(devices)])  17.4 us
    ppermute x11, starting transfers between devices, swap_by(): return lax.ppermute(value, 'space', [(i, i ^ mask) for i in range(devices)])  11.4 us
    ppermute x2, starting transfers between devices, far_swap(): return lax.ppermute(value, 'space', [(i, other(i)) for i in range(devices)])  10.4 us
    unnamed x16, local copies, waits for them, and re-layouts  3.86 us
  transfers between devices with their start and end apart: 15, of which 3 were waited for; matrix products, arithmetic and copies ran while one was open for 0% of the time, Pallas kernels for 29%

profile of v10, /device:TPU:0, one launch (start us, length us, event | category | flops | bytes accessed | tf_op | source)
XLA Modules:
  0.0 63.0 jit_solution(14741151300535767757)
XLA Ops:
  0.7 5.5 %collective-permute-start = (bf16[256,1024]{1,0:T(8,128)(2,1)}, bf16[256,1024]{1,0:T(8,128)(2,1)}, u32[]{:S(2)}, u32[]{:S(2)}) collective-permute-start(bf16[256,1024]{1,0:T(8,128)(2,1)} %x.3), channel_id=1, source_target_pairs={{0,15},{1,2},{2,1},{3,4},{4,3},{5,6},{6,5},{7,8},{8,7},{9,10},{10,... | collective-permute-start | bytes 1572872 | tf_op jit(solution)/shard_map/ppermute | solution.py:297
  6.2 0.5 collective-permute-start.5
  6.7 0.1 pad_add_fusion.1.place
  6.8 1.0 %copy-done.2 = bf16[256,1024]{1,0:T(8,128)(2,1)S(1)} copy-done((bf16[256,1024]{1,0:T(8,128)(2,1)S(1)}, bf16[256,1024]{1,0:T(8,128)(2,1)}, u32[]{:S(2)}) %copy-start.2) | copy-done | bytes 524312
  7.8 0.7 %copy-done.4 = bf16[7,16,16]{2,1,0:T(8,128)(2,1)S(1)} copy-done((bf16[7,16,16]{2,1,0:T(8,128)(2,1)S(1)}, bf16[7,16,16]{2,1,0:T(8,128)(2,1)}, u32[]{:S(2)}) %copy-start.4) | copy-done | bytes 3608
  8.6 0.7 %copy-done.5 = s32[256,7]{0,1:T(8,128)S(1)} copy-done((s32[256,7]{0,1:T(8,128)S(1)}, s32[256,7]{0,1:T(8,128)}, u32[]{:S(2)}) %copy-start.5) | copy-done | bytes 7192
  9.3 0.7 %copy-done.6 = s32[256]{0:T(256)S(1)} copy-done((s32[256]{0:T(256)S(1)}, s32[256]{0:T(256)}, u32[]{:S(2)}) %copy-start.6) | copy-done | bytes 1048
  9.9 0.7 %copy-done.7 = s32[256]{0:T(256)S(1)} copy-done((s32[256]{0:T(256)S(1)}, s32[256]{0:T(256)}, u32[]{:S(2)}) %copy-start.7) | copy-done | bytes 1048
  10.6 3.5 %shard_map.95 = (bf16[1536,512]{1,0:T(8,128)(2,1)S(1)}, s32[8,256]{1,0:T(8,128)S(1)}, bf16[1536,1024]{1,0:T(8,128)(2,1)S(1)}, bf16[1792,256]{1,0:T(8,128)(2,1)S(1)}) custom-call(s32[4]{0:T(128)S(1)} %pad_add_fusion.1.place, s32[7,256]{1,0:T(8,128)S(1)} %bitcast.10, s32[1,256]{1,0:T(1,128)S(1)} %bitcast.11, s32[1,256]{1,0:T(1,128)S(1)} %bitcast.12, ...), custom_call_target="tpu_custom_call" | custom-call | flops 1073741824 | bytes 8388608 | tf_op jit(solution)/shard_map/pallas_call | solution.py:41
  14.2 0.8 %shard_map.98.back_sel = bf16[512,1536]{1,0:T(8,128)(2,1)S(1)} custom-call(s32[4]{0:T(128)S(1)} %pad_add_fusion.1.place, s32[8,256]{1,0:T(8,128)S(1)} %get-tuple-element.36.sources), custom_call_target="tpu_custom_call" | custom-call | flops 67108864 | bytes 8388608 | tf_op jit(solution)/shard_map/pallas_call | solution.py:41
  15.0 0.7 %shard_map.94.up = f32[256,1024]{1,0:T(8,128)S(1)} custom-call(bf16[256,1024]{1,0:T(8,128)(2,1)S(1)} %copy-done, bf16[1024,1024]{1,0:T(8,128)(2,1)S(1)} %copy-done.1), custom_call_target="tpu_custom_call" | custom-call | flops 536870912 | bytes 8388608 | tf_op jit(solution)/shard_map/pallas_call | solution.py:41
  15.8 0.1 pad_add_fusion.me
  15.8 4.3 %shard_map.96 = (bf16[1536,1024]{1,0:T(8,128)(2,1)S(1)}, f32[256,1024]{1,0:T(8,128)S(1)}, bf16[512,256]{1,0:T(8,128)(2,1)S(1)}, bf16[512,256]{1,0:T(8,128)(2,1)S(1)}) custom-call(s32[4]{0:T(128)S(1)} %pad_add_fusion.me, bf16[256,1024]{1,0:T(8,128)(2,1)} %collective-permute-done.far, bf16[256,1024]{1,0:T(8,128)(2,1)} %collective-permute-done.1.near, ...), custom_call_target="tpu_custom_call" | custom-call | flops 3221225472 | bytes 8388608 | tf_op jit(solution)/shard_map/pallas_call | solution.py:41
  20.2 0.8 %collective-permute-start.4 = (bf16[512,256]{1,0:T(8,128)(2,1)S(1)}, bf16[512,256]{1,0:T(8,128)(2,1)S(1)}, u32[]{:S(2)}, u32[]{:S(2)}) collective-permute-start(bf16[512,256]{1,0:T(8,128)(2,1)S(1)} %get-tuple-element.41), channel_id=1, source_target_pairs={{0,1},{1,0},{2,3},{3,2},{4,5},{5,4},{6,7},{7,6},{8,9},{9,8},{10,11... | collective-permute-start | bytes 786440 | tf_op jit(solution)/shard_map/ppermute | solution.py:300
  21.0 2.0 %shard_map.97 = (bf16[256,1024]{1,0:T(8,128)(2,1)S(1)}, f32[16,128]{1,0:T(8,128)S(1)}) custom-call(f32[256,1024]{1,0:T(8,128)S(1)} %shard_map.94.up, f32[256,1024]{1,0:T(8,128)S(1)} %get-tuple-element.33.pre, bf16[256,1024]{1,0:T(8,128)(2,1)S(1)} %copy-done.3, bf16[1536,1024]{1,0:T(8,128)(2,1)S(1)} %get-tuple-element.34.rows), custom_call_target="tpu_custom_call" | custom-call | flops 2147483648 | bytes 8388608 | tf_op jit(solution)/shard_map/pallas_call | solution.py:41
  23.1 2.7 %shard_map.99 = (bf16[1536,1024]{1,0:T(8,128)(2,1)S(1)}, bf16[256,1024]{1,0:T(8,128)(2,1)S(1)}, bf16[256,1024]{1,0:T(8,128)(2,1)S(1)}) custom-call(bf16[256,1024]{1,0:T(8,128)(2,1)S(1)} %get-tuple-element.35.grad, bf16[1792,256]{1,0:T(8,128)(2,1)S(1)} %get-tuple-element.32.wk, bf16[512,1536]{1,0:T(8,128)(2,1)S(1)} %shard_map.98.back_sel), custom_call_target="tpu_custom_call" | custom-call | flops 3221225472 | bytes 8388608 | tf_op jit(solution)/shard_map/pallas_call | solution.py:41
  25.8 4.8 %collective-permute-start.2 = (bf16[256,1024]{1,0:T(8,128)(2,1)S(1)}, bf16[256,1024]{1,0:T(8,128)(2,1)S(1)}, u32[]{:S(2)}, u32[]{:S(2)}) collective-permute-start(bf16[256,1024]{1,0:T(8,128)(2,1)S(1)} %get-tuple-element.38), channel_id=1, source_target_pairs={{0,15},{1,2},{2,1},{3,4},{4,3},{5,6},{6,5},{7,8},{8,7},{9,10},{10,... | collective-permute-start | bytes 1572872 | tf_op jit(solution)/shard_map/ppermute | solution.py:297
  30.7 1.3 %shard_map.102 = (bf16[256,512]{1,0:T(8,128)(2,1)S(1)}, f32[256,512]{1,0:T(8,128)S(1)}, bf16[256,512]{1,0:T(8,128)(2,1)S(1)}, f32[256,512]{1,0:T(8,128)S(1)}) custom-call(s32[4]{0:T(128)S(1)} %pad_add_fusion.me, bf16[512,256]{1,0:T(8,128)(2,1)S(1)} %get-tuple-element.40.act, bf16[512,256]{1,0:T(8,128)(2,1)S(1)} %collective-permute-done.4.act_got, ...), custom_call_target="tpu_custom_call" | custom-call | flops 1073741824 | bytes 8388608 | tf_op jit(solution)/shard_map/pallas_call | solution.py:41
  31.9 0.1 collective-permute-start.6
  32.1 0.6 collective-permute-start.8
  32.6 0.8 %collective-permute-done.8 = f32[16,128]{1,0:T(8,128)S(1)} collective-permute-done((f32[16,128]{1,0:T(8,128)S(1)}, f32[16,128]{1,0:T(8,128)S(1)}, u32[]{:S(2)}, u32[]{:S(2)}) %collective-permute-start.8) | collective-permute-done | bytes 8224 | tf_op jit(solution)/shard_map/ppermute | solution.py:300
  33.5 1.7 %collective-permute-start.9 = (f32[16,128]{1,0:T(8,128)S(1)}, f32[16,128]{1,0:T(8,128)S(1)}, u32[]{:S(2)}, u32[]{:S(2)}) collective-permute-start(f32[16,128]{1,0:T(8,128)S(1)} %add.3.refs_4_), channel_id=1, source_target_pairs={{0,2},{1,3},{2,0},{3,1},{4,6},{5,7},{6,4},{7,5},{8,10},{9,11},{10,... | collective-permute-start | bytes 24584 | tf_op jit(solution)/shard_map/ppermute | solution.py:300
  35.2 10.9 %collective-permute-done.9.refs_5_ = f32[16,128]{1,0:T(8,128)S(1)} collective-permute-done((f32[16,128]{1,0:T(8,128)S(1)}, f32[16,128]{1,0:T(8,128)S(1)}, u32[]{:S(2)}, u32[]{:S(2)}) %collective-permute-start.9) | collective-permute-done | bytes 8224 | tf_op jit(solution)/shard_map/ppermute | solution.py:300
  46.1 0.7 %shard_map.103 = (bf16[80,512]{1,0:T(8,128)(2,1)S(1)}, bf16[144,512]{1,0:T(8,128)(2,1)S(1)}, bf16[80,512]{1,0:T(8,128)(2,1)S(1)}, f32[64,512]{1,0:T(8,128)S(1)},...) custom-call(s32[4]{0:T(128)S(1)} %pad_add_fusion.me, ...), custom_call_target="tpu_custom_call" | custom-call | flops 1048576 | bytes 8388608 | tf_op jit(solution)/shard_map/pallas_call | solution.py:41
  46.8 2.7 %collective-permute-start.11 = (bf16[144,512]{1,0:T(8,128)(2,1)S(1)}, bf16[144,512]{1,0:T(8,128)(2,1)S(1)}, u32[]{:S(2)}, u32[]{:S(2)}) collective-permute-start(bf16[144,512]{1,0:T(8,128)(2,1)S(1)} %get-tuple-element.49), channel_id=1, source_target_pairs={{0,8},{1,9},{2,10},{3,11},{4,12},{5,13},{6,14},{7,15},{8,0},{9,1},... | collective-permute-start | bytes 442376 | tf_op jit(solution)/shard_map/ppermute | solution.py:300
  49.4 1.6 %collective-permute-start.10 = (bf16[80,512]{1,0:T(8,128)(2,1)S(1)}, bf16[80,512]{1,0:T(8,128)(2,1)S(1)}, u32[]{:S(2)}, u32[]{:S(2)}) collective-permute-start(bf16[80,512]{1,0:T(8,128)(2,1)S(1)} %get-tuple-element.48), channel_id=1, source_target_pairs={{0,4},{1,5},{2,6},{3,7},{4,0},{5,1},{6,2},{7,3},{8,12},{9,13},{10,... | collective-permute-start | bytes 245768 | tf_op jit(solution)/shard_map/ppermute | solution.py:300
  51.0 0.2 collective-permute-start.12
  51.2 3.2 %collective-permute-start.14 = (bf16[64,512]{1,0:T(8,128)(2,1)S(1)}, bf16[64,512]{1,0:T(8,128)(2,1)S(1)}, u32[]{:S(2)}, u32[]{:S(2)}) collective-permute-start(bf16[64,512]{1,0:T(8,128)(2,1)S(1)} %get-tuple-element.53), channel_id=1, source_target_pairs={{0,10},{1,11},{2,8},{3,9},{4,14},{5,15},{6,12},{7,13},{8,2},{9,3},... | collective-permute-start | bytes 196616 | tf_op jit(solution)/shard_map/ppermute | solution.py:300
  54.4 1.1 %shard_map.100.inner = f32[256,1024]{1,0:T(8,128)S(1)} custom-call(bf16[256,1024]{1,0:T(8,128)(2,1)S(1)} %get-tuple-element.35.grad, bf16[1536,1024]{1,0:T(8,128)(2,1)S(1)} %get-tuple-element.37.terms, bf16[1792,256]{1,0:T(8,128)(2,1)S(1)} %get-tuple-element.32.wk, s32[8,256]{1,0:T(8,128)S(1)} %get-tuple-element.36.sources, bf16[256,1024]{1,0:T(8,128)(2,1)S(1)} %copy-done), custom_call_target="tpu_custom_call" | custom-call | flops 1073741824 | bytes 8388608 | tf_op jit(solution)/shard_map/pallas_call | solution.py:41
  55.5 1.0 %shard_map.101 = bf16[256,1024]{1,0:T(8,128)(2,1)} custom-call(f32[256,1024]{1,0:T(8,128)S(1)} %shard_map.100.inner, bf16[256,1024]{1,0:T(8,128)(2,1)S(1)} %collective-permute-done.2.first, bf16[256,1024]{1,0:T(8,128)(2,1)S(1)} %collective-permute-done.3.second), custom_call_target="tpu_custom_call" | custom-call | flops 1048576 | bytes 8388608 | tf_op jit(solution)/shard_map/pallas_call | solution.py:41
  56.5 5.7 %collective-permute-done.14.three_b = bf16[64,512]{1,0:T(8,128)(2,1)S(1)} collective-permute-done((bf16[64,512]{1,0:T(8,128)(2,1)S(1)}, bf16[64,512]{1,0:T(8,128)(2,1)S(1)}, u32[]{:S(2)}, u32[]{:S(2)}) %collective-permute-start.14) | collective-permute-done | bytes 65568 | tf_op jit(solution)/shard_map/ppermute | solution.py:300
  62.2 0.8 %shard_map.104 = (f32[64,1024]{1,0:T(8,128)}, f32[7,16,16]{2,1,0:T(8,128)}) custom-call(f32[64,512]{1,0:T(8,128)S(1)} %get-tuple-element.47.kept_a, bf16[80,512]{1,0:T(8,128)(2,1)S(1)} %collective-permute-done.10.one, bf16[144,512]{1,0:T(8,128)(2,1)S(1)} %collective-permute-done.11.shared, bf16[80,512]{1,0:T(8,128)(2,1)S(1)} %collective-permute-done.12.three, ...), custom_call_target="tpu_custom_call" | custom-call | flops 1048576 | bytes 8388608 | tf_op jit(solution)/shard_map/pallas_call | solution.py:41
  (28 shorter events, 0.1 us)
Async XLA Ops:
  0.6 14.4 %copy-start = (bf16[256,1024]{1,0:T(8,128)(2,1)S(1)}, bf16[256,1024]{1,0:T(8,128)(2,1)}, u32[]{:S(2)}) copy-start(bf16[256,1024]{1,0:T(8,128)(2,1)} %cot.5) | copy-start | bytes 1572868
  0.6 14.4 %copy-start.1 = (bf16[1024,1024]{1,0:T(8,128)(2,1)S(1)}, bf16[1024,1024]{1,0:T(8,128)(2,1)}, u32[]{:S(2)}) copy-start(bf16[1024,1024]{1,0:T(8,128)(2,1)} %mix.1) | copy-start | bytes 6291460
  0.7 15.2 %collective-permute-start = (bf16[256,1024]{1,0:T(8,128)(2,1)}, bf16[256,1024]{1,0:T(8,128)(2,1)}, u32[]{:S(2)}, u32[]{:S(2)}) collective-permute-start(bf16[256,1024]{1,0:T(8,128)(2,1)} %x.3), channel_id=1, source_target_pairs={{0,15},{1,2},{2,1},{3,4},{4,3},{5,6},{6,5},{7,8},{8,7},{9,10},{10,... | collective-permute-start | bytes 1572872 | tf_op jit(solution)/shard_map/ppermute | solution.py:297
  6.2 9.7 %collective-permute-start.1 = (bf16[256,1024]{1,0:T(8,128)(2,1)}, bf16[256,1024]{1,0:T(8,128)(2,1)}, u32[]{:S(2)}, u32[]{:S(2)}) collective-permute-start(bf16[256,1024]{1,0:T(8,128)(2,1)} %x.3), channel_id=1, source_target_pairs={{0,1},{1,0},{2,3},{3,2},{4,5},{5,4},{6,7},{7,6},{8,9},{9,8},{10,11... | collective-permute-start | bytes 1572872 | tf_op jit(solution)/shard_map/ppermute | solution.py:293
  6.2 24.5 %collective-permute-start.5 = (bf16[256,1024]{1,0:T(8,128)(2,1)}, bf16[256,1024]{1,0:T(8,128)(2,1)S(1)}, u32[]{:S(2)}, u32[]{:S(2)}) collective-permute-start(bf16[256,1024]{1,0:T(8,128)(2,1)} %cot.5), channel_id=1, source_target_pairs={{0,1},{1,0},{2,3},{3,2},{4,5},{5,4},{6,7},{7,6},{8,9},{9,8},{10,11... | collective-permute-start | bytes 1572872 | tf_op jit(solution)/shard_map/ppermute | solution.py:300
  6.8 1.0 %copy-start.2 = (bf16[256,1024]{1,0:T(8,128)(2,1)S(1)}, bf16[256,1024]{1,0:T(8,128)(2,1)}, u32[]{:S(2)}) copy-start(bf16[256,1024]{1,0:T(8,128)(2,1)} %x.3) | copy-start | bytes 1572868
  7.8 0.7 %copy-start.4 = (bf16[7,16,16]{2,1,0:T(8,128)(2,1)S(1)}, bf16[7,16,16]{2,1,0:T(8,128)(2,1)}, u32[]{:S(2)}) copy-start(bf16[7,16,16]{2,1,0:T(8,128)(2,1)} %conv_hbm.1) | copy-start | bytes 10756
  8.6 0.7 %copy-start.5 = (s32[256,7]{0,1:T(8,128)S(1)}, s32[256,7]{0,1:T(8,128)}, u32[]{:S(2)}) copy-start(s32[256,7]{0,1:T(8,128)} %param.11) | copy-start | bytes 21508
  9.3 0.7 %copy-start.6 = (s32[256]{0:T(256)S(1)}, s32[256]{0:T(256)}, u32[]{:S(2)}) copy-start(s32[256]{0:T(256)} %param.12) | copy-start | bytes 3076
  9.9 0.7 %copy-start.7 = (s32[256]{0:T(256)S(1)}, s32[256]{0:T(256)}, u32[]{:S(2)}) copy-start(s32[256]{0:T(256)} %param.13) | copy-start | bytes 3076
  14.2 1.7 %copy-start.3 = (bf16[256,1024]{1,0:T(8,128)(2,1)S(1)}, bf16[256,1024]{1,0:T(8,128)(2,1)}, u32[]{:S(2)}) copy-start(bf16[256,1024]{1,0:T(8,128)(2,1)} %x.3) | copy-start | bytes 1572868
  20.2 10.5 %collective-permute-start.4 = (bf16[512,256]{1,0:T(8,128)(2,1)S(1)}, bf16[512,256]{1,0:T(8,128)(2,1)S(1)}, u32[]{:S(2)}, u32[]{:S(2)}) collective-permute-start(bf16[512,256]{1,0:T(8,128)(2,1)S(1)} %get-tuple-element.41), channel_id=1, source_target_pairs={{0,1},{1,0},{2,3},{3,2},{4,5},{5,4},{6,7},{7,6},{8,9},{9,8},{10,11... | collective-permute-start | bytes 786440 | tf_op jit(solution)/shard_map/ppermute | solution.py:300
  25.8 25.4 %collective-permute-start.2 = (bf16[256,1024]{1,0:T(8,128)(2,1)S(1)}, bf16[256,1024]{1,0:T(8,128)(2,1)S(1)}, u32[]{:S(2)}, u32[]{:S(2)}) collective-permute-start(bf16[256,1024]{1,0:T(8,128)(2,1)S(1)} %get-tuple-element.38), channel_id=1, source_target_pairs={{0,15},{1,2},{2,1},{3,4},{4,3},{5,6},{6,5},{7,8},{8,7},{9,10},{10,... | collective-permute-start | bytes 1572872 | tf_op jit(solution)/shard_map/ppermute | solution.py:297
  30.6 20.6 %collective-permute-start.3 = (bf16[256,1024]{1,0:T(8,128)(2,1)S(1)}, bf16[256,1024]{1,0:T(8,128)(2,1)S(1)}, u32[]{:S(2)}, u32[]{:S(2)}) collective-permute-start(bf16[256,1024]{1,0:T(8,128)(2,1)S(1)} %get-tuple-element.39), channel_id=1, source_target_pairs={{0,1},{1,0},{2,3},{3,2},{4,5},{5,4},{6,7},{7,6},{8,9},{9,8},{10,11... | collective-permute-start | bytes 1572872 | tf_op jit(solution)/shard_map/ppermute | solution.py:293
  31.9 14.2 %collective-permute-start.6 = (bf16[256,512]{1,0:T(8,128)(2,1)S(1)}, bf16[256,512]{1,0:T(8,128)(2,1)S(1)}, u32[]{:S(2)}, u32[]{:S(2)}) collective-permute-start(bf16[256,512]{1,0:T(8,128)(2,1)S(1)} %get-tuple-element.43), channel_id=1, source_target_pairs={{0,2},{1,3},{2,0},{3,1},{4,6},{5,7},{6,4},{7,5},{8,10},{9,11},{10,... | collective-permute-start | bytes 786440 | tf_op jit(solution)/shard_map/ppermute | solution.py:300
  32.0 14.1 %collective-permute-start.7 = (bf16[256,512]{1,0:T(8,128)(2,1)S(1)}, bf16[256,512]{1,0:T(8,128)(2,1)S(1)}, u32[]{:S(2)}, u32[]{:S(2)}) collective-permute-start(bf16[256,512]{1,0:T(8,128)(2,1)S(1)} %get-tuple-element.45), channel_id=1, source_target_pairs={{0,4},{1,5},{2,6},{3,7},{4,0},{5,1},{6,2},{7,3},{8,12},{9,13},{10,... | collective-permute-start | bytes 786440 | tf_op jit(solution)/shard_map/ppermute | solution.py:300
  32.1 1.4 %collective-permute-start.8 = (f32[16,128]{1,0:T(8,128)S(1)}, f32[16,128]{1,0:T(8,128)S(1)}, u32[]{:S(2)}, u32[]{:S(2)}) collective-permute-start(f32[16,128]{1,0:T(8,128)S(1)} %get-tuple-element.46), channel_id=1, source_target_pairs={{0,1},{1,0},{2,3},{3,2},{4,5},{5,4},{6,7},{7,6},{8,9},{9,8},{10,11... | collective-permute-start | bytes 24584 | tf_op jit(solution)/shard_map/ppermute | solution.py:300
  33.5 12.6 %collective-permute-start.9 = (f32[16,128]{1,0:T(8,128)S(1)}, f32[16,128]{1,0:T(8,128)S(1)}, u32[]{:S(2)}, u32[]{:S(2)}) collective-permute-start(f32[16,128]{1,0:T(8,128)S(1)} %add.3.refs_4_), channel_id=1, source_target_pairs={{0,2},{1,3},{2,0},{3,1},{4,6},{5,7},{6,4},{7,5},{8,10},{9,11},{10,... | collective-permute-start | bytes 24584 | tf_op jit(solution)/shard_map/ppermute | solution.py:300
  46.8 15.4 %collective-permute-start.11 = (bf16[144,512]{1,0:T(8,128)(2,1)S(1)}, bf16[144,512]{1,0:T(8,128)(2,1)S(1)}, u32[]{:S(2)}, u32[]{:S(2)}) collective-permute-start(bf16[144,512]{1,0:T(8,128)(2,1)S(1)} %get-tuple-element.49), channel_id=1, source_target_pairs={{0,8},{1,9},{2,10},{3,11},{4,12},{5,13},{6,14},{7,15},{8,0},{9,1},... | collective-permute-start | bytes 442376 | tf_op jit(solution)/shard_map/ppermute | solution.py:300
  49.4 12.7 %collective-permute-start.10 = (bf16[80,512]{1,0:T(8,128)(2,1)S(1)}, bf16[80,512]{1,0:T(8,128)(2,1)S(1)}, u32[]{:S(2)}, u32[]{:S(2)}) collective-permute-start(bf16[80,512]{1,0:T(8,128)(2,1)S(1)} %get-tuple-element.48), channel_id=1, source_target_pairs={{0,4},{1,5},{2,6},{3,7},{4,0},{5,1},{6,2},{7,3},{8,12},{9,13},{10,... | collective-permute-start | bytes 245768 | tf_op jit(solution)/shard_map/ppermute | solution.py:300
  51.0 11.2 %collective-permute-start.12 = (bf16[80,512]{1,0:T(8,128)(2,1)S(1)}, bf16[80,512]{1,0:T(8,128)(2,1)S(1)}, u32[]{:S(2)}, u32[]{:S(2)}) collective-permute-start(bf16[80,512]{1,0:T(8,128)(2,1)S(1)} %get-tuple-element.50), channel_id=1, source_target_pairs={{0,12},{1,13},{2,14},{3,15},{4,8},{5,9},{6,10},{7,11},{8,4},{9,5},... | collective-permute-start | bytes 245768 | tf_op jit(solution)/shard_map/ppermute | solution.py:300
  51.2 5.3 %collective-permute-start.13 = (bf16[64,512]{1,0:T(8,128)(2,1)S(1)}, bf16[64,512]{1,0:T(8,128)(2,1)S(1)}, u32[]{:S(2)}, u32[]{:S(2)}) collective-permute-start(bf16[64,512]{1,0:T(8,128)(2,1)S(1)} %get-tuple-element.52), channel_id=1, source_target_pairs={{0,2},{1,3},{2,0},{3,1},{4,6},{5,7},{6,4},{7,5},{8,10},{9,11},{10,... | collective-permute-start | bytes 196616 | tf_op jit(solution)/shard_map/ppermute | solution.py:300
  51.2 10.9 %collective-permute-start.14 = (bf16[64,512]{1,0:T(8,128)(2,1)S(1)}, bf16[64,512]{1,0:T(8,128)(2,1)S(1)}, u32[]{:S(2)}, u32[]{:S(2)}) collective-permute-start(bf16[64,512]{1,0:T(8,128)(2,1)S(1)} %get-tuple-element.53), channel_id=1, source_target_pairs={{0,10},{1,11},{2,8},{3,9},{4,14},{5,15},{6,12},{7,13},{8,2},{9,3},... | collective-permute-start | bytes 196616 | tf_op jit(solution)/shard_map/ppermute | solution.py:300
